TPU v7x, 128 devices: a whole 4x4x4 slice. The times are simulated.
128 devices in a mesh: cent: 4 (over y), rows: 32 (over z, x, core).
Axes of the slice: x: 4, y: 4, z: 4, core: 2. Of those that a mesh axis runs over, the one named last changes fastest.
Arguments:
- embeddings: bfloat16 [32768, 2048], P(('cent', 'rows')), may hold values from -6 to 6
- centroids: bfloat16 [16384, 2048], P(('cent', 'rows')), may hold values from -0.125 to 0.125
- cluster: int32 [32768, 1], P(('cent', 'rows')), may hold values from 0 to 127; in each aligned block of 256 rows (0 to 255, 256 to 511, ...) at most 4 rows name the same one
- noise_salt: int32 [1], replicated, may hold values from 0 to 1048575
Outputs:
- perturbed_max: float32 [32768], P(('cent', 'rows'))
- dedup_score: float32 [32768], P(('cent', 'rows'))
- new_centroids: float32 [128, 2048], P(('cent', 'rows'))
Inputs may be any that keep to these rules, and one draw needn't show every extreme that they name: In every aligned block of 256 rows (the rows of one device) no cluster is named by more than 4 rows, and in some block some cluster by exactly 4; every cluster is named by some row.
All inputs are finite; a program needn't handle non-finite values.
Results may differ from a plain program's by a relative error of at most 0.0003.
Values may be sent and summed in bfloat16 or wider, within the bound.
A program may use at most 128 MiB of HBM per device.

v0:
```python
import math

import jax
import jax.numpy as jnp
from jax import lax
from jax.sharding import PartitionSpec as P

inverse_temp = 3.0
epsilon = 1e-06


def logical_shift(word, amount):
    return lax.shift_right_logical(word, jnp.full(word.shape, amount, jnp.int32))


def gumbel_noise(row_ids, cent_ids, salt_word):
    mixed = row_ids * 1103515245 + cent_ids * 739982445 + salt_word
    mixed = mixed ^ logical_shift(mixed, 16)
    mixed = mixed * 2146121005
    mixed = mixed ^ logical_shift(mixed, 15)
    mixed = mixed * 1759714725
    mixed = mixed ^ logical_shift(mixed, 16)
    low_bits = mixed & 8388607
    uniform = (low_bits.astype(jnp.float32) + 0.5) * (1.0 / 8388608.0)
    return -jnp.log(-jnp.log(uniform))


def cluster_stats(members, valid):
    feature_dim = members.shape[1]
    widened = members.astype(jnp.float32)
    scale = lax.rsqrt(jnp.mean(widened * widened, axis=1) + epsilon)
    gram = lax.dot_general(
        members, members, (((1,), (1,)), ((), ())), preferred_element_type=jnp.float32
    )
    similar = gram * scale[:, None] * scale[None, :] * (1.0 / math.sqrt(feature_dim))
    order = jnp.arange(members.shape[0], dtype=jnp.int32)
    usable = valid[None, :] & (order[:, None] != order[None, :])
    highest = jnp.max(jnp.where(usable, similar, -1e30), axis=1)
    scores = jnp.where(jnp.any(usable, axis=1), highest, 0.0)
    total = jnp.sum(jnp.where(valid[:, None], widened, 0.0), axis=0)
    center = total * lax.rsqrt(jnp.mean(total * total) + epsilon)
    return (scores, center)


def shards(embeddings, centroids, cluster, noise_salt):
    rows_dev, feature_dim = embeddings.shape
    cent_dev = centroids.shape[0]
    cent_count = lax.axis_size("cent")
    rows_count = lax.axis_size("rows")
    devices = cent_count * rows_count
    capacity = max(2, 2 * rows_dev // devices)
    cent_index = lax.axis_index("cent")
    rows_index = lax.axis_index("rows")
    salt_word = noise_salt[0]
    group = lax.all_gather(embeddings, "cent", axis=0, tiled=True)
    position = jnp.arange(cent_count * rows_dev, dtype=jnp.int32)
    group_ids = (position // rows_dev * rows_count + rows_index) * rows_dev + position % rows_dev
    panel_base = cent_index * (rows_count * cent_dev)
    initial = jnp.full((cent_count * rows_dev,), -1e30, jnp.float32)
    piece = lax.all_gather(centroids, "rows", axis=0, tiled=True)
    piece_rows = piece.shape[0]
    block = math.gcd(piece_rows, 512)
    tiles = piece.reshape(piece_rows // block, block, feature_dim)
    offsets = jnp.arange(piece_rows // block, dtype=jnp.int32) * block

    def step(carry, item):
        tile, offset = item
        scores = lax.dot_general(
            group, tile, (((1,), (1,)), ((), ())), preferred_element_type=jnp.float32
        )
        cent_ids = panel_base + offset + jnp.arange(block, dtype=jnp.int32)
        perturbed = inverse_temp * scores + gumbel_noise(
            group_ids[:, None], cent_ids[None, :], salt_word
        )
        return (jnp.maximum(carry, jnp.max(perturbed, axis=1)), None)

    result, unused = lax.scan(step, initial, (tiles, offsets))
    merged = lax.pmax(result, "cent")
    perturbed_max = lax.dynamic_slice_in_dim(merged, cent_index * rows_dev, rows_dev)
    assigned = cluster[:, 0]
    order = jnp.arange(rows_dev, dtype=jnp.int32)
    same = (assigned[:, None] == assigned[None, :]) & (order[None, :] < order[:, None])
    rank = jnp.sum(same.astype(jnp.int32), axis=1)
    slot = assigned * capacity + rank
    outgoing = jnp.zeros((devices * capacity, feature_dim), jnp.bfloat16).at[slot].set(embeddings)
    present = (
        jnp.zeros((devices * capacity,), jnp.bfloat16)
        .at[slot]
        .set(jnp.ones((rows_dev,), jnp.bfloat16))
    )
    received, arrived = (
        lax.all_to_all(
            outgoing.reshape(devices, capacity, feature_dim),
            ("cent", "rows"),
            split_axis=0,
            concat_axis=0,
            tiled=True,
        ),
        lax.all_to_all(
            present.reshape(devices, capacity),
            ("cent", "rows"),
            split_axis=0,
            concat_axis=0,
            tiled=True,
        ),
    )
    members = received.reshape(devices * capacity, feature_dim)
    valid = arrived.reshape(devices * capacity) > 0.5
    scores, center = cluster_stats(members, valid)
    returned = lax.all_to_all(
        scores.reshape(devices, capacity), ("cent", "rows"), split_axis=0, concat_axis=0, tiled=True
    )
    dedup_score = returned.reshape(devices * capacity)[slot]
    return (perturbed_max, dedup_score, center[None, :])


def solution(mesh):
    in_specs = (
        P(("cent", "rows"), None),
        P(("cent", "rows"), None),
        P(("cent", "rows"), None),
        P(),
    )
    out_specs = (P(("cent", "rows")), P(("cent", "rows")), P(("cent", "rows"), None))
    return jax.shard_map(shards, mesh=mesh, in_specs=in_specs, out_specs=out_specs, check_vma=False)
```

profile of v0, /device:TPU:1, one launch (start us, length us, event | category | flops | bytes accessed | tf_op | source)
XLA Modules:
  0.0 241.7 jit_solution(4939791693935059020)
XLA Ops:
  7.2 0.0 all-gather.5.cloned.1.call-start
  7.2 0.7 all-gather.5.cloned.1.call-update
  7.9 0.0 all-gather.3.cloned.1.call-start
  7.9 0.7 all-gather.3.cloned.1.call-update
  8.6 0.9 convert_reduce_fusion
  9.6 0.7 compare_select_fusion
  10.3 2.2 scatter_custom_fusion
  12.4 0.8 all_to_all.17
  13.2 11.5 %all-to-all-start = ((bf16[128,1,4]{2,1,0:T(2,128)(2,1)}), bf16[128,1,4]{2,1,0:T(2,128)(2,1)S(1)}, u32[]{:S(2)}, u32[]{:S(2)}) async-start(bf16[128,1,4]{2,1,0:T(2,128)(2,1)} %all_to_all.17), calls=%async_computation | async-start | bytes 131072 | tf_op jit(solution)/shard_map/all_to_all | solution.py:99
  24.7 3.6 %scatter_custom_fusion.1 = bf16[512,2048]{1,0:T(8,128)(2,1)S(1)} fusion(s32[256]{0:T(256)S(1)} %bitcast.32, bf16[256,2048]{1,0:T(8,128)(2,1)} %param.6, bf16[]{:T(256)} %constant.99.clone.1), kind=kCustom, calls=%fused_computation.50 | custom fusion | bytes 2097664 | tf_op jit(solution)/shard_map/scatter | solution.py:85
  28.3 2.2 reshape.113
  30.5 3.7 %all-to-all-done = bf16[128,1,4]{2,1,0:T(2,128)(2,1)S(1)} async-done(((bf16[128,1,4]{2,1,0:T(2,128)(2,1)}), bf16[128,1,4]{2,1,0:T(2,128)(2,1)S(1)}, u32[]{:S(2)}, u32[]{:S(2)}) %all-to-all-start) | async-done | bytes 1056 | tf_op jit(solution)/shard_map/all_to_all | solution.py:99
  34.2 6.1 %all-to-all-start.1 = ((bf16[128,4,2048]{2,1,0:T(4,128)(2,1)}), bf16[128,4,2048]{2,1,0:T(4,128)(2,1)S(1)}, u32[]{:S(2)}, u32[]{:S(2)}) async-start(bf16[128,4,2048]{2,1,0:T(4,128)(2,1)} %reshape.113), calls=%async_computation.1 | async-start | bytes 4194304 | tf_op jit(solution)/shard_map/all_to_all | solution.py:92
  40.3 0.3 broadcast_compare_fusion
  40.6 0.1 gt.22
  40.7 0.1 copy.15
  40.8 0.1 copy.16
  40.9 0.2 fusion.41
  41.1 33.1 %all-to-all-done.1 = bf16[128,4,2048]{2,1,0:T(4,128)(2,1)S(1)} async-done(((bf16[128,4,2048]{2,1,0:T(4,128)(2,1)}), bf16[128,4,2048]{2,1,0:T(4,128)(2,1)S(1)}, u32[]{:S(2)}, u32[]{:S(2)}) %all-to-all-start.1) | async-done | bytes 2097184 | tf_op jit(solution)/shard_map/all_to_all | solution.py:92
  74.2 2.1 fusion.33
  76.4 0.1 rsqrt.18
  76.5 2.1 reshape.114
  78.6 3.6 %fusion.37 = f32[512]{0:T(512)S(1)} fusion(bf16[512,2048]{1,0:T(8,128)(2,1)} %reshape.114, f32[512]{0:T(512)S(1)} %rsqrt.18, pred[512]{0:T(512)(128)(4,1)S(1)} %gt.22), kind=kOutput, calls=%fused_computation.49 | convolution fusion | flops 1075576320 | bytes 2101760 | tf_op jit(solution)/shard_map/dot_general | solution.py:32
  82.2 0.7 select_n.51
  82.9 6.0 %all-to-all-start.2 = ((f32[128,1,4]{2,1,0:T(1,128)}), f32[128,1,4]{2,1,0:T(1,128)S(1)}, u32[]{:S(2)}, u32[]{:S(2)}) async-start(f32[128,1,4]{2,1,0:T(1,128)} %bitcast.5), calls=%async_computation.2 | async-start | bytes 131072 | tf_op jit(solution)/shard_map/all_to_all | solution.py:110
  88.9 0.6 multiply_reduce_fusion
  90.2 0.6 broadcast_multiply_fusion
  90.8 7.6 %all-to-all-done.2 = f32[128,1,4]{2,1,0:T(1,128)S(1)} async-done(((f32[128,1,4]{2,1,0:T(1,128)}), f32[128,1,4]{2,1,0:T(1,128)S(1)}, u32[]{:S(2)}, u32[]{:S(2)}) %all-to-all-start.2) | async-done | bytes 2080 | tf_op jit(solution)/shard_map/all_to_all | solution.py:110
  98.4 0.5 broadcast.166
  98.9 0.8 reduce.7
  99.7 0.1 reshape.115
  99.8 2.5 %gather_fusion = f32[256]{0:T(256)} fusion(f32[512]{0:T(512)S(1)} %reshape.115, s32[1024]{0:T(1024)S(1)} %pad_clamp_fusion), kind=kCustom, calls=%fused_computation | custom fusion | bytes 3072 | tf_op jit(solution)/shard_map/gather | solution.py:113
  102.3 0.0 all-gather.5.cloned.1.call-done
  102.3 57.7 %all-gather.3.cloned.1.call-done = bf16[4096,2048]{1,0:T(8,128)(2,1)} async-done(((bf16[128,2048]{1,0:T(8,128)(2,1)}), bf16[4096,2048]{1,0:T(8,128)(2,1)}) %all-gather.3.cloned.1.call-update) | async-done | bytes 16777232 | tf_op jit(solution)/shard_map/all_gather | solution.py:60
  160.0 65.8 %while.11 = (s32[]{:T(128)}, f32[1024]{0:T(1024)S(1)}, bf16[8,512,2048]{2,1,0:T(8,128)(2,1)}, bf16[1024,2048]{1,0:T(8,128)(2,1)}, s32[8]{0:T(128)S(1)}, /*index=...) while((s32[]{:T(128)}, f32[1024]{0:T(1024)S(1)}, bf16[8,512,2048]{2,1,0:T(8,128)(2,1)}, ...), condition=%wide.region_2.3_spmd.clone, body=%wide.region_0.2_spmd.clone.sunk | while | flops 2157464576 | bytes 6320795 | solution.py:77
  160.0 0.6 dynamic_slice.23
  161.3 6.9 %fusion.56 = f32[1024]{0:T(1024)S(1)} fusion(bf16[1024,2048]{1,0:T(8,128)(2,1)} %get-tuple-element.168, bf16[8,512,2048]{2,1,0:T(8,128)(2,1)} %get-tuple-element.167, s32[]{:T(128)S(6)} %copy.19, s32[]{:T(128)} %get-tuple-element.171, s32[512]{0:T(512)S(1)} %add_multiply_fusion.2, s32[1024]{0:T(1024)S(1)} %fusion.55), kind=kOutput, calls=%fused_computation.21.clone.1 | convolution fusion | flops 2157444096 | bytes 6302212 | tf_op jit(solution)/shard_map/while/body/eval_jaxpr/dot_general | solution.py:68
  168.2 0.6 dynamic_slice.23
  169.5 6.9 %fusion.56 = f32[1024]{0:T(1024)S(1)} fusion(bf16[1024,2048]{1,0:T(8,128)(2,1)} %get-tuple-element.168, bf16[8,512,2048]{2,1,0:T(8,128)(2,1)} %get-tuple-element.167, s32[]{:T(128)S(6)} %copy.19, s32[]{:T(128)} %get-tuple-element.171, s32[512]{0:T(512)S(1)} %add_multiply_fusion.2, s32[1024]{0:T(1024)S(1)} %fusion.55), kind=kOutput, calls=%fused_computation.21.clone.1 | convolution fusion | flops 2157444096 | bytes 6302212 | tf_op jit(solution)/shard_map/while/body/eval_jaxpr/dot_general | solution.py:68
  176.5 0.6 dynamic_slice.23
  177.7 6.9 %fusion.56 = f32[1024]{0:T(1024)S(1)} fusion(bf16[1024,2048]{1,0:T(8,128)(2,1)} %get-tuple-element.168, bf16[8,512,2048]{2,1,0:T(8,128)(2,1)} %get-tuple-element.167, s32[]{:T(128)S(6)} %copy.19, s32[]{:T(128)} %get-tuple-element.171, s32[512]{0:T(512)S(1)} %add_multiply_fusion.2, s32[1024]{0:T(1024)S(1)} %fusion.55), kind=kOutput, calls=%fused_computation.21.clone.1 | convolution fusion | flops 2157444096 | bytes 6302212 | tf_op jit(solution)/shard_map/while/body/eval_jaxpr/dot_general | solution.py:68
  184.7 0.6 dynamic_slice.23
  185.9 6.9 %fusion.56 = f32[1024]{0:T(1024)S(1)} fusion(bf16[1024,2048]{1,0:T(8,128)(2,1)} %get-tuple-element.168, bf16[8,512,2048]{2,1,0:T(8,128)(2,1)} %get-tuple-element.167, s32[]{:T(128)S(6)} %copy.19, s32[]{:T(128)} %get-tuple-element.171, s32[512]{0:T(512)S(1)} %add_multiply_fusion.2, s32[1024]{0:T(1024)S(1)} %fusion.55), kind=kOutput, calls=%fused_computation.21.clone.1 | convolution fusion | flops 2157444096 | bytes 6302212 | tf_op jit(solution)/shard_map/while/body/eval_jaxpr/dot_general | solution.py:68
  192.9 0.6 dynamic_slice.23
  194.2 6.9 %fusion.56 = f32[1024]{0:T(1024)S(1)} fusion(bf16[1024,2048]{1,0:T(8,128)(2,1)} %get-tuple-element.168, bf16[8,512,2048]{2,1,0:T(8,128)(2,1)} %get-tuple-element.167, s32[]{:T(128)S(6)} %copy.19, s32[]{:T(128)} %get-tuple-element.171, s32[512]{0:T(512)S(1)} %add_multiply_fusion.2, s32[1024]{0:T(1024)S(1)} %fusion.55), kind=kOutput, calls=%fused_computation.21.clone.1 | convolution fusion | flops 2157444096 | bytes 6302212 | tf_op jit(solution)/shard_map/while/body/eval_jaxpr/dot_general | solution.py:68
  201.1 0.6 dynamic_slice.23
  202.4 6.9 %fusion.56 = f32[1024]{0:T(1024)S(1)} fusion(bf16[1024,2048]{1,0:T(8,128)(2,1)} %get-tuple-element.168, bf16[8,512,2048]{2,1,0:T(8,128)(2,1)} %get-tuple-element.167, s32[]{:T(128)S(6)} %copy.19, s32[]{:T(128)} %get-tuple-element.171, s32[512]{0:T(512)S(1)} %add_multiply_fusion.2, s32[1024]{0:T(1024)S(1)} %fusion.55), kind=kOutput, calls=%fused_computation.21.clone.1 | convolution fusion | flops 2157444096 | bytes 6302212 | tf_op jit(solution)/shard_map/while/body/eval_jaxpr/dot_general | solution.py:68
  209.4 0.6 dynamic_slice.23
  210.6 6.9 %fusion.56 = f32[1024]{0:T(1024)S(1)} fusion(bf16[1024,2048]{1,0:T(8,128)(2,1)} %get-tuple-element.168, bf16[8,512,2048]{2,1,0:T(8,128)(2,1)} %get-tuple-element.167, s32[]{:T(128)S(6)} %copy.19, s32[]{:T(128)} %get-tuple-element.171, s32[512]{0:T(512)S(1)} %add_multiply_fusion.2, s32[1024]{0:T(1024)S(1)} %fusion.55), kind=kOutput, calls=%fused_computation.21.clone.1 | convolution fusion | flops 2157444096 | bytes 6302212 | tf_op jit(solution)/shard_map/while/body/eval_jaxpr/dot_general | solution.py:68
  217.6 0.6 dynamic_slice.23
  218.9 6.9 %fusion.56 = f32[1024]{0:T(1024)S(1)} fusion(bf16[1024,2048]{1,0:T(8,128)(2,1)} %get-tuple-element.168, bf16[8,512,2048]{2,1,0:T(8,128)(2,1)} %get-tuple-element.167, s32[]{:T(128)S(6)} %copy.19, s32[]{:T(128)} %get-tuple-element.171, s32[512]{0:T(512)S(1)} %add_multiply_fusion.2, s32[1024]{0:T(1024)S(1)} %fusion.55), kind=kOutput, calls=%fused_computation.21.clone.1 | convolution fusion | flops 2157444096 | bytes 6302212 | tf_op jit(solution)/shard_map/while/body/eval_jaxpr/dot_general | solution.py:68
  225.8 8.5 %pmax.7 = f32[1024]{0:T(1024)S(1)} all-reduce(f32[1024]{0:T(1024)S(1)} %get-tuple-element.45), channel_id=1, replica_groups=mesh['cent'=4,'rows'=32] {'cent'}, use_global_device_ids=true, to_apply=%region_3.4 | all-reduce | flops 1024 | bytes 8192 | tf_op jit(solution)/shard_map/pmax | solution.py:78
  234.3 0.6 dynamic_slice.11
  (30 shorter events, 0.2 us)
Async XLA Ops:
  7.2 95.2 %all-gather.5.cloned.1.call-start = ((), (), s32[]{:S(2)}) async-start(), calls=%async_computation.4 | async-start | bytes 5242880 | tf_op jit(solution)/shard_map/all_gather | solution.py:55
  7.9 152.1 %all-gather.3.cloned.1.call-start = ((), (), s32[]{:S(2)}) async-start(), calls=%async_computation.3 | async-start | bytes 17301504 | tf_op jit(solution)/shard_map/all_gather | solution.py:60
  13.2 21.0 %all-to-all-start = ((bf16[128,1,4]{2,1,0:T(2,128)(2,1)}), bf16[128,1,4]{2,1,0:T(2,128)(2,1)S(1)}, u32[]{:S(2)}, u32[]{:S(2)}) async-start(bf16[128,1,4]{2,1,0:T(2,128)(2,1)} %all_to_all.17), calls=%async_computation | async-start | bytes 131072 | tf_op jit(solution)/shard_map/all_to_all | solution.py:99
  34.2 40.0 %all-to-all-start.1 = ((bf16[128,4,2048]{2,1,0:T(4,128)(2,1)}), bf16[128,4,2048]{2,1,0:T(4,128)(2,1)S(1)}, u32[]{:S(2)}, u32[]{:S(2)}) async-start(bf16[128,4,2048]{2,1,0:T(4,128)(2,1)} %reshape.113), calls=%async_computation.1 | async-start | bytes 4194304 | tf_op jit(solution)/shard_map/all_to_all | solution.py:92
  82.9 15.5 %all-to-all-start.2 = ((f32[128,1,4]{2,1,0:T(1,128)}), f32[128,1,4]{2,1,0:T(1,128)S(1)}, u32[]{:S(2)}, u32[]{:S(2)}) async-start(f32[128,1,4]{2,1,0:T(1,128)} %bitcast.5), calls=%async_computation.2 | async-start | bytes 131072 | tf_op jit(solution)/shard_map/all_to_all | solution.py:110
Sparse Core Ops, SparseCore 0:
  9.7 74.6 all-gather.4
  86.6 73.3 all-gather.2
where the time goes:
time: 243 us; the launch traced here: 242 us
  waiting for transfers between devices  103 us (42%)
  matrix products  59 us (24%)
  starting transfers between devices  23.6 us (10%)
  local copies, waits for them, and re-layouts  20.7 us (9%)
  between operations  14.9 us (6%)
  blocking collectives  8.46 us (3%)
  other arithmetic  6.36 us (3%)
  loops' own time  5.28 us (2%)
    all_gather x1, waiting for transfers between devices, shards(): piece = lax.all_gather(centroids, 'rows', axis=0, tiled=True)  57.7 us
    dot_general x8, matrix products, step(): lax.dot_general(group, tile, (((1,), (1,)), ((), ())), preferred_element_...  55.4 us
    all_to_all x1, waiting for transfers between devices, shards(): lax.all_to_all(outgoing.reshape(devices, capacity, feature_dim), ('cent',...  33.1 us
    all_to_all x1, starting transfers between devices, shards(): lax.all_to_all(present.reshape(devices, capacity), ('cent', 'rows'), spli...  11.5 us
    pmax x1, blocking collectives, shards(): merged = lax.pmax(result, 'cent')  8.46 us
    all_to_all x1, waiting for transfers between devices, shards(): lax.all_to_all(scores.reshape(devices, capacity), ('cent', 'rows'), split...  7.6 us
    all_to_all x1, starting transfers between devices, shards(): lax.all_to_all(outgoing.reshape(devices, capacity, feature_dim), ('cent',...  6.07 us
    all_to_all x1, starting transfers between devices, shards(): lax.all_to_all(scores.reshape(devices, capacity), ('cent', 'rows'), split...  5.97 us
  transfers between devices with their start and end apart: 5, of which 4 were waited for; matrix products, arithmetic and copies ran while one was open for 10% of the time, Pallas kernels for 0%

commit v1 on v0

v1 whole, which is shorter than its diff:
```python
import math

import jax
import jax.numpy as jnp
from jax import lax
from jax.sharding import Mesh
from jax.sharding import PartitionSpec as P

inverse_temp = 3.0
epsilon = 1e-06
ALL = ("y", "z", "x", "c")


def logical_shift(word, amount):
    return lax.shift_right_logical(word, jnp.full(word.shape, amount, jnp.int32))


def gumbel_noise(row_ids, cent_ids, salt_word):
    mixed = row_ids * 1103515245 + cent_ids * 739982445 + salt_word
    mixed = mixed ^ logical_shift(mixed, 16)
    mixed = mixed * 2146121005
    mixed = mixed ^ logical_shift(mixed, 15)
    mixed = mixed * 1759714725
    mixed = mixed ^ logical_shift(mixed, 16)
    low_bits = mixed & 8388607
    uniform = (low_bits.astype(jnp.float32) + 0.5) * (1.0 / 8388608.0)
    return -jnp.log(-jnp.log(uniform))


def cluster_stats(members, valid):
    feature_dim = members.shape[1]
    widened = members.astype(jnp.float32)
    scale = lax.rsqrt(jnp.mean(widened * widened, axis=1) + epsilon)
    gram = lax.dot_general(
        members, members, (((1,), (1,)), ((), ())), preferred_element_type=jnp.float32
    )
    similar = gram * scale[:, None] * scale[None, :] * (1.0 / math.sqrt(feature_dim))
    order = jnp.arange(members.shape[0], dtype=jnp.int32)
    usable = valid[None, :] & (order[:, None] != order[None, :])
    highest = jnp.max(jnp.where(usable, similar, -1e30), axis=1)
    scores = jnp.where(jnp.any(usable, axis=1), highest, 0.0)
    total = jnp.sum(jnp.where(valid[:, None], widened, 0.0), axis=0)
    center = total * lax.rsqrt(jnp.mean(total * total) + epsilon)
    return (scores, center)


def shards(embeddings, centroids, cluster, noise_salt):
    rows_dev, feature_dim = embeddings.shape
    cent_dev = centroids.shape[0]
    ny, nz, nx, nc = (lax.axis_size(a) for a in ALL)
    devices = ny * nz * nx * nc
    capacity = max(2, 2 * rows_dev // devices)
    iy, iz, ix, ic = (lax.axis_index(a) for a in ALL)
    me = ((iy * nz + iz) * nx + ix) * nc + ic
    salt_word = noise_salt[0]
    group = lax.all_gather(lax.all_gather(embeddings, "y", axis=0, tiled=True), "c", axis=0, tiled=True)
    piece = lax.all_gather(centroids, ("z", "x"), axis=0, tiled=True)
    position = jnp.arange(nc * ny * rows_dev, dtype=jnp.int32)
    src_c = position // (ny * rows_dev)
    src_y = position // rows_dev % ny
    row_dev = ((src_y * nz + iz) * nx + ix) * nc + src_c
    group_ids = row_dev * rows_dev + position % rows_dev
    cpos = jnp.arange(nz * nx * cent_dev, dtype=jnp.int32)
    cent_dev_ids = ((iy * nz + cpos // (nx * cent_dev)) * nx + cpos // cent_dev % nx) * nc + ic
    cent_ids = cent_dev_ids * cent_dev + cpos % cent_dev
    piece_rows = piece.shape[0]
    block = math.gcd(piece_rows, 512)
    steps = piece_rows // block
    tiles = piece.reshape(steps, block, feature_dim)
    noise = gumbel_noise(group_ids[:, None], cent_ids[None, :], salt_word)
    noise_tiles = noise.reshape(group.shape[0], steps, block).transpose(1, 0, 2)
    initial = jnp.full((group.shape[0],), -1e30, jnp.float32)

    def step(carry, item):
        tile, noise_tile = item
        scores = lax.dot_general(
            group, tile, (((1,), (1,)), ((), ())), preferred_element_type=jnp.float32
        )
        perturbed = inverse_temp * scores + noise_tile
        return (jnp.maximum(carry, jnp.max(perturbed, axis=1)), None)

    result, unused = lax.scan(step, initial, (tiles, noise_tiles))
    merged = lax.pmax(result, ("c", "y"))
    perturbed_max = lax.dynamic_slice_in_dim(merged, (ic * ny + iy) * rows_dev, rows_dev)
    assigned = cluster[:, 0]
    order = jnp.arange(rows_dev, dtype=jnp.int32)
    same = (assigned[:, None] == assigned[None, :]) & (order[None, :] < order[:, None])
    rank = jnp.sum(same.astype(jnp.int32), axis=1)
    slot = assigned * capacity + rank
    outgoing = jnp.zeros((devices * capacity, feature_dim), jnp.bfloat16).at[slot].set(embeddings)
    present = (
        jnp.zeros((devices * capacity,), jnp.bfloat16)
        .at[slot]
        .set(jnp.ones((rows_dev,), jnp.bfloat16))
    )
    received = lax.all_to_all(
        outgoing.reshape(devices, capacity, feature_dim), ALL, split_axis=0, concat_axis=0, tiled=True
    )
    arrived = lax.all_to_all(
        present.reshape(devices, capacity), ALL, split_axis=0, concat_axis=0, tiled=True
    )
    members = received.reshape(devices * capacity, feature_dim)
    valid = arrived.reshape(devices * capacity) > 0.5
    scores, center = cluster_stats(members, valid)
    returned = lax.all_to_all(
        scores.reshape(devices, capacity), ALL, split_axis=0, concat_axis=0, tiled=True
    )
    dedup_score = returned.reshape(devices * capacity)[slot]
    return (perturbed_max, dedup_score, center[None, :])


def solution(mesh):
    cent_count, rows_count = mesh.devices.shape
    cores = 2
    side = math.isqrt(rows_count // cores)
    view = Mesh(mesh.devices.reshape(cent_count, side, rows_count // cores // side, cores), ALL)
    spec = P(ALL, None)
    in_specs = (spec, spec, spec, P())
    out_specs = (P(ALL), P(ALL), spec)
    return jax.shard_map(shards, mesh=view, in_specs=in_specs, out_specs=out_specs, check_vma=False)
```

time: 243 us -> 236 us (0.971)
  matrix products: 59 us -> 43.1 us
  other arithmetic: 6.36 us -> 18.5 us
  blocking collectives: 8.46 us -> 15.8 us
  loops' own time: 5.28 us -> 0.12 us
  local copies, waits for them, and re-layouts: 20.7 us -> 15.8 us
  waiting for transfers between devices: 103 us -> 107 us
  starting transfers between devices: 23.6 us -> 20.1 us
    dot_general x8 -> x4, matrix products: 55.4 us -> 38.8 us  [step(): lax.dot_general(group, tile, (((1,), (1,)), ((), ())), preferred_element_...]
    neg x0 -> x1, other arithmetic: none -> 12.2 us  [gumbel_noise(): return -jnp.log(-jnp.log(uniform))]
    all_gather x2 -> x3, waiting for transfers between devices: 57.7 us -> 69 us  [the longest x1 53.2 us: shards(): lax.all_gather(embeddings, 'y', axis=0, tiled=True)]
    all_to_all x3, waiting for transfers between devices: 44.4 us -> 36.3 us  [the longest x1 25.5 us: shards(): lax.all_to_all(outgoing.reshape(devices, capacity, feature_dim), ALL, spl...]
    pmax x1, blocking collectives: 8.46 us -> 15.8 us  [shards(): merged = lax.pmax(result, ('c', 'y'))]
    another operation x1, loops' own time: 5.28 us -> 0.12 us  [shards(): result, unused = lax.scan(step, initial, (tiles, noise_tiles))]
    dynamic_slice x9 -> x1, local copies, waits for them, and re-layouts: 5.59 us -> 0.64 us  [shards(): lax.dynamic_slice_in_dim(merged, (ic * ny + iy) * rows_dev, rows_dev)]
    all_to_all x3, starting transfers between devices: 23.5 us -> 20 us  [the longest x1 8.6 us: shards(): lax.all_to_all(present.reshape(devices, capacity), ALL, split_axis=0, con...]
  transfers between devices with their start and end apart: 5 -> 6, of which waited for: 4 -> 5; matrix products, arithmetic and copies ran while one was open for 10% -> 16% of each run, Pallas kernels for 0% -> 0%
where the time goes in v1:
time: 236 us; the launch traced here: 235 us
  waiting for transfers between devices  107 us (45%)
  matrix products  43.1 us (18%)
  starting transfers between devices  20.1 us (9%)
  other arithmetic  18.5 us (8%)
  local copies, waits for them, and re-layouts  15.8 us (7%)
  blocking collectives  15.8 us (7%)
  between operations  15.2 us (6%)
    all_gather x1, waiting for transfers between devices, shards(): lax.all_gather(embeddings, 'y', axis=0, tiled=True)  53.2 us
    dot_general x4, matrix products, step(): lax.dot_general(group, tile, (((1,), (1,)), ((), ())), preferred_element_...  38.8 us
    all_to_all x1, waiting for transfers between devices, shards(): lax.all_to_all(outgoing.reshape(devices, capacity, feature_dim), ALL, spl...  25.5 us
    all_gather x1, waiting for transfers between devices, shards(): piece = lax.all_gather(centroids, ('z', 'x'), axis=0, tiled=True)  15.8 us
    pmax x1, blocking collectives, shards(): merged = lax.pmax(result, ('c', 'y'))  15.8 us
    neg x1, other arithmetic, gumbel_noise(): return -jnp.log(-jnp.log(uniform))  12.2 us
    all_to_all x1, starting transfers between devices, shards(): lax.all_to_all(present.reshape(devices, capacity), ALL, split_axis=0, con...  8.6 us
    all_to_all x1, waiting for transfers between devices, shards(): lax.all_to_all(scores.reshape(devices, capacity), ALL, split_axis=0, conc...  8.01 us
  transfers between devices with their start and end apart: 6, of which 5 were waited for; matrix products, arithmetic and copies ran while one was open for 16% of the time, Pallas kernels for 0%

profile of v1, /device:TPU:1, one launch (start us, length us, event | category | flops | bytes accessed | tf_op | source)
XLA Modules:
  0.0 235.4 jit_solution(165970841655316677)
XLA Ops:
  7.2 0.0 all-gather.6.cloned.1.call-start
  7.2 0.7 all-gather.6.cloned.1.call-update
  7.9 0.0 all-gather.8.cloned.1.call-start
  7.9 53.2 %all-gather.6.cloned.1.call-done = bf16[1024,2048]{1,0:T(8,128)(2,1)} async-done(((bf16[256,2048]{1,0:T(8,128)(2,1)}), bf16[1024,2048]{1,0:T(8,128)(2,1)}) %all-gather.6.cloned.1.call-update) | async-done | bytes 4194320 | tf_op jit(solution)/shard_map/all_gather | solution.py:56
  61.2 0.0 all-gather.8.cloned.1.call-update
  61.2 0.0 all-gather.4.cloned.1.call-start
  61.3 0.7 all-gather.4.cloned.1.call-update
  62.0 0.9 convert_reduce_fusion
  62.9 0.7 compare_select_fusion
  63.6 2.2 scatter_custom_fusion
  65.7 0.8 all_to_all.17
  66.5 8.6 %all-to-all-start = ((bf16[128,1,4]{2,1,0:T(2,128)(2,1)}), bf16[128,1,4]{2,1,0:T(2,128)(2,1)S(1)}, u32[]{:S(2)}, u32[]{:S(2)}) async-start(bf16[128,1,4]{2,1,0:T(2,128)(2,1)} %all_to_all.17), calls=%async_computation | async-start | bytes 131072 | tf_op jit(solution)/shard_map/all_to_all | solution.py:99
  75.2 3.7 %scatter_custom_fusion.1 = bf16[512,2048]{1,0:T(8,128)(2,1)S(1)} fusion(s32[256]{0:T(256)S(1)} %bitcast.33, bf16[256,2048]{1,0:T(8,128)(2,1)} %param.6, bf16[]{:T(256)} %constant.177.clone.1), kind=kCustom, calls=%fused_computation.31 | custom fusion | bytes 2097664 | tf_op jit(solution)/shard_map/scatter | solution.py:90
  79.6 2.2 reshape.217
  81.8 2.8 %all-to-all-done = bf16[128,1,4]{2,1,0:T(2,128)(2,1)S(1)} async-done(((bf16[128,1,4]{2,1,0:T(2,128)(2,1)}), bf16[128,1,4]{2,1,0:T(2,128)(2,1)S(1)}, u32[]{:S(2)}, u32[]{:S(2)}) %all-to-all-start) | async-done | bytes 1056 | tf_op jit(solution)/shard_map/all_to_all | solution.py:99
  84.6 6.9 %all-to-all-start.1 = ((bf16[128,4,2048]{2,1,0:T(4,128)(2,1)}), bf16[128,4,2048]{2,1,0:T(4,128)(2,1)S(1)}, u32[]{:S(2)}, u32[]{:S(2)}) async-start(bf16[128,4,2048]{2,1,0:T(4,128)(2,1)} %reshape.217), calls=%async_computation.1 | async-start | bytes 4194304 | tf_op jit(solution)/shard_map/all_to_all | solution.py:96
  91.5 12.2 %fusion.13 = f32[4,2048,512]{1,2,0:T(8,128)} fusion(s32[]{:T(128)} %bitcast.28, s32[4,512]{1,0:T(4,128)S(1)} %fusion.55, s32[2048]{0:T(1024)S(1)} %fusion.40), kind=kLoop, calls=%fused_computation.21 | loop fusion | flops 67108864 | bytes 16793604 | tf_op jit(solution)/shard_map/neg | solution.py:27
  103.7 0.3 broadcast_compare_fusion
  104.0 0.1 copy.15
  104.1 0.1 copy.16
  104.2 0.1 gt.22
  104.4 0.2 fusion.23
  104.5 25.5 %all-to-all-done.1 = bf16[128,4,2048]{2,1,0:T(4,128)(2,1)S(1)} async-done(((bf16[128,4,2048]{2,1,0:T(4,128)(2,1)}), bf16[128,4,2048]{2,1,0:T(4,128)(2,1)S(1)}, u32[]{:S(2)}, u32[]{:S(2)}) %all-to-all-start.1) | async-done | bytes 2097184 | tf_op jit(solution)/shard_map/all_to_all | solution.py:96
  130.0 2.1 fusion.15
  132.1 0.1 rsqrt.18
  132.2 2.0 reshape.218
  134.3 4.3 %fusion.19 = f32[512]{0:T(512)S(1)} fusion(bf16[512,2048]{1,0:T(8,128)(2,1)} %reshape.218, f32[512]{0:T(512)S(1)} %rsqrt.18, pred[512]{0:T(512)(128)(4,1)S(1)} %gt.22), kind=kOutput, calls=%fused_computation.30 | convolution fusion | flops 1075576320 | bytes 2101760 | tf_op jit(solution)/shard_map/dot_general | solution.py:34
  138.6 0.7 select_n.110
  139.3 4.5 %all-to-all-start.2 = ((f32[128,1,4]{2,1,0:T(1,128)}), f32[128,1,4]{2,1,0:T(1,128)S(1)}, u32[]{:S(2)}, u32[]{:S(2)}) async-start(f32[128,1,4]{2,1,0:T(1,128)} %bitcast.5), calls=%async_computation.2 | async-start | bytes 131072 | tf_op jit(solution)/shard_map/all_to_all | solution.py:105
  143.8 0.6 multiply_reduce_fusion
  145.1 0.6 broadcast_multiply_fusion
  145.7 8.0 %all-to-all-done.2 = f32[128,1,4]{2,1,0:T(1,128)S(1)} async-done(((f32[128,1,4]{2,1,0:T(1,128)}), f32[128,1,4]{2,1,0:T(1,128)S(1)}, u32[]{:S(2)}, u32[]{:S(2)}) %all-to-all-start.2) | async-done | bytes 2080 | tf_op jit(solution)/shard_map/all_to_all | solution.py:105
  153.7 0.5 broadcast.395
  154.3 0.8 reduce.7
  155.1 0.1 reshape.219
  155.2 2.5 %gather_fusion = f32[256]{0:T(256)} fusion(f32[512]{0:T(512)S(1)} %reshape.219, s32[1024]{0:T(1024)S(1)} %pad_clamp_fusion), kind=kCustom, calls=%fused_computation | custom fusion | bytes 3072 | tf_op jit(solution)/shard_map/gather | solution.py:108
  157.7 0.0 all-gather.8.cloned.1.call-done
  157.7 15.8 %all-gather.4.cloned.1.call-done = bf16[2048,2048]{1,0:T(8,128)(2,1)} async-done(((bf16[128,2048]{1,0:T(8,128)(2,1)}), bf16[2048,2048]{1,0:T(8,128)(2,1)}) %all-gather.4.cloned.1.call-update) | async-done | bytes 8388624 | tf_op jit(solution)/shard_map/all_gather | solution.py:57
  173.5 39.0 %while.11 = (s32[]{:T(128)}, f32[2048]{0:T(1024)S(1)}, bf16[4,512,2048]{2,1,0:T(8,128)(2,1)}, bf16[2048,2048]{1,0:T(8,128)(2,1)}, f32[4,2048,512]{1,2,0:T(8,128)}, /*index=5*/s32[]{:T(128)}, s32[]{:T(128)}) while((s32[]{:T(128)}, f32[2048]{0:T(1024)S(1)}, bf16[4,512,2048]{2,1,0:T(8,128)(2,1)}, bf16[2048,2048]{1,0:T(8,128)(2,1)}, ...), condition=%wide.region_2.3_spmd.clone, body=%wide.region_0.2_spmd.clone.sunk | while | flops 4298115072 | bytes 14713943 | solution.py:82
  173.5 9.7 %fusion.69 = f32[2048]{0:T(1024)S(1)} fusion(f32[4,2048,512]{1,2,0:T(8,128)} %get-tuple-element.112, s32[]{:T(128)} %get-tuple-element.101, bf16[2048,2048]{1,0:T(8,128)(2,1)} %get-tuple-element.111, bf16[4,512,2048]{2,1,0:T(8,128)(2,1)} %get-tuple-element.110), kind=kOutput, calls=%fused_computation.4.clone.1 | convolution fusion | flops 4298110976 | bytes 14689280 | tf_op jit(solution)/shard_map/while/body/eval_jaxpr/dot_general | solution.py:76
  183.2 9.7 %fusion.69 = f32[2048]{0:T(1024)S(1)} fusion(f32[4,2048,512]{1,2,0:T(8,128)} %get-tuple-element.112, s32[]{:T(128)} %get-tuple-element.101, bf16[2048,2048]{1,0:T(8,128)(2,1)} %get-tuple-element.111, bf16[4,512,2048]{2,1,0:T(8,128)(2,1)} %get-tuple-element.110), kind=kOutput, calls=%fused_computation.4.clone.1 | convolution fusion | flops 4298110976 | bytes 14689280 | tf_op jit(solution)/shard_map/while/body/eval_jaxpr/dot_general | solution.py:76
  193.0 9.7 %fusion.69 = f32[2048]{0:T(1024)S(1)} fusion(f32[4,2048,512]{1,2,0:T(8,128)} %get-tuple-element.112, s32[]{:T(128)} %get-tuple-element.101, bf16[2048,2048]{1,0:T(8,128)(2,1)} %get-tuple-element.111, bf16[4,512,2048]{2,1,0:T(8,128)(2,1)} %get-tuple-element.110), kind=kOutput, calls=%fused_computation.4.clone.1 | convolution fusion | flops 4298110976 | bytes 14689280 | tf_op jit(solution)/shard_map/while/body/eval_jaxpr/dot_general | solution.py:76
  202.7 9.7 %fusion.69 = f32[2048]{0:T(1024)S(1)} fusion(f32[4,2048,512]{1,2,0:T(8,128)} %get-tuple-element.112, s32[]{:T(128)} %get-tuple-element.101, bf16[2048,2048]{1,0:T(8,128)(2,1)} %get-tuple-element.111, bf16[4,512,2048]{2,1,0:T(8,128)(2,1)} %get-tuple-element.110), kind=kOutput, calls=%fused_computation.4.clone.1 | convolution fusion | flops 4298110976 | bytes 14689280 | tf_op jit(solution)/shard_map/while/body/eval_jaxpr/dot_general | solution.py:76
  212.5 15.8 %pmax.7 = f32[2048]{0:T(1024)S(1)} all-reduce(f32[2048]{0:T(1024)S(1)} %get-tuple-element.30), channel_id=1, replica_groups=mesh['y'=4,'z'=4,'x'=4,'c'=2] {'c','y'}, use_global_device_ids=true, to_apply=%region_3.4 | all-reduce | flops 2048 | bytes 16384 | tf_op jit(solution)/shard_map/pmax | solution.py:83
  228.2 0.6 dynamic_slice.11
  (11 shorter events, 0.1 us)
Async XLA Ops:
  7.2 54.0 %all-gather.6.cloned.1.call-start = ((), (), s32[]{:S(2)}) async-start(), calls=%async_computation.4 | async-start | bytes 5242880 | tf_op jit(solution)/shard_map/all_gather | solution.py:56
  7.9 149.8 %all-gather.8.cloned.1.call-start = ((), (), s32[]{:S(2)}) async-start(), calls=%async_computation.5 | async-start | bytes 12582912 | tf_op jit(solution)/shard_map/all_gather | solution.py:56
  61.2 112.3 %all-gather.4.cloned.1.call-start = ((), (), s32[]{:S(2)}) async-start(), calls=%async_computation.3 | async-start | bytes 8912896 | tf_op jit(solution)/shard_map/all_gather | solution.py:57
  66.5 18.1 %all-to-all-start = ((bf16[128,1,4]{2,1,0:T(2,128)(2,1)}), bf16[128,1,4]{2,1,0:T(2,128)(2,1)S(1)}, u32[]{:S(2)}, u32[]{:S(2)}) async-start(bf16[128,1,4]{2,1,0:T(2,128)(2,1)} %all_to_all.17), calls=%async_computation | async-start | bytes 131072 | tf_op jit(solution)/shard_map/all_to_all | solution.py:99
  84.6 45.4 %all-to-all-start.1 = ((bf16[128,4,2048]{2,1,0:T(4,128)(2,1)}), bf16[128,4,2048]{2,1,0:T(4,128)(2,1)S(1)}, u32[]{:S(2)}, u32[]{:S(2)}) async-start(bf16[128,4,2048]{2,1,0:T(4,128)(2,1)} %reshape.217), calls=%async_computation.1 | async-start | bytes 4194304 | tf_op jit(solution)/shard_map/all_to_all | solution.py:96
  139.3 14.4 %all-to-all-start.2 = ((f32[128,1,4]{2,1,0:T(1,128)}), f32[128,1,4]{2,1,0:T(1,128)S(1)}, u32[]{:S(2)}, u32[]{:S(2)}) async-start(f32[128,1,4]{2,1,0:T(1,128)} %bitcast.5), calls=%async_computation.2 | async-start | bytes 131072 | tf_op jit(solution)/shard_map/all_to_all | solution.py:105
Sparse Core Ops, SparseCore 0:
  9.7 51.4 all-gather.5
  62.8 23.2 all-gather.7
  88.3 85.1 all-gather.3

commit v2 on v1

--- a/solution.py
+++ b/solution.py
@@ -1,8 +1,11 @@
+import functools
 import math
 
 import jax
 import jax.numpy as jnp
 from jax import lax
+from jax.experimental import pallas as pl
+from jax.experimental.pallas import tpu as pltpu
 from jax.sharding import Mesh
 from jax.sharding import PartitionSpec as P
 
@@ -25,6 +28,72 @@
     low_bits = mixed & 8388607
     uniform = (low_bits.astype(jnp.float32) + 0.5) * (1.0 / 8388608.0)
     return -jnp.log(-jnp.log(uniform))
+
+
+def gather_kernel(axes, sizes, x_ref, out_ref, send_sem, recv_sem, local_sem):
+    n = math.prod(sizes)
+    where = {a: lax.axis_index(a) for a in ALL}
+    me = 0
+    for a, size in zip(axes, sizes):
+        me = me * size + where[a]
+
+    def device_of(index):
+        coords = dict(where)
+        for a, size in reversed(list(zip(axes, sizes))):
+            coords[a] = lax.rem(index, size)
+            index = index // size
+        return tuple(coords[a] for a in ALL)
+
+    peers = [lax.rem(me + k, n) for k in range(n)]
+    barrier = pltpu.get_barrier_semaphore()
+    for k in range(1, n):
+        pl.semaphore_signal(barrier, inc=1, device_id=device_of(peers[k]), device_id_type=pl.DeviceIdType.MESH)
+    pl.semaphore_wait(barrier, n - 1)
+    local = pltpu.make_async_copy(x_ref, out_ref.at[me], local_sem)
+    local.start()
+    sends = []
+    for k in range(1, n):
+        copy = pltpu.make_async_remote_copy(
+            src_ref=x_ref,
+            dst_ref=out_ref.at[me],
+            send_sem=send_sem.at[k],
+            recv_sem=recv_sem.at[me],
+            device_id=device_of(peers[k]),
+            device_id_type=pl.DeviceIdType.MESH,
+        )
+        copy.start()
+        sends.append(copy)
+    for k in range(1, n):
+        source = lax.rem(me + n - k, n)
+        pltpu.make_async_remote_copy(
+            src_ref=x_ref,
+            dst_ref=out_ref.at[source],
+            send_sem=send_sem.at[k],
+            recv_sem=recv_sem.at[source],
+            device_id=device_of(source),
+            device_id_type=pl.DeviceIdType.MESH,
+        ).wait_recv()
+    for copy in sends:
+        copy.wait_send()
+    local.wait()
+
+
+def gather(x, axes, collective_id):
+    sizes = tuple(lax.axis_size(a) for a in axes)
+    n = math.prod(sizes)
+    out = pl.pallas_call(
+        functools.partial(gather_kernel, axes, sizes),
+        out_shape=jax.ShapeDtypeStruct((n,) + x.shape, x.dtype),
+        in_specs=[pl.BlockSpec(memory_space=pl.ANY)],
+        out_specs=pl.BlockSpec(memory_space=pl.ANY),
+        scratch_shapes=[
+            pltpu.SemaphoreType.DMA((n,)),
+            pltpu.SemaphoreType.DMA((n,)),
+            pltpu.SemaphoreType.DMA,
+        ],
+        compiler_params=pltpu.CompilerParams(collective_id=collective_id, has_side_effects=True),
+    )(x)
+    return out.reshape((n * x.shape[0],) + x.shape[1:])
 
 
 def cluster_stats(members, valid):
@@ -53,8 +122,8 @@
     iy, iz, ix, ic = (lax.axis_index(a) for a in ALL)
     me = ((iy * nz + iz) * nx + ix) * nc + ic
     salt_word = noise_salt[0]
-    group = lax.all_gather(lax.all_gather(embeddings, "y", axis=0, tiled=True), "c", axis=0, tiled=True)
-    piece = lax.all_gather(centroids, ("z", "x"), axis=0, tiled=True)
+    group = gather(gather(embeddings, ("y",), 0), ("c",), 1)
+    piece = gather(centroids, ("z", "x"), 2)
     position = jnp.arange(nc * ny * rows_dev, dtype=jnp.int32)
     src_c = position // (ny * rows_dev)
     src_y = position // rows_dev % ny

time: 236 us -> 461 us (1.95)
  Pallas kernels: 0 us -> 321 us
  waiting for transfers between devices: 107 us -> 7.61 us
  starting transfers between devices: 20.1 us -> 37.6 us
  between operations: 15.2 us -> 2.12 us
    pallas_call x0 -> x3, Pallas kernels: none -> 321 us  [gather(): pl.pallas_call(functools.partial(gather_kernel, axes, sizes), out_shape=j...]
    all_gather x3 -> x0, waiting for transfers between devices: 69 us -> none  [the longest x1 53.2 us: shards(): lax.all_gather(embeddings, 'y', axis=0, tiled=True)]
    all_to_all x1, waiting for transfers between devices: 25.5 us -> 0.01 us  [shards(): lax.all_to_all(outgoing.reshape(devices, capacity, feature_dim), ALL, spl...]
    all_to_all x1, starting transfers between devices: 6.92 us -> 18 us  [shards(): lax.all_to_all(outgoing.reshape(devices, capacity, feature_dim), ALL, spl...]
  transfers between devices with their start and end apart: 6 -> 3, of which waited for: 5 -> 1; matrix products, arithmetic and copies ran while one was open for 16% -> 13% of each run, Pallas kernels for 0% -> 70%
where the time goes in v2:
time: 461 us
  Pallas kernels  321 us (70%)
  matrix products  42.4 us (9%)
  starting transfers between devices  37.6 us (8%)
  other arithmetic  18.5 us (4%)
  local copies, waits for them, and re-layouts  15.7 us (3%)
  blocking collectives  15.6 us (3%)
  waiting for transfers between devices  7.61 us (2%)
    pallas_call x3, Pallas kernels, gather(): pl.pallas_call(functools.partial(gather_kernel, axes, sizes), out_shape=j...  321 us
    dot_general x4, matrix products, step(): lax.dot_general(group, tile, (((1,), (1,)), ((), ())), preferred_element_...  38.8 us
    all_to_all x1, starting transfers between devices, shards(): lax.all_to_all(outgoing.reshape(devices, capacity, feature_dim), ALL, spl...  18 us
    pmax x1, blocking collectives, shards(): merged = lax.pmax(result, ('c', 'y'))  15.6 us
    neg x1, other arithmetic, gumbel_noise(): return -jnp.log(-jnp.log(uniform))  12.2 us
    all_to_all x1, starting transfers between devices, shards(): lax.all_to_all(present.reshape(devices, capacity), ALL, split_axis=0, con...  11.5 us
  transfers between devices with their start and end apart: 3, of which 1 were waited for; matrix products, arithmetic and copies ran while one was open for 13% of the time, Pallas kernels for 70%

profile of v2, /device:TPU:1, one launch (start us, length us, event | category | flops | bytes accessed | tf_op | source)
XLA Modules:
  0.0 460.6 jit_solution(16098816587715956672)
XLA Ops:
  0.6 0.9 convert_reduce_fusion
  1.6 0.7 compare_select_fusion
  2.3 2.2 scatter_custom_fusion
  4.4 0.8 all_to_all.17
  5.2 11.5 %all-to-all-start = ((bf16[128,1,4]{2,1,0:T(2,128)(2,1)}), bf16[128,1,4]{2,1,0:T(2,128)(2,1)S(1)}, u32[]{:S(2)}, u32[]{:S(2)}) async-start(bf16[128,1,4]{2,1,0:T(2,128)(2,1)} %all_to_all.17), calls=%async_computation | async-start | bytes 131072 | tf_op jit(solution)/shard_map/all_to_all | solution.py:168
  17.4 12.2 %fusion.13 = f32[4,2048,512]{1,2,0:T(8,128)} fusion(s32[]{:T(128)} %bitcast.30, s32[4,512]{1,0:T(4,128)S(1)} %fusion.55, s32[2048]{0:T(1024)S(1)} %fusion.40), kind=kLoop, calls=%fused_computation.21 | loop fusion | flops 67108864 | bytes 16793604 | tf_op jit(solution)/shard_map/neg | solution.py:30
  29.6 49.6 %shard_map.68 = bf16[4,256,2048]{2,1,0:T(8,128)(2,1)} custom-call(bf16[256,2048]{1,0:T(8,128)(2,1)} %x_ref.3), custom_call_target="tpu_custom_call" | custom-call | tf_op jit(solution)/shard_map/pallas_call | solution.py:84
  79.2 3.5 scatter_custom_fusion.1
  82.7 129.5 %shard_map.69 = bf16[2,1024,2048]{2,1,0:T(8,128)(2,1)} custom-call(bf16[1024,2048]{1,0:T(8,128)(2,1)} %bitcast.31), custom_call_target="tpu_custom_call" | custom-call | tf_op jit(solution)/shard_map/pallas_call | solution.py:84
  212.2 141.9 %shard_map.67 = bf16[16,128,2048]{2,1,0:T(8,128)(2,1)} custom-call(bf16[128,2048]{1,0:T(8,128)(2,1)} %x_ref.2), custom_call_target="tpu_custom_call" | custom-call | tf_op jit(solution)/shard_map/pallas_call | solution.py:84
  354.1 2.2 reshape.221
  356.4 0.0 all-to-all-done
  356.4 18.0 %all-to-all-start.1 = ((bf16[128,4,2048]{2,1,0:T(4,128)(2,1)}), bf16[128,4,2048]{2,1,0:T(4,128)(2,1)S(1)}, u32[]{:S(2)}, u32[]{:S(2)}) async-start(bf16[128,4,2048]{2,1,0:T(4,128)(2,1)} %reshape.221), calls=%async_computation.1 | async-start | bytes 4194304 | tf_op jit(solution)/shard_map/all_to_all | solution.py:165
  374.3 39.0 %while.11 = (s32[]{:T(128)}, f32[2048]{0:T(1024)S(1)}, bf16[4,512,2048]{2,1,0:T(8,128)(2,1)}, bf16[2048,2048]{1,0:T(8,128)(2,1)}, f32[4,2048,512]{1,2,0:T(8,128)}, /*index=5*/s32[]{:T(128)}, s32[]{:T(128)}) while((s32[]{:T(128)}, f32[2048]{0:T(1024)S(1)}, bf16[4,512,2048]{2,1,0:T(8,128)(2,1)}, bf16[2048,2048]{1,0:T(8,128)(2,1)}, ...), condition=%wide.region_2.3_spmd.clone, body=%wide.region_0.2_spmd.clone.sunk | while | flops 4298115072 | bytes 14713943 | solution.py:151
  374.4 9.7 %fusion.69 = f32[2048]{0:T(1024)S(1)} fusion(f32[4,2048,512]{1,2,0:T(8,128)} %get-tuple-element.112, s32[]{:T(128)} %get-tuple-element.101, bf16[2048,2048]{1,0:T(8,128)(2,1)} %get-tuple-element.111, bf16[4,512,2048]{2,1,0:T(8,128)(2,1)} %get-tuple-element.110), kind=kOutput, calls=%fused_computation.4.clone.1 | convolution fusion | flops 4298110976 | bytes 14689280 | tf_op jit(solution)/shard_map/while/body/eval_jaxpr/dot_general | solution.py:145
  384.1 9.7 %fusion.69 = f32[2048]{0:T(1024)S(1)} fusion(f32[4,2048,512]{1,2,0:T(8,128)} %get-tuple-element.112, s32[]{:T(128)} %get-tuple-element.101, bf16[2048,2048]{1,0:T(8,128)(2,1)} %get-tuple-element.111, bf16[4,512,2048]{2,1,0:T(8,128)(2,1)} %get-tuple-element.110), kind=kOutput, calls=%fused_computation.4.clone.1 | convolution fusion | flops 4298110976 | bytes 14689280 | tf_op jit(solution)/shard_map/while/body/eval_jaxpr/dot_general | solution.py:145
  393.9 9.7 %fusion.69 = f32[2048]{0:T(1024)S(1)} fusion(f32[4,2048,512]{1,2,0:T(8,128)} %get-tuple-element.112, s32[]{:T(128)} %get-tuple-element.101, bf16[2048,2048]{1,0:T(8,128)(2,1)} %get-tuple-element.111, bf16[4,512,2048]{2,1,0:T(8,128)(2,1)} %get-tuple-element.110), kind=kOutput, calls=%fused_computation.4.clone.1 | convolution fusion | flops 4298110976 | bytes 14689280 | tf_op jit(solution)/shard_map/while/body/eval_jaxpr/dot_general | solution.py:145
  403.6 9.7 %fusion.69 = f32[2048]{0:T(1024)S(1)} fusion(f32[4,2048,512]{1,2,0:T(8,128)} %get-tuple-element.112, s32[]{:T(128)} %get-tuple-element.101, bf16[2048,2048]{1,0:T(8,128)(2,1)} %get-tuple-element.111, bf16[4,512,2048]{2,1,0:T(8,128)(2,1)} %get-tuple-element.110), kind=kOutput, calls=%fused_computation.4.clone.1 | convolution fusion | flops 4298110976 | bytes 14689280 | tf_op jit(solution)/shard_map/while/body/eval_jaxpr/dot_general | solution.py:145
  413.4 15.6 %pmax.7 = f32[2048]{0:T(1024)S(1)} all-reduce(f32[2048]{0:T(1024)S(1)} %get-tuple-element.30), channel_id=1, replica_groups=mesh['y'=4,'z'=4,'x'=4,'c'=2] {'c','y'}, use_global_device_ids=true, to_apply=%region_3.4 | all-reduce | flops 2048 | bytes 16384 | tf_op jit(solution)/shard_map/pmax | solution.py:152
  428.9 0.6 dynamic_slice.11
  429.6 0.3 broadcast_compare_fusion
  429.8 0.1 copy.15
  429.9 0.1 copy.16
  430.1 0.1 gt.22
  430.2 0.2 fusion.23
  430.4 0.0 all-to-all-done.1
  430.4 2.1 fusion.15
  432.5 0.1 rsqrt.18
  432.6 2.1 reshape.222
  434.7 3.6 fusion.19
  438.3 0.7 select_n.110
  439.1 8.1 %all-to-all-start.2 = ((f32[128,1,4]{2,1,0:T(1,128)}), f32[128,1,4]{2,1,0:T(1,128)S(1)}, u32[]{:S(2)}, u32[]{:S(2)}) async-start(f32[128,1,4]{2,1,0:T(1,128)} %bitcast.7), calls=%async_computation.2 | async-start | bytes 131072 | tf_op jit(solution)/shard_map/all_to_all | solution.py:174
  447.2 0.6 multiply_reduce_fusion
  448.5 0.6 broadcast_multiply_fusion
  449.1 7.6 %all-to-all-done.2 = f32[128,1,4]{2,1,0:T(1,128)S(1)} async-done(((f32[128,1,4]{2,1,0:T(1,128)}), f32[128,1,4]{2,1,0:T(1,128)S(1)}, u32[]{:S(2)}, u32[]{:S(2)}) %all-to-all-start.2) | async-done | bytes 2080 | tf_op jit(solution)/shard_map/all_to_all | solution.py:174
  456.7 0.5 broadcast.395
  457.2 0.8 reduce.7
  458.0 0.1 reshape.223
  458.1 2.5 gather_fusion
  (11 shorter events, 0.1 us)
Async XLA Ops:
  5.2 351.2 %all-to-all-start = ((bf16[128,1,4]{2,1,0:T(2,128)(2,1)}), bf16[128,1,4]{2,1,0:T(2,128)(2,1)S(1)}, u32[]{:S(2)}, u32[]{:S(2)}) async-start(bf16[128,1,4]{2,1,0:T(2,128)(2,1)} %all_to_all.17), calls=%async_computation | async-start | bytes 131072 | tf_op jit(solution)/shard_map/all_to_all | solution.py:168
  356.4 74.0 %all-to-all-start.1 = ((bf16[128,4,2048]{2,1,0:T(4,128)(2,1)}), bf16[128,4,2048]{2,1,0:T(4,128)(2,1)S(1)}, u32[]{:S(2)}, u32[]{:S(2)}) async-start(bf16[128,4,2048]{2,1,0:T(4,128)(2,1)} %reshape.221), calls=%async_computation.1 | async-start | bytes 4194304 | tf_op jit(solution)/shard_map/all_to_all | solution.py:165
  439.1 17.6 %all-to-all-start.2 = ((f32[128,1,4]{2,1,0:T(1,128)}), f32[128,1,4]{2,1,0:T(1,128)S(1)}, u32[]{:S(2)}, u32[]{:S(2)}) async-start(f32[128,1,4]{2,1,0:T(1,128)} %bitcast.7), calls=%async_computation.2 | async-start | bytes 131072 | tf_op jit(solution)/shard_map/all_to_all | solution.py:174

commit v3 on v2

--- a/solution.py
+++ b/solution.py
@@ -122,13 +122,14 @@
     iy, iz, ix, ic = (lax.axis_index(a) for a in ALL)
     me = ((iy * nz + iz) * nx + ix) * nc + ic
     salt_word = noise_salt[0]
-    group = gather(gather(embeddings, ("y",), 0), ("c",), 1)
-    piece = gather(centroids, ("z", "x"), 2)
-    position = jnp.arange(nc * ny * rows_dev, dtype=jnp.int32)
-    src_c = position // (ny * rows_dev)
-    src_y = position // rows_dev % ny
-    row_dev = ((src_y * nz + iz) * nx + ix) * nc + src_c
-    group_ids = row_dev * rows_dev + position % rows_dev
+    own_rows = gather(embeddings, ("y",), 0)
+    other_rows = lax.ppermute(own_rows, "c", [(i, (i + 1) % nc) for i in range(nc)])
+    group = jnp.concatenate([own_rows, other_rows], axis=0)
+    piece = lax.all_gather(centroids, ("z", "x"), axis=0, tiled=True)
+    src_c = jnp.stack([ic, (ic + nc - 1) % nc])
+    src_y = jnp.arange(ny, dtype=jnp.int32)
+    row_dev = ((src_y[None, :] * nz + iz) * nx + ix) * nc + src_c[:, None]
+    group_ids = (row_dev[:, :, None] * rows_dev + jnp.arange(rows_dev, dtype=jnp.int32)).reshape(-1)
     cpos = jnp.arange(nz * nx * cent_dev, dtype=jnp.int32)
     cent_dev_ids = ((iy * nz + cpos // (nx * cent_dev)) * nx + cpos // cent_dev % nx) * nc + ic
     cent_ids = cent_dev_ids * cent_dev + cpos % cent_dev
@@ -149,6 +150,7 @@
         return (jnp.maximum(carry, jnp.max(perturbed, axis=1)), None)
 
     result, unused = lax.scan(step, initial, (tiles, noise_tiles))
+    result = jnp.roll(result, ic * (ny * rows_dev))
     merged = lax.pmax(result, ("c", "y"))
     perturbed_max = lax.dynamic_slice_in_dim(merged, (ic * ny + iy) * rows_dev, rows_dev)
     assigned = cluster[:, 0]

time: 461 us -> 217 us (0.47)
  Pallas kernels: 321 us -> 50.3 us
  waiting for transfers between devices: 7.61 us -> 28.8 us
  starting transfers between devices: 37.6 us -> 22 us
  between operations: 2.12 us -> 15.6 us
  other arithmetic: 18.5 us -> 27 us
    pallas_call x3 -> x1, Pallas kernels: 321 us -> 50.3 us  [gather(): pl.pallas_call(functools.partial(gather_kernel, axes, sizes), out_shape=j...]
    all_to_all x1, waiting for transfers between devices: 0.01 us -> 17.5 us  [shards(): lax.all_to_all(outgoing.reshape(devices, capacity, feature_dim), ALL, spl...]
    all_to_all x1, starting transfers between devices: 18 us -> 6.77 us  [shards(): lax.all_to_all(outgoing.reshape(devices, capacity, feature_dim), ALL, spl...]
    concatenate x0 -> x2, other arithmetic: none -> 8.36 us  [the longest x1 8.34 us: shards(): group = jnp.concatenate([own_rows, other_rows], axis=0)]
  transfers between devices with their start and end apart: 3 -> 5, of which waited for: 1 -> 3; matrix products, arithmetic and copies ran while one was open for 13% -> 21% of each run, Pallas kernels for 70% -> 23%
where the time goes in v3:
time: 217 us; the launch traced here: 216 us
  Pallas kernels  50.3 us (23%)
  matrix products  42.5 us (20%)
  waiting for transfers between devices  28.8 us (13%)
  other arithmetic  27 us (12%)
  starting transfers between devices  22 us (10%)
  local copies, waits for them, and re-layouts  15.8 us (7%)
  between operations  15.6 us (7%)
  blocking collectives  14.2 us (7%)
    pallas_call x1, Pallas kernels, gather(): pl.pallas_call(functools.partial(gather_kernel, axes, sizes), out_shape=j...  50.3 us
    dot_general x4, matrix products, step(): lax.dot_general(group, tile, (((1,), (1,)), ((), ())), preferred_element_...  38.8 us
    all_to_all x1, waiting for transfers between devices, shards(): lax.all_to_all(outgoing.reshape(devices, capacity, feature_dim), ALL, spl...  17.5 us
    pmax x1, blocking collectives, shards(): merged = lax.pmax(result, ('c', 'y'))  14.2 us
    neg x1, other arithmetic, gumbel_noise(): return -jnp.log(-jnp.log(uniform))  12.2 us
    all_to_all x1, starting transfers between devices, shards(): lax.all_to_all(present.reshape(devices, capacity), ALL, split_axis=0, con...  9.15 us
    concatenate x1, other arithmetic, shards(): group = jnp.concatenate([own_rows, other_rows], axis=0)  8.34 us
    all_to_all x1, waiting for transfers between devices, shards(): lax.all_to_all(scores.reshape(devices, capacity), ALL, split_axis=0, conc...  7.62 us
  transfers between devices with their start and end apart: 5, of which 3 were waited for; matrix products, arithmetic and copies ran while one was open for 21% of the time, Pallas kernels for 23%

profile of v3, /device:TPU:1, one launch (start us, length us, event | category | flops | bytes accessed | tf_op | source)
XLA Modules:
  0.0 216.3 jit_solution(9628602595488818327)
XLA Ops:
  7.2 0.0 all-gather.2.cloned.1.call-start
  7.2 0.7 all-gather.2.cloned.1.call-update
  7.9 50.3 %shard_map.67 = bf16[4,256,2048]{2,1,0:T(8,128)(2,1)} custom-call(bf16[256,2048]{1,0:T(8,128)(2,1)} %x_ref.1), custom_call_target="tpu_custom_call" | custom-call | tf_op jit(solution)/shard_map/pallas_call | solution.py:84
  58.2 1.6 collective-permute-start
  59.8 0.9 convert_reduce_fusion
  60.8 0.7 compare_select_fusion
  61.5 2.2 scatter_custom_fusion
  63.6 0.8 all_to_all.17
  64.4 9.1 %all-to-all-start = ((bf16[128,1,4]{2,1,0:T(2,128)(2,1)}), bf16[128,1,4]{2,1,0:T(2,128)(2,1)S(1)}, u32[]{:S(2)}, u32[]{:S(2)}) async-start(bf16[128,1,4]{2,1,0:T(2,128)(2,1)} %all_to_all.17), calls=%async_computation | async-start | bytes 131072 | tf_op jit(solution)/shard_map/all_to_all | solution.py:170
  73.6 0.1 pad_add_fusion
  73.7 0.1 add_multiply_fusion
  73.8 0.1 multiply_bitcast_fusion
  73.9 3.5 %scatter_custom_fusion.1 = bf16[512,2048]{1,0:T(8,128)(2,1)S(1)} fusion(s32[256]{0:T(256)S(1)} %bitcast.42, bf16[256,2048]{1,0:T(8,128)(2,1)} %x_ref.1, bf16[]{:T(256)} %constant.175.clone.1), kind=kCustom, calls=%fused_computation.32 | custom fusion | bytes 2097664 | tf_op jit(solution)/shard_map/scatter | solution.py:161
  78.1 2.3 %reshape.231 = bf16[128,4,2048]{2,1,0:T(4,128)(2,1)} reshape(bf16[512,2048]{1,0:T(8,128)(2,1)S(1)} %scatter_custom_fusion.1) | data formatting | bytes 4194304 | tf_op jit(solution)/shard_map/reshape | solution.py:168
  80.3 3.0 %all-to-all-done = bf16[128,1,4]{2,1,0:T(2,128)(2,1)S(1)} async-done(((bf16[128,1,4]{2,1,0:T(2,128)(2,1)}), bf16[128,1,4]{2,1,0:T(2,128)(2,1)S(1)}, u32[]{:S(2)}, u32[]{:S(2)}) %all-to-all-start) | async-done | bytes 1056 | tf_op jit(solution)/shard_map/all_to_all | solution.py:170
  83.3 6.8 %all-to-all-start.1 = ((bf16[128,4,2048]{2,1,0:T(4,128)(2,1)}), bf16[128,4,2048]{2,1,0:T(4,128)(2,1)S(1)}, u32[]{:S(2)}, u32[]{:S(2)}) async-start(bf16[128,4,2048]{2,1,0:T(4,128)(2,1)} %reshape.231), calls=%async_computation.1 | async-start | bytes 4194304 | tf_op jit(solution)/shard_map/all_to_all | solution.py:167
  90.1 12.2 %fusion.13 = f32[4,2048,512]{1,2,0:T(8,128)} fusion(s32[]{:T(128)} %bitcast.34, s32[4,512]{1,0:T(4,128)S(1)} %fusion.37, s32[2048]{0:T(1024)S(1)} %bitcast.37), kind=kLoop, calls=%fused_computation.21 | loop fusion | flops 67108864 | bytes 16793604 | tf_op jit(solution)/shard_map/neg | solution.py:30
  102.3 0.3 broadcast_compare_fusion
  102.5 0.1 copy.15
  102.6 0.1 copy.16
  102.8 0.1 gt.22
  102.9 0.2 fusion.23
  103.1 17.5 %all-to-all-done.1 = bf16[128,4,2048]{2,1,0:T(4,128)(2,1)S(1)} async-done(((bf16[128,4,2048]{2,1,0:T(4,128)(2,1)}), bf16[128,4,2048]{2,1,0:T(4,128)(2,1)S(1)}, u32[]{:S(2)}, u32[]{:S(2)}) %all-to-all-start.1) | async-done | bytes 2097184 | tf_op jit(solution)/shard_map/all_to_all | solution.py:167
  120.6 2.1 fusion.15
  122.7 0.1 rsqrt.18
  122.8 2.1 reshape.232
  125.0 3.7 %fusion.19 = f32[512]{0:T(512)S(1)} fusion(bf16[512,2048]{1,0:T(8,128)(2,1)} %reshape.232, f32[512]{0:T(512)S(1)} %rsqrt.18, pred[512]{0:T(512)(128)(4,1)S(1)} %gt.22), kind=kOutput, calls=%fused_computation.31 | convolution fusion | flops 1075576320 | bytes 2101760 | tf_op jit(solution)/shard_map/dot_general | solution.py:103
  128.6 0.7 select_n.97
  129.4 4.4 %all-to-all-start.2 = ((f32[128,1,4]{2,1,0:T(1,128)}), f32[128,1,4]{2,1,0:T(1,128)S(1)}, u32[]{:S(2)}, u32[]{:S(2)}) async-start(f32[128,1,4]{2,1,0:T(1,128)} %bitcast.8), calls=%async_computation.2 | async-start | bytes 131072 | tf_op jit(solution)/shard_map/all_to_all | solution.py:176
  133.8 0.6 multiply_reduce_fusion
  135.1 0.6 broadcast_multiply_fusion
  135.7 7.6 %all-to-all-done.2 = f32[128,1,4]{2,1,0:T(1,128)S(1)} async-done(((f32[128,1,4]{2,1,0:T(1,128)}), f32[128,1,4]{2,1,0:T(1,128)S(1)}, u32[]{:S(2)}, u32[]{:S(2)}) %all-to-all-start.2) | async-done | bytes 2080 | tf_op jit(solution)/shard_map/all_to_all | solution.py:176
  143.3 0.5 broadcast.334
  143.8 0.8 reduce.7
  144.6 0.1 reshape.233
  144.7 2.5 %gather_fusion = f32[256]{0:T(256)} fusion(f32[512]{0:T(512)S(1)} %reshape.233, s32[1024]{0:T(1024)S(1)} %pad_clamp_fusion), kind=kCustom, calls=%fused_computation | custom fusion | bytes 3072 | tf_op jit(solution)/shard_map/gather | solution.py:179
  147.2 0.0 collective-permute-done
  147.2 8.3 %pad_maximum_fusion = bf16[2048,2048]{1,0:T(8,128)(2,1)} fusion(bf16[1024,2048]{1,0:T(8,128)(2,1)} %collective-permute-done, bf16[1024,2048]{1,0:T(8,128)(2,1)} %bitcast.36), kind=kLoop, calls=%fused_computation.22 | loop fusion | flops 16777216 | bytes 16777216 | tf_op jit(solution)/shard_map/concatenate | solution.py:127
  155.6 0.0 all-gather.2.cloned.1.call-done
  155.6 39.0 %while.11 = (s32[]{:T(128)}, f32[2048]{0:T(1024)S(1)}, bf16[4,512,2048]{2,1,0:T(8,128)(2,1)}, bf16[2048,2048]{1,0:T(8,128)(2,1)}, f32[4,2048,512]{1,2,0:T(8,128)}, /*index=5*/s32[]{:T(128)}, s32[]{:T(128)}) while((s32[]{:T(128)}, f32[2048]{0:T(1024)S(1)}, bf16[4,512,2048]{2,1,0:T(8,128)(2,1)}, bf16[2048,2048]{1,0:T(8,128)(2,1)}, ...), condition=%wide.region_2.3_spmd.clone, body=%wide.region_0.2_spmd.clone.sunk | while | flops 4298115072 | bytes 14713943 | solution.py:152
  155.6 9.7 %fusion.51 = f32[2048]{0:T(1024)S(1)} fusion(f32[4,2048,512]{1,2,0:T(8,128)} %get-tuple-element.112, s32[]{:T(128)} %get-tuple-element.101, bf16[2048,2048]{1,0:T(8,128)(2,1)} %get-tuple-element.111, bf16[4,512,2048]{2,1,0:T(8,128)(2,1)} %get-tuple-element.110), kind=kOutput, calls=%fused_computation.4.clone.1 | convolution fusion | flops 4298110976 | bytes 14689280 | tf_op jit(solution)/shard_map/while/body/eval_jaxpr/dot_general | solution.py:146
  165.3 9.7 %fusion.51 = f32[2048]{0:T(1024)S(1)} fusion(f32[4,2048,512]{1,2,0:T(8,128)} %get-tuple-element.112, s32[]{:T(128)} %get-tuple-element.101, bf16[2048,2048]{1,0:T(8,128)(2,1)} %get-tuple-element.111, bf16[4,512,2048]{2,1,0:T(8,128)(2,1)} %get-tuple-element.110), kind=kOutput, calls=%fused_computation.4.clone.1 | convolution fusion | flops 4298110976 | bytes 14689280 | tf_op jit(solution)/shard_map/while/body/eval_jaxpr/dot_general | solution.py:146
  175.1 9.7 %fusion.51 = f32[2048]{0:T(1024)S(1)} fusion(f32[4,2048,512]{1,2,0:T(8,128)} %get-tuple-element.112, s32[]{:T(128)} %get-tuple-element.101, bf16[2048,2048]{1,0:T(8,128)(2,1)} %get-tuple-element.111, bf16[4,512,2048]{2,1,0:T(8,128)(2,1)} %get-tuple-element.110), kind=kOutput, calls=%fused_computation.4.clone.1 | convolution fusion | flops 4298110976 | bytes 14689280 | tf_op jit(solution)/shard_map/while/body/eval_jaxpr/dot_general | solution.py:146
  184.8 9.7 %fusion.51 = f32[2048]{0:T(1024)S(1)} fusion(f32[4,2048,512]{1,2,0:T(8,128)} %get-tuple-element.112, s32[]{:T(128)} %get-tuple-element.101, bf16[2048,2048]{1,0:T(8,128)(2,1)} %get-tuple-element.111, bf16[4,512,2048]{2,1,0:T(8,128)(2,1)} %get-tuple-element.110), kind=kOutput, calls=%fused_computation.4.clone.1 | convolution fusion | flops 4298110976 | bytes 14689280 | tf_op jit(solution)/shard_map/while/body/eval_jaxpr/dot_general | solution.py:146
  194.6 14.2 %pmax.7 = f32[2048]{0:T(1024)S(1)} all-reduce(f32[2048]{0:T(1024)S(1)} %fusion.33), channel_id=1, replica_groups=mesh['y'=4,'z'=4,'x'=4,'c'=2] {'c','y'}, use_global_device_ids=true, to_apply=%region_3.4 | all-reduce | flops 2048 | bytes 16384 | tf_op jit(solution)/shard_map/pmax | solution.py:154
  208.8 0.6 dynamic_slice.16
  (13 shorter events, 0.1 us)
Async XLA Ops:
  7.2 148.4 %all-gather.2.cloned.1.call-start = ((), (), s32[]{:S(2)}) async-start(), calls=%async_computation.3 | async-start | bytes 8912896 | tf_op jit(solution)/shard_map/all_gather | solution.py:128
  58.2 89.0 %collective-permute-start = (bf16[1024,2048]{1,0:T(8,128)(2,1)}, bf16[1024,2048]{1,0:T(8,128)(2,1)}, u32[]{:S(2)}, u32[]{:S(2)}) collective-permute-start(bf16[1024,2048]{1,0:T(8,128)(2,1)} %bitcast.35), channel_id=1, source_target_pairs={{0,1},{1,0},{2,3},{3,2},{4,5},{5,4},{6,7},{7,6},{8,9},{9,8},{10,11... | collective-permute-start | bytes 12582920 | tf_op jit(solution)/shard_map/ppermute | solution.py:126
  64.4 18.9 %all-to-all-start = ((bf16[128,1,4]{2,1,0:T(2,128)(2,1)}), bf16[128,1,4]{2,1,0:T(2,128)(2,1)S(1)}, u32[]{:S(2)}, u32[]{:S(2)}) async-start(bf16[128,1,4]{2,1,0:T(2,128)(2,1)} %all_to_all.17), calls=%async_computation | async-start | bytes 131072 | tf_op jit(solution)/shard_map/all_to_all | solution.py:170
  83.3 37.3 %all-to-all-start.1 = ((bf16[128,4,2048]{2,1,0:T(4,128)(2,1)}), bf16[128,4,2048]{2,1,0:T(4,128)(2,1)S(1)}, u32[]{:S(2)}, u32[]{:S(2)}) async-start(bf16[128,4,2048]{2,1,0:T(4,128)(2,1)} %reshape.231), calls=%async_computation.1 | async-start | bytes 4194304 | tf_op jit(solution)/shard_map/all_to_all | solution.py:167
  129.4 13.9 %all-to-all-start.2 = ((f32[128,1,4]{2,1,0:T(1,128)}), f32[128,1,4]{2,1,0:T(1,128)S(1)}, u32[]{:S(2)}, u32[]{:S(2)}) async-start(f32[128,1,4]{2,1,0:T(1,128)} %bitcast.8), calls=%async_computation.2 | async-start | bytes 131072 | tf_op jit(solution)/shard_map/all_to_all | solution.py:176
Sparse Core Ops, SparseCore 0:
  10.1 74.7 all-gather.1

commit v4 on v3

--- a/solution.py
+++ b/solution.py
@@ -122,14 +122,19 @@
     iy, iz, ix, ic = (lax.axis_index(a) for a in ALL)
     me = ((iy * nz + iz) * nx + ix) * nc + ic
     salt_word = noise_salt[0]
-    own_rows = gather(embeddings, ("y",), 0)
-    other_rows = lax.ppermute(own_rows, "c", [(i, (i + 1) % nc) for i in range(nc)])
-    group = jnp.concatenate([own_rows, other_rows], axis=0)
+    swap = [(i, (i + 1) % nc) for i in range(nc)]
+    ring_y = [
+        embeddings if s == 0 else lax.ppermute(embeddings, "y", [(i, (i + s) % ny) for i in range(ny)])
+        for s in range(ny)
+    ]
+    group = jnp.concatenate(ring_y + [lax.ppermute(p, "c", swap) for p in ring_y], axis=0)
     piece = lax.all_gather(centroids, ("z", "x"), axis=0, tiled=True)
     src_c = jnp.stack([ic, (ic + nc - 1) % nc])
-    src_y = jnp.arange(ny, dtype=jnp.int32)
+    src_y = (iy - jnp.arange(ny, dtype=jnp.int32)) % ny
     row_dev = ((src_y[None, :] * nz + iz) * nx + ix) * nc + src_c[:, None]
     group_ids = (row_dev[:, :, None] * rows_dev + jnp.arange(rows_dev, dtype=jnp.int32)).reshape(-1)
+    canonical = ((src_c[:, None] * ny + src_y[None, :])[:, :, None] * rows_dev
+                 + jnp.arange(rows_dev, dtype=jnp.int32)).reshape(-1)
     cpos = jnp.arange(nz * nx * cent_dev, dtype=jnp.int32)
     cent_dev_ids = ((iy * nz + cpos // (nx * cent_dev)) * nx + cpos // cent_dev % nx) * nc + ic
     cent_ids = cent_dev_ids * cent_dev + cpos % cent_dev
@@ -150,7 +155,7 @@
         return (jnp.maximum(carry, jnp.max(perturbed, axis=1)), None)
 
     result, unused = lax.scan(step, initial, (tiles, noise_tiles))
-    result = jnp.roll(result, ic * (ny * rows_dev))
+    result = jnp.zeros_like(result).at[canonical].set(result, unique_indices=True)
     merged = lax.pmax(result, ("c", "y"))
     perturbed_max = lax.dynamic_slice_in_dim(merged, (ic * ny + iy) * rows_dev, rows_dev)
     assigned = cluster[:, 0]

time: 217 us -> 212 us (0.977)
  Pallas kernels: 50.3 us -> 0 us
  waiting for transfers between devices: 28.8 us -> 53.1 us
  local copies, waits for them, and re-layouts: 15.8 us -> 39.2 us
  other arithmetic: 27 us -> 18.8 us
  starting transfers between devices: 22 us -> 28.2 us
    pallas_call x1 -> x0, Pallas kernels: 50.3 us -> none  [gather(): pl.pallas_call(functools.partial(gather_kernel, axes, sizes), out_shape=j...]
    all_to_all x1, waiting for transfers between devices: 2.98 us -> 17.2 us  [shards(): lax.all_to_all(present.reshape(devices, capacity), ALL, split_axis=0, con...]
    unnamed x1 -> x10, local copies, waits for them, and re-layouts: 0.01 us -> 13.8 us
    all_to_all x1, waiting for transfers between devices: 17.5 us -> 27.4 us  [shards(): lax.all_to_all(outgoing.reshape(devices, capacity, feature_dim), ALL, spl...]
    concatenate x2 -> x0, other arithmetic: 8.36 us -> none  [the longest x1 8.34 us: shards(): group = jnp.concatenate([own_rows, other_rows], axis=0)]
    scatter x0 -> x1, local copies, waits for them, and re-layouts: none -> 8.05 us  [shards(): jnp.zeros_like(result).at[canonical].set(result, unique_indices=True)]
    ppermute x1 -> x7, starting transfers between devices: 1.63 us -> 9.08 us  [the longest x3 5.88 us: shards(): lax.ppermute(embeddings, 'y', [(i, (i + s) % ny) for i in range(ny)])]
    concatenate x0 -> x1, local copies, waits for them, and re-layouts: none -> 2.33 us  [shards(): jnp.concatenate(ring_y + [lax.ppermute(p, 'c', swap) for p in ring_y], ax...]
  transfers between devices with their start and end apart: 5 -> 11, of which waited for: 3 -> 3; matrix products, arithmetic and copies ran while one was open for 21% -> 25% of each run, Pallas kernels for 23% -> 0%
where the time goes in v4:
time: 212 us
  waiting for transfers between devices  53.1 us (25%)
  matrix products  42.4 us (20%)
  local copies, waits for them, and re-layouts  39.2 us (18%)
  starting transfers between devices  28.2 us (13%)
  other arithmetic  18.8 us (9%)
  between operations  15.5 us (7%)
  blocking collectives  14.2 us (7%)
    dot_general x4, matrix products, step(): lax.dot_general(group, tile, (((1,), (1,)), ((), ())), preferred_element_...  38.8 us
    all_to_all x1, waiting for transfers between devices, shards(): lax.all_to_all(outgoing.reshape(devices, capacity, feature_dim), ALL, spl...  27.4 us
    all_to_all x1, waiting for transfers between devices, shards(): lax.all_to_all(present.reshape(devices, capacity), ALL, split_axis=0, con...  17.2 us
    pmax x1, blocking collectives, shards(): merged = lax.pmax(result, ('c', 'y'))  14.2 us
    unnamed x10, local copies, waits for them, and re-layouts  13.8 us
    neg x1, other arithmetic, gumbel_noise(): return -jnp.log(-jnp.log(uniform))  12.2 us
    scatter x1, local copies, waits for them, and re-layouts, shards(): jnp.zeros_like(result).at[canonical].set(result, unique_indices=True)  8.05 us
    all_to_all x1, waiting for transfers between devices, shards(): lax.all_to_all(scores.reshape(devices, capacity), ALL, split_axis=0, conc...  7.74 us
  transfers between devices with their start and end apart: 11, of which 3 were waited for; matrix products, arithmetic and copies ran while one was open for 25% of the time, Pallas kernels for 0%

profile of v4, /device:TPU:1, one launch (start us, length us, event | category | flops | bytes accessed | tf_op | source)
XLA Modules:
  0.0 211.6 jit_solution(18075964598048970508)
XLA Ops:
  7.2 0.0 all-gather.2.cloned.1.call-start
  7.2 0.7 all-gather.2.cloned.1.call-update
  7.9 2.2 %collective-permute-start = (bf16[256,2048]{1,0:T(8,128)(2,1)}, bf16[256,2048]{1,0:T(8,128)(2,1)}, u32[]{:S(2)}, u32[]{:S(2)}) collective-permute-start(bf16[256,2048]{1,0:T(8,128)(2,1)} %param.6), channel_id=1, source_target_pairs={{0,32},{32,64},{64,96},{96,0},{1,33},{33,65},{65,97},{97,1},{2,34}... | collective-permute-start | bytes 3145736 | tf_op jit(solution)/shard_map/ppermute | solution.py:127
  10.1 2.6 %collective-permute-start.1 = (bf16[256,2048]{1,0:T(8,128)(2,1)}, bf16[256,2048]{1,0:T(8,128)(2,1)}, u32[]{:S(2)}, u32[]{:S(2)}) collective-permute-start(bf16[256,2048]{1,0:T(8,128)(2,1)} %param.6), channel_id=1, source_target_pairs={{0,64},{32,96},{64,0},{96,32},{1,65},{33,97},{65,1},{97,33},{2,66}... | collective-permute-start | bytes 3145736 | tf_op jit(solution)/shard_map/ppermute | solution.py:127
  12.7 1.1 collective-permute-start.2
  13.8 1.5 collective-permute-start.3
  15.3 0.9 convert_reduce_fusion
  16.3 0.7 compare_select_fusion.1
  17.0 2.2 %scatter_custom_fusion.1 = bf16[512]{0:T(512)(128)(2,1)S(1)} fusion(s32[256]{0:T(256)S(1)} %bitcast.39, bf16[256]{0:T(256)(128)(2,1)S(1)} %broadcast.401, bf16[]{:T(256)} %constant.166.clone.1), kind=kCustom, calls=%fused_computation.90 | custom fusion | bytes 1026 | tf_op jit(solution)/shard_map/scatter | solution.py:170
  19.1 0.7 all_to_all.17
  19.9 7.6 %all-to-all-start = ((bf16[128,1,4]{2,1,0:T(2,128)(2,1)}), bf16[128,1,4]{2,1,0:T(2,128)(2,1)S(1)}, u32[]{:S(2)}, u32[]{:S(2)}) async-start(bf16[128,1,4]{2,1,0:T(2,128)(2,1)} %all_to_all.17), calls=%async_computation | async-start | bytes 131072 | tf_op jit(solution)/shard_map/all_to_all | solution.py:175
  28.1 0.1 broadcast_multiply_fusion.1
  28.2 0.1 add_multiply_fusion
  28.3 0.1 multiply_bitcast_fusion
  28.4 0.1 add_multiply_fusion.1
  28.5 12.2 %fusion.13 = f32[4,2048,512]{1,2,0:T(8,128)} fusion(s32[]{:T(128)} %bitcast.34, s32[4,512]{1,0:T(4,128)S(1)} %fusion.36, s32[2048]{0:T(1024)S(1)} %bitcast.35), kind=kLoop, calls=%fused_computation.22 | loop fusion | flops 67108864 | bytes 16793604 | tf_op jit(solution)/shard_map/neg | solution.py:30
  40.6 0.1 iota_add_fusion
  40.7 2.8 %scatter_custom_fusion.2 = bf16[512,2048]{1,0:T(8,128)(2,1)S(1)} fusion(s32[256]{0:T(256)S(1)} %bitcast.40, bf16[256,2048]{1,0:T(8,128)(2,1)S(1)} %copy-done, bf16[]{:T(256)} %constant.166.clone.1), kind=kCustom, calls=%fused_computation.32 | custom fusion | bytes 2097154 | tf_op jit(solution)/shard_map/scatter | solution.py:166
  43.5 2.2 %reshape.318 = bf16[128,4,2048]{2,1,0:T(4,128)(2,1)} reshape(bf16[512,2048]{1,0:T(8,128)(2,1)S(1)} %scatter_custom_fusion.2) | data formatting | bytes 4194304 | tf_op jit(solution)/shard_map/reshape | solution.py:173
  45.8 17.2 %all-to-all-done = bf16[128,1,4]{2,1,0:T(2,128)(2,1)S(1)} async-done(((bf16[128,1,4]{2,1,0:T(2,128)(2,1)}), bf16[128,1,4]{2,1,0:T(2,128)(2,1)S(1)}, u32[]{:S(2)}, u32[]{:S(2)}) %all-to-all-start) | async-done | bytes 1056 | tf_op jit(solution)/shard_map/all_to_all | solution.py:175
  63.0 7.5 %all-to-all-start.1 = ((bf16[128,4,2048]{2,1,0:T(4,128)(2,1)}), bf16[128,4,2048]{2,1,0:T(4,128)(2,1)S(1)}, u32[]{:S(2)}, u32[]{:S(2)}) async-start(bf16[128,4,2048]{2,1,0:T(4,128)(2,1)} %reshape.318), calls=%async_computation.1 | async-start | bytes 4194304 | tf_op jit(solution)/shard_map/all_to_all | solution.py:172
  70.5 1.1 constant_dynamic-update-slice_fusion.7
  71.6 0.3 broadcast_compare_fusion
  71.9 0.1 gt.22
  72.0 0.1 copy.15
  72.1 0.1 copy.16
  72.3 0.2 fusion.23
  72.4 0.0 collective-permute-done
  72.4 1.1 collective-permute-start.4
  73.6 0.0 collective-permute-done.1
  73.6 0.1 collective-permute-start.5
  73.7 0.0 collective-permute-done.2
  73.7 0.4 collective-permute-start.6
  74.1 2.3 %constant_dynamic-update-slice_fusion.6 = bf16[2048,2048]{1,0:T(8,128)(2,1)} fusion(bf16[2048,2048]{1,0:T(8,128)(2,1)} %constant_dynamic-update-slice_fusion.7, bf16[256,2048]{1,0:T(8,128)(2,1)} %collective-permute-done), kind=kLoop, calls=%fused_computation.49 | loop fusion | bytes 2097152
  76.4 2.3 %constant_dynamic-update-slice_fusion.5 = bf16[2048,2048]{1,0:T(8,128)(2,1)} fusion(bf16[2048,2048]{1,0:T(8,128)(2,1)} %constant_dynamic-update-slice_fusion.6, bf16[256,2048]{1,0:T(8,128)(2,1)} %collective-permute-done.1), kind=kLoop, calls=%fused_computation.48 | loop fusion | bytes 2097152
  78.7 2.3 %constant_dynamic-update-slice_fusion.4 = bf16[2048,2048]{1,0:T(8,128)(2,1)} fusion(bf16[2048,2048]{1,0:T(8,128)(2,1)} %constant_dynamic-update-slice_fusion.5, bf16[256,2048]{1,0:T(8,128)(2,1)} %collective-permute-done.2), kind=kLoop, calls=%fused_computation.47 | loop fusion | bytes 2097152
  81.0 2.4 %constant_dynamic-update-slice_fusion.3 = bf16[2048,2048]{1,0:T(8,128)(2,1)} fusion(bf16[2048,2048]{1,0:T(8,128)(2,1)} %constant_dynamic-update-slice_fusion.4, bf16[256,2048]{1,0:T(8,128)(2,1)} %collective-permute-done.3), kind=kLoop, calls=%fused_computation.46 | loop fusion | bytes 2097152
  83.4 27.4 %all-to-all-done.1 = bf16[128,4,2048]{2,1,0:T(4,128)(2,1)S(1)} async-done(((bf16[128,4,2048]{2,1,0:T(4,128)(2,1)}), bf16[128,4,2048]{2,1,0:T(4,128)(2,1)S(1)}, u32[]{:S(2)}, u32[]{:S(2)}) %all-to-all-start.1) | async-done | bytes 2097184 | tf_op jit(solution)/shard_map/all_to_all | solution.py:172
  110.9 2.1 fusion.15
  113.0 0.1 rsqrt.18
  113.1 2.1 reshape.319
  115.2 3.6 %fusion.19 = f32[512]{0:T(512)S(1)} fusion(bf16[512,2048]{1,0:T(8,128)(2,1)} %reshape.319, f32[512]{0:T(512)S(1)} %rsqrt.18, pred[512]{0:T(512)(128)(4,1)S(1)} %gt.22), kind=kOutput, calls=%fused_computation.31 | convolution fusion | flops 1075576320 | bytes 2101760 | tf_op jit(solution)/shard_map/dot_general | solution.py:103
  118.8 0.7 select_n.108
  119.5 4.1 %all-to-all-start.2 = ((f32[128,1,4]{2,1,0:T(1,128)}), f32[128,1,4]{2,1,0:T(1,128)S(1)}, u32[]{:S(2)}, u32[]{:S(2)}) async-start(f32[128,1,4]{2,1,0:T(1,128)} %bitcast.8), calls=%async_computation.2 | async-start | bytes 131072 | tf_op jit(solution)/shard_map/all_to_all | solution.py:181
  123.6 0.6 multiply_reduce_fusion
  124.9 0.6 broadcast_multiply_fusion
  125.5 7.7 %all-to-all-done.2 = f32[128,1,4]{2,1,0:T(1,128)S(1)} async-done(((f32[128,1,4]{2,1,0:T(1,128)}), f32[128,1,4]{2,1,0:T(1,128)S(1)}, u32[]{:S(2)}, u32[]{:S(2)}) %all-to-all-start.2) | async-done | bytes 2080 | tf_op jit(solution)/shard_map/all_to_all | solution.py:181
  133.2 0.5 broadcast.429
  133.7 0.8 reduce.7
  134.6 0.1 reshape.320
  134.7 2.5 %gather_fusion = f32[256]{0:T(256)} fusion(f32[512]{0:T(512)S(1)} %reshape.320, s32[1024]{0:T(1024)S(1)} %pad_clamp_fusion), kind=kCustom, calls=%fused_computation | custom fusion | bytes 3072 | tf_op jit(solution)/shard_map/gather | solution.py:184
  137.2 1.0 constant_dynamic-update-slice_fusion.2
  138.2 0.0 collective-permute-done.5
  138.2 2.3 %constant_dynamic-update-slice_fusion.1 = bf16[2048,2048]{1,0:T(8,128)(2,1)} fusion(bf16[2048,2048]{1,0:T(8,128)(2,1)} %constant_dynamic-update-slice_fusion.2, bf16[256,2048]{1,0:T(8,128)(2,1)} %collective-permute-done.5), kind=kLoop, calls=%fused_computation.44 | loop fusion | bytes 2097152
  140.5 0.0 collective-permute-done.6
  140.5 2.3 %constant_dynamic-update-slice_fusion = bf16[2048,2048]{1,0:T(8,128)(2,1)} fusion(bf16[2048,2048]{1,0:T(8,128)(2,1)} %constant_dynamic-update-slice_fusion.1, bf16[256,2048]{1,0:T(8,128)(2,1)} %collective-permute-done.6), kind=kLoop, calls=%fused_computation.43 | loop fusion | bytes 2097152 | tf_op jit(solution)/shard_map/concatenate | solution.py:130
  142.9 39.0 %while.11 = (s32[]{:T(128)}, f32[2048]{0:T(1024)S(1)}, bf16[4,512,2048]{2,1,0:T(8,128)(2,1)}, bf16[2048,2048]{1,0:T(8,128)(2,1)}, f32[4,2048,512]{1,2,0:T(8,128)}, /*index=5*/s32[]{:T(128)}, s32[]{:T(128)}) while((s32[]{:T(128)}, f32[2048]{0:T(1024)S(1)}, bf16[4,512,2048]{2,1,0:T(8,128)(2,1)}, bf16[2048,2048]{1,0:T(8,128)(2,1)}, ...), condition=%wide.region_2.3_spmd.clone, body=%wide.region_0.2_spmd.clone.sunk | while | flops 4298115072 | bytes 14713951 | solution.py:157
  142.9 9.7 %fusion.53 = f32[2048]{0:T(1024)S(1)} fusion(f32[4,2048,512]{1,2,0:T(8,128)} %get-tuple-element.116, s32[]{:T(128)S(6)} %copy.27, bf16[2048,2048]{1,0:T(8,128)(2,1)} %get-tuple-element.115, bf16[4,512,2048]{2,1,0:T(8,128)(2,1)} %get-tuple-element.114), kind=kOutput, calls=%fused_computation.5.clone.1 | convolution fusion | flops 4298110976 | bytes 14689280 | tf_op jit(solution)/shard_map/while/body/eval_jaxpr/dot_general | solution.py:151
  152.6 9.7 %fusion.53 = f32[2048]{0:T(1024)S(1)} fusion(f32[4,2048,512]{1,2,0:T(8,128)} %get-tuple-element.116, s32[]{:T(128)S(6)} %copy.27, bf16[2048,2048]{1,0:T(8,128)(2,1)} %get-tuple-element.115, bf16[4,512,2048]{2,1,0:T(8,128)(2,1)} %get-tuple-element.114), kind=kOutput, calls=%fused_computation.5.clone.1 | convolution fusion | flops 4298110976 | bytes 14689280 | tf_op jit(solution)/shard_map/while/body/eval_jaxpr/dot_general | solution.py:151
  162.4 9.7 %fusion.53 = f32[2048]{0:T(1024)S(1)} fusion(f32[4,2048,512]{1,2,0:T(8,128)} %get-tuple-element.116, s32[]{:T(128)S(6)} %copy.27, bf16[2048,2048]{1,0:T(8,128)(2,1)} %get-tuple-element.115, bf16[4,512,2048]{2,1,0:T(8,128)(2,1)} %get-tuple-element.114), kind=kOutput, calls=%fused_computation.5.clone.1 | convolution fusion | flops 4298110976 | bytes 14689280 | tf_op jit(solution)/shard_map/while/body/eval_jaxpr/dot_general | solution.py:151
  172.1 9.7 %fusion.53 = f32[2048]{0:T(1024)S(1)} fusion(f32[4,2048,512]{1,2,0:T(8,128)} %get-tuple-element.116, s32[]{:T(128)S(6)} %copy.27, bf16[2048,2048]{1,0:T(8,128)(2,1)} %get-tuple-element.115, bf16[4,512,2048]{2,1,0:T(8,128)(2,1)} %get-tuple-element.114), kind=kOutput, calls=%fused_computation.5.clone.1 | convolution fusion | flops 4298110976 | bytes 14689280 | tf_op jit(solution)/shard_map/while/body/eval_jaxpr/dot_general | solution.py:151
  181.9 8.0 %scatter_custom_fusion = f32[2048]{0:T(1024)S(1)} fusion(s32[2048]{0:T(1024)S(1)} %bitcast.37, f32[2048]{0:T(1024)S(1)} %get-tuple-element.30, f32[]{:T(128)} %constant.138.clone.1), kind=kCustom, calls=%fused_computation.80 | custom fusion | bytes 8196 | tf_op jit(solution)/shard_map/scatter | solution.py:158
  189.9 14.2 %pmax.7 = f32[2048]{0:T(1024)S(1)} all-reduce(f32[2048]{0:T(1024)S(1)} %scatter_custom_fusion), channel_id=1, replica_groups=mesh['y'=4,'z'=4,'x'=4,'c'=2] {'c','y'}, use_global_device_ids=true, to_apply=%region_4.5 | all-reduce | flops 2048 | bytes 16384 | tf_op jit(solution)/shard_map/pmax | solution.py:159
  204.1 0.6 dynamic_slice.11
  (19 shorter events, 0.2 us)
Async XLA Ops:
  7.2 135.7 %all-gather.2.cloned.1.call-start = ((), (), s32[]{:S(2)}) async-start(), calls=%async_computation.3 | async-start | bytes 8912896 | tf_op jit(solution)/shard_map/all_gather | solution.py:131
  7.9 64.5 %collective-permute-start = (bf16[256,2048]{1,0:T(8,128)(2,1)}, bf16[256,2048]{1,0:T(8,128)(2,1)}, u32[]{:S(2)}, u32[]{:S(2)}) collective-permute-start(bf16[256,2048]{1,0:T(8,128)(2,1)} %param.6), channel_id=1, source_target_pairs={{0,32},{32,64},{64,96},{96,0},{1,33},{33,65},{65,97},{97,1},{2,34}... | collective-permute-start | bytes 3145736 | tf_op jit(solution)/shard_map/ppermute | solution.py:127
  10.1 63.5 %collective-permute-start.1 = (bf16[256,2048]{1,0:T(8,128)(2,1)}, bf16[256,2048]{1,0:T(8,128)(2,1)}, u32[]{:S(2)}, u32[]{:S(2)}) collective-permute-start(bf16[256,2048]{1,0:T(8,128)(2,1)} %param.6), channel_id=1, source_target_pairs={{0,64},{32,96},{64,0},{96,32},{1,65},{33,97},{65,1},{97,33},{2,66}... | collective-permute-start | bytes 3145736 | tf_op jit(solution)/shard_map/ppermute | solution.py:127
  12.7 61.0 %collective-permute-start.2 = (bf16[256,2048]{1,0:T(8,128)(2,1)}, bf16[256,2048]{1,0:T(8,128)(2,1)}, u32[]{:S(2)}, u32[]{:S(2)}) collective-permute-start(bf16[256,2048]{1,0:T(8,128)(2,1)} %param.6), channel_id=1, source_target_pairs={{0,96},{32,0},{64,32},{96,64},{1,97},{33,1},{65,33},{97,65},{2,98}... | collective-permute-start | bytes 3145736 | tf_op jit(solution)/shard_map/ppermute | solution.py:127
  13.8 67.3 %collective-permute-start.3 = (bf16[256,2048]{1,0:T(8,128)(2,1)}, bf16[256,2048]{1,0:T(8,128)(2,1)}, u32[]{:S(2)}, u32[]{:S(2)}) collective-permute-start(bf16[256,2048]{1,0:T(8,128)(2,1)} %param.6), channel_id=1, source_target_pairs={{0,1},{1,0},{2,3},{3,2},{4,5},{5,4},{6,7},{7,6},{8,9},{9,8},{10,11... | collective-permute-start | bytes 3145736 | tf_op jit(solution)/shard_map/ppermute | solution.py:130
  19.9 43.1 %all-to-all-start = ((bf16[128,1,4]{2,1,0:T(2,128)(2,1)}), bf16[128,1,4]{2,1,0:T(2,128)(2,1)S(1)}, u32[]{:S(2)}, u32[]{:S(2)}) async-start(bf16[128,1,4]{2,1,0:T(2,128)(2,1)} %all_to_all.17), calls=%async_computation | async-start | bytes 131072 | tf_op jit(solution)/shard_map/all_to_all | solution.py:175
  28.5 12.2 %copy-start = (bf16[256,2048]{1,0:T(8,128)(2,1)S(1)}, bf16[256,2048]{1,0:T(8,128)(2,1)}, u32[]{:S(2)}) copy-start(bf16[256,2048]{1,0:T(8,128)(2,1)} %param.6) | copy-start | bytes 3145732
  63.0 47.9 %all-to-all-start.1 = ((bf16[128,4,2048]{2,1,0:T(4,128)(2,1)}), bf16[128,4,2048]{2,1,0:T(4,128)(2,1)S(1)}, u32[]{:S(2)}, u32[]{:S(2)}) async-start(bf16[128,4,2048]{2,1,0:T(4,128)(2,1)} %reshape.318), calls=%async_computation.1 | async-start | bytes 4194304 | tf_op jit(solution)/shard_map/all_to_all | solution.py:172
  72.4 64.8 %collective-permute-start.4 = (bf16[256,2048]{1,0:T(8,128)(2,1)}, bf16[256,2048]{1,0:T(8,128)(2,1)S(1)}, u32[]{:S(2)}, u32[]{:S(2)}) collective-permute-start(bf16[256,2048]{1,0:T(8,128)(2,1)} %collective-permute-done), channel_id=1, source_target_pairs={{0,1},{1,0},{2,3},{3,2},{4,5},{5,4},{6,7},{7,6},{8,9},{9,8},{10,11... | collective-permute-start | bytes 3145736 | tf_op jit(solution)/shard_map/ppermute | solution.py:130
  73.6 64.7 %collective-permute-start.5 = (bf16[256,2048]{1,0:T(8,128)(2,1)}, bf16[256,2048]{1,0:T(8,128)(2,1)}, u32[]{:S(2)}, u32[]{:S(2)}) collective-permute-start(bf16[256,2048]{1,0:T(8,128)(2,1)} %collective-permute-done.1), channel_id=1, source_target_pairs={{0,1},{1,0},{2,3},{3,2},{4,5},{5,4},{6,7},{7,6},{8,9},{9,8},{10,11... | collective-permute-start | bytes 3145736 | tf_op jit(solution)/shard_map/ppermute | solution.py:130
  73.7 66.9 %collective-permute-start.6 = (bf16[256,2048]{1,0:T(8,128)(2,1)}, bf16[256,2048]{1,0:T(8,128)(2,1)}, u32[]{:S(2)}, u32[]{:S(2)}) collective-permute-start(bf16[256,2048]{1,0:T(8,128)(2,1)} %collective-permute-done.2), channel_id=1, source_target_pairs={{0,1},{1,0},{2,3},{3,2},{4,5},{5,4},{6,7},{7,6},{8,9},{9,8},{10,11... | collective-permute-start | bytes 3145736 | tf_op jit(solution)/shard_map/ppermute | solution.py:130
  119.5 13.7 %all-to-all-start.2 = ((f32[128,1,4]{2,1,0:T(1,128)}), f32[128,1,4]{2,1,0:T(1,128)S(1)}, u32[]{:S(2)}, u32[]{:S(2)}) async-start(f32[128,1,4]{2,1,0:T(1,128)} %bitcast.8), calls=%async_computation.2 | async-start | bytes 131072 | tf_op jit(solution)/shard_map/all_to_all | solution.py:181
Sparse Core Ops, SparseCore 0:
  10.1 92.8 all-gather.1

commit v5 on v4

--- a/solution.py
+++ b/solution.py
@@ -133,8 +133,6 @@
     src_y = (iy - jnp.arange(ny, dtype=jnp.int32)) % ny
     row_dev = ((src_y[None, :] * nz + iz) * nx + ix) * nc + src_c[:, None]
     group_ids = (row_dev[:, :, None] * rows_dev + jnp.arange(rows_dev, dtype=jnp.int32)).reshape(-1)
-    canonical = ((src_c[:, None] * ny + src_y[None, :])[:, :, None] * rows_dev
-                 + jnp.arange(rows_dev, dtype=jnp.int32)).reshape(-1)
     cpos = jnp.arange(nz * nx * cent_dev, dtype=jnp.int32)
     cent_dev_ids = ((iy * nz + cpos // (nx * cent_dev)) * nx + cpos // cent_dev % nx) * nc + ic
     cent_ids = cent_dev_ids * cent_dev + cpos % cent_dev
@@ -155,28 +153,28 @@
         return (jnp.maximum(carry, jnp.max(perturbed, axis=1)), None)
 
     result, unused = lax.scan(step, initial, (tiles, noise_tiles))
-    result = jnp.zeros_like(result).at[canonical].set(result, unique_indices=True)
-    merged = lax.pmax(result, ("c", "y"))
-    perturbed_max = lax.dynamic_slice_in_dim(merged, (ic * ny + iy) * rows_dev, rows_dev)
+    blocks = result.reshape(nc, ny, rows_dev)
+    best = blocks[0, 0]
+    for sc in range(nc):
+        for sy in range(ny):
+            if sc == 0 and sy == 0:
+                continue
+            perm = [(yy * nc + cc, (yy - sy) % ny * nc + (cc - sc) % nc) for yy in range(ny) for cc in range(nc)]
+            best = jnp.maximum(best, lax.ppermute(blocks[sc, sy], ("y", "c"), perm))
+    perturbed_max = best
     assigned = cluster[:, 0]
     order = jnp.arange(rows_dev, dtype=jnp.int32)
     same = (assigned[:, None] == assigned[None, :]) & (order[None, :] < order[:, None])
     rank = jnp.sum(same.astype(jnp.int32), axis=1)
     slot = assigned * capacity + rank
-    outgoing = jnp.zeros((devices * capacity, feature_dim), jnp.bfloat16).at[slot].set(embeddings)
-    present = (
-        jnp.zeros((devices * capacity,), jnp.bfloat16)
-        .at[slot]
-        .set(jnp.ones((rows_dev,), jnp.bfloat16))
-    )
+    flag_width = 128
+    tagged = jnp.concatenate([embeddings, jnp.ones((rows_dev, flag_width), jnp.bfloat16)], axis=1)
+    outgoing = jnp.zeros((devices * capacity, feature_dim + flag_width), jnp.bfloat16).at[slot].set(tagged)
     received = lax.all_to_all(
-        outgoing.reshape(devices, capacity, feature_dim), ALL, split_axis=0, concat_axis=0, tiled=True
-    )
-    arrived = lax.all_to_all(
-        present.reshape(devices, capacity), ALL, split_axis=0, concat_axis=0, tiled=True
-    )
-    members = received.reshape(devices * capacity, feature_dim)
-    valid = arrived.reshape(devices * capacity) > 0.5
+        outgoing.reshape(devices, capacity, feature_dim + flag_width), ALL, split_axis=0, concat_axis=0, tiled=True
+    ).reshape(devices * capacity, feature_dim + flag_width)
+    members = received[:, :feature_dim]
+    valid = received[:, feature_dim] > 0.5
     scores, center = cluster_stats(members, valid)
     returned = lax.all_to_all(
         scores.reshape(devices, capacity), ALL, split_axis=0, concat_axis=0, tiled=True

time: 212 us -> 172 us (0.81)
  waiting for transfers between devices: 53.1 us -> 31 us
  blocking collectives: 14.2 us -> 0 us
  local copies, waits for them, and re-layouts: 39.2 us -> 25.4 us
  starting transfers between devices: 28.2 us -> 37.1 us
    all_to_all x2 -> x1, waiting for transfers between devices: 44.6 us -> 0.01 us  [shards(): lax.all_to_all(outgoing.reshape(devices, capacity, feature_dim + flag_wid...]
    ppermute x3, waiting for transfers between devices: 0.01 us -> 30.3 us  [shards(): lax.ppermute(embeddings, 'y', [(i, (i + s) % ny) for i in range(ny)])]
    pmax x1 -> x0, blocking collectives: 14.2 us -> none  [shards(): merged = lax.pmax(result, ('c', 'y'))]
    scatter x3 -> x1, local copies, waits for them, and re-layouts: 13 us -> 3.63 us  [shards(): jnp.zeros((devices * capacity, feature_dim + flag_width), jnp.bfloat16)]
    ppermute x0 -> x7, starting transfers between devices: none -> 8.54 us  [shards(): best = jnp.maximum(best, lax.ppermute(blocks[sc, sy], ('y', 'c'), perm))]
    all_to_all x1, waiting for transfers between devices: 7.74 us -> 0.01 us  [shards(): lax.all_to_all(scores.reshape(devices, capacity), ALL, split_axis=0, conc...]
    all_to_all x2 -> x1, starting transfers between devices: 15 us -> 7.56 us  [shards(): lax.all_to_all(outgoing.reshape(devices, capacity, feature_dim + flag_wid...]
    all_to_all x1, starting transfers between devices: 4.08 us -> 9.7 us  [shards(): lax.all_to_all(scores.reshape(devices, capacity), ALL, split_axis=0, conc...]
  transfers between devices with their start and end apart: 11 -> 17, of which waited for: 3 -> 1; matrix products, arithmetic and copies ran while one was open for 25% -> 51% of each run, Pallas kernels for 0% -> 0%
where the time goes in v5:
time: 172 us
  matrix products  42.5 us (25%)
  starting transfers between devices  37.1 us (22%)
  waiting for transfers between devices  31 us (18%)
  local copies, waits for them, and re-layouts  25.4 us (15%)
  other arithmetic  20.4 us (12%)
  between operations  15.5 us (9%)
    dot_general x4, matrix products, step(): lax.dot_general(group, tile, (((1,), (1,)), ((), ())), preferred_element_...  38.8 us
    ppermute x3, waiting for transfers between devices, shards(): lax.ppermute(embeddings, 'y', [(i, (i + s) % ny) for i in range(ny)])  30.3 us
    unnamed x10, local copies, waits for them, and re-layouts  12.6 us
    neg x1, other arithmetic, gumbel_noise(): return -jnp.log(-jnp.log(uniform))  12.2 us
    all_to_all x1, starting transfers between devices, shards(): lax.all_to_all(scores.reshape(devices, capacity), ALL, split_axis=0, conc...  9.7 us
    ppermute x7, starting transfers between devices, shards(): best = jnp.maximum(best, lax.ppermute(blocks[sc, sy], ('y', 'c'), perm))  8.54 us
    all_to_all x1, starting transfers between devices, shards(): lax.all_to_all(outgoing.reshape(devices, capacity, feature_dim + flag_wid...  7.56 us
    ppermute x3, starting transfers between devices, shards(): lax.ppermute(embeddings, 'y', [(i, (i + s) % ny) for i in range(ny)])  5.88 us
  transfers between devices with their start and end apart: 17, of which 1 were waited for; matrix products, arithmetic and copies ran while one was open for 51% of the time, Pallas kernels for 0%

profile of v5, /device:TPU:1, one launch (start us, length us, event | category | flops | bytes accessed | tf_op | source)
XLA Modules:
  0.0 171.9 jit_solution(11611983352579418298)
XLA Ops:
  7.2 0.0 all-gather.2.cloned.1.call-start
  7.2 0.7 all-gather.2.cloned.1.call-update
  7.9 2.2 %collective-permute-start = (bf16[256,2048]{1,0:T(8,128)(2,1)}, bf16[256,2048]{1,0:T(8,128)(2,1)}, u32[]{:S(2)}, u32[]{:S(2)}) collective-permute-start(bf16[256,2048]{1,0:T(8,128)(2,1)} %param.6), channel_id=1, source_target_pairs={{0,32},{32,64},{64,96},{96,0},{1,33},{33,65},{65,97},{97,1},{2,34}... | collective-permute-start | bytes 3145736 | tf_op jit(solution)/shard_map/ppermute | solution.py:127
  10.1 2.6 %collective-permute-start.1 = (bf16[256,2048]{1,0:T(8,128)(2,1)}, bf16[256,2048]{1,0:T(8,128)(2,1)}, u32[]{:S(2)}, u32[]{:S(2)}) collective-permute-start(bf16[256,2048]{1,0:T(8,128)(2,1)} %param.6), channel_id=1, source_target_pairs={{0,64},{32,96},{64,0},{96,32},{1,65},{33,97},{65,1},{97,33},{2,66}... | collective-permute-start | bytes 3145736 | tf_op jit(solution)/shard_map/ppermute | solution.py:127
  12.7 1.1 collective-permute-start.2
  13.8 1.5 collective-permute-start.3
  15.3 0.9 convert_reduce_fusion
  16.3 0.7 compare_select_fusion
  16.9 3.6 %scatter_custom_fusion = bf16[512,2176]{1,0:T(8,128)(2,1)S(1)} fusion(s32[256]{0:T(256)S(1)} %bitcast.42, bf16[256,2048]{1,0:T(8,128)(2,1)} %param.6, bf16[]{:T(256)} %constant.158.clone.1, bf16[]{:T(256)} %constant.157.clone.1), kind=kCustom, calls=%fused_computation.32 | custom fusion | bytes 3276804 | tf_op jit(solution)/shard_map/scatter | solution.py:172
  20.6 2.1 %reshape.212 = bf16[128,4,2176]{2,1,0:T(4,128)(2,1)} reshape(bf16[512,2176]{1,0:T(8,128)(2,1)S(1)} %scatter_custom_fusion) | data formatting | bytes 4456448 | tf_op jit(solution)/shard_map/reshape | solution.py:174
  22.7 7.6 %all-to-all-start = ((bf16[128,4,2176]{2,1,0:T(4,128)(2,1)}), bf16[128,4,2176]{2,1,0:T(4,128)(2,1)S(1)}, u32[]{:S(2)}, u32[]{:S(2)}) async-start(bf16[128,4,2176]{2,1,0:T(4,128)(2,1)} %reshape.212), calls=%async_computation | async-start | bytes 4456448 | tf_op jit(solution)/shard_map/all_to_all | solution.py:173
  31.0 0.1 pad_add_fusion
  31.1 0.1 add_multiply_fusion
  31.1 0.1 multiply_bitcast_fusion
  31.3 0.0 copy-start
  31.3 12.2 %fusion.13 = f32[4,2048,512]{1,2,0:T(8,128)} fusion(s32[]{:T(128)} %bitcast.38, s32[4,512]{1,0:T(4,128)S(1)} %fusion.50, s32[2048]{0:T(1024)S(1)} %bitcast.39), kind=kLoop, calls=%fused_computation.20 | loop fusion | flops 67108864 | bytes 16793604 | tf_op jit(solution)/shard_map/neg | solution.py:30
  43.5 1.1 constant_dynamic-update-slice_fusion.7
  44.6 0.0 collective-permute-done
  44.6 1.1 collective-permute-start.4
  45.7 30.3 %collective-permute-done.1 = bf16[256,2048]{1,0:T(8,128)(2,1)} collective-permute-done((bf16[256,2048]{1,0:T(8,128)(2,1)}, bf16[256,2048]{1,0:T(8,128)(2,1)}, u32[]{:S(2)}, u32[]{:S(2)}) %collective-permute-start.1) | collective-permute-done | bytes 1048608 | tf_op jit(solution)/shard_map/ppermute | solution.py:127
  76.0 2.7 %collective-permute-start.5 = (bf16[256,2048]{1,0:T(8,128)(2,1)}, bf16[256,2048]{1,0:T(8,128)(2,1)S(1)}, u32[]{:S(2)}, u32[]{:S(2)}) collective-permute-start(bf16[256,2048]{1,0:T(8,128)(2,1)} %collective-permute-done.1), channel_id=1, source_target_pairs={{0,1},{1,0},{2,3},{3,2},{4,5},{5,4},{6,7},{7,6},{8,9},{9,8},{10,11... | collective-permute-start | bytes 3145736 | tf_op jit(solution)/shard_map/ppermute | solution.py:130
  78.7 2.3 %constant_dynamic-update-slice_fusion.6 = bf16[2048,2048]{1,0:T(8,128)(2,1)} fusion(bf16[2048,2048]{1,0:T(8,128)(2,1)} %constant_dynamic-update-slice_fusion.7, bf16[256,2048]{1,0:T(8,128)(2,1)} %collective-permute-done), kind=kLoop, calls=%fused_computation.48 | loop fusion | bytes 2097152
  81.0 0.0 collective-permute-done.2
  81.0 0.0 collective-permute-start.6
  81.0 2.4 %constant_dynamic-update-slice_fusion.5 = bf16[2048,2048]{1,0:T(8,128)(2,1)} fusion(bf16[2048,2048]{1,0:T(8,128)(2,1)} %constant_dynamic-update-slice_fusion.6, bf16[256,2048]{1,0:T(8,128)(2,1)} %collective-permute-done.1), kind=kLoop, calls=%fused_computation.47 | loop fusion | bytes 2097152
  83.4 2.3 %constant_dynamic-update-slice_fusion.4 = bf16[2048,2048]{1,0:T(8,128)(2,1)} fusion(bf16[2048,2048]{1,0:T(8,128)(2,1)} %constant_dynamic-update-slice_fusion.5, bf16[256,2048]{1,0:T(8,128)(2,1)} %collective-permute-done.2), kind=kLoop, calls=%fused_computation.46 | loop fusion | bytes 2097152
  85.7 0.0 collective-permute-done.3
  85.7 2.4 %constant_dynamic-update-slice_fusion.3 = bf16[2048,2048]{1,0:T(8,128)(2,1)} fusion(bf16[2048,2048]{1,0:T(8,128)(2,1)} %constant_dynamic-update-slice_fusion.4, bf16[256,2048]{1,0:T(8,128)(2,1)} %collective-permute-done.3), kind=kLoop, calls=%fused_computation.45 | loop fusion | bytes 2097152
  88.1 0.0 collective-permute-done.4
  88.1 1.0 constant_dynamic-update-slice_fusion.2
  89.1 1.0 constant_dynamic-update-slice_fusion.1
  90.1 0.0 collective-permute-done.6
  90.2 1.1 constant_dynamic-update-slice_fusion
  91.2 2.1 %reshape.213 = bf16[512,2176]{1,0:T(8,128)(2,1)} reshape(bf16[128,4,2176]{2,1,0:T(4,128)(2,1)S(1)} %all-to-all-done) | data formatting | bytes 4456448 | tf_op jit(solution)/shard_map/reshape | solution.py:175
  93.3 1.1 compare_reduce_fusion
  94.4 0.2 fusion.37
  94.5 2.4 %fusion.15 = (f32[2048]{0:T(1024)S(1)}, f32[512]{0:T(512)S(1)}) fusion(pred[512]{0:T(512)(128)(4,1)S(1)} %compare_reduce_fusion, bf16[512,2176]{1,0:T(8,128)(2,1)} %reshape.213), kind=kLoop, calls=%fused_computation.24 | loop fusion | flops 5240320 | bytes 2107904 | tf_op jit(solution)/shard_map/reduce_sum | solution.py:111
  97.0 3.6 %fusion.30 = f32[512]{0:T(512)S(1)} fusion(bf16[512,2176]{1,0:T(8,128)(2,1)} %reshape.213, f32[512]{0:T(512)S(1)} %add_rsqrt_fusion, pred[512]{0:T(512)(128)(4,1)S(1)} %compare_reduce_fusion), kind=kOutput, calls=%fused_computation.31 | convolution fusion | flops 1075576320 | bytes 2103808 | tf_op jit(solution)/shard_map/dot_general | solution.py:103
  100.6 0.7 select_n.88
  101.3 9.7 %all-to-all-start.1 = ((f32[128,1,4]{2,1,0:T(1,128)}), f32[128,1,4]{2,1,0:T(1,128)S(1)}, u32[]{:S(2)}, u32[]{:S(2)}) async-start(f32[128,1,4]{2,1,0:T(1,128)} %bitcast.15), calls=%async_computation.1 | async-start | bytes 131072 | tf_op jit(solution)/shard_map/all_to_all | solution.py:179
  111.0 0.0 all-gather.2.cloned.1.call-done
  111.1 39.0 %while.11 = (s32[]{:T(128)}, f32[2048]{0:T(1024)S(1)}, bf16[4,512,2048]{2,1,0:T(8,128)(2,1)}, bf16[2048,2048]{1,0:T(8,128)(2,1)}, f32[4,2048,512]{1,2,0:T(8,128)}, /*index=5*/s32[]{:T(128)}, s32[]{:T(128)}) while((s32[]{:T(128)}, f32[2048]{0:T(1024)S(1)}, bf16[4,512,2048]{2,1,0:T(8,128)(2,1)}, bf16[2048,2048]{1,0:T(8,128)(2,1)}, ...), condition=%wide.region_2.3_spmd.clone, body=%wide.region_0.2_spmd.clone.sunk | while | flops 4298115072 | bytes 14713951 | solution.py:155
  111.1 9.7 %fusion.66 = f32[2048]{0:T(1024)S(1)} fusion(f32[4,2048,512]{1,2,0:T(8,128)} %get-tuple-element.118, s32[]{:T(128)S(6)} %copy.20, bf16[2048,2048]{1,0:T(8,128)(2,1)} %get-tuple-element.117, bf16[4,512,2048]{2,1,0:T(8,128)(2,1)} %get-tuple-element.116), kind=kOutput, calls=%fused_computation.3.clone.1 | convolution fusion | flops 4298110976 | bytes 14689280 | tf_op jit(solution)/shard_map/while/body/eval_jaxpr/dot_general | solution.py:149
  120.8 9.7 %fusion.66 = f32[2048]{0:T(1024)S(1)} fusion(f32[4,2048,512]{1,2,0:T(8,128)} %get-tuple-element.118, s32[]{:T(128)S(6)} %copy.20, bf16[2048,2048]{1,0:T(8,128)(2,1)} %get-tuple-element.117, bf16[4,512,2048]{2,1,0:T(8,128)(2,1)} %get-tuple-element.116), kind=kOutput, calls=%fused_computation.3.clone.1 | convolution fusion | flops 4298110976 | bytes 14689280 | tf_op jit(solution)/shard_map/while/body/eval_jaxpr/dot_general | solution.py:149
  130.6 9.7 %fusion.66 = f32[2048]{0:T(1024)S(1)} fusion(f32[4,2048,512]{1,2,0:T(8,128)} %get-tuple-element.118, s32[]{:T(128)S(6)} %copy.20, bf16[2048,2048]{1,0:T(8,128)(2,1)} %get-tuple-element.117, bf16[4,512,2048]{2,1,0:T(8,128)(2,1)} %get-tuple-element.116), kind=kOutput, calls=%fused_computation.3.clone.1 | convolution fusion | flops 4298110976 | bytes 14689280 | tf_op jit(solution)/shard_map/while/body/eval_jaxpr/dot_general | solution.py:149
  140.3 9.7 %fusion.66 = f32[2048]{0:T(1024)S(1)} fusion(f32[4,2048,512]{1,2,0:T(8,128)} %get-tuple-element.118, s32[]{:T(128)S(6)} %copy.20, bf16[2048,2048]{1,0:T(8,128)(2,1)} %get-tuple-element.117, bf16[4,512,2048]{2,1,0:T(8,128)(2,1)} %get-tuple-element.116), kind=kOutput, calls=%fused_computation.3.clone.1 | convolution fusion | flops 4298110976 | bytes 14689280 | tf_op jit(solution)/shard_map/while/body/eval_jaxpr/dot_general | solution.py:149
  150.1 1.7 collective-permute-start.13
  151.8 2.5 %collective-permute-start.12 = (f32[256]{0:T(256)S(1)}, f32[256]{0:T(256)S(1)}, u32[]{:S(2)}, u32[]{:S(2)}) collective-permute-start(f32[256]{0:T(256)S(1)} %bitcast.51), channel_id=1, source_target_pairs={{0,65},{1,64},{32,97},{33,96},{64,1},{65,0},{96,33},{97,32},{2,67}... | collective-permute-start | bytes 3080 | tf_op jit(solution)/shard_map/ppermute | solution.py:163
  154.3 0.6 multiply_reduce_fusion
  155.6 1.4 collective-permute-start.11
  157.0 0.2 collective-permute-start.10
  157.2 0.3 collective-permute-start.9
  157.5 0.0 collective-permute-done.13
  157.5 0.9 collective-permute-start.8
  158.4 1.5 collective-permute-start.7
  159.9 0.6 broadcast_multiply_fusion
  160.5 0.5 broadcast.349
  161.0 0.8 reduce.5
  161.9 0.1 reshape.214
  162.0 2.5 %gather_fusion = f32[256]{0:T(256)} fusion(f32[512]{0:T(512)S(1)} %reshape.214, s32[1024]{0:T(1024)S(1)} %pad_clamp_fusion), kind=kCustom, calls=%fused_computation | custom fusion | bytes 3072 | tf_op jit(solution)/shard_map/gather | solution.py:182
  164.5 0.0 collective-permute-done.11
  164.5 0.0 collective-permute-done.10
  164.5 0.0 collective-permute-done.8
  164.5 0.6 maximum_maximum_fusion
  (20 shorter events, 0.1 us)
Async XLA Ops:
  7.2 103.9 %all-gather.2.cloned.1.call-start = ((), (), s32[]{:S(2)}) async-start(), calls=%async_computation.2 | async-start | bytes 8912896 | tf_op jit(solution)/shard_map/all_gather | solution.py:131
  7.9 36.7 %collective-permute-start = (bf16[256,2048]{1,0:T(8,128)(2,1)}, bf16[256,2048]{1,0:T(8,128)(2,1)}, u32[]{:S(2)}, u32[]{:S(2)}) collective-permute-start(bf16[256,2048]{1,0:T(8,128)(2,1)} %param.6), channel_id=1, source_target_pairs={{0,32},{32,64},{64,96},{96,0},{1,33},{33,65},{65,97},{97,1},{2,34}... | collective-permute-start | bytes 3145736 | tf_op jit(solution)/shard_map/ppermute | solution.py:127
  10.1 65.9 %collective-permute-start.1 = (bf16[256,2048]{1,0:T(8,128)(2,1)}, bf16[256,2048]{1,0:T(8,128)(2,1)}, u32[]{:S(2)}, u32[]{:S(2)}) collective-permute-start(bf16[256,2048]{1,0:T(8,128)(2,1)} %param.6), channel_id=1, source_target_pairs={{0,64},{32,96},{64,0},{96,32},{1,65},{33,97},{65,1},{97,33},{2,66}... | collective-permute-start | bytes 3145736 | tf_op jit(solution)/shard_map/ppermute | solution.py:127
  12.7 68.3 %collective-permute-start.2 = (bf16[256,2048]{1,0:T(8,128)(2,1)}, bf16[256,2048]{1,0:T(8,128)(2,1)}, u32[]{:S(2)}, u32[]{:S(2)}) collective-permute-start(bf16[256,2048]{1,0:T(8,128)(2,1)} %param.6), channel_id=1, source_target_pairs={{0,96},{32,0},{64,32},{96,64},{1,97},{33,1},{65,33},{97,65},{2,98}... | collective-permute-start | bytes 3145736 | tf_op jit(solution)/shard_map/ppermute | solution.py:127
  13.8 71.9 %collective-permute-start.3 = (bf16[256,2048]{1,0:T(8,128)(2,1)}, bf16[256,2048]{1,0:T(8,128)(2,1)}, u32[]{:S(2)}, u32[]{:S(2)}) collective-permute-start(bf16[256,2048]{1,0:T(8,128)(2,1)} %param.6), channel_id=1, source_target_pairs={{0,1},{1,0},{2,3},{3,2},{4,5},{5,4},{6,7},{7,6},{8,9},{9,8},{10,11... | collective-permute-start | bytes 3145736 | tf_op jit(solution)/shard_map/ppermute | solution.py:130
  22.7 68.5 %all-to-all-start = ((bf16[128,4,2176]{2,1,0:T(4,128)(2,1)}), bf16[128,4,2176]{2,1,0:T(4,128)(2,1)S(1)}, u32[]{:S(2)}, u32[]{:S(2)}) async-start(bf16[128,4,2176]{2,1,0:T(4,128)(2,1)} %reshape.212), calls=%async_computation | async-start | bytes 4456448 | tf_op jit(solution)/shard_map/all_to_all | solution.py:173
  31.3 12.2 %copy-start = (bf16[256,2048]{1,0:T(8,128)(2,1)S(1)}, bf16[256,2048]{1,0:T(8,128)(2,1)}, u32[]{:S(2)}) copy-start(bf16[256,2048]{1,0:T(8,128)(2,1)} %param.6) | copy-start | bytes 3145732
  44.6 43.5 %collective-permute-start.4 = (bf16[256,2048]{1,0:T(8,128)(2,1)}, bf16[256,2048]{1,0:T(8,128)(2,1)S(1)}, u32[]{:S(2)}, u32[]{:S(2)}) collective-permute-start(bf16[256,2048]{1,0:T(8,128)(2,1)} %collective-permute-done), channel_id=1, source_target_pairs={{0,1},{1,0},{2,3},{3,2},{4,5},{5,4},{6,7},{7,6},{8,9},{9,8},{10,11... | collective-permute-start | bytes 3145736 | tf_op jit(solution)/shard_map/ppermute | solution.py:130
  76.0 13.1 %collective-permute-start.5 = (bf16[256,2048]{1,0:T(8,128)(2,1)}, bf16[256,2048]{1,0:T(8,128)(2,1)S(1)}, u32[]{:S(2)}, u32[]{:S(2)}) collective-permute-start(bf16[256,2048]{1,0:T(8,128)(2,1)} %collective-permute-done.1), channel_id=1, source_target_pairs={{0,1},{1,0},{2,3},{3,2},{4,5},{5,4},{6,7},{7,6},{8,9},{9,8},{10,11... | collective-permute-start | bytes 3145736 | tf_op jit(solution)/shard_map/ppermute | solution.py:130
  81.0 9.2 %collective-permute-start.6 = (bf16[256,2048]{1,0:T(8,128)(2,1)}, bf16[256,2048]{1,0:T(8,128)(2,1)S(1)}, u32[]{:S(2)}, u32[]{:S(2)}) collective-permute-start(bf16[256,2048]{1,0:T(8,128)(2,1)} %collective-permute-done.2), channel_id=1, source_target_pairs={{0,1},{1,0},{2,3},{3,2},{4,5},{5,4},{6,7},{7,6},{8,9},{9,8},{10,11... | collective-permute-start | bytes 3145736 | tf_op jit(solution)/shard_map/ppermute | solution.py:130
  101.3 59.2 %all-to-all-start.1 = ((f32[128,1,4]{2,1,0:T(1,128)}), f32[128,1,4]{2,1,0:T(1,128)S(1)}, u32[]{:S(2)}, u32[]{:S(2)}) async-start(f32[128,1,4]{2,1,0:T(1,128)} %bitcast.15), calls=%async_computation.1 | async-start | bytes 131072 | tf_op jit(solution)/shard_map/all_to_all | solution.py:179
  150.1 7.4 %collective-permute-start.13 = (f32[256]{0:T(256)S(1)}, f32[256]{0:T(256)S(1)}, u32[]{:S(2)}, u32[]{:S(2)}) collective-permute-start(f32[256]{0:T(256)S(1)} %bitcast.52), channel_id=1, source_target_pairs={{0,33},{1,32},{32,65},{33,64},{64,97},{65,96},{96,1},{97,0},{2,35}... | collective-permute-start | bytes 3080 | tf_op jit(solution)/shard_map/ppermute | solution.py:163
  151.8 6.6 %collective-permute-start.12 = (f32[256]{0:T(256)S(1)}, f32[256]{0:T(256)S(1)}, u32[]{:S(2)}, u32[]{:S(2)}) collective-permute-start(f32[256]{0:T(256)S(1)} %bitcast.51), channel_id=1, source_target_pairs={{0,65},{1,64},{32,97},{33,96},{64,1},{65,0},{96,33},{97,32},{2,67}... | collective-permute-start | bytes 3080 | tf_op jit(solution)/shard_map/ppermute | solution.py:163
  155.6 8.9 %collective-permute-start.11 = (f32[256]{0:T(256)S(1)}, f32[256]{0:T(256)S(1)}, u32[]{:S(2)}, u32[]{:S(2)}) collective-permute-start(f32[256]{0:T(256)S(1)} %bitcast.50), channel_id=1, source_target_pairs={{0,97},{1,96},{32,1},{33,0},{64,33},{65,32},{96,65},{97,64},{2,99}... | collective-permute-start | bytes 3080 | tf_op jit(solution)/shard_map/ppermute | solution.py:163
  157.0 7.5 %collective-permute-start.10 = (f32[256]{0:T(256)S(1)}, f32[256]{0:T(256)S(1)}, u32[]{:S(2)}, u32[]{:S(2)}) collective-permute-start(f32[256]{0:T(256)S(1)} %bitcast.49), channel_id=1, source_target_pairs={{0,1},{1,0},{32,33},{33,32},{64,65},{65,64},{96,97},{97,96},{2,3},... | collective-permute-start | bytes 3080 | tf_op jit(solution)/shard_map/ppermute | solution.py:163
  157.2 7.3 %collective-permute-start.9 = (f32[256]{0:T(256)S(1)}, f32[256]{0:T(256)S(1)}, u32[]{:S(2)}, u32[]{:S(2)}) collective-permute-start(f32[256]{0:T(256)S(1)} %bitcast.48), channel_id=1, source_target_pairs={{0,32},{1,33},{32,64},{33,65},{64,96},{65,97},{96,0},{97,1},{2,34}... | collective-permute-start | bytes 3080 | tf_op jit(solution)/shard_map/ppermute | solution.py:163
  157.5 7.0 %collective-permute-start.8 = (f32[256]{0:T(256)S(1)}, f32[256]{0:T(256)S(1)}, u32[]{:S(2)}, u32[]{:S(2)}) collective-permute-start(f32[256]{0:T(256)S(1)} %bitcast.47), channel_id=1, source_target_pairs={{0,64},{1,65},{32,96},{33,97},{64,0},{65,1},{96,32},{97,33},{2,66}... | collective-permute-start | bytes 3080 | tf_op jit(solution)/shard_map/ppermute | solution.py:163
  158.4 6.1 %collective-permute-start.7 = (f32[256]{0:T(256)S(1)}, f32[256]{0:T(256)S(1)}, u32[]{:S(2)}, u32[]{:S(2)}) collective-permute-start(f32[256]{0:T(256)S(1)} %bitcast.46), channel_id=1, source_target_pairs={{0,96},{1,97},{32,0},{33,1},{64,32},{65,33},{96,64},{97,65},{2,98}... | collective-permute-start | bytes 3080 | tf_op jit(solution)/shard_map/ppermute | solution.py:163
Sparse Core Ops, SparseCore 0:
  10.1 90.6 all-gather.1

commit v6 on v5

--- a/solution.py
+++ b/solution.py
@@ -128,21 +128,16 @@
         for s in range(ny)
     ]
     group = jnp.concatenate(ring_y + [lax.ppermute(p, "c", swap) for p in ring_y], axis=0)
-    piece = lax.all_gather(centroids, ("z", "x"), axis=0, tiled=True)
     src_c = jnp.stack([ic, (ic + nc - 1) % nc])
     src_y = (iy - jnp.arange(ny, dtype=jnp.int32)) % ny
     row_dev = ((src_y[None, :] * nz + iz) * nx + ix) * nc + src_c[:, None]
     group_ids = (row_dev[:, :, None] * rows_dev + jnp.arange(rows_dev, dtype=jnp.int32)).reshape(-1)
-    cpos = jnp.arange(nz * nx * cent_dev, dtype=jnp.int32)
-    cent_dev_ids = ((iy * nz + cpos // (nx * cent_dev)) * nx + cpos // cent_dev % nx) * nc + ic
-    cent_ids = cent_dev_ids * cent_dev + cpos % cent_dev
-    piece_rows = piece.shape[0]
-    block = math.gcd(piece_rows, 512)
-    steps = piece_rows // block
-    tiles = piece.reshape(steps, block, feature_dim)
-    noise = gumbel_noise(group_ids[:, None], cent_ids[None, :], salt_word)
-    noise_tiles = noise.reshape(group.shape[0], steps, block).transpose(1, 0, 2)
-    initial = jnp.full((group.shape[0],), -1e30, jnp.float32)
+    halves = 2
+    share = cent_dev // halves
+    spread = nz * nx
+    cpos = jnp.arange(spread * share, dtype=jnp.int32)
+    cent_dev_ids = ((iy * nz + cpos // (nx * share)) * nx + cpos // share % nx) * nc + ic
+    result = jnp.full((group.shape[0],), -1e30, jnp.float32)
 
     def step(carry, item):
         tile, noise_tile = item
@@ -152,7 +147,16 @@
         perturbed = inverse_temp * scores + noise_tile
         return (jnp.maximum(carry, jnp.max(perturbed, axis=1)), None)
 
-    result, unused = lax.scan(step, initial, (tiles, noise_tiles))
+    for h in range(halves):
+        piece = lax.all_gather(centroids[h * share:(h + 1) * share], ("z", "x"), axis=0, tiled=True)
+        cent_ids = cent_dev_ids * cent_dev + h * share + cpos % share
+        piece_rows = piece.shape[0]
+        block = math.gcd(piece_rows, 512)
+        steps = piece_rows // block
+        tiles = piece.reshape(steps, block, feature_dim)
+        noise = gumbel_noise(group_ids[:, None], cent_ids[None, :], salt_word)
+        noise_tiles = noise.reshape(group.shape[0], steps, block).transpose(1, 0, 2)
+        result, unused = lax.scan(step, result, (tiles, noise_tiles))
     blocks = result.reshape(nc, ny, rows_dev)
     best = blocks[0, 0]
     for sc in range(nc):

time: 172 us -> 174 us (1.012)
  local copies, waits for them, and re-layouts: 25.4 us -> 27.3 us
    slice x0 -> x1, local copies, waits for them, and re-layouts: none -> 1.9 us  [shards(): centroids[h * share:(h + 1) * share]]
  transfers between devices with their start and end apart: 17 -> 18, of which waited for: 1 -> 1; matrix products, arithmetic and copies ran while one was open for 51% -> 51% of each run, Pallas kernels for 0% -> 0%
where the time goes in v6:
time: 174 us
  matrix products  42.9 us (25%)
  starting transfers between devices  37 us (21%)
  waiting for transfers between devices  30.5 us (18%)
  local copies, waits for them, and re-layouts  27.3 us (16%)
  other arithmetic  20.4 us (12%)
  between operations  15.5 us (9%)
    dot_general x4, matrix products, step(): lax.dot_general(group, tile, (((1,), (1,)), ((), ())), preferred_element_...  39.2 us
    ppermute x3, waiting for transfers between devices, shards(): lax.ppermute(embeddings, 'y', [(i, (i + s) % ny) for i in range(ny)])  29.7 us
    unnamed x10, local copies, waits for them, and re-layouts  12.5 us
    neg x1, other arithmetic, gumbel_noise(): return -jnp.log(-jnp.log(uniform))  12.2 us
    all_to_all x1, starting transfers between devices, shards(): lax.all_to_all(scores.reshape(devices, capacity), ALL, split_axis=0, conc...  9.54 us
    ppermute x7, starting transfers between devices, shards(): best = jnp.maximum(best, lax.ppermute(blocks[sc, sy], ('y', 'c'), perm))  8.55 us
    all_to_all x1, starting transfers between devices, shards(): lax.all_to_all(outgoing.reshape(devices, capacity, feature_dim + flag_wid...  7.59 us
    ppermute x3, starting transfers between devices, shards(): lax.ppermute(embeddings, 'y', [(i, (i + s) % ny) for i in range(ny)])  5.88 us
  transfers between devices with their start and end apart: 18, of which 1 were waited for; matrix products, arithmetic and copies ran while one was open for 51% of the time, Pallas kernels for 0%

profile of v6, /device:TPU:1, one launch (start us, length us, event | category | flops | bytes accessed | tf_op | source)
XLA Modules:
  0.0 173.7 jit_solution(16202825823252211019)
XLA Ops:
  7.2 0.0 all-gather.3.cloned.1.call-start
  7.2 1.9 %fusion.64 = (bf16[64,2048]{1,0:T(8,128)(2,1)}, bf16[64,2048]{1,0:T(8,128)(2,1)}) fusion(bf16[128,2048]{1,0:T(8,128)(2,1)} %param.9), kind=kLoop, calls=%fused_computation.102 | loop fusion | bytes 1048576 | tf_op jit(solution)/shard_map/slice | solution.py:151
  9.1 0.0 all-gather.3.cloned.1.call-update
  9.1 2.2 %collective-permute-start = (bf16[256,2048]{1,0:T(8,128)(2,1)}, bf16[256,2048]{1,0:T(8,128)(2,1)}, u32[]{:S(2)}, u32[]{:S(2)}) collective-permute-start(bf16[256,2048]{1,0:T(8,128)(2,1)} %param.8), channel_id=1, source_target_pairs={{0,32},{32,64},{64,96},{96,0},{1,33},{33,65},{65,97},{97,1},{2,34}... | collective-permute-start | bytes 3145736 | tf_op jit(solution)/shard_map/ppermute | solution.py:127
  11.3 2.6 %collective-permute-start.1 = (bf16[256,2048]{1,0:T(8,128)(2,1)}, bf16[256,2048]{1,0:T(8,128)(2,1)}, u32[]{:S(2)}, u32[]{:S(2)}) collective-permute-start(bf16[256,2048]{1,0:T(8,128)(2,1)} %param.8), channel_id=1, source_target_pairs={{0,64},{32,96},{64,0},{96,32},{1,65},{33,97},{65,1},{97,33},{2,66}... | collective-permute-start | bytes 3145736 | tf_op jit(solution)/shard_map/ppermute | solution.py:127
  14.0 1.1 collective-permute-start.2
  15.0 1.5 collective-permute-start.3
  16.5 0.9 convert_reduce_fusion
  17.5 0.7 compare_select_fusion.2
  18.2 3.6 %scatter_custom_fusion = bf16[512,2176]{1,0:T(8,128)(2,1)S(1)} fusion(s32[256]{0:T(256)S(1)} %bitcast.61, bf16[256,2048]{1,0:T(8,128)(2,1)} %param.8, bf16[]{:T(256)} %constant.184.clone.1, bf16[]{:T(256)} %constant.183.clone.1), kind=kCustom, calls=%fused_computation.50 | custom fusion | bytes 3276804 | tf_op jit(solution)/shard_map/scatter | solution.py:176
  21.8 2.1 %reshape.238 = bf16[128,4,2176]{2,1,0:T(4,128)(2,1)} reshape(bf16[512,2176]{1,0:T(8,128)(2,1)S(1)} %scatter_custom_fusion) | data formatting | bytes 4456448 | tf_op jit(solution)/shard_map/reshape | solution.py:178
  23.9 7.6 %all-to-all-start = ((bf16[128,4,2176]{2,1,0:T(4,128)(2,1)}), bf16[128,4,2176]{2,1,0:T(4,128)(2,1)S(1)}, u32[]{:S(2)}, u32[]{:S(2)}) async-start(bf16[128,4,2176]{2,1,0:T(4,128)(2,1)} %reshape.238), calls=%async_computation | async-start | bytes 4456448 | tf_op jit(solution)/shard_map/all_to_all | solution.py:177
  31.5 0.0 all-gather.5.cloned.1.call-start
  31.6 0.7 all-gather.5.cloned.1.call-update
  33.0 0.1 pad_add_fusion
  33.1 0.1 add_multiply_fusion.3
  33.2 0.1 multiply_bitcast_fusion
  33.3 12.2 %fusion.27 = (f32[2,2048,512]{1,2,0:T(8,128)}, f32[2,2048,512]{1,2,0:T(8,128)}) fusion(s32[2,512]{1,0:T(2,128)S(1)} %get-tuple-element.111, s32[]{:T(128)} %bitcast.57, s32[2048]{0:T(1024)S(1)} %bitcast.58, s32[2,512]{1,0:T(2,128)S(1)} %get-tuple-element.112), kind=kLoop, calls=%fused_computation.38 | loop fusion | flops 67108864 | bytes 16793604 | tf_op jit(solution)/shard_map/neg | solution.py:30
  45.5 1.1 constant_dynamic-update-slice_fusion.7
  46.6 0.0 collective-permute-done
  46.6 1.1 collective-permute-start.4
  47.6 29.7 %collective-permute-done.1 = bf16[256,2048]{1,0:T(8,128)(2,1)} collective-permute-done((bf16[256,2048]{1,0:T(8,128)(2,1)}, bf16[256,2048]{1,0:T(8,128)(2,1)}, u32[]{:S(2)}, u32[]{:S(2)}) %collective-permute-start.1) | collective-permute-done | bytes 1048608 | tf_op jit(solution)/shard_map/ppermute | solution.py:127
  77.4 2.7 %collective-permute-start.5 = (bf16[256,2048]{1,0:T(8,128)(2,1)}, bf16[256,2048]{1,0:T(8,128)(2,1)S(1)}, u32[]{:S(2)}, u32[]{:S(2)}) collective-permute-start(bf16[256,2048]{1,0:T(8,128)(2,1)} %collective-permute-done.1), channel_id=1, source_target_pairs={{0,1},{1,0},{2,3},{3,2},{4,5},{5,4},{6,7},{7,6},{8,9},{9,8},{10,11... | collective-permute-start | bytes 3145736 | tf_op jit(solution)/shard_map/ppermute | solution.py:130
  80.1 2.4 %constant_dynamic-update-slice_fusion.6 = bf16[2048,2048]{1,0:T(8,128)(2,1)} fusion(bf16[2048,2048]{1,0:T(8,128)(2,1)} %constant_dynamic-update-slice_fusion.7, bf16[256,2048]{1,0:T(8,128)(2,1)} %collective-permute-done), kind=kLoop, calls=%fused_computation.66 | loop fusion | bytes 2097152
  82.4 0.0 collective-permute-done.2
  82.4 0.0 collective-permute-start.6
  82.5 2.3 %constant_dynamic-update-slice_fusion.5 = bf16[2048,2048]{1,0:T(8,128)(2,1)} fusion(bf16[2048,2048]{1,0:T(8,128)(2,1)} %constant_dynamic-update-slice_fusion.6, bf16[256,2048]{1,0:T(8,128)(2,1)} %collective-permute-done.1), kind=kLoop, calls=%fused_computation.65 | loop fusion | bytes 2097152
  84.8 2.3 %constant_dynamic-update-slice_fusion.4 = bf16[2048,2048]{1,0:T(8,128)(2,1)} fusion(bf16[2048,2048]{1,0:T(8,128)(2,1)} %constant_dynamic-update-slice_fusion.5, bf16[256,2048]{1,0:T(8,128)(2,1)} %collective-permute-done.2), kind=kLoop, calls=%fused_computation.64 | loop fusion | bytes 2097152
  87.1 2.3 %constant_dynamic-update-slice_fusion.3 = bf16[2048,2048]{1,0:T(8,128)(2,1)} fusion(bf16[2048,2048]{1,0:T(8,128)(2,1)} %constant_dynamic-update-slice_fusion.4, bf16[256,2048]{1,0:T(8,128)(2,1)} %collective-permute-done.3), kind=kLoop, calls=%fused_computation.63 | loop fusion | bytes 2097152
  89.4 1.1 constant_dynamic-update-slice_fusion.2
  90.5 0.0 collective-permute-done.5
  90.5 1.1 constant_dynamic-update-slice_fusion.1
  91.6 0.0 collective-permute-done.6
  91.6 1.1 constant_dynamic-update-slice_fusion
  92.6 0.0 all-to-all-done
  92.6 2.1 %reshape.239 = bf16[512,2176]{1,0:T(8,128)(2,1)} reshape(bf16[128,4,2176]{2,1,0:T(4,128)(2,1)S(1)} %all-to-all-done) | data formatting | bytes 4456448 | tf_op jit(solution)/shard_map/reshape | solution.py:179
  94.8 1.1 compare_reduce_fusion
  95.8 0.2 fusion.51
  96.0 2.4 %fusion.29 = (f32[2048]{0:T(1024)S(1)}, f32[512]{0:T(512)S(1)}) fusion(pred[512]{0:T(512)(128)(4,1)S(1)} %compare_reduce_fusion, bf16[512,2176]{1,0:T(8,128)(2,1)} %reshape.239), kind=kLoop, calls=%fused_computation.42 | loop fusion | flops 5240320 | bytes 2107904 | tf_op jit(solution)/shard_map/reduce_sum | solution.py:111
  98.4 3.6 %fusion.44 = f32[512]{0:T(512)S(1)} fusion(bf16[512,2176]{1,0:T(8,128)(2,1)} %reshape.239, f32[512]{0:T(512)S(1)} %add_rsqrt_fusion, pred[512]{0:T(512)(128)(4,1)S(1)} %compare_reduce_fusion), kind=kOutput, calls=%fused_computation.49 | convolution fusion | flops 1075576320 | bytes 2103808 | tf_op jit(solution)/shard_map/dot_general | solution.py:103
  102.1 0.7 select_n.104
  102.8 9.5 %all-to-all-start.1 = ((f32[128,1,4]{2,1,0:T(1,128)}), f32[128,1,4]{2,1,0:T(1,128)S(1)}, u32[]{:S(2)}, u32[]{:S(2)}) async-start(f32[128,1,4]{2,1,0:T(1,128)} %bitcast.19), calls=%async_computation.1 | async-start | bytes 131072 | tf_op jit(solution)/shard_map/all_to_all | solution.py:183
  112.4 0.0 all-gather.3.cloned.1.call-done
  112.4 19.9 %while.22 = (s32[]{:T(128)}, f32[2048]{0:T(1024)S(1)}, bf16[2,512,2048]{2,1,0:T(8,128)(2,1)}, bf16[2048,2048]{1,0:T(8,128)(2,1)}, f32[2,2048,512]{1,2,0:T(8,128)}, /*index=5*/s32[]{:T(128)}, s32[]{:T(128)}) while((s32[]{:T(128)}, f32[2048]{0:T(1024)S(1)}, bf16[2,512,2048]{2,1,0:T(8,128)(2,1)}, bf16[2048,2048]{1,0:T(8,128)(2,1)}, ...), condition=%wide.region_2.3_spmd.clone, body=%wide.region_0.2_spmd.clone.sunk | while | flops 4298115072 | bytes 14713951 | solution.py:159
  112.4 9.8 %fusion.79 = f32[2048]{0:T(1024)S(1)} fusion(f32[2,2048,512]{1,2,0:T(8,128)} %get-tuple-element.193, s32[]{:T(128)S(6)} %copy.20, bf16[2048,2048]{1,0:T(8,128)(2,1)} %get-tuple-element.192, bf16[2,512,2048]{2,1,0:T(8,128)(2,1)} %get-tuple-element.191), kind=kOutput, calls=%fused_computation.8.clone.1 | convolution fusion | flops 4298110976 | bytes 14689280 | tf_op jit(solution)/shard_map/while/body/eval_jaxpr/dot_general | solution.py:144
  122.3 10.0 %fusion.79 = f32[2048]{0:T(1024)S(1)} fusion(f32[2,2048,512]{1,2,0:T(8,128)} %get-tuple-element.193, s32[]{:T(128)S(6)} %copy.20, bf16[2048,2048]{1,0:T(8,128)(2,1)} %get-tuple-element.192, bf16[2,512,2048]{2,1,0:T(8,128)(2,1)} %get-tuple-element.191), kind=kOutput, calls=%fused_computation.8.clone.1 | convolution fusion | flops 4298110976 | bytes 14689280 | tf_op jit(solution)/shard_map/while/body/eval_jaxpr/dot_general | solution.py:144
  132.3 0.0 all-gather.5.cloned.1.call-done
  132.3 19.5 %while.21 = (s32[]{:T(128)}, f32[2048]{0:T(1024)S(1)}, bf16[2,512,2048]{2,1,0:T(8,128)(2,1)}, bf16[2048,2048]{1,0:T(8,128)(2,1)}, f32[2,2048,512]{1,2,0:T(8,128)}, /*index=5*/s32[]{:T(128)}) while((s32[]{:T(128)}, f32[2048]{0:T(1024)S(1)}, bf16[2,512,2048]{2,1,0:T(8,128)(2,1)}, bf16[2048,2048]{1,0:T(8,128)(2,1)}, f32[2,2048,512]{1,2,0:T(8,128)}, ...), condition=%wide.region_5.6_spmd, body=%wide.region_3.5_spmd.sunk | while | flops 4298113024 | bytes 14713933 | solution.py:159
  132.3 9.7 %fusion.76 = f32[2048]{0:T(1024)S(1)} fusion(f32[2,2048,512]{1,2,0:T(8,128)} %get-tuple-element.212, s32[]{:T(128)S(6)} %copy.26, bf16[2048,2048]{1,0:T(8,128)(2,1)} %get-tuple-element.211, bf16[2,512,2048]{2,1,0:T(8,128)(2,1)} %get-tuple-element.210), kind=kOutput, calls=%fused_computation.3.clone.1 | convolution fusion | flops 4298110976 | bytes 14689280 | tf_op jit(solution)/shard_map/while/body/eval_jaxpr/dot_general | solution.py:144
  142.1 9.7 %fusion.76 = f32[2048]{0:T(1024)S(1)} fusion(f32[2,2048,512]{1,2,0:T(8,128)} %get-tuple-element.212, s32[]{:T(128)S(6)} %copy.26, bf16[2048,2048]{1,0:T(8,128)(2,1)} %get-tuple-element.211, bf16[2,512,2048]{2,1,0:T(8,128)(2,1)} %get-tuple-element.210), kind=kOutput, calls=%fused_computation.3.clone.1 | convolution fusion | flops 4298110976 | bytes 14689280 | tf_op jit(solution)/shard_map/while/body/eval_jaxpr/dot_general | solution.py:144
  151.8 1.7 collective-permute-start.13
  153.5 2.5 %collective-permute-start.12 = (f32[256]{0:T(256)S(1)}, f32[256]{0:T(256)S(1)}, u32[]{:S(2)}, u32[]{:S(2)}) collective-permute-start(f32[256]{0:T(256)S(1)} %bitcast.70), channel_id=1, source_target_pairs={{0,65},{1,64},{32,97},{33,96},{64,1},{65,0},{96,33},{97,32},{2,67}... | collective-permute-start | bytes 3080 | tf_op jit(solution)/shard_map/ppermute | solution.py:167
  156.0 0.6 multiply_reduce_fusion
  157.3 1.4 collective-permute-start.11
  158.7 0.2 collective-permute-start.10
  158.9 0.3 collective-permute-start.9
  159.3 0.9 collective-permute-start.8
  160.1 1.5 collective-permute-start.7
  161.7 0.6 broadcast_multiply_fusion
  162.3 0.5 broadcast.540
  162.8 0.8 reduce.5
  163.6 0.1 reshape.240
  163.7 2.5 %gather_fusion = f32[256]{0:T(256)} fusion(f32[512]{0:T(512)S(1)} %reshape.240, s32[1024]{0:T(1024)S(1)} %pad_clamp_fusion), kind=kCustom, calls=%fused_computation | custom fusion | bytes 3072 | tf_op jit(solution)/shard_map/gather | solution.py:186
  166.3 0.6 maximum_maximum_fusion
  (25 shorter events, 0.2 us)
Async XLA Ops:
  7.2 105.2 %all-gather.3.cloned.1.call-start = ((), (), s32[]{:S(2)}) async-start(), calls=%async_computation.2 | async-start | bytes 4456448 | tf_op jit(solution)/shard_map/all_gather | solution.py:151
  9.1 37.4 %collective-permute-start = (bf16[256,2048]{1,0:T(8,128)(2,1)}, bf16[256,2048]{1,0:T(8,128)(2,1)}, u32[]{:S(2)}, u32[]{:S(2)}) collective-permute-start(bf16[256,2048]{1,0:T(8,128)(2,1)} %param.8), channel_id=1, source_target_pairs={{0,32},{32,64},{64,96},{96,0},{1,33},{33,65},{65,97},{97,1},{2,34}... | collective-permute-start | bytes 3145736 | tf_op jit(solution)/shard_map/ppermute | solution.py:127
  11.3 66.0 %collective-permute-start.1 = (bf16[256,2048]{1,0:T(8,128)(2,1)}, bf16[256,2048]{1,0:T(8,128)(2,1)}, u32[]{:S(2)}, u32[]{:S(2)}) collective-permute-start(bf16[256,2048]{1,0:T(8,128)(2,1)} %param.8), channel_id=1, source_target_pairs={{0,64},{32,96},{64,0},{96,32},{1,65},{33,97},{65,1},{97,33},{2,66}... | collective-permute-start | bytes 3145736 | tf_op jit(solution)/shard_map/ppermute | solution.py:127
  14.0 68.5 %collective-permute-start.2 = (bf16[256,2048]{1,0:T(8,128)(2,1)}, bf16[256,2048]{1,0:T(8,128)(2,1)}, u32[]{:S(2)}, u32[]{:S(2)}) collective-permute-start(bf16[256,2048]{1,0:T(8,128)(2,1)} %param.8), channel_id=1, source_target_pairs={{0,96},{32,0},{64,32},{96,64},{1,97},{33,1},{65,33},{97,65},{2,98}... | collective-permute-start | bytes 3145736 | tf_op jit(solution)/shard_map/ppermute | solution.py:127
  15.0 72.1 %collective-permute-start.3 = (bf16[256,2048]{1,0:T(8,128)(2,1)}, bf16[256,2048]{1,0:T(8,128)(2,1)}, u32[]{:S(2)}, u32[]{:S(2)}) collective-permute-start(bf16[256,2048]{1,0:T(8,128)(2,1)} %param.8), channel_id=1, source_target_pairs={{0,1},{1,0},{2,3},{3,2},{4,5},{5,4},{6,7},{7,6},{8,9},{9,8},{10,11... | collective-permute-start | bytes 3145736 | tf_op jit(solution)/shard_map/ppermute | solution.py:130
  23.9 68.7 %all-to-all-start = ((bf16[128,4,2176]{2,1,0:T(4,128)(2,1)}), bf16[128,4,2176]{2,1,0:T(4,128)(2,1)S(1)}, u32[]{:S(2)}, u32[]{:S(2)}) async-start(bf16[128,4,2176]{2,1,0:T(4,128)(2,1)} %reshape.238), calls=%async_computation | async-start | bytes 4456448 | tf_op jit(solution)/shard_map/all_to_all | solution.py:177
  31.5 100.7 %all-gather.5.cloned.1.call-start = ((), (), s32[]{:S(2)}) async-start(), calls=%async_computation.3 | async-start | bytes 4456448 | tf_op jit(solution)/shard_map/all_gather | solution.py:151
  33.3 12.2 %copy-start = (bf16[256,2048]{1,0:T(8,128)(2,1)S(1)}, bf16[256,2048]{1,0:T(8,128)(2,1)}, u32[]{:S(2)}) copy-start(bf16[256,2048]{1,0:T(8,128)(2,1)} %param.8) | copy-start | bytes 3145732
  46.6 42.9 %collective-permute-start.4 = (bf16[256,2048]{1,0:T(8,128)(2,1)}, bf16[256,2048]{1,0:T(8,128)(2,1)S(1)}, u32[]{:S(2)}, u32[]{:S(2)}) collective-permute-start(bf16[256,2048]{1,0:T(8,128)(2,1)} %collective-permute-done), channel_id=1, source_target_pairs={{0,1},{1,0},{2,3},{3,2},{4,5},{5,4},{6,7},{7,6},{8,9},{9,8},{10,11... | collective-permute-start | bytes 3145736 | tf_op jit(solution)/shard_map/ppermute | solution.py:130
  77.4 13.1 %collective-permute-start.5 = (bf16[256,2048]{1,0:T(8,128)(2,1)}, bf16[256,2048]{1,0:T(8,128)(2,1)S(1)}, u32[]{:S(2)}, u32[]{:S(2)}) collective-permute-start(bf16[256,2048]{1,0:T(8,128)(2,1)} %collective-permute-done.1), channel_id=1, source_target_pairs={{0,1},{1,0},{2,3},{3,2},{4,5},{5,4},{6,7},{7,6},{8,9},{9,8},{10,11... | collective-permute-start | bytes 3145736 | tf_op jit(solution)/shard_map/ppermute | solution.py:130
  82.4 9.1 %collective-permute-start.6 = (bf16[256,2048]{1,0:T(8,128)(2,1)}, bf16[256,2048]{1,0:T(8,128)(2,1)S(1)}, u32[]{:S(2)}, u32[]{:S(2)}) collective-permute-start(bf16[256,2048]{1,0:T(8,128)(2,1)} %collective-permute-done.2), channel_id=1, source_target_pairs={{0,1},{1,0},{2,3},{3,2},{4,5},{5,4},{6,7},{7,6},{8,9},{9,8},{10,11... | collective-permute-start | bytes 3145736 | tf_op jit(solution)/shard_map/ppermute | solution.py:130
  102.8 59.5 %all-to-all-start.1 = ((f32[128,1,4]{2,1,0:T(1,128)}), f32[128,1,4]{2,1,0:T(1,128)S(1)}, u32[]{:S(2)}, u32[]{:S(2)}) async-start(f32[128,1,4]{2,1,0:T(1,128)} %bitcast.19), calls=%async_computation.1 | async-start | bytes 131072 | tf_op jit(solution)/shard_map/all_to_all | solution.py:183
  151.8 7.4 %collective-permute-start.13 = (f32[256]{0:T(256)S(1)}, f32[256]{0:T(256)S(1)}, u32[]{:S(2)}, u32[]{:S(2)}) collective-permute-start(f32[256]{0:T(256)S(1)} %bitcast.71), channel_id=1, source_target_pairs={{0,33},{1,32},{32,65},{33,64},{64,97},{65,96},{96,1},{97,0},{2,35}... | collective-permute-start | bytes 3080 | tf_op jit(solution)/shard_map/ppermute | solution.py:167
  153.5 6.6 %collective-permute-start.12 = (f32[256]{0:T(256)S(1)}, f32[256]{0:T(256)S(1)}, u32[]{:S(2)}, u32[]{:S(2)}) collective-permute-start(f32[256]{0:T(256)S(1)} %bitcast.70), channel_id=1, source_target_pairs={{0,65},{1,64},{32,97},{33,96},{64,1},{65,0},{96,33},{97,32},{2,67}... | collective-permute-start | bytes 3080 | tf_op jit(solution)/shard_map/ppermute | solution.py:167
  157.3 8.9 %collective-permute-start.11 = (f32[256]{0:T(256)S(1)}, f32[256]{0:T(256)S(1)}, u32[]{:S(2)}, u32[]{:S(2)}) collective-permute-start(f32[256]{0:T(256)S(1)} %bitcast.69), channel_id=1, source_target_pairs={{0,97},{1,96},{32,1},{33,0},{64,33},{65,32},{96,65},{97,64},{2,99}... | collective-permute-start | bytes 3080 | tf_op jit(solution)/shard_map/ppermute | solution.py:167
  158.7 7.5 %collective-permute-start.10 = (f32[256]{0:T(256)S(1)}, f32[256]{0:T(256)S(1)}, u32[]{:S(2)}, u32[]{:S(2)}) collective-permute-start(f32[256]{0:T(256)S(1)} %bitcast.68), channel_id=1, source_target_pairs={{0,1},{1,0},{32,33},{33,32},{64,65},{65,64},{96,97},{97,96},{2,3},... | collective-permute-start | bytes 3080 | tf_op jit(solution)/shard_map/ppermute | solution.py:167
  158.9 7.3 %collective-permute-start.9 = (f32[256]{0:T(256)S(1)}, f32[256]{0:T(256)S(1)}, u32[]{:S(2)}, u32[]{:S(2)}) collective-permute-start(f32[256]{0:T(256)S(1)} %bitcast.67), channel_id=1, source_target_pairs={{0,32},{1,33},{32,64},{33,65},{64,96},{65,97},{96,0},{97,1},{2,34}... | collective-permute-start | bytes 3080 | tf_op jit(solution)/shard_map/ppermute | solution.py:167
  159.3 7.0 %collective-permute-start.8 = (f32[256]{0:T(256)S(1)}, f32[256]{0:T(256)S(1)}, u32[]{:S(2)}, u32[]{:S(2)}) collective-permute-start(f32[256]{0:T(256)S(1)} %bitcast.66), channel_id=1, source_target_pairs={{0,64},{1,65},{32,96},{33,97},{64,0},{65,1},{96,32},{97,33},{2,66}... | collective-permute-start | bytes 3080 | tf_op jit(solution)/shard_map/ppermute | solution.py:167
  160.1 6.1 %collective-permute-start.7 = (f32[256]{0:T(256)S(1)}, f32[256]{0:T(256)S(1)}, u32[]{:S(2)}, u32[]{:S(2)}) collective-permute-start(f32[256]{0:T(256)S(1)} %bitcast.65), channel_id=1, source_target_pairs={{0,96},{1,97},{32,0},{33,1},{64,32},{65,33},{96,64},{97,65},{2,98}... | collective-permute-start | bytes 3080 | tf_op jit(solution)/shard_map/ppermute | solution.py:167
Sparse Core Ops, SparseCore 0:
  10.1 68.2 all-gather.2
  80.6 50.6 all-gather.4

commit v7 on v6

--- a/solution.py
+++ b/solution.py
@@ -123,10 +123,21 @@
     me = ((iy * nz + iz) * nx + ix) * nc + ic
     salt_word = noise_salt[0]
     swap = [(i, (i + 1) % nc) for i in range(nc)]
-    ring_y = [
-        embeddings if s == 0 else lax.ppermute(embeddings, "y", [(i, (i + s) % ny) for i in range(ny)])
-        for s in range(ny)
-    ]
+    def shift_y(x, s):
+        return lax.ppermute(x, "y", [(i, (i + s) % ny) for i in range(ny)])
+
+    ring_y = []
+    for s in range(ny):
+        if s == 0:
+            ring_y.append(embeddings)
+        elif 2 * s == ny:
+            cut = rows_dev // 2
+            ahead, behind = embeddings[:cut], embeddings[cut:]
+            for unused in range(s):
+                ahead, behind = shift_y(ahead, 1), shift_y(behind, -1)
+            ring_y.append(jnp.concatenate([ahead, behind], axis=0))
+        else:
+            ring_y.append(shift_y(embeddings, s))
     group = jnp.concatenate(ring_y + [lax.ppermute(p, "c", swap) for p in ring_y], axis=0)
     src_c = jnp.stack([ic, (ic + nc - 1) % nc])
     src_y = (iy - jnp.arange(ny, dtype=jnp.int32)) % ny

time: 174 us -> 182 us (1.046)
  starting transfers between devices: 37 us -> 40 us
  local copies, waits for them, and re-layouts: 27.3 us -> 30 us
    ppermute x3 -> x6, starting transfers between devices: 5.88 us -> 10.3 us  [shift_y(): return lax.ppermute(x, 'y', [(i, (i + s) % ny) for i in range(ny)])]
    unnamed x10 -> x11, local copies, waits for them, and re-layouts: 12.5 us -> 14 us
    ppermute x3 -> x6, waiting for transfers between devices: 29.7 us -> 29.9 us  [shift_y(): return lax.ppermute(x, 'y', [(i, (i + s) % ny) for i in range(ny)])]
  transfers between devices with their start and end apart: 18 -> 21, of which waited for: 1 -> 3; matrix products, arithmetic and copies ran while one was open for 51% -> 51% of each run, Pallas kernels for 0% -> 0%
where the time goes in v7:
time: 182 us; the launch traced here: 181 us
  matrix products  42.8 us (24%)
  starting transfers between devices  40 us (22%)
  waiting for transfers between devices  30.7 us (17%)
  local copies, waits for them, and re-layouts  30 us (16%)
  other arithmetic  21.6 us (12%)
  between operations  15.6 us (9%)
    dot_general x4, matrix products, step(): lax.dot_general(group, tile, (((1,), (1,)), ((), ())), preferred_element_...  39.2 us
    ppermute x6, waiting for transfers between devices, shift_y(): return lax.ppermute(x, 'y', [(i, (i + s) % ny) for i in range(ny)])  29.9 us
    unnamed x11, local copies, waits for them, and re-layouts  14 us
    neg x1, other arithmetic, gumbel_noise(): return -jnp.log(-jnp.log(uniform))  12.2 us
    ppermute x6, starting transfers between devices, shift_y(): return lax.ppermute(x, 'y', [(i, (i + s) % ny) for i in range(ny)])  10.3 us
    ppermute x7, starting transfers between devices, shards(): best = jnp.maximum(best, lax.ppermute(blocks[sc, sy], ('y', 'c'), perm))  8.53 us
    all_to_all x1, starting transfers between devices, shards(): lax.all_to_all(scores.reshape(devices, capacity), ALL, split_axis=0, conc...  8.53 us
    all_to_all x1, starting transfers between devices, shards(): lax.all_to_all(outgoing.reshape(devices, capacity, feature_dim + flag_wid...  8.22 us
  transfers between devices with their start and end apart: 21, of which 3 were waited for; matrix products, arithmetic and copies ran while one was open for 51% of the time, Pallas kernels for 0%

profile of v7, /device:TPU:1, one launch (start us, length us, event | category | flops | bytes accessed | tf_op | source)
XLA Modules:
  0.0 180.9 jit_solution(1850641943603521534)
XLA Ops:
  7.2 0.0 all-gather.3.cloned.1.call-start
  7.2 1.9 %fusion.65 = (bf16[64,2048]{1,0:T(8,128)(2,1)}, bf16[64,2048]{1,0:T(8,128)(2,1)}) fusion(bf16[128,2048]{1,0:T(8,128)(2,1)} %param.9), kind=kLoop, calls=%fused_computation.105 | loop fusion | bytes 1048576 | tf_op jit(solution)/shard_map/slice | solution.py:162
  9.1 2.2 %collective-permute-start = (bf16[256,2048]{1,0:T(8,128)(2,1)}, bf16[256,2048]{1,0:T(8,128)(2,1)}, u32[]{:S(2)}, u32[]{:S(2)}) collective-permute-start(bf16[256,2048]{1,0:T(8,128)(2,1)} %param.8), channel_id=1, source_target_pairs={{0,32},{32,64},{64,96},{96,0},{1,33},{33,65},{65,97},{97,1},{2,34}... | collective-permute-start | bytes 3145736 | tf_op jit(solution)/shard_map/ppermute | solution.py:127
  11.3 1.5 collective-permute-start.5
  12.8 1.0 collective-permute-start.6
  13.8 1.3 fusion.64
  15.1 0.2 collective-permute-start.1
  15.3 2.5 %collective-permute-start.3 = (bf16[128,2048]{1,0:T(8,128)(2,1)S(1)}, bf16[128,2048]{1,0:T(8,128)(2,1)}, u32[]{:S(2)}, u32[]{:S(2)}) collective-permute-start(bf16[128,2048]{1,0:T(8,128)(2,1)S(1)} %get-tuple-element.99), channel_id=1, source_target_pairs={{0,96},{32,0},{64,32},{96,64},{1,97},{33,1},{65,33},{97,65},{2,98}... | collective-permute-start | bytes 1572872 | tf_op jit(solution)/shard_map/ppermute | solution.py:127
  17.9 0.9 convert_reduce_fusion
  18.8 0.7 compare_select_fusion.2
  19.5 3.6 %scatter_custom_fusion = bf16[512,2176]{1,0:T(8,128)(2,1)S(1)} fusion(s32[256]{0:T(256)S(1)} %bitcast.61, bf16[256,2048]{1,0:T(8,128)(2,1)} %param.8, bf16[]{:T(256)} %constant.184.clone.1, bf16[]{:T(256)} %constant.183.clone.1), kind=kCustom, calls=%fused_computation.50 | custom fusion | bytes 3276804 | tf_op jit(solution)/shard_map/scatter | solution.py:187
  23.1 2.1 %reshape.238 = bf16[128,4,2176]{2,1,0:T(4,128)(2,1)} reshape(bf16[512,2176]{1,0:T(8,128)(2,1)S(1)} %scatter_custom_fusion) | data formatting | bytes 4456448 | tf_op jit(solution)/shard_map/reshape | solution.py:189
  25.2 8.2 %all-to-all-start = ((bf16[128,4,2176]{2,1,0:T(4,128)(2,1)}), bf16[128,4,2176]{2,1,0:T(4,128)(2,1)S(1)}, u32[]{:S(2)}, u32[]{:S(2)}) async-start(bf16[128,4,2176]{2,1,0:T(4,128)(2,1)} %reshape.238), calls=%async_computation | async-start | bytes 4456448 | tf_op jit(solution)/shard_map/all_to_all | solution.py:188
  33.5 0.0 all-gather.5.cloned.1.call-start
  33.5 0.7 all-gather.5.cloned.1.call-update
  34.9 0.1 pad_add_fusion
  35.0 0.1 add_multiply_fusion.3
  35.1 0.1 multiply_bitcast_fusion
  35.2 27.0 %collective-permute-done.1 = bf16[128,2048]{1,0:T(8,128)(2,1)} collective-permute-done((bf16[128,2048]{1,0:T(8,128)(2,1)S(1)}, bf16[128,2048]{1,0:T(8,128)(2,1)}, u32[]{:S(2)}, u32[]{:S(2)}) %collective-permute-start.1) | collective-permute-done | bytes 524320 | tf_op jit(solution)/shard_map/ppermute | solution.py:127
  62.2 0.6 collective-permute-start.2
  62.8 0.1 collective-permute-done.3
  62.9 3.2 %collective-permute-start.4 = (bf16[128,2048]{1,0:T(8,128)(2,1)}, bf16[128,2048]{1,0:T(8,128)(2,1)}, u32[]{:S(2)}, u32[]{:S(2)}) collective-permute-start(bf16[128,2048]{1,0:T(8,128)(2,1)} %collective-permute-done.3), channel_id=1, source_target_pairs={{0,96},{32,0},{64,32},{96,64},{1,97},{33,1},{65,33},{97,65},{2,98}... | collective-permute-start | bytes 1572872 | tf_op jit(solution)/shard_map/ppermute | solution.py:127
  66.2 12.2 %fusion.27 = (f32[2,2048,512]{1,2,0:T(8,128)}, f32[2,2048,512]{1,2,0:T(8,128)}) fusion(s32[2,512]{1,0:T(2,128)S(1)} %get-tuple-element.113, s32[]{:T(128)} %bitcast.57, s32[2048]{0:T(1024)S(1)} %bitcast.58, s32[2,512]{1,0:T(2,128)S(1)} %get-tuple-element.114), kind=kLoop, calls=%fused_computation.38 | loop fusion | flops 67108864 | bytes 16793604 | tf_op jit(solution)/shard_map/neg | solution.py:30
  78.4 1.0 constant_dynamic-update-slice_fusion.8
  79.4 2.8 %collective-permute-done.2 = bf16[128,2048]{1,0:T(8,128)(2,1)} collective-permute-done((bf16[128,2048]{1,0:T(8,128)(2,1)}, bf16[128,2048]{1,0:T(8,128)(2,1)}, u32[]{:S(2)}, u32[]{:S(2)}) %collective-permute-start.2) | collective-permute-done | bytes 524320 | tf_op jit(solution)/shard_map/ppermute | solution.py:127
  82.2 1.3 pad_maximum_fusion
  83.5 2.9 %collective-permute-start.8 = (bf16[256,2048]{1,0:T(8,128)(2,1)S(1)}, bf16[256,2048]{1,0:T(8,128)(2,1)S(1)}, u32[]{:S(2)}, u32[]{:S(2)}) collective-permute-start(bf16[256,2048]{1,0:T(8,128)(2,1)S(1)} %pad_maximum_fusion), channel_id=1, source_target_pairs={{0,1},{1,0},{2,3},{3,2},{4,5},{5,4},{6,7},{7,6},{8,9},{9,8},{10,11... | collective-permute-start | bytes 3145736 | tf_op jit(solution)/shard_map/ppermute | solution.py:141
  86.3 0.1 collective-permute-start.7
  86.4 2.3 %constant_dynamic-update-slice_fusion.7 = bf16[2048,2048]{1,0:T(8,128)(2,1)} fusion(bf16[2048,2048]{1,0:T(8,128)(2,1)} %constant_dynamic-update-slice_fusion.8, bf16[256,2048]{1,0:T(8,128)(2,1)} %collective-permute-done), kind=kLoop, calls=%fused_computation.68 | loop fusion | bytes 2097152
  88.8 1.9 %constant_dynamic-update-slice_fusion.6 = bf16[2048,2048]{1,0:T(8,128)(2,1)} fusion(bf16[2048,2048]{1,0:T(8,128)(2,1)} %constant_dynamic-update-slice_fusion.7, bf16[128,2048]{1,0:T(8,128)(2,1)} %collective-permute-done.2), kind=kLoop, calls=%fused_computation.67 | loop fusion | bytes 1048576
  90.7 0.4 collective-permute-start.9
  91.1 1.9 %constant_dynamic-update-slice_fusion.5 = bf16[2048,2048]{1,0:T(8,128)(2,1)} fusion(bf16[2048,2048]{1,0:T(8,128)(2,1)} %constant_dynamic-update-slice_fusion.6, bf16[128,2048]{1,0:T(8,128)(2,1)} %collective-permute-done.4), kind=kLoop, calls=%fused_computation.66 | loop fusion | bytes 1048576
  93.0 2.4 %constant_dynamic-update-slice_fusion.4 = bf16[2048,2048]{1,0:T(8,128)(2,1)} fusion(bf16[2048,2048]{1,0:T(8,128)(2,1)} %constant_dynamic-update-slice_fusion.5, bf16[256,2048]{1,0:T(8,128)(2,1)} %collective-permute-done.5), kind=kLoop, calls=%fused_computation.65 | loop fusion | bytes 2097152
  95.4 2.3 %constant_dynamic-update-slice_fusion.3 = bf16[2048,2048]{1,0:T(8,128)(2,1)} fusion(bf16[2048,2048]{1,0:T(8,128)(2,1)} %constant_dynamic-update-slice_fusion.4, bf16[256,2048]{1,0:T(8,128)(2,1)} %collective-permute-done.6), kind=kLoop, calls=%fused_computation.64 | loop fusion | bytes 2097152
  97.7 1.1 constant_dynamic-update-slice_fusion.2
  98.8 1.1 constant_dynamic-update-slice_fusion.1
  99.9 1.1 constant_dynamic-update-slice_fusion
  101.0 2.1 %reshape.239 = bf16[512,2176]{1,0:T(8,128)(2,1)} reshape(bf16[128,4,2176]{2,1,0:T(4,128)(2,1)S(1)} %all-to-all-done) | data formatting | bytes 4456448 | tf_op jit(solution)/shard_map/reshape | solution.py:190
  103.1 1.1 compare_reduce_fusion
  104.1 0.2 fusion.51
  104.3 2.4 %fusion.29 = (f32[2048]{0:T(1024)S(1)}, f32[512]{0:T(512)S(1)}) fusion(pred[512]{0:T(512)(128)(4,1)S(1)} %compare_reduce_fusion, bf16[512,2176]{1,0:T(8,128)(2,1)} %reshape.239), kind=kLoop, calls=%fused_computation.42 | loop fusion | flops 5240320 | bytes 2107904 | tf_op jit(solution)/shard_map/reduce_sum | solution.py:111
  106.7 3.6 %fusion.44 = f32[512]{0:T(512)S(1)} fusion(bf16[512,2176]{1,0:T(8,128)(2,1)} %reshape.239, f32[512]{0:T(512)S(1)} %add_rsqrt_fusion, pred[512]{0:T(512)(128)(4,1)S(1)} %compare_reduce_fusion), kind=kOutput, calls=%fused_computation.49 | convolution fusion | flops 1075576320 | bytes 2103808 | tf_op jit(solution)/shard_map/dot_general | solution.py:103
  110.4 0.7 select_n.104
  111.1 8.5 %all-to-all-start.1 = ((f32[128,1,4]{2,1,0:T(1,128)}), f32[128,1,4]{2,1,0:T(1,128)S(1)}, u32[]{:S(2)}, u32[]{:S(2)}) async-start(f32[128,1,4]{2,1,0:T(1,128)} %bitcast.19), calls=%async_computation.1 | async-start | bytes 131072 | tf_op jit(solution)/shard_map/all_to_all | solution.py:194
  119.6 19.9 %while.22 = (s32[]{:T(128)}, f32[2048]{0:T(1024)S(1)}, bf16[2,512,2048]{2,1,0:T(8,128)(2,1)}, bf16[2048,2048]{1,0:T(8,128)(2,1)}, f32[2,2048,512]{1,2,0:T(8,128)}, /*index=5*/s32[]{:T(128)}, s32[]{:T(128)}) while((s32[]{:T(128)}, f32[2048]{0:T(1024)S(1)}, bf16[2,512,2048]{2,1,0:T(8,128)(2,1)}, bf16[2048,2048]{1,0:T(8,128)(2,1)}, ...), condition=%wide.region_2.3_spmd.clone, body=%wide.region_0.2_spmd.clone.sunk | while | flops 4298115072 | bytes 14713951 | solution.py:170
  119.7 10.0 %fusion.80 = f32[2048]{0:T(1024)S(1)} fusion(f32[2,2048,512]{1,2,0:T(8,128)} %get-tuple-element.195, s32[]{:T(128)S(6)} %copy.21, bf16[2048,2048]{1,0:T(8,128)(2,1)} %get-tuple-element.194, bf16[2,512,2048]{2,1,0:T(8,128)(2,1)} %get-tuple-element.193), kind=kOutput, calls=%fused_computation.8.clone.1 | convolution fusion | flops 4298110976 | bytes 14689280 | tf_op jit(solution)/shard_map/while/body/eval_jaxpr/dot_general | solution.py:155
  129.7 9.8 %fusion.80 = f32[2048]{0:T(1024)S(1)} fusion(f32[2,2048,512]{1,2,0:T(8,128)} %get-tuple-element.195, s32[]{:T(128)S(6)} %copy.21, bf16[2048,2048]{1,0:T(8,128)(2,1)} %get-tuple-element.194, bf16[2,512,2048]{2,1,0:T(8,128)(2,1)} %get-tuple-element.193), kind=kOutput, calls=%fused_computation.8.clone.1 | convolution fusion | flops 4298110976 | bytes 14689280 | tf_op jit(solution)/shard_map/while/body/eval_jaxpr/dot_general | solution.py:155
  139.6 19.5 %while.21 = (s32[]{:T(128)}, f32[2048]{0:T(1024)S(1)}, bf16[2,512,2048]{2,1,0:T(8,128)(2,1)}, bf16[2048,2048]{1,0:T(8,128)(2,1)}, f32[2,2048,512]{1,2,0:T(8,128)}, /*index=5*/s32[]{:T(128)}) while((s32[]{:T(128)}, f32[2048]{0:T(1024)S(1)}, bf16[2,512,2048]{2,1,0:T(8,128)(2,1)}, bf16[2048,2048]{1,0:T(8,128)(2,1)}, f32[2,2048,512]{1,2,0:T(8,128)}, ...), condition=%wide.region_5.6_spmd, body=%wide.region_3.5_spmd.sunk | while | flops 4298113024 | bytes 14713933 | solution.py:170
  139.6 9.7 %fusion.77 = f32[2048]{0:T(1024)S(1)} fusion(f32[2,2048,512]{1,2,0:T(8,128)} %get-tuple-element.214, s32[]{:T(128)S(6)} %copy.27, bf16[2048,2048]{1,0:T(8,128)(2,1)} %get-tuple-element.213, bf16[2,512,2048]{2,1,0:T(8,128)(2,1)} %get-tuple-element.212), kind=kOutput, calls=%fused_computation.3.clone.1 | convolution fusion | flops 4298110976 | bytes 14689280 | tf_op jit(solution)/shard_map/while/body/eval_jaxpr/dot_general | solution.py:155
  149.3 9.7 %fusion.77 = f32[2048]{0:T(1024)S(1)} fusion(f32[2,2048,512]{1,2,0:T(8,128)} %get-tuple-element.214, s32[]{:T(128)S(6)} %copy.27, bf16[2048,2048]{1,0:T(8,128)(2,1)} %get-tuple-element.213, bf16[2,512,2048]{2,1,0:T(8,128)(2,1)} %get-tuple-element.212), kind=kOutput, calls=%fused_computation.3.clone.1 | convolution fusion | flops 4298110976 | bytes 14689280 | tf_op jit(solution)/shard_map/while/body/eval_jaxpr/dot_general | solution.py:155
  159.1 1.7 collective-permute-start.16
  160.8 2.5 %collective-permute-start.15 = (f32[256]{0:T(256)S(1)}, f32[256]{0:T(256)S(1)}, u32[]{:S(2)}, u32[]{:S(2)}) collective-permute-start(f32[256]{0:T(256)S(1)} %bitcast.70), channel_id=1, source_target_pairs={{0,65},{1,64},{32,97},{33,96},{64,1},{65,0},{96,33},{97,32},{2,67}... | collective-permute-start | bytes 3080 | tf_op jit(solution)/shard_map/ppermute | solution.py:178
  163.3 0.6 multiply_reduce_fusion
  164.6 1.4 collective-permute-start.14
  166.0 0.2 collective-permute-start.13
  166.2 0.3 collective-permute-start.12
  166.5 0.9 collective-permute-start.11
  167.4 1.5 collective-permute-start.10
  168.9 0.6 broadcast_multiply_fusion
  169.5 0.5 broadcast.540
  170.0 0.8 reduce.5
  170.8 0.1 reshape.240
  170.9 2.5 %gather_fusion = f32[256]{0:T(256)} fusion(f32[512]{0:T(512)S(1)} %reshape.240, s32[1024]{0:T(1024)S(1)} %pad_clamp_fusion), kind=kCustom, calls=%fused_computation | custom fusion | bytes 3072 | tf_op jit(solution)/shard_map/gather | solution.py:197
  173.5 0.6 maximum_maximum_fusion
  (34 shorter events, 0.2 us)
Async XLA Ops:
  7.2 112.5 %all-gather.3.cloned.1.call-start = ((), (), s32[]{:S(2)}) async-start(), calls=%async_computation.2 | async-start | bytes 4456448 | tf_op jit(solution)/shard_map/all_gather | solution.py:162
  9.1 77.2 %collective-permute-start = (bf16[256,2048]{1,0:T(8,128)(2,1)}, bf16[256,2048]{1,0:T(8,128)(2,1)}, u32[]{:S(2)}, u32[]{:S(2)}) collective-permute-start(bf16[256,2048]{1,0:T(8,128)(2,1)} %param.8), channel_id=1, source_target_pairs={{0,32},{32,64},{64,96},{96,0},{1,33},{33,65},{65,97},{97,1},{2,34}... | collective-permute-start | bytes 3145736 | tf_op jit(solution)/shard_map/ppermute | solution.py:127
  11.3 79.4 %collective-permute-start.5 = (bf16[256,2048]{1,0:T(8,128)(2,1)}, bf16[256,2048]{1,0:T(8,128)(2,1)}, u32[]{:S(2)}, u32[]{:S(2)}) collective-permute-start(bf16[256,2048]{1,0:T(8,128)(2,1)} %param.8), channel_id=1, source_target_pairs={{0,96},{32,0},{64,32},{96,64},{1,97},{33,1},{65,33},{97,65},{2,98}... | collective-permute-start | bytes 3145736 | tf_op jit(solution)/shard_map/ppermute | solution.py:127
  12.8 82.5 %collective-permute-start.6 = (bf16[256,2048]{1,0:T(8,128)(2,1)}, bf16[256,2048]{1,0:T(8,128)(2,1)}, u32[]{:S(2)}, u32[]{:S(2)}) collective-permute-start(bf16[256,2048]{1,0:T(8,128)(2,1)} %param.8), channel_id=1, source_target_pairs={{0,1},{1,0},{2,3},{3,2},{4,5},{5,4},{6,7},{7,6},{8,9},{9,8},{10,11... | collective-permute-start | bytes 3145736 | tf_op jit(solution)/shard_map/ppermute | solution.py:141
  15.1 47.1 %collective-permute-start.1 = (bf16[128,2048]{1,0:T(8,128)(2,1)S(1)}, bf16[128,2048]{1,0:T(8,128)(2,1)}, u32[]{:S(2)}, u32[]{:S(2)}) collective-permute-start(bf16[128,2048]{1,0:T(8,128)(2,1)S(1)} %get-tuple-element.100), channel_id=1, source_target_pairs={{0,32},{32,64},{64,96},{96,0},{1,33},{33,65},{65,97},{97,1},{2,34}... | collective-permute-start | bytes 1572872 | tf_op jit(solution)/shard_map/ppermute | solution.py:127
  15.3 47.6 %collective-permute-start.3 = (bf16[128,2048]{1,0:T(8,128)(2,1)S(1)}, bf16[128,2048]{1,0:T(8,128)(2,1)}, u32[]{:S(2)}, u32[]{:S(2)}) collective-permute-start(bf16[128,2048]{1,0:T(8,128)(2,1)S(1)} %get-tuple-element.99), channel_id=1, source_target_pairs={{0,96},{32,0},{64,32},{96,64},{1,97},{33,1},{65,33},{97,65},{2,98}... | collective-permute-start | bytes 1572872 | tf_op jit(solution)/shard_map/ppermute | solution.py:127
  25.2 75.7 %all-to-all-start = ((bf16[128,4,2176]{2,1,0:T(4,128)(2,1)}), bf16[128,4,2176]{2,1,0:T(4,128)(2,1)S(1)}, u32[]{:S(2)}, u32[]{:S(2)}) async-start(bf16[128,4,2176]{2,1,0:T(4,128)(2,1)} %reshape.238), calls=%async_computation | async-start | bytes 4456448 | tf_op jit(solution)/shard_map/all_to_all | solution.py:188
  33.5 106.1 %all-gather.5.cloned.1.call-start = ((), (), s32[]{:S(2)}) async-start(), calls=%async_computation.3 | async-start | bytes 4456448 | tf_op jit(solution)/shard_map/all_gather | solution.py:162
  62.2 19.9 %collective-permute-start.2 = (bf16[128,2048]{1,0:T(8,128)(2,1)}, bf16[128,2048]{1,0:T(8,128)(2,1)}, u32[]{:S(2)}, u32[]{:S(2)}) collective-permute-start(bf16[128,2048]{1,0:T(8,128)(2,1)} %collective-permute-done.1), channel_id=1, source_target_pairs={{0,32},{32,64},{64,96},{96,0},{1,33},{33,65},{65,97},{97,1},{2,34}... | collective-permute-start | bytes 1572872 | tf_op jit(solution)/shard_map/ppermute | solution.py:127
  62.9 19.2 %collective-permute-start.4 = (bf16[128,2048]{1,0:T(8,128)(2,1)}, bf16[128,2048]{1,0:T(8,128)(2,1)}, u32[]{:S(2)}, u32[]{:S(2)}) collective-permute-start(bf16[128,2048]{1,0:T(8,128)(2,1)} %collective-permute-done.3), channel_id=1, source_target_pairs={{0,96},{32,0},{64,32},{96,64},{1,97},{33,1},{65,33},{97,65},{2,98}... | collective-permute-start | bytes 1572872 | tf_op jit(solution)/shard_map/ppermute | solution.py:127
  66.2 12.2 %copy-start = (bf16[256,2048]{1,0:T(8,128)(2,1)S(1)}, bf16[256,2048]{1,0:T(8,128)(2,1)}, u32[]{:S(2)}) copy-start(bf16[256,2048]{1,0:T(8,128)(2,1)} %param.8) | copy-start | bytes 3145732
  83.5 15.3 %collective-permute-start.8 = (bf16[256,2048]{1,0:T(8,128)(2,1)S(1)}, bf16[256,2048]{1,0:T(8,128)(2,1)S(1)}, u32[]{:S(2)}, u32[]{:S(2)}) collective-permute-start(bf16[256,2048]{1,0:T(8,128)(2,1)S(1)} %pad_maximum_fusion), channel_id=1, source_target_pairs={{0,1},{1,0},{2,3},{3,2},{4,5},{5,4},{6,7},{7,6},{8,9},{9,8},{10,11... | collective-permute-start | bytes 3145736 | tf_op jit(solution)/shard_map/ppermute | solution.py:141
  86.3 11.3 %collective-permute-start.7 = (bf16[256,2048]{1,0:T(8,128)(2,1)}, bf16[256,2048]{1,0:T(8,128)(2,1)S(1)}, u32[]{:S(2)}, u32[]{:S(2)}) collective-permute-start(bf16[256,2048]{1,0:T(8,128)(2,1)} %collective-permute-done), channel_id=1, source_target_pairs={{0,1},{1,0},{2,3},{3,2},{4,5},{5,4},{6,7},{7,6},{8,9},{9,8},{10,11... | collective-permute-start | bytes 3145736 | tf_op jit(solution)/shard_map/ppermute | solution.py:141
  90.7 9.2 %collective-permute-start.9 = (bf16[256,2048]{1,0:T(8,128)(2,1)}, bf16[256,2048]{1,0:T(8,128)(2,1)S(1)}, u32[]{:S(2)}, u32[]{:S(2)}) collective-permute-start(bf16[256,2048]{1,0:T(8,128)(2,1)} %collective-permute-done.5), channel_id=1, source_target_pairs={{0,1},{1,0},{2,3},{3,2},{4,5},{5,4},{6,7},{7,6},{8,9},{9,8},{10,11... | collective-permute-start | bytes 3145736 | tf_op jit(solution)/shard_map/ppermute | solution.py:141
  111.1 58.4 %all-to-all-start.1 = ((f32[128,1,4]{2,1,0:T(1,128)}), f32[128,1,4]{2,1,0:T(1,128)S(1)}, u32[]{:S(2)}, u32[]{:S(2)}) async-start(f32[128,1,4]{2,1,0:T(1,128)} %bitcast.19), calls=%async_computation.1 | async-start | bytes 131072 | tf_op jit(solution)/shard_map/all_to_all | solution.py:194
  159.1 7.4 %collective-permute-start.16 = (f32[256]{0:T(256)S(1)}, f32[256]{0:T(256)S(1)}, u32[]{:S(2)}, u32[]{:S(2)}) collective-permute-start(f32[256]{0:T(256)S(1)} %bitcast.71), channel_id=1, source_target_pairs={{0,33},{1,32},{32,65},{33,64},{64,97},{65,96},{96,1},{97,0},{2,35}... | collective-permute-start | bytes 3080 | tf_op jit(solution)/shard_map/ppermute | solution.py:178
  160.8 6.6 %collective-permute-start.15 = (f32[256]{0:T(256)S(1)}, f32[256]{0:T(256)S(1)}, u32[]{:S(2)}, u32[]{:S(2)}) collective-permute-start(f32[256]{0:T(256)S(1)} %bitcast.70), channel_id=1, source_target_pairs={{0,65},{1,64},{32,97},{33,96},{64,1},{65,0},{96,33},{97,32},{2,67}... | collective-permute-start | bytes 3080 | tf_op jit(solution)/shard_map/ppermute | solution.py:178
  164.6 8.9 %collective-permute-start.14 = (f32[256]{0:T(256)S(1)}, f32[256]{0:T(256)S(1)}, u32[]{:S(2)}, u32[]{:S(2)}) collective-permute-start(f32[256]{0:T(256)S(1)} %bitcast.69), channel_id=1, source_target_pairs={{0,97},{1,96},{32,1},{33,0},{64,33},{65,32},{96,65},{97,64},{2,99}... | collective-permute-start | bytes 3080 | tf_op jit(solution)/shard_map/ppermute | solution.py:178
  166.0 7.5 %collective-permute-start.13 = (f32[256]{0:T(256)S(1)}, f32[256]{0:T(256)S(1)}, u32[]{:S(2)}, u32[]{:S(2)}) collective-permute-start(f32[256]{0:T(256)S(1)} %bitcast.68), channel_id=1, source_target_pairs={{0,1},{1,0},{32,33},{33,32},{64,65},{65,64},{96,97},{97,96},{2,3},... | collective-permute-start | bytes 3080 | tf_op jit(solution)/shard_map/ppermute | solution.py:178
  166.2 7.3 %collective-permute-start.12 = (f32[256]{0:T(256)S(1)}, f32[256]{0:T(256)S(1)}, u32[]{:S(2)}, u32[]{:S(2)}) collective-permute-start(f32[256]{0:T(256)S(1)} %bitcast.67), channel_id=1, source_target_pairs={{0,32},{1,33},{32,64},{33,65},{64,96},{65,97},{96,0},{97,1},{2,34}... | collective-permute-start | bytes 3080 | tf_op jit(solution)/shard_map/ppermute | solution.py:178
  166.5 7.0 %collective-permute-start.11 = (f32[256]{0:T(256)S(1)}, f32[256]{0:T(256)S(1)}, u32[]{:S(2)}, u32[]{:S(2)}) collective-permute-start(f32[256]{0:T(256)S(1)} %bitcast.66), channel_id=1, source_target_pairs={{0,64},{1,65},{32,96},{33,97},{64,0},{65,1},{96,32},{97,33},{2,66}... | collective-permute-start | bytes 3080 | tf_op jit(solution)/shard_map/ppermute | solution.py:178
  167.4 6.1 %collective-permute-start.10 = (f32[256]{0:T(256)S(1)}, f32[256]{0:T(256)S(1)}, u32[]{:S(2)}, u32[]{:S(2)}) collective-permute-start(f32[256]{0:T(256)S(1)} %bitcast.65), channel_id=1, source_target_pairs={{0,96},{1,97},{32,0},{33,1},{64,32},{65,33},{96,64},{97,65},{2,98}... | collective-permute-start | bytes 3080 | tf_op jit(solution)/shard_map/ppermute | solution.py:178
Sparse Core Ops, SparseCore 0:
  10.1 73.4 all-gather.2
  85.8 49.9 all-gather.4

commit v8 on v5

--- a/solution.py
+++ b/solution.py
@@ -96,6 +96,40 @@
     return out.reshape((n * x.shape[0],) + x.shape[1:])
 
 
+def score_kernel(rows_ref, cents_ref, noise_ref, out_ref):
+    scores = lax.dot_general(
+        rows_ref[...], cents_ref[...], (((1,), (1,)), ((), ())), preferred_element_type=jnp.float32
+    )
+    best = jnp.max(inverse_temp * scores + noise_ref[...], axis=1, keepdims=True)
+
+    @pl.when(pl.program_id(1) == 0)
+    def _():
+        out_ref[...] = best
+
+    @pl.when(pl.program_id(1) > 0)
+    def _():
+        out_ref[...] = jnp.maximum(out_ref[...], best)
+
+
+def score_max(rows, cents, noise):
+    count, width = rows.shape
+    tm = min(512, count)
+    tn = min(512, cents.shape[0])
+    out = pl.pallas_call(
+        score_kernel,
+        out_shape=jax.ShapeDtypeStruct((count, 1), jnp.float32),
+        grid=(count // tm, cents.shape[0] // tn),
+        in_specs=[
+            pl.BlockSpec((tm, width), lambda i, j: (i, 0)),
+            pl.BlockSpec((tn, width), lambda i, j: (j, 0)),
+            pl.BlockSpec((tm, tn), lambda i, j: (i, j)),
+        ],
+        out_specs=pl.BlockSpec((tm, 1), lambda i, j: (i, 0)),
+        compiler_params=pltpu.CompilerParams(dimension_semantics=("parallel", "arbitrary")),
+    )(rows, cents, noise)
+    return out[:, 0]
+
+
 def cluster_stats(members, valid):
     feature_dim = members.shape[1]
     widened = members.astype(jnp.float32)
@@ -136,23 +170,8 @@
     cpos = jnp.arange(nz * nx * cent_dev, dtype=jnp.int32)
     cent_dev_ids = ((iy * nz + cpos // (nx * cent_dev)) * nx + cpos // cent_dev % nx) * nc + ic
     cent_ids = cent_dev_ids * cent_dev + cpos % cent_dev
-    piece_rows = piece.shape[0]
-    block = math.gcd(piece_rows, 512)
-    steps = piece_rows // block
-    tiles = piece.reshape(steps, block, feature_dim)
     noise = gumbel_noise(group_ids[:, None], cent_ids[None, :], salt_word)
-    noise_tiles = noise.reshape(group.shape[0], steps, block).transpose(1, 0, 2)
-    initial = jnp.full((group.shape[0],), -1e30, jnp.float32)
-
-    def step(carry, item):
-        tile, noise_tile = item
-        scores = lax.dot_general(
-            group, tile, (((1,), (1,)), ((), ())), preferred_element_type=jnp.float32
-        )
-        perturbed = inverse_temp * scores + noise_tile
-        return (jnp.maximum(carry, jnp.max(perturbed, axis=1)), None)
-
-    result, unused = lax.scan(step, initial, (tiles, noise_tiles))
+    result = score_max(group, piece, noise)
     blocks = result.reshape(nc, ny, rows_dev)
     best = blocks[0, 0]
     for sc in range(nc):

time: 172 us -> 165 us (0.959)
  matrix products: 42.5 us -> 3.61 us
  Pallas kernels: 0 us -> 31 us
    dot_general x4 -> x0, matrix products: 38.8 us -> none  [step(): lax.dot_general(group, tile, (((1,), (1,)), ((), ())), preferred_element_...]
    pallas_call x0 -> x1, Pallas kernels: none -> 31 us  [score_max(): pl.pallas_call(score_kernel, out_shape=jax.ShapeDtypeStruct((count, 1), j...]
  transfers between devices with their start and end apart: 17 -> 17, of which waited for: 1 -> 1; matrix products, arithmetic and copies ran while one was open for 51% -> 30% of each run, Pallas kernels for 0% -> 19%
where the time goes in v8:
time: 165 us; the launch traced here: 164 us
  starting transfers between devices  37.2 us (23%)
  waiting for transfers between devices  31.2 us (19%)
  Pallas kernels  31 us (19%)
  local copies, waits for them, and re-layouts  24.1 us (15%)
  other arithmetic  21.7 us (13%)
  between operations  15.5 us (9%)
  matrix products  3.61 us (2%)
    pallas_call x1, Pallas kernels, score_max(): pl.pallas_call(score_kernel, out_shape=jax.ShapeDtypeStruct((count, 1), j...  31 us
    ppermute x3, waiting for transfers between devices, shards(): lax.ppermute(embeddings, 'y', [(i, (i + s) % ny) for i in range(ny)])  30.5 us
    neg x1, other arithmetic, gumbel_noise(): return -jnp.log(-jnp.log(uniform))  12 us
    unnamed x10, local copies, waits for them, and re-layouts  11.3 us
    all_to_all x1, starting transfers between devices, shards(): lax.all_to_all(scores.reshape(devices, capacity), ALL, split_axis=0, conc...  9.71 us
    ppermute x7, starting transfers between devices, shards(): best = jnp.maximum(best, lax.ppermute(blocks[sc, sy], ('y', 'c'), perm))  8.67 us
    all_to_all x1, starting transfers between devices, shards(): lax.all_to_all(outgoing.reshape(devices, capacity, feature_dim + flag_wid...  7.56 us
    ppermute x3, starting transfers between devices, shards(): lax.ppermute(embeddings, 'y', [(i, (i + s) % ny) for i in range(ny)])  5.88 us
  transfers between devices with their start and end apart: 17, of which 1 were waited for; matrix products, arithmetic and copies ran while one was open for 30% of the time, Pallas kernels for 19%

profile of v8, /device:TPU:1, one launch (start us, length us, event | category | flops | bytes accessed | tf_op | source)
XLA Modules:
  0.0 164.4 jit_solution(7358121011544769)
XLA Ops:
  7.2 0.0 all-gather.2.cloned.1.call-start
  7.2 0.7 all-gather.2.cloned.1.call-update
  7.9 2.2 %collective-permute-start = (bf16[256,2048]{1,0:T(8,128)(2,1)}, bf16[256,2048]{1,0:T(8,128)(2,1)}, u32[]{:S(2)}, u32[]{:S(2)}) collective-permute-start(bf16[256,2048]{1,0:T(8,128)(2,1)} %param.4), channel_id=1, source_target_pairs={{0,32},{32,64},{64,96},{96,0},{1,33},{33,65},{65,97},{97,1},{2,34}... | collective-permute-start | bytes 3145736 | tf_op jit(solution)/shard_map/ppermute | solution.py:161
  10.1 2.6 %collective-permute-start.1 = (bf16[256,2048]{1,0:T(8,128)(2,1)}, bf16[256,2048]{1,0:T(8,128)(2,1)}, u32[]{:S(2)}, u32[]{:S(2)}) collective-permute-start(bf16[256,2048]{1,0:T(8,128)(2,1)} %param.4), channel_id=1, source_target_pairs={{0,64},{32,96},{64,0},{96,32},{1,65},{33,97},{65,1},{97,33},{2,66}... | collective-permute-start | bytes 3145736 | tf_op jit(solution)/shard_map/ppermute | solution.py:161
  12.7 1.1 collective-permute-start.2
  13.8 1.5 collective-permute-start.3
  15.3 0.9 convert_reduce_fusion
  16.3 0.7 compare_select_fusion
  16.9 3.6 %scatter_custom_fusion = bf16[512,2176]{1,0:T(8,128)(2,1)S(1)} fusion(s32[256]{0:T(256)S(1)} %bitcast.23, bf16[256,2048]{1,0:T(8,128)(2,1)} %param.4, bf16[]{:T(256)} %constant.137.clone.1, bf16[]{:T(256)} %constant.135.clone.1), kind=kCustom, calls=%fused_computation.26 | custom fusion | bytes 3276804 | tf_op jit(solution)/shard_map/scatter | solution.py:191
  20.6 2.1 %reshape.188 = bf16[128,4,2176]{2,1,0:T(4,128)(2,1)} reshape(bf16[512,2176]{1,0:T(8,128)(2,1)S(1)} %scatter_custom_fusion) | data formatting | bytes 4456448 | tf_op jit(solution)/shard_map/reshape | solution.py:193
  22.7 7.6 %all-to-all-start = ((bf16[128,4,2176]{2,1,0:T(4,128)(2,1)}), bf16[128,4,2176]{2,1,0:T(4,128)(2,1)S(1)}, u32[]{:S(2)}, u32[]{:S(2)}) async-start(bf16[128,4,2176]{2,1,0:T(4,128)(2,1)} %reshape.188), calls=%async_computation | async-start | bytes 4456448 | tf_op jit(solution)/shard_map/all_to_all | solution.py:192
  31.0 0.1 pad_add_fusion
  31.1 0.1 add_multiply_fusion
  31.1 0.1 multiply_bitcast_fusion
  31.2 0.0 copy-start
  31.2 12.0 %fusion.9.noise_ref = f32[2048,2048]{1,0:T(8,128)} fusion(s32[]{:T(128)} %bitcast.19, s32[2048]{0:T(1024)S(1)} %fusion.46, s32[2048]{0:T(1024)S(1)} %bitcast.20), kind=kLoop, calls=%fused_computation.14 | loop fusion | flops 67108864 | bytes 16793604 | tf_op jit(solution)/shard_map/neg | solution.py:30
  43.3 1.1 constant_dynamic-update-slice_fusion.7
  44.4 0.0 collective-permute-done
  44.4 1.1 collective-permute-start.4
  45.5 30.5 %collective-permute-done.1 = bf16[256,2048]{1,0:T(8,128)(2,1)} collective-permute-done((bf16[256,2048]{1,0:T(8,128)(2,1)}, bf16[256,2048]{1,0:T(8,128)(2,1)}, u32[]{:S(2)}, u32[]{:S(2)}) %collective-permute-start.1) | collective-permute-done | bytes 1048608 | tf_op jit(solution)/shard_map/ppermute | solution.py:161
  76.0 2.7 %collective-permute-start.5 = (bf16[256,2048]{1,0:T(8,128)(2,1)}, bf16[256,2048]{1,0:T(8,128)(2,1)S(1)}, u32[]{:S(2)}, u32[]{:S(2)}) collective-permute-start(bf16[256,2048]{1,0:T(8,128)(2,1)} %collective-permute-done.1), channel_id=1, source_target_pairs={{0,1},{1,0},{2,3},{3,2},{4,5},{5,4},{6,7},{7,6},{8,9},{9,8},{10,11... | collective-permute-start | bytes 3145736 | tf_op jit(solution)/shard_map/ppermute | solution.py:164
  78.7 2.3 %constant_dynamic-update-slice_fusion.6 = bf16[2048,2048]{1,0:T(8,128)(2,1)} fusion(bf16[2048,2048]{1,0:T(8,128)(2,1)} %constant_dynamic-update-slice_fusion.7, bf16[256,2048]{1,0:T(8,128)(2,1)} %collective-permute-done), kind=kLoop, calls=%fused_computation.42 | loop fusion | bytes 2097152
  81.0 0.0 collective-permute-done.2
  81.0 0.0 collective-permute-start.6
  81.0 2.4 %constant_dynamic-update-slice_fusion.5 = bf16[2048,2048]{1,0:T(8,128)(2,1)} fusion(bf16[2048,2048]{1,0:T(8,128)(2,1)} %constant_dynamic-update-slice_fusion.6, bf16[256,2048]{1,0:T(8,128)(2,1)} %collective-permute-done.1), kind=kLoop, calls=%fused_computation.41 | loop fusion | bytes 2097152
  83.4 1.0 constant_dynamic-update-slice_fusion.4
  84.4 0.0 collective-permute-done.3
  84.4 2.4 %constant_dynamic-update-slice_fusion.3 = bf16[2048,2048]{1,0:T(8,128)(2,1)} fusion(bf16[2048,2048]{1,0:T(8,128)(2,1)} %constant_dynamic-update-slice_fusion.4, bf16[256,2048]{1,0:T(8,128)(2,1)} %collective-permute-done.3), kind=kLoop, calls=%fused_computation.39 | loop fusion | bytes 2097152
  86.8 0.0 collective-permute-done.4
  86.8 1.0 constant_dynamic-update-slice_fusion.2
  87.8 0.0 collective-permute-done.5
  87.8 1.0 constant_dynamic-update-slice_fusion.1
  88.9 0.0 collective-permute-done.6
  88.9 1.1 constant_dynamic-update-slice_fusion.rows_ref
  90.0 0.0 all-to-all-done
  90.0 2.1 %reshape.189 = bf16[512,2176]{1,0:T(8,128)(2,1)} reshape(bf16[128,4,2176]{2,1,0:T(4,128)(2,1)S(1)} %all-to-all-done) | data formatting | bytes 4456448 | tf_op jit(solution)/shard_map/reshape | solution.py:194
  92.1 1.1 compare_reduce_fusion
  93.1 0.2 fusion.33
  93.3 2.4 %fusion.11 = (f32[2048]{0:T(1024)S(1)}, f32[512]{0:T(512)S(1)}) fusion(pred[512]{0:T(512)(128)(4,1)S(1)} %compare_reduce_fusion, bf16[512,2176]{1,0:T(8,128)(2,1)} %reshape.189), kind=kLoop, calls=%fused_computation.18 | loop fusion | flops 5240320 | bytes 2107904 | tf_op jit(solution)/shard_map/reduce_sum | solution.py:145
  95.7 3.6 %fusion.26 = f32[512]{0:T(512)S(1)} fusion(bf16[512,2176]{1,0:T(8,128)(2,1)} %reshape.189, f32[512]{0:T(512)S(1)} %add_rsqrt_fusion, pred[512]{0:T(512)(128)(4,1)S(1)} %compare_reduce_fusion), kind=kOutput, calls=%fused_computation.25 | convolution fusion | flops 1075576320 | bytes 2103808 | tf_op jit(solution)/shard_map/dot_general | solution.py:137
  99.3 0.7 select_n.88
  100.1 9.7 %all-to-all-start.1 = ((f32[128,1,4]{2,1,0:T(1,128)}), f32[128,1,4]{2,1,0:T(1,128)S(1)}, u32[]{:S(2)}, u32[]{:S(2)}) async-start(f32[128,1,4]{2,1,0:T(1,128)} %bitcast.14), calls=%async_computation.1 | async-start | bytes 131072 | tf_op jit(solution)/shard_map/all_to_all | solution.py:198
  109.8 0.0 all-gather.2.cloned.1.call-done.cents_ref
  109.8 31.0 %shard_map.67 = f32[2048,1]{1,0:T(8,128)} custom-call(bf16[2048,2048]{1,0:T(8,128)(2,1)} %constant_dynamic-update-slice_fusion.rows_ref, bf16[2048,2048]{1,0:T(8,128)(2,1)} %all-gather.2.cloned.1.call-done.cents_ref, f32[2048,2048]{1,0:T(8,128)} %fusion.9.noise_ref), custom_call_target="tpu_custom_call" | custom-call | tf_op jit(solution)/shard_map/pallas_call | solution.py:118
  140.8 1.6 reduce
  142.4 1.7 %collective-permute-start.13 = (f32[256]{0:T(256)S(1)}, f32[256]{0:T(256)S(1)}, u32[]{:S(2)}, u32[]{:S(2)}) collective-permute-start(f32[256]{0:T(256)S(1)} %bitcast.33), channel_id=1, source_target_pairs={{0,33},{1,32},{32,65},{33,64},{64,97},{65,96},{96,1},{97,0},{2,35}... | collective-permute-start | bytes 3080 | tf_op jit(solution)/shard_map/ppermute | solution.py:182
  144.1 2.5 %collective-permute-start.12 = (f32[256]{0:T(256)S(1)}, f32[256]{0:T(256)S(1)}, u32[]{:S(2)}, u32[]{:S(2)}) collective-permute-start(f32[256]{0:T(256)S(1)} %bitcast.32), channel_id=1, source_target_pairs={{0,65},{1,64},{32,97},{33,96},{64,1},{65,0},{96,33},{97,32},{2,67}... | collective-permute-start | bytes 3080 | tf_op jit(solution)/shard_map/ppermute | solution.py:182
  146.7 0.6 multiply_reduce_fusion
  147.9 1.4 collective-permute-start.11
  149.4 0.2 collective-permute-start.10
  149.5 0.4 collective-permute-start.9
  149.9 0.0 collective-permute-done.13
  149.9 0.9 collective-permute-start.8
  150.8 1.6 collective-permute-start.7
  152.4 0.6 broadcast_multiply_fusion
  153.0 0.5 broadcast.300
  153.5 0.8 reduce.6
  154.3 0.1 reshape.190
  154.4 2.5 %gather_fusion = f32[256]{0:T(256)} fusion(f32[512]{0:T(512)S(1)} %reshape.190, s32[1024]{0:T(1024)S(1)} %pad_clamp_fusion), kind=kCustom, calls=%fused_computation | custom fusion | bytes 3072 | tf_op jit(solution)/shard_map/gather | solution.py:201
  156.9 0.0 collective-permute-done.11
  156.9 0.0 collective-permute-done.10
  156.9 0.0 collective-permute-done.9
  157.0 0.0 collective-permute-done.8
  157.0 0.6 maximum_maximum_fusion
  (12 shorter events, 0.1 us)
Async XLA Ops:
  7.2 102.6 %all-gather.2.cloned.1.call-start = ((), (), s32[]{:S(2)}) async-start(), calls=%async_computation.2 | async-start | bytes 8912896 | tf_op jit(solution)/shard_map/all_gather | solution.py:165
  7.9 36.5 %collective-permute-start = (bf16[256,2048]{1,0:T(8,128)(2,1)}, bf16[256,2048]{1,0:T(8,128)(2,1)}, u32[]{:S(2)}, u32[]{:S(2)}) collective-permute-start(bf16[256,2048]{1,0:T(8,128)(2,1)} %param.4), channel_id=1, source_target_pairs={{0,32},{32,64},{64,96},{96,0},{1,33},{33,65},{65,97},{97,1},{2,34}... | collective-permute-start | bytes 3145736 | tf_op jit(solution)/shard_map/ppermute | solution.py:161
  10.1 65.9 %collective-permute-start.1 = (bf16[256,2048]{1,0:T(8,128)(2,1)}, bf16[256,2048]{1,0:T(8,128)(2,1)}, u32[]{:S(2)}, u32[]{:S(2)}) collective-permute-start(bf16[256,2048]{1,0:T(8,128)(2,1)} %param.4), channel_id=1, source_target_pairs={{0,64},{32,96},{64,0},{96,32},{1,65},{33,97},{65,1},{97,33},{2,66}... | collective-permute-start | bytes 3145736 | tf_op jit(solution)/shard_map/ppermute | solution.py:161
  12.7 68.3 %collective-permute-start.2 = (bf16[256,2048]{1,0:T(8,128)(2,1)}, bf16[256,2048]{1,0:T(8,128)(2,1)S(1)}, u32[]{:S(2)}, u32[]{:S(2)}) collective-permute-start(bf16[256,2048]{1,0:T(8,128)(2,1)} %param.4), channel_id=1, source_target_pairs={{0,96},{32,0},{64,32},{96,64},{1,97},{33,1},{65,33},{97,65},{2,98}... | collective-permute-start | bytes 3145736 | tf_op jit(solution)/shard_map/ppermute | solution.py:161
  13.8 70.6 %collective-permute-start.3 = (bf16[256,2048]{1,0:T(8,128)(2,1)}, bf16[256,2048]{1,0:T(8,128)(2,1)}, u32[]{:S(2)}, u32[]{:S(2)}) collective-permute-start(bf16[256,2048]{1,0:T(8,128)(2,1)} %param.4), channel_id=1, source_target_pairs={{0,1},{1,0},{2,3},{3,2},{4,5},{5,4},{6,7},{7,6},{8,9},{9,8},{10,11... | collective-permute-start | bytes 3145736 | tf_op jit(solution)/shard_map/ppermute | solution.py:164
  22.7 67.2 %all-to-all-start = ((bf16[128,4,2176]{2,1,0:T(4,128)(2,1)}), bf16[128,4,2176]{2,1,0:T(4,128)(2,1)S(1)}, u32[]{:S(2)}, u32[]{:S(2)}) async-start(bf16[128,4,2176]{2,1,0:T(4,128)(2,1)} %reshape.188), calls=%async_computation | async-start | bytes 4456448 | tf_op jit(solution)/shard_map/all_to_all | solution.py:192
  31.2 12.0 %copy-start = (bf16[256,2048]{1,0:T(8,128)(2,1)S(1)}, bf16[256,2048]{1,0:T(8,128)(2,1)}, u32[]{:S(2)}) copy-start(bf16[256,2048]{1,0:T(8,128)(2,1)} %param.4) | copy-start | bytes 3145732
  44.4 42.4 %collective-permute-start.4 = (bf16[256,2048]{1,0:T(8,128)(2,1)}, bf16[256,2048]{1,0:T(8,128)(2,1)S(1)}, u32[]{:S(2)}, u32[]{:S(2)}) collective-permute-start(bf16[256,2048]{1,0:T(8,128)(2,1)} %collective-permute-done), channel_id=1, source_target_pairs={{0,1},{1,0},{2,3},{3,2},{4,5},{5,4},{6,7},{7,6},{8,9},{9,8},{10,11... | collective-permute-start | bytes 3145736 | tf_op jit(solution)/shard_map/ppermute | solution.py:164
  76.0 11.9 %collective-permute-start.5 = (bf16[256,2048]{1,0:T(8,128)(2,1)}, bf16[256,2048]{1,0:T(8,128)(2,1)S(1)}, u32[]{:S(2)}, u32[]{:S(2)}) collective-permute-start(bf16[256,2048]{1,0:T(8,128)(2,1)} %collective-permute-done.1), channel_id=1, source_target_pairs={{0,1},{1,0},{2,3},{3,2},{4,5},{5,4},{6,7},{7,6},{8,9},{9,8},{10,11... | collective-permute-start | bytes 3145736 | tf_op jit(solution)/shard_map/ppermute | solution.py:164
  81.0 7.9 %collective-permute-start.6 = (bf16[256,2048]{1,0:T(8,128)(2,1)S(1)}, bf16[256,2048]{1,0:T(8,128)(2,1)S(1)}, u32[]{:S(2)}, u32[]{:S(2)}) collective-permute-start(bf16[256,2048]{1,0:T(8,128)(2,1)S(1)} %collective-permute-done.2), channel_id=1, source_target_pairs={{0,1},{1,0},{2,3},{3,2},{4,5},{5,4},{6,7},{7,6},{8,9},{9,8},{10,11... | collective-permute-start | bytes 3145736 | tf_op jit(solution)/shard_map/ppermute | solution.py:164
  100.1 52.9 %all-to-all-start.1 = ((f32[128,1,4]{2,1,0:T(1,128)}), f32[128,1,4]{2,1,0:T(1,128)S(1)}, u32[]{:S(2)}, u32[]{:S(2)}) async-start(f32[128,1,4]{2,1,0:T(1,128)} %bitcast.14), calls=%async_computation.1 | async-start | bytes 131072 | tf_op jit(solution)/shard_map/all_to_all | solution.py:198
  142.4 7.4 %collective-permute-start.13 = (f32[256]{0:T(256)S(1)}, f32[256]{0:T(256)S(1)}, u32[]{:S(2)}, u32[]{:S(2)}) collective-permute-start(f32[256]{0:T(256)S(1)} %bitcast.33), channel_id=1, source_target_pairs={{0,33},{1,32},{32,65},{33,64},{64,97},{65,96},{96,1},{97,0},{2,35}... | collective-permute-start | bytes 3080 | tf_op jit(solution)/shard_map/ppermute | solution.py:182
  144.1 6.6 %collective-permute-start.12 = (f32[256]{0:T(256)S(1)}, f32[256]{0:T(256)S(1)}, u32[]{:S(2)}, u32[]{:S(2)}) collective-permute-start(f32[256]{0:T(256)S(1)} %bitcast.32), channel_id=1, source_target_pairs={{0,65},{1,64},{32,97},{33,96},{64,1},{65,0},{96,33},{97,32},{2,67}... | collective-permute-start | bytes 3080 | tf_op jit(solution)/shard_map/ppermute | solution.py:182
  147.9 9.0 %collective-permute-start.11 = (f32[256]{0:T(256)S(1)}, f32[256]{0:T(256)S(1)}, u32[]{:S(2)}, u32[]{:S(2)}) collective-permute-start(f32[256]{0:T(256)S(1)} %bitcast.31), channel_id=1, source_target_pairs={{0,97},{1,96},{32,1},{33,0},{64,33},{65,32},{96,65},{97,64},{2,99}... | collective-permute-start | bytes 3080 | tf_op jit(solution)/shard_map/ppermute | solution.py:182
  149.4 7.6 %collective-permute-start.10 = (f32[256]{0:T(256)S(1)}, f32[256]{0:T(256)S(1)}, u32[]{:S(2)}, u32[]{:S(2)}) collective-permute-start(f32[256]{0:T(256)S(1)} %bitcast.30), channel_id=1, source_target_pairs={{0,1},{1,0},{32,33},{33,32},{64,65},{65,64},{96,97},{97,96},{2,3},... | collective-permute-start | bytes 3080 | tf_op jit(solution)/shard_map/ppermute | solution.py:182
  149.5 7.4 %collective-permute-start.9 = (f32[256]{0:T(256)S(1)}, f32[256]{0:T(256)S(1)}, u32[]{:S(2)}, u32[]{:S(2)}) collective-permute-start(f32[256]{0:T(256)S(1)} %bitcast.29), channel_id=1, source_target_pairs={{0,32},{1,33},{32,64},{33,65},{64,96},{65,97},{96,0},{97,1},{2,34}... | collective-permute-start | bytes 3080 | tf_op jit(solution)/shard_map/ppermute | solution.py:182
  149.9 7.1 %collective-permute-start.8 = (f32[256]{0:T(256)S(1)}, f32[256]{0:T(256)S(1)}, u32[]{:S(2)}, u32[]{:S(2)}) collective-permute-start(f32[256]{0:T(256)S(1)} %bitcast.28), channel_id=1, source_target_pairs={{0,64},{1,65},{32,96},{33,97},{64,0},{65,1},{96,32},{97,33},{2,66}... | collective-permute-start | bytes 3080 | tf_op jit(solution)/shard_map/ppermute | solution.py:182
  150.8 6.2 %collective-permute-start.7 = (f32[256]{0:T(256)S(1)}, f32[256]{0:T(256)S(1)}, u32[]{:S(2)}, u32[]{:S(2)}) collective-permute-start(f32[256]{0:T(256)S(1)} %bitcast.27), channel_id=1, source_target_pairs={{0,96},{1,97},{32,0},{33,1},{64,32},{65,33},{96,64},{97,65},{2,98}... | collective-permute-start | bytes 3080 | tf_op jit(solution)/shard_map/ppermute | solution.py:182
Sparse Core Ops, SparseCore 0:
  10.1 90.6 all-gather.1

commit v9 on v8

--- a/solution.py
+++ b/solution.py
@@ -113,7 +113,7 @@
 
 def score_max(rows, cents, noise):
     count, width = rows.shape
-    tm = min(512, count)
+    tm = min(1024, count)
     tn = min(512, cents.shape[0])
     out = pl.pallas_call(
         score_kernel,

time: 165 us -> 159 us (0.964)
  Pallas kernels: 31 us -> 25.4 us
    pallas_call x1, Pallas kernels: 31 us -> 25.4 us  [score_max(): pl.pallas_call(score_kernel, out_shape=jax.ShapeDtypeStruct((count, 1), j...]
  transfers between devices with their start and end apart: 17 -> 17, of which waited for: 1 -> 1; matrix products, arithmetic and copies ran while one was open for 30% -> 31% of each run, Pallas kernels for 19% -> 16%
where the time goes in v9:
time: 159 us
  starting transfers between devices  37.2 us (23%)
  waiting for transfers between devices  31.2 us (20%)
  Pallas kernels  25.4 us (16%)
  local copies, waits for them, and re-layouts  24.1 us (15%)
  other arithmetic  21.7 us (14%)
  between operations  15.5 us (10%)
  matrix products  3.61 us (2%)
    ppermute x3, waiting for transfers between devices, shards(): lax.ppermute(embeddings, 'y', [(i, (i + s) % ny) for i in range(ny)])  30.5 us
    pallas_call x1, Pallas kernels, score_max(): pl.pallas_call(score_kernel, out_shape=jax.ShapeDtypeStruct((count, 1), j...  25.4 us
    neg x1, other arithmetic, gumbel_noise(): return -jnp.log(-jnp.log(uniform))  12 us
    unnamed x10, local copies, waits for them, and re-layouts  11.3 us
    all_to_all x1, starting transfers between devices, shards(): lax.all_to_all(scores.reshape(devices, capacity), ALL, split_axis=0, conc...  9.71 us
    ppermute x7, starting transfers between devices, shards(): best = jnp.maximum(best, lax.ppermute(blocks[sc, sy], ('y', 'c'), perm))  8.66 us
    all_to_all x1, starting transfers between devices, shards(): lax.all_to_all(outgoing.reshape(devices, capacity, feature_dim + flag_wid...  7.56 us
    ppermute x3, starting transfers between devices, shards(): lax.ppermute(embeddings, 'y', [(i, (i + s) % ny) for i in range(ny)])  5.88 us
  transfers between devices with their start and end apart: 17, of which 1 were waited for; matrix products, arithmetic and copies ran while one was open for 31% of the time, Pallas kernels for 16%

profile of v9, /device:TPU:1, one launch (start us, length us, event | category | flops | bytes accessed | tf_op | source)
XLA Modules:
  0.0 158.7 jit_solution(10051332731997575475)
XLA Ops:
  7.2 0.0 all-gather.2.cloned.1.call-start
  7.2 0.7 all-gather.2.cloned.1.call-update
  7.9 2.2 %collective-permute-start = (bf16[256,2048]{1,0:T(8,128)(2,1)}, bf16[256,2048]{1,0:T(8,128)(2,1)}, u32[]{:S(2)}, u32[]{:S(2)}) collective-permute-start(bf16[256,2048]{1,0:T(8,128)(2,1)} %param.4), channel_id=1, source_target_pairs={{0,32},{32,64},{64,96},{96,0},{1,33},{33,65},{65,97},{97,1},{2,34}... | collective-permute-start | bytes 3145736 | tf_op jit(solution)/shard_map/ppermute | solution.py:161
  10.1 2.6 %collective-permute-start.1 = (bf16[256,2048]{1,0:T(8,128)(2,1)}, bf16[256,2048]{1,0:T(8,128)(2,1)}, u32[]{:S(2)}, u32[]{:S(2)}) collective-permute-start(bf16[256,2048]{1,0:T(8,128)(2,1)} %param.4), channel_id=1, source_target_pairs={{0,64},{32,96},{64,0},{96,32},{1,65},{33,97},{65,1},{97,33},{2,66}... | collective-permute-start | bytes 3145736 | tf_op jit(solution)/shard_map/ppermute | solution.py:161
  12.7 1.1 collective-permute-start.2
  13.8 1.5 collective-permute-start.3
  15.3 0.9 convert_reduce_fusion
  16.3 0.7 compare_select_fusion
  16.9 3.6 %scatter_custom_fusion = bf16[512,2176]{1,0:T(8,128)(2,1)S(1)} fusion(s32[256]{0:T(256)S(1)} %bitcast.23, bf16[256,2048]{1,0:T(8,128)(2,1)} %param.4, bf16[]{:T(256)} %constant.137.clone.1, bf16[]{:T(256)} %constant.135.clone.1), kind=kCustom, calls=%fused_computation.26 | custom fusion | bytes 3276804 | tf_op jit(solution)/shard_map/scatter | solution.py:191
  20.6 2.1 %reshape.188 = bf16[128,4,2176]{2,1,0:T(4,128)(2,1)} reshape(bf16[512,2176]{1,0:T(8,128)(2,1)S(1)} %scatter_custom_fusion) | data formatting | bytes 4456448 | tf_op jit(solution)/shard_map/reshape | solution.py:193
  22.7 7.6 %all-to-all-start = ((bf16[128,4,2176]{2,1,0:T(4,128)(2,1)}), bf16[128,4,2176]{2,1,0:T(4,128)(2,1)S(1)}, u32[]{:S(2)}, u32[]{:S(2)}) async-start(bf16[128,4,2176]{2,1,0:T(4,128)(2,1)} %reshape.188), calls=%async_computation | async-start | bytes 4456448 | tf_op jit(solution)/shard_map/all_to_all | solution.py:192
  31.0 0.1 pad_add_fusion
  31.1 0.1 add_multiply_fusion
  31.1 0.1 multiply_bitcast_fusion
  31.2 0.0 copy-start
  31.2 12.0 %fusion.9.noise_ref = f32[2048,2048]{1,0:T(8,128)} fusion(s32[]{:T(128)} %bitcast.19, s32[2048]{0:T(1024)S(1)} %fusion.46, s32[2048]{0:T(1024)S(1)} %bitcast.20), kind=kLoop, calls=%fused_computation.14 | loop fusion | flops 67108864 | bytes 16793604 | tf_op jit(solution)/shard_map/neg | solution.py:30
  43.3 1.1 constant_dynamic-update-slice_fusion.7
  44.4 0.0 collective-permute-done
  44.4 1.1 collective-permute-start.4
  45.5 30.5 %collective-permute-done.1 = bf16[256,2048]{1,0:T(8,128)(2,1)} collective-permute-done((bf16[256,2048]{1,0:T(8,128)(2,1)}, bf16[256,2048]{1,0:T(8,128)(2,1)}, u32[]{:S(2)}, u32[]{:S(2)}) %collective-permute-start.1) | collective-permute-done | bytes 1048608 | tf_op jit(solution)/shard_map/ppermute | solution.py:161
  76.0 2.7 %collective-permute-start.5 = (bf16[256,2048]{1,0:T(8,128)(2,1)}, bf16[256,2048]{1,0:T(8,128)(2,1)S(1)}, u32[]{:S(2)}, u32[]{:S(2)}) collective-permute-start(bf16[256,2048]{1,0:T(8,128)(2,1)} %collective-permute-done.1), channel_id=1, source_target_pairs={{0,1},{1,0},{2,3},{3,2},{4,5},{5,4},{6,7},{7,6},{8,9},{9,8},{10,11... | collective-permute-start | bytes 3145736 | tf_op jit(solution)/shard_map/ppermute | solution.py:164
  78.7 2.3 %constant_dynamic-update-slice_fusion.6 = bf16[2048,2048]{1,0:T(8,128)(2,1)} fusion(bf16[2048,2048]{1,0:T(8,128)(2,1)} %constant_dynamic-update-slice_fusion.7, bf16[256,2048]{1,0:T(8,128)(2,1)} %collective-permute-done), kind=kLoop, calls=%fused_computation.42 | loop fusion | bytes 2097152
  81.0 0.0 collective-permute-done.2
  81.0 0.0 collective-permute-start.6
  81.0 2.4 %constant_dynamic-update-slice_fusion.5 = bf16[2048,2048]{1,0:T(8,128)(2,1)} fusion(bf16[2048,2048]{1,0:T(8,128)(2,1)} %constant_dynamic-update-slice_fusion.6, bf16[256,2048]{1,0:T(8,128)(2,1)} %collective-permute-done.1), kind=kLoop, calls=%fused_computation.41 | loop fusion | bytes 2097152
  83.4 1.0 constant_dynamic-update-slice_fusion.4
  84.4 0.0 collective-permute-done.3
  84.4 2.4 %constant_dynamic-update-slice_fusion.3 = bf16[2048,2048]{1,0:T(8,128)(2,1)} fusion(bf16[2048,2048]{1,0:T(8,128)(2,1)} %constant_dynamic-update-slice_fusion.4, bf16[256,2048]{1,0:T(8,128)(2,1)} %collective-permute-done.3), kind=kLoop, calls=%fused_computation.39 | loop fusion | bytes 2097152
  86.8 0.0 collective-permute-done.4
  86.8 1.0 constant_dynamic-update-slice_fusion.2
  87.8 0.0 collective-permute-done.5
  87.8 1.0 constant_dynamic-update-slice_fusion.1
  88.9 0.0 collective-permute-done.6
  88.9 1.1 constant_dynamic-update-slice_fusion.rows_ref
  90.0 0.0 all-to-all-done
  90.0 2.1 %reshape.189 = bf16[512,2176]{1,0:T(8,128)(2,1)} reshape(bf16[128,4,2176]{2,1,0:T(4,128)(2,1)S(1)} %all-to-all-done) | data formatting | bytes 4456448 | tf_op jit(solution)/shard_map/reshape | solution.py:194
  92.1 1.1 compare_reduce_fusion
  93.1 0.2 fusion.33
  93.3 2.4 %fusion.11 = (f32[2048]{0:T(1024)S(1)}, f32[512]{0:T(512)S(1)}) fusion(pred[512]{0:T(512)(128)(4,1)S(1)} %compare_reduce_fusion, bf16[512,2176]{1,0:T(8,128)(2,1)} %reshape.189), kind=kLoop, calls=%fused_computation.18 | loop fusion | flops 5240320 | bytes 2107904 | tf_op jit(solution)/shard_map/reduce_sum | solution.py:145
  95.7 3.6 %fusion.26 = f32[512]{0:T(512)S(1)} fusion(bf16[512,2176]{1,0:T(8,128)(2,1)} %reshape.189, f32[512]{0:T(512)S(1)} %add_rsqrt_fusion, pred[512]{0:T(512)(128)(4,1)S(1)} %compare_reduce_fusion), kind=kOutput, calls=%fused_computation.25 | convolution fusion | flops 1075576320 | bytes 2103808 | tf_op jit(solution)/shard_map/dot_general | solution.py:137
  99.3 0.7 select_n.88
  100.1 9.7 %all-to-all-start.1 = ((f32[128,1,4]{2,1,0:T(1,128)}), f32[128,1,4]{2,1,0:T(1,128)S(1)}, u32[]{:S(2)}, u32[]{:S(2)}) async-start(f32[128,1,4]{2,1,0:T(1,128)} %bitcast.14), calls=%async_computation.1 | async-start | bytes 131072 | tf_op jit(solution)/shard_map/all_to_all | solution.py:198
  109.8 0.0 all-gather.2.cloned.1.call-done.cents_ref
  109.8 25.4 %shard_map.67 = f32[2048,1]{1,0:T(8,128)} custom-call(bf16[2048,2048]{1,0:T(8,128)(2,1)} %constant_dynamic-update-slice_fusion.rows_ref, bf16[2048,2048]{1,0:T(8,128)(2,1)} %all-gather.2.cloned.1.call-done.cents_ref, f32[2048,2048]{1,0:T(8,128)} %fusion.9.noise_ref), custom_call_target="tpu_custom_call" | custom-call | tf_op jit(solution)/shard_map/pallas_call | solution.py:118
  135.2 1.6 reduce
  136.8 1.7 %collective-permute-start.13 = (f32[256]{0:T(256)S(1)}, f32[256]{0:T(256)S(1)}, u32[]{:S(2)}, u32[]{:S(2)}) collective-permute-start(f32[256]{0:T(256)S(1)} %bitcast.33), channel_id=1, source_target_pairs={{0,33},{1,32},{32,65},{33,64},{64,97},{65,96},{96,1},{97,0},{2,35}... | collective-permute-start | bytes 3080 | tf_op jit(solution)/shard_map/ppermute | solution.py:182
  138.5 2.5 %collective-permute-start.12 = (f32[256]{0:T(256)S(1)}, f32[256]{0:T(256)S(1)}, u32[]{:S(2)}, u32[]{:S(2)}) collective-permute-start(f32[256]{0:T(256)S(1)} %bitcast.32), channel_id=1, source_target_pairs={{0,65},{1,64},{32,97},{33,96},{64,1},{65,0},{96,33},{97,32},{2,67}... | collective-permute-start | bytes 3080 | tf_op jit(solution)/shard_map/ppermute | solution.py:182
  141.0 0.6 multiply_reduce_fusion
  142.3 1.4 collective-permute-start.11
  143.7 0.2 collective-permute-start.10
  143.9 0.3 collective-permute-start.9
  144.2 0.0 collective-permute-done.13
  144.2 0.9 collective-permute-start.8
  145.1 1.6 %collective-permute-start.7 = (f32[256]{0:T(256)S(1)}, f32[256]{0:T(256)S(1)}, u32[]{:S(2)}, u32[]{:S(2)}) collective-permute-start(f32[256]{0:T(256)S(1)} %bitcast.27), channel_id=1, source_target_pairs={{0,96},{1,97},{32,0},{33,1},{64,32},{65,33},{96,64},{97,65},{2,98}... | collective-permute-start | bytes 3080 | tf_op jit(solution)/shard_map/ppermute | solution.py:182
  146.8 0.6 broadcast_multiply_fusion
  147.4 0.0 all-to-all-done.1
  147.4 0.5 broadcast.300
  147.9 0.8 reduce.6
  148.7 0.1 reshape.190
  148.8 2.5 %gather_fusion = f32[256]{0:T(256)} fusion(f32[512]{0:T(512)S(1)} %reshape.190, s32[1024]{0:T(1024)S(1)} %pad_clamp_fusion), kind=kCustom, calls=%fused_computation | custom fusion | bytes 3072 | tf_op jit(solution)/shard_map/gather | solution.py:201
  151.3 0.0 collective-permute-done.11
  151.3 0.0 collective-permute-done.10
  151.3 0.0 collective-permute-done.8
  151.3 0.6 maximum_maximum_fusion
  (12 shorter events, 0.1 us)
Async XLA Ops:
  7.2 102.6 %all-gather.2.cloned.1.call-start = ((), (), s32[]{:S(2)}) async-start(), calls=%async_computation.2 | async-start | bytes 8912896 | tf_op jit(solution)/shard_map/all_gather | solution.py:165
  7.9 36.5 %collective-permute-start = (bf16[256,2048]{1,0:T(8,128)(2,1)}, bf16[256,2048]{1,0:T(8,128)(2,1)}, u32[]{:S(2)}, u32[]{:S(2)}) collective-permute-start(bf16[256,2048]{1,0:T(8,128)(2,1)} %param.4), channel_id=1, source_target_pairs={{0,32},{32,64},{64,96},{96,0},{1,33},{33,65},{65,97},{97,1},{2,34}... | collective-permute-start | bytes 3145736 | tf_op jit(solution)/shard_map/ppermute | solution.py:161
  10.1 65.9 %collective-permute-start.1 = (bf16[256,2048]{1,0:T(8,128)(2,1)}, bf16[256,2048]{1,0:T(8,128)(2,1)}, u32[]{:S(2)}, u32[]{:S(2)}) collective-permute-start(bf16[256,2048]{1,0:T(8,128)(2,1)} %param.4), channel_id=1, source_target_pairs={{0,64},{32,96},{64,0},{96,32},{1,65},{33,97},{65,1},{97,33},{2,66}... | collective-permute-start | bytes 3145736 | tf_op jit(solution)/shard_map/ppermute | solution.py:161
  12.7 68.3 %collective-permute-start.2 = (bf16[256,2048]{1,0:T(8,128)(2,1)}, bf16[256,2048]{1,0:T(8,128)(2,1)S(1)}, u32[]{:S(2)}, u32[]{:S(2)}) collective-permute-start(bf16[256,2048]{1,0:T(8,128)(2,1)} %param.4), channel_id=1, source_target_pairs={{0,96},{32,0},{64,32},{96,64},{1,97},{33,1},{65,33},{97,65},{2,98}... | collective-permute-start | bytes 3145736 | tf_op jit(solution)/shard_map/ppermute | solution.py:161
  13.8 70.6 %collective-permute-start.3 = (bf16[256,2048]{1,0:T(8,128)(2,1)}, bf16[256,2048]{1,0:T(8,128)(2,1)}, u32[]{:S(2)}, u32[]{:S(2)}) collective-permute-start(bf16[256,2048]{1,0:T(8,128)(2,1)} %param.4), channel_id=1, source_target_pairs={{0,1},{1,0},{2,3},{3,2},{4,5},{5,4},{6,7},{7,6},{8,9},{9,8},{10,11... | collective-permute-start | bytes 3145736 | tf_op jit(solution)/shard_map/ppermute | solution.py:164
  22.7 67.2 %all-to-all-start = ((bf16[128,4,2176]{2,1,0:T(4,128)(2,1)}), bf16[128,4,2176]{2,1,0:T(4,128)(2,1)S(1)}, u32[]{:S(2)}, u32[]{:S(2)}) async-start(bf16[128,4,2176]{2,1,0:T(4,128)(2,1)} %reshape.188), calls=%async_computation | async-start | bytes 4456448 | tf_op jit(solution)/shard_map/all_to_all | solution.py:192
  31.2 12.0 %copy-start = (bf16[256,2048]{1,0:T(8,128)(2,1)S(1)}, bf16[256,2048]{1,0:T(8,128)(2,1)}, u32[]{:S(2)}) copy-start(bf16[256,2048]{1,0:T(8,128)(2,1)} %param.4) | copy-start | bytes 3145732
  44.4 42.4 %collective-permute-start.4 = (bf16[256,2048]{1,0:T(8,128)(2,1)}, bf16[256,2048]{1,0:T(8,128)(2,1)S(1)}, u32[]{:S(2)}, u32[]{:S(2)}) collective-permute-start(bf16[256,2048]{1,0:T(8,128)(2,1)} %collective-permute-done), channel_id=1, source_target_pairs={{0,1},{1,0},{2,3},{3,2},{4,5},{5,4},{6,7},{7,6},{8,9},{9,8},{10,11... | collective-permute-start | bytes 3145736 | tf_op jit(solution)/shard_map/ppermute | solution.py:164
  76.0 11.9 %collective-permute-start.5 = (bf16[256,2048]{1,0:T(8,128)(2,1)}, bf16[256,2048]{1,0:T(8,128)(2,1)S(1)}, u32[]{:S(2)}, u32[]{:S(2)}) collective-permute-start(bf16[256,2048]{1,0:T(8,128)(2,1)} %collective-permute-done.1), channel_id=1, source_target_pairs={{0,1},{1,0},{2,3},{3,2},{4,5},{5,4},{6,7},{7,6},{8,9},{9,8},{10,11... | collective-permute-start | bytes 3145736 | tf_op jit(solution)/shard_map/ppermute | solution.py:164
  81.0 7.9 %collective-permute-start.6 = (bf16[256,2048]{1,0:T(8,128)(2,1)S(1)}, bf16[256,2048]{1,0:T(8,128)(2,1)S(1)}, u32[]{:S(2)}, u32[]{:S(2)}) collective-permute-start(bf16[256,2048]{1,0:T(8,128)(2,1)S(1)} %collective-permute-done.2), channel_id=1, source_target_pairs={{0,1},{1,0},{2,3},{3,2},{4,5},{5,4},{6,7},{7,6},{8,9},{9,8},{10,11... | collective-permute-start | bytes 3145736 | tf_op jit(solution)/shard_map/ppermute | solution.py:164
  100.1 47.3 %all-to-all-start.1 = ((f32[128,1,4]{2,1,0:T(1,128)}), f32[128,1,4]{2,1,0:T(1,128)S(1)}, u32[]{:S(2)}, u32[]{:S(2)}) async-start(f32[128,1,4]{2,1,0:T(1,128)} %bitcast.14), calls=%async_computation.1 | async-start | bytes 131072 | tf_op jit(solution)/shard_map/all_to_all | solution.py:198
  136.8 7.4 %collective-permute-start.13 = (f32[256]{0:T(256)S(1)}, f32[256]{0:T(256)S(1)}, u32[]{:S(2)}, u32[]{:S(2)}) collective-permute-start(f32[256]{0:T(256)S(1)} %bitcast.33), channel_id=1, source_target_pairs={{0,33},{1,32},{32,65},{33,64},{64,97},{65,96},{96,1},{97,0},{2,35}... | collective-permute-start | bytes 3080 | tf_op jit(solution)/shard_map/ppermute | solution.py:182
  138.5 6.6 %collective-permute-start.12 = (f32[256]{0:T(256)S(1)}, f32[256]{0:T(256)S(1)}, u32[]{:S(2)}, u32[]{:S(2)}) collective-permute-start(f32[256]{0:T(256)S(1)} %bitcast.32), channel_id=1, source_target_pairs={{0,65},{1,64},{32,97},{33,96},{64,1},{65,0},{96,33},{97,32},{2,67}... | collective-permute-start | bytes 3080 | tf_op jit(solution)/shard_map/ppermute | solution.py:182
  142.3 9.0 %collective-permute-start.11 = (f32[256]{0:T(256)S(1)}, f32[256]{0:T(256)S(1)}, u32[]{:S(2)}, u32[]{:S(2)}) collective-permute-start(f32[256]{0:T(256)S(1)} %bitcast.31), channel_id=1, source_target_pairs={{0,97},{1,96},{32,1},{33,0},{64,33},{65,32},{96,65},{97,64},{2,99}... | collective-permute-start | bytes 3080 | tf_op jit(solution)/shard_map/ppermute | solution.py:182
  143.7 7.6 %collective-permute-start.10 = (f32[256]{0:T(256)S(1)}, f32[256]{0:T(256)S(1)}, u32[]{:S(2)}, u32[]{:S(2)}) collective-permute-start(f32[256]{0:T(256)S(1)} %bitcast.30), channel_id=1, source_target_pairs={{0,1},{1,0},{32,33},{33,32},{64,65},{65,64},{96,97},{97,96},{2,3},... | collective-permute-start | bytes 3080 | tf_op jit(solution)/shard_map/ppermute | solution.py:182
  143.9 7.4 %collective-permute-start.9 = (f32[256]{0:T(256)S(1)}, f32[256]{0:T(256)S(1)}, u32[]{:S(2)}, u32[]{:S(2)}) collective-permute-start(f32[256]{0:T(256)S(1)} %bitcast.29), channel_id=1, source_target_pairs={{0,32},{1,33},{32,64},{33,65},{64,96},{65,97},{96,0},{97,1},{2,34}... | collective-permute-start | bytes 3080 | tf_op jit(solution)/shard_map/ppermute | solution.py:182
  144.2 7.1 %collective-permute-start.8 = (f32[256]{0:T(256)S(1)}, f32[256]{0:T(256)S(1)}, u32[]{:S(2)}, u32[]{:S(2)}) collective-permute-start(f32[256]{0:T(256)S(1)} %bitcast.28), channel_id=1, source_target_pairs={{0,64},{1,65},{32,96},{33,97},{64,0},{65,1},{96,32},{97,33},{2,66}... | collective-permute-start | bytes 3080 | tf_op jit(solution)/shard_map/ppermute | solution.py:182
  145.1 6.2 %collective-permute-start.7 = (f32[256]{0:T(256)S(1)}, f32[256]{0:T(256)S(1)}, u32[]{:S(2)}, u32[]{:S(2)}) collective-permute-start(f32[256]{0:T(256)S(1)} %bitcast.27), channel_id=1, source_target_pairs={{0,96},{1,97},{32,0},{33,1},{64,32},{65,33},{96,64},{97,65},{2,98}... | collective-permute-start | bytes 3080 | tf_op jit(solution)/shard_map/ppermute | solution.py:182
Sparse Core Ops, SparseCore 0:
  10.1 90.6 all-gather.1

commit v10 on v9

--- a/solution.py
+++ b/solution.py
@@ -113,8 +113,8 @@
 
 def score_max(rows, cents, noise):
     count, width = rows.shape
-    tm = min(1024, count)
-    tn = min(512, cents.shape[0])
+    tm = min(2048, count)
+    tn = min(256, cents.shape[0])
     out = pl.pallas_call(
         score_kernel,
         out_shape=jax.ShapeDtypeStruct((count, 1), jnp.float32),

time: 159 us -> 160 us (level)
  no operation moved by 1% of the time
where the time goes in v10:
time: 160 us; the launch traced here: 159 us
  starting transfers between devices  37.2 us (23%)
  waiting for transfers between devices  31.2 us (20%)
  Pallas kernels  26.1 us (16%)
  local copies, waits for them, and re-layouts  24.1 us (15%)
  other arithmetic  21.7 us (14%)
  between operations  15.5 us (10%)
  matrix products  3.61 us (2%)
    ppermute x3, waiting for transfers between devices, shards(): lax.ppermute(embeddings, 'y', [(i, (i + s) % ny) for i in range(ny)])  30.5 us
    pallas_call x1, Pallas kernels, score_max(): pl.pallas_call(score_kernel, out_shape=jax.ShapeDtypeStruct((count, 1), j...  26.1 us
    neg x1, other arithmetic, gumbel_noise(): return -jnp.log(-jnp.log(uniform))  12 us
    unnamed x10, local copies, waits for them, and re-layouts  11.3 us
    all_to_all x1, starting transfers between devices, shards(): lax.all_to_all(scores.reshape(devices, capacity), ALL, split_axis=0, conc...  9.71 us
    ppermute x7, starting transfers between devices, shards(): best = jnp.maximum(best, lax.ppermute(blocks[sc, sy], ('y', 'c'), perm))  8.66 us
    all_to_all x1, starting transfers between devices, shards(): lax.all_to_all(outgoing.reshape(devices, capacity, feature_dim + flag_wid...  7.56 us
    ppermute x3, starting transfers between devices, shards(): lax.ppermute(embeddings, 'y', [(i, (i + s) % ny) for i in range(ny)])  5.88 us
  transfers between devices with their start and end apart: 17, of which 1 were waited for; matrix products, arithmetic and copies ran while one was open for 31% of the time, Pallas kernels for 16%

profile of v10, /device:TPU:1, one launch (start us, length us, event | category | flops | bytes accessed | tf_op | source)
XLA Modules:
  0.0 159.4 jit_solution(8526212651232167619)
XLA Ops:
  7.2 0.0 all-gather.2.cloned.1.call-start
  7.2 0.7 all-gather.2.cloned.1.call-update
  7.9 2.2 %collective-permute-start = (bf16[256,2048]{1,0:T(8,128)(2,1)}, bf16[256,2048]{1,0:T(8,128)(2,1)}, u32[]{:S(2)}, u32[]{:S(2)}) collective-permute-start(bf16[256,2048]{1,0:T(8,128)(2,1)} %param.4), channel_id=1, source_target_pairs={{0,32},{32,64},{64,96},{96,0},{1,33},{33,65},{65,97},{97,1},{2,34}... | collective-permute-start | bytes 3145736 | tf_op jit(solution)/shard_map/ppermute | solution.py:161
  10.1 2.6 %collective-permute-start.1 = (bf16[256,2048]{1,0:T(8,128)(2,1)}, bf16[256,2048]{1,0:T(8,128)(2,1)}, u32[]{:S(2)}, u32[]{:S(2)}) collective-permute-start(bf16[256,2048]{1,0:T(8,128)(2,1)} %param.4), channel_id=1, source_target_pairs={{0,64},{32,96},{64,0},{96,32},{1,65},{33,97},{65,1},{97,33},{2,66}... | collective-permute-start | bytes 3145736 | tf_op jit(solution)/shard_map/ppermute | solution.py:161
  12.7 1.1 collective-permute-start.2
  13.8 1.5 collective-permute-start.3
  15.3 0.9 convert_reduce_fusion
  16.3 0.7 compare_select_fusion
  16.9 3.6 %scatter_custom_fusion = bf16[512,2176]{1,0:T(8,128)(2,1)S(1)} fusion(s32[256]{0:T(256)S(1)} %bitcast.23, bf16[256,2048]{1,0:T(8,128)(2,1)} %param.4, bf16[]{:T(256)} %constant.137.clone.1, bf16[]{:T(256)} %constant.135.clone.1), kind=kCustom, calls=%fused_computation.26 | custom fusion | bytes 3276804 | tf_op jit(solution)/shard_map/scatter | solution.py:191
  20.6 2.1 %reshape.188 = bf16[128,4,2176]{2,1,0:T(4,128)(2,1)} reshape(bf16[512,2176]{1,0:T(8,128)(2,1)S(1)} %scatter_custom_fusion) | data formatting | bytes 4456448 | tf_op jit(solution)/shard_map/reshape | solution.py:193
  22.7 7.6 %all-to-all-start = ((bf16[128,4,2176]{2,1,0:T(4,128)(2,1)}), bf16[128,4,2176]{2,1,0:T(4,128)(2,1)S(1)}, u32[]{:S(2)}, u32[]{:S(2)}) async-start(bf16[128,4,2176]{2,1,0:T(4,128)(2,1)} %reshape.188), calls=%async_computation | async-start | bytes 4456448 | tf_op jit(solution)/shard_map/all_to_all | solution.py:192
  31.0 0.1 pad_add_fusion
  31.1 0.1 add_multiply_fusion
  31.1 0.1 multiply_bitcast_fusion
  31.2 0.0 copy-start
  31.2 12.0 %fusion.9.noise_ref = f32[2048,2048]{1,0:T(8,128)} fusion(s32[]{:T(128)} %bitcast.19, s32[2048]{0:T(1024)S(1)} %fusion.46, s32[2048]{0:T(1024)S(1)} %bitcast.20), kind=kLoop, calls=%fused_computation.14 | loop fusion | flops 67108864 | bytes 16793604 | tf_op jit(solution)/shard_map/neg | solution.py:30
  43.3 1.1 constant_dynamic-update-slice_fusion.7
  44.4 0.0 collective-permute-done
  44.4 1.1 collective-permute-start.4
  45.5 30.5 %collective-permute-done.1 = bf16[256,2048]{1,0:T(8,128)(2,1)} collective-permute-done((bf16[256,2048]{1,0:T(8,128)(2,1)}, bf16[256,2048]{1,0:T(8,128)(2,1)}, u32[]{:S(2)}, u32[]{:S(2)}) %collective-permute-start.1) | collective-permute-done | bytes 1048608 | tf_op jit(solution)/shard_map/ppermute | solution.py:161
  76.0 2.7 %collective-permute-start.5 = (bf16[256,2048]{1,0:T(8,128)(2,1)}, bf16[256,2048]{1,0:T(8,128)(2,1)S(1)}, u32[]{:S(2)}, u32[]{:S(2)}) collective-permute-start(bf16[256,2048]{1,0:T(8,128)(2,1)} %collective-permute-done.1), channel_id=1, source_target_pairs={{0,1},{1,0},{2,3},{3,2},{4,5},{5,4},{6,7},{7,6},{8,9},{9,8},{10,11... | collective-permute-start | bytes 3145736 | tf_op jit(solution)/shard_map/ppermute | solution.py:164
  78.7 2.3 %constant_dynamic-update-slice_fusion.6 = bf16[2048,2048]{1,0:T(8,128)(2,1)} fusion(bf16[2048,2048]{1,0:T(8,128)(2,1)} %constant_dynamic-update-slice_fusion.7, bf16[256,2048]{1,0:T(8,128)(2,1)} %collective-permute-done), kind=kLoop, calls=%fused_computation.42 | loop fusion | bytes 2097152
  81.0 0.0 collective-permute-done.2
  81.0 0.0 collective-permute-start.6
  81.0 2.4 %constant_dynamic-update-slice_fusion.5 = bf16[2048,2048]{1,0:T(8,128)(2,1)} fusion(bf16[2048,2048]{1,0:T(8,128)(2,1)} %constant_dynamic-update-slice_fusion.6, bf16[256,2048]{1,0:T(8,128)(2,1)} %collective-permute-done.1), kind=kLoop, calls=%fused_computation.41 | loop fusion | bytes 2097152
  83.4 1.0 constant_dynamic-update-slice_fusion.4
  84.4 0.0 collective-permute-done.3
  84.4 2.4 %constant_dynamic-update-slice_fusion.3 = bf16[2048,2048]{1,0:T(8,128)(2,1)} fusion(bf16[2048,2048]{1,0:T(8,128)(2,1)} %constant_dynamic-update-slice_fusion.4, bf16[256,2048]{1,0:T(8,128)(2,1)} %collective-permute-done.3), kind=kLoop, calls=%fused_computation.39 | loop fusion | bytes 2097152
  86.8 0.0 collective-permute-done.4
  86.8 1.0 constant_dynamic-update-slice_fusion.2
  87.8 0.0 collective-permute-done.5
  87.8 1.0 constant_dynamic-update-slice_fusion.1
  88.9 0.0 collective-permute-done.6
  88.9 1.1 constant_dynamic-update-slice_fusion.rows_ref
  90.0 0.0 all-to-all-done
  90.0 2.1 %reshape.189 = bf16[512,2176]{1,0:T(8,128)(2,1)} reshape(bf16[128,4,2176]{2,1,0:T(4,128)(2,1)S(1)} %all-to-all-done) | data formatting | bytes 4456448 | tf_op jit(solution)/shard_map/reshape | solution.py:194
  92.1 1.1 compare_reduce_fusion
  93.1 0.2 fusion.33
  93.3 2.4 %fusion.11 = (f32[2048]{0:T(1024)S(1)}, f32[512]{0:T(512)S(1)}) fusion(pred[512]{0:T(512)(128)(4,1)S(1)} %compare_reduce_fusion, bf16[512,2176]{1,0:T(8,128)(2,1)} %reshape.189), kind=kLoop, calls=%fused_computation.18 | loop fusion | flops 5240320 | bytes 2107904 | tf_op jit(solution)/shard_map/reduce_sum | solution.py:145
  95.7 3.6 %fusion.26 = f32[512]{0:T(512)S(1)} fusion(bf16[512,2176]{1,0:T(8,128)(2,1)} %reshape.189, f32[512]{0:T(512)S(1)} %add_rsqrt_fusion, pred[512]{0:T(512)(128)(4,1)S(1)} %compare_reduce_fusion), kind=kOutput, calls=%fused_computation.25 | convolution fusion | flops 1075576320 | bytes 2103808 | tf_op jit(solution)/shard_map/dot_general | solution.py:137
  99.3 0.7 select_n.88
  100.1 9.7 %all-to-all-start.1 = ((f32[128,1,4]{2,1,0:T(1,128)}), f32[128,1,4]{2,1,0:T(1,128)S(1)}, u32[]{:S(2)}, u32[]{:S(2)}) async-start(f32[128,1,4]{2,1,0:T(1,128)} %bitcast.14), calls=%async_computation.1 | async-start | bytes 131072 | tf_op jit(solution)/shard_map/all_to_all | solution.py:198
  109.8 0.0 all-gather.2.cloned.1.call-done.cents_ref
  109.8 26.1 %shard_map.67 = f32[2048,1]{1,0:T(8,128)} custom-call(bf16[2048,2048]{1,0:T(8,128)(2,1)} %constant_dynamic-update-slice_fusion.rows_ref, bf16[2048,2048]{1,0:T(8,128)(2,1)} %all-gather.2.cloned.1.call-done.cents_ref, f32[2048,2048]{1,0:T(8,128)} %fusion.9.noise_ref), custom_call_target="tpu_custom_call" | custom-call | tf_op jit(solution)/shard_map/pallas_call | solution.py:118
  135.9 1.6 reduce
  137.5 1.7 %collective-permute-start.13 = (f32[256]{0:T(256)S(1)}, f32[256]{0:T(256)S(1)}, u32[]{:S(2)}, u32[]{:S(2)}) collective-permute-start(f32[256]{0:T(256)S(1)} %bitcast.33), channel_id=1, source_target_pairs={{0,33},{1,32},{32,65},{33,64},{64,97},{65,96},{96,1},{97,0},{2,35}... | collective-permute-start | bytes 3080 | tf_op jit(solution)/shard_map/ppermute | solution.py:182
  139.2 2.5 %collective-permute-start.12 = (f32[256]{0:T(256)S(1)}, f32[256]{0:T(256)S(1)}, u32[]{:S(2)}, u32[]{:S(2)}) collective-permute-start(f32[256]{0:T(256)S(1)} %bitcast.32), channel_id=1, source_target_pairs={{0,65},{1,64},{32,97},{33,96},{64,1},{65,0},{96,33},{97,32},{2,67}... | collective-permute-start | bytes 3080 | tf_op jit(solution)/shard_map/ppermute | solution.py:182
  141.7 0.6 multiply_reduce_fusion
  143.0 1.4 collective-permute-start.11
  144.4 0.2 collective-permute-start.10
  144.5 0.3 collective-permute-start.9
  144.9 0.0 collective-permute-done.13
  144.9 0.9 collective-permute-start.8
  145.8 0.0 collective-permute-done.12
  145.8 1.6 %collective-permute-start.7 = (f32[256]{0:T(256)S(1)}, f32[256]{0:T(256)S(1)}, u32[]{:S(2)}, u32[]{:S(2)}) collective-permute-start(f32[256]{0:T(256)S(1)} %bitcast.27), channel_id=1, source_target_pairs={{0,96},{1,97},{32,0},{33,1},{64,32},{65,33},{96,64},{97,65},{2,98}... | collective-permute-start | bytes 3080 | tf_op jit(solution)/shard_map/ppermute | solution.py:182
  147.4 0.6 broadcast_multiply_fusion
  148.0 0.5 broadcast.300
  148.5 0.8 reduce.6
  149.4 0.1 reshape.190
  149.5 2.5 %gather_fusion = f32[256]{0:T(256)} fusion(f32[512]{0:T(512)S(1)} %reshape.190, s32[1024]{0:T(1024)S(1)} %pad_clamp_fusion), kind=kCustom, calls=%fused_computation | custom fusion | bytes 3072 | tf_op jit(solution)/shard_map/gather | solution.py:201
  152.0 0.0 collective-permute-done.11
  152.0 0.0 collective-permute-done.10
  152.0 0.0 collective-permute-done.9
  152.0 0.6 maximum_maximum_fusion
  (12 shorter events, 0.1 us)
Async XLA Ops:
  7.2 102.6 %all-gather.2.cloned.1.call-start = ((), (), s32[]{:S(2)}) async-start(), calls=%async_computation.2 | async-start | bytes 8912896 | tf_op jit(solution)/shard_map/all_gather | solution.py:165
  7.9 36.5 %collective-permute-start = (bf16[256,2048]{1,0:T(8,128)(2,1)}, bf16[256,2048]{1,0:T(8,128)(2,1)}, u32[]{:S(2)}, u32[]{:S(2)}) collective-permute-start(bf16[256,2048]{1,0:T(8,128)(2,1)} %param.4), channel_id=1, source_target_pairs={{0,32},{32,64},{64,96},{96,0},{1,33},{33,65},{65,97},{97,1},{2,34}... | collective-permute-start | bytes 3145736 | tf_op jit(solution)/shard_map/ppermute | solution.py:161
  10.1 65.9 %collective-permute-start.1 = (bf16[256,2048]{1,0:T(8,128)(2,1)}, bf16[256,2048]{1,0:T(8,128)(2,1)}, u32[]{:S(2)}, u32[]{:S(2)}) collective-permute-start(bf16[256,2048]{1,0:T(8,128)(2,1)} %param.4), channel_id=1, source_target_pairs={{0,64},{32,96},{64,0},{96,32},{1,65},{33,97},{65,1},{97,33},{2,66}... | collective-permute-start | bytes 3145736 | tf_op jit(solution)/shard_map/ppermute | solution.py:161
  12.7 68.3 %collective-permute-start.2 = (bf16[256,2048]{1,0:T(8,128)(2,1)}, bf16[256,2048]{1,0:T(8,128)(2,1)S(1)}, u32[]{:S(2)}, u32[]{:S(2)}) collective-permute-start(bf16[256,2048]{1,0:T(8,128)(2,1)} %param.4), channel_id=1, source_target_pairs={{0,96},{32,0},{64,32},{96,64},{1,97},{33,1},{65,33},{97,65},{2,98}... | collective-permute-start | bytes 3145736 | tf_op jit(solution)/shard_map/ppermute | solution.py:161
  13.8 70.6 %collective-permute-start.3 = (bf16[256,2048]{1,0:T(8,128)(2,1)}, bf16[256,2048]{1,0:T(8,128)(2,1)}, u32[]{:S(2)}, u32[]{:S(2)}) collective-permute-start(bf16[256,2048]{1,0:T(8,128)(2,1)} %param.4), channel_id=1, source_target_pairs={{0,1},{1,0},{2,3},{3,2},{4,5},{5,4},{6,7},{7,6},{8,9},{9,8},{10,11... | collective-permute-start | bytes 3145736 | tf_op jit(solution)/shard_map/ppermute | solution.py:164
  22.7 67.2 %all-to-all-start = ((bf16[128,4,2176]{2,1,0:T(4,128)(2,1)}), bf16[128,4,2176]{2,1,0:T(4,128)(2,1)S(1)}, u32[]{:S(2)}, u32[]{:S(2)}) async-start(bf16[128,4,2176]{2,1,0:T(4,128)(2,1)} %reshape.188), calls=%async_computation | async-start | bytes 4456448 | tf_op jit(solution)/shard_map/all_to_all | solution.py:192
  31.2 12.0 %copy-start = (bf16[256,2048]{1,0:T(8,128)(2,1)S(1)}, bf16[256,2048]{1,0:T(8,128)(2,1)}, u32[]{:S(2)}) copy-start(bf16[256,2048]{1,0:T(8,128)(2,1)} %param.4) | copy-start | bytes 3145732
  44.4 42.4 %collective-permute-start.4 = (bf16[256,2048]{1,0:T(8,128)(2,1)}, bf16[256,2048]{1,0:T(8,128)(2,1)S(1)}, u32[]{:S(2)}, u32[]{:S(2)}) collective-permute-start(bf16[256,2048]{1,0:T(8,128)(2,1)} %collective-permute-done), channel_id=1, source_target_pairs={{0,1},{1,0},{2,3},{3,2},{4,5},{5,4},{6,7},{7,6},{8,9},{9,8},{10,11... | collective-permute-start | bytes 3145736 | tf_op jit(solution)/shard_map/ppermute | solution.py:164
  76.0 11.9 %collective-permute-start.5 = (bf16[256,2048]{1,0:T(8,128)(2,1)}, bf16[256,2048]{1,0:T(8,128)(2,1)S(1)}, u32[]{:S(2)}, u32[]{:S(2)}) collective-permute-start(bf16[256,2048]{1,0:T(8,128)(2,1)} %collective-permute-done.1), channel_id=1, source_target_pairs={{0,1},{1,0},{2,3},{3,2},{4,5},{5,4},{6,7},{7,6},{8,9},{9,8},{10,11... | collective-permute-start | bytes 3145736 | tf_op jit(solution)/shard_map/ppermute | solution.py:164
  81.0 7.9 %collective-permute-start.6 = (bf16[256,2048]{1,0:T(8,128)(2,1)S(1)}, bf16[256,2048]{1,0:T(8,128)(2,1)S(1)}, u32[]{:S(2)}, u32[]{:S(2)}) collective-permute-start(bf16[256,2048]{1,0:T(8,128)(2,1)S(1)} %collective-permute-done.2), channel_id=1, source_target_pairs={{0,1},{1,0},{2,3},{3,2},{4,5},{5,4},{6,7},{7,6},{8,9},{9,8},{10,11... | collective-permute-start | bytes 3145736 | tf_op jit(solution)/shard_map/ppermute | solution.py:164
  100.1 48.0 %all-to-all-start.1 = ((f32[128,1,4]{2,1,0:T(1,128)}), f32[128,1,4]{2,1,0:T(1,128)S(1)}, u32[]{:S(2)}, u32[]{:S(2)}) async-start(f32[128,1,4]{2,1,0:T(1,128)} %bitcast.14), calls=%async_computation.1 | async-start | bytes 131072 | tf_op jit(solution)/shard_map/all_to_all | solution.py:198
  137.5 7.4 %collective-permute-start.13 = (f32[256]{0:T(256)S(1)}, f32[256]{0:T(256)S(1)}, u32[]{:S(2)}, u32[]{:S(2)}) collective-permute-start(f32[256]{0:T(256)S(1)} %bitcast.33), channel_id=1, source_target_pairs={{0,33},{1,32},{32,65},{33,64},{64,97},{65,96},{96,1},{97,0},{2,35}... | collective-permute-start | bytes 3080 | tf_op jit(solution)/shard_map/ppermute | solution.py:182
  139.2 6.6 %collective-permute-start.12 = (f32[256]{0:T(256)S(1)}, f32[256]{0:T(256)S(1)}, u32[]{:S(2)}, u32[]{:S(2)}) collective-permute-start(f32[256]{0:T(256)S(1)} %bitcast.32), channel_id=1, source_target_pairs={{0,65},{1,64},{32,97},{33,96},{64,1},{65,0},{96,33},{97,32},{2,67}... | collective-permute-start | bytes 3080 | tf_op jit(solution)/shard_map/ppermute | solution.py:182
  143.0 9.0 %collective-permute-start.11 = (f32[256]{0:T(256)S(1)}, f32[256]{0:T(256)S(1)}, u32[]{:S(2)}, u32[]{:S(2)}) collective-permute-start(f32[256]{0:T(256)S(1)} %bitcast.31), channel_id=1, source_target_pairs={{0,97},{1,96},{32,1},{33,0},{64,33},{65,32},{96,65},{97,64},{2,99}... | collective-permute-start | bytes 3080 | tf_op jit(solution)/shard_map/ppermute | solution.py:182
  144.4 7.6 %collective-permute-start.10 = (f32[256]{0:T(256)S(1)}, f32[256]{0:T(256)S(1)}, u32[]{:S(2)}, u32[]{:S(2)}) collective-permute-start(f32[256]{0:T(256)S(1)} %bitcast.30), channel_id=1, source_target_pairs={{0,1},{1,0},{32,33},{33,32},{64,65},{65,64},{96,97},{97,96},{2,3},... | collective-permute-start | bytes 3080 | tf_op jit(solution)/shard_map/ppermute | solution.py:182
  144.5 7.4 %collective-permute-start.9 = (f32[256]{0:T(256)S(1)}, f32[256]{0:T(256)S(1)}, u32[]{:S(2)}, u32[]{:S(2)}) collective-permute-start(f32[256]{0:T(256)S(1)} %bitcast.29), channel_id=1, source_target_pairs={{0,32},{1,33},{32,64},{33,65},{64,96},{65,97},{96,0},{97,1},{2,34}... | collective-permute-start | bytes 3080 | tf_op jit(solution)/shard_map/ppermute | solution.py:182
  144.9 7.1 %collective-permute-start.8 = (f32[256]{0:T(256)S(1)}, f32[256]{0:T(256)S(1)}, u32[]{:S(2)}, u32[]{:S(2)}) collective-permute-start(f32[256]{0:T(256)S(1)} %bitcast.28), channel_id=1, source_target_pairs={{0,64},{1,65},{32,96},{33,97},{64,0},{65,1},{96,32},{97,33},{2,66}... | collective-permute-start | bytes 3080 | tf_op jit(solution)/shard_map/ppermute | solution.py:182
  145.8 6.2 %collective-permute-start.7 = (f32[256]{0:T(256)S(1)}, f32[256]{0:T(256)S(1)}, u32[]{:S(2)}, u32[]{:S(2)}) collective-permute-start(f32[256]{0:T(256)S(1)} %bitcast.27), channel_id=1, source_target_pairs={{0,96},{1,97},{32,0},{33,1},{64,32},{65,33},{96,64},{97,65},{2,98}... | collective-permute-start | bytes 3080 | tf_op jit(solution)/shard_map/ppermute | solution.py:182
Sparse Core Ops, SparseCore 0:
  10.1 90.6 all-gather.1

commit v11 on v9

--- a/solution.py
+++ b/solution.py
@@ -172,15 +172,11 @@
     cent_ids = cent_dev_ids * cent_dev + cpos % cent_dev
     noise = gumbel_noise(group_ids[:, None], cent_ids[None, :], salt_word)
     result = score_max(group, piece, noise)
-    blocks = result.reshape(nc, ny, rows_dev)
-    best = blocks[0, 0]
-    for sc in range(nc):
-        for sy in range(ny):
-            if sc == 0 and sy == 0:
-                continue
-            perm = [(yy * nc + cc, (yy - sy) % ny * nc + (cc - sc) % nc) for yy in range(ny) for cc in range(nc)]
-            best = jnp.maximum(best, lax.ppermute(blocks[sc, sy], ("y", "c"), perm))
-    perturbed_max = best
+    owner = jnp.arange(ny * nc, dtype=jnp.int32)
+    picked = (ic - owner % nc) % nc * ny + (iy - owner // nc) % ny
+    outbound = jnp.take(result.reshape(nc * ny, rows_dev), picked, axis=0)
+    inbound = lax.all_to_all(outbound, ("y", "c"), split_axis=0, concat_axis=0, tiled=True)
+    perturbed_max = jnp.max(inbound, axis=0)
     assigned = cluster[:, 0]
     order = jnp.arange(rows_dev, dtype=jnp.int32)
     same = (assigned[:, None] == assigned[None, :]) & (order[None, :] < order[:, None])

time: 159 us -> 157 us (0.987)
  starting transfers between devices: 37.2 us -> 33.4 us
    ppermute x7 -> x0, starting transfers between devices: 8.66 us -> none  [shards(): best = jnp.maximum(best, lax.ppermute(blocks[sc, sy], ('y', 'c'), perm))]
    all_to_all x0 -> x1, starting transfers between devices: none -> 4.81 us  [shards(): lax.all_to_all(outbound, ('y', 'c'), split_axis=0, concat_axis=0, tiled=T...]
  transfers between devices with their start and end apart: 17 -> 11, of which waited for: 1 -> 2; matrix products, arithmetic and copies ran while one was open for 31% -> 32% of each run, Pallas kernels for 16% -> 16%
where the time goes in v11:
time: 157 us; the launch traced here: 156 us
  starting transfers between devices  33.4 us (21%)
  waiting for transfers between devices  31.2 us (20%)
  Pallas kernels  25.4 us (16%)
  local copies, waits for them, and re-layouts  25.3 us (16%)
  other arithmetic  21.8 us (14%)
  between operations  15.5 us (10%)
  matrix products  3.61 us (2%)
    ppermute x3, waiting for transfers between devices, shards(): lax.ppermute(embeddings, 'y', [(i, (i + s) % ny) for i in range(ny)])  30.4 us
    pallas_call x1, Pallas kernels, score_max(): pl.pallas_call(score_kernel, out_shape=jax.ShapeDtypeStruct((count, 1), j...  25.4 us
    neg x1, other arithmetic, gumbel_noise(): return -jnp.log(-jnp.log(uniform))  12 us
    unnamed x10, local copies, waits for them, and re-layouts  11.3 us
    all_to_all x1, starting transfers between devices, shards(): lax.all_to_all(scores.reshape(devices, capacity), ALL, split_axis=0, conc...  9.73 us
    all_to_all x1, starting transfers between devices, shards(): lax.all_to_all(outgoing.reshape(devices, capacity, feature_dim + flag_wid...  7.56 us
    ppermute x3, starting transfers between devices, shards(): lax.ppermute(embeddings, 'y', [(i, (i + s) % ny) for i in range(ny)])  5.88 us
    ppermute x4, starting transfers between devices, shards(): lax.ppermute(p, 'c', swap)  5.35 us
  transfers between devices with their start and end apart: 11, of which 2 were waited for; matrix products, arithmetic and copies ran while one was open for 32% of the time, Pallas kernels for 16%

profile of v11, /device:TPU:1, one launch (start us, length us, event | category | flops | bytes accessed | tf_op | source)
XLA Modules:
  0.0 156.2 jit_solution(17452918555125739815)
XLA Ops:
  7.2 0.0 all-gather.2.cloned.1.call-start
  7.2 0.7 all-gather.2.cloned.1.call-update
  7.9 2.2 %collective-permute-start = (bf16[256,2048]{1,0:T(8,128)(2,1)}, bf16[256,2048]{1,0:T(8,128)(2,1)}, u32[]{:S(2)}, u32[]{:S(2)}) collective-permute-start(bf16[256,2048]{1,0:T(8,128)(2,1)} %param.4), channel_id=1, source_target_pairs={{0,32},{32,64},{64,96},{96,0},{1,33},{33,65},{65,97},{97,1},{2,34}... | collective-permute-start | bytes 3145736 | tf_op jit(solution)/shard_map/ppermute | solution.py:161
  10.1 2.6 %collective-permute-start.1 = (bf16[256,2048]{1,0:T(8,128)(2,1)}, bf16[256,2048]{1,0:T(8,128)(2,1)}, u32[]{:S(2)}, u32[]{:S(2)}) collective-permute-start(bf16[256,2048]{1,0:T(8,128)(2,1)} %param.4), channel_id=1, source_target_pairs={{0,64},{32,96},{64,0},{96,32},{1,65},{33,97},{65,1},{97,33},{2,66}... | collective-permute-start | bytes 3145736 | tf_op jit(solution)/shard_map/ppermute | solution.py:161
  12.7 1.1 collective-permute-start.2
  13.8 1.5 collective-permute-start.3
  15.3 0.9 convert_reduce_fusion
  16.3 0.7 compare_select_fusion
  16.9 3.6 %scatter_custom_fusion = bf16[512,2176]{1,0:T(8,128)(2,1)S(1)} fusion(s32[256]{0:T(256)S(1)} %bitcast.19, bf16[256,2048]{1,0:T(8,128)(2,1)} %param.4, bf16[]{:T(256)} %constant.193.clone.1, bf16[]{:T(256)} %constant.191.clone.1), kind=kCustom, calls=%fused_computation.27 | custom fusion | bytes 3276804 | tf_op jit(solution)/shard_map/scatter | solution.py:187
  20.6 2.1 %reshape.354 = bf16[128,4,2176]{2,1,0:T(4,128)(2,1)} reshape(bf16[512,2176]{1,0:T(8,128)(2,1)S(1)} %scatter_custom_fusion) | data formatting | bytes 4456448 | tf_op jit(solution)/shard_map/reshape | solution.py:189
  22.7 7.6 %all-to-all-start.1 = ((bf16[128,4,2176]{2,1,0:T(4,128)(2,1)}), bf16[128,4,2176]{2,1,0:T(4,128)(2,1)S(1)}, u32[]{:S(2)}, u32[]{:S(2)}) async-start(bf16[128,4,2176]{2,1,0:T(4,128)(2,1)} %reshape.354), calls=%async_computation.1 | async-start | bytes 4456448 | tf_op jit(solution)/shard_map/all_to_all | solution.py:188
  31.0 0.1 pad_add_fusion
  31.1 0.1 add_multiply_fusion
  31.1 0.1 multiply_bitcast_fusion
  31.2 0.0 copy-start
  31.2 12.0 %fusion.9.noise_ref = f32[2048,2048]{1,0:T(8,128)} fusion(s32[]{:T(128)} %bitcast.15, s32[2048]{0:T(1024)S(1)} %fusion.46, s32[2048]{0:T(1024)S(1)} %bitcast.16), kind=kLoop, calls=%fused_computation.15 | loop fusion | flops 67108864 | bytes 16793604 | tf_op jit(solution)/shard_map/neg | solution.py:30
  43.3 0.0 copy-done
  43.3 1.1 constant_dynamic-update-slice_fusion.7
  44.4 0.0 collective-permute-done
  44.5 1.1 collective-permute-start.4
  45.5 30.4 %collective-permute-done.1 = bf16[256,2048]{1,0:T(8,128)(2,1)} collective-permute-done((bf16[256,2048]{1,0:T(8,128)(2,1)}, bf16[256,2048]{1,0:T(8,128)(2,1)}, u32[]{:S(2)}, u32[]{:S(2)}) %collective-permute-start.1) | collective-permute-done | bytes 1048608 | tf_op jit(solution)/shard_map/ppermute | solution.py:161
  76.0 2.7 %collective-permute-start.5 = (bf16[256,2048]{1,0:T(8,128)(2,1)}, bf16[256,2048]{1,0:T(8,128)(2,1)S(1)}, u32[]{:S(2)}, u32[]{:S(2)}) collective-permute-start(bf16[256,2048]{1,0:T(8,128)(2,1)} %collective-permute-done.1), channel_id=1, source_target_pairs={{0,1},{1,0},{2,3},{3,2},{4,5},{5,4},{6,7},{7,6},{8,9},{9,8},{10,11... | collective-permute-start | bytes 3145736 | tf_op jit(solution)/shard_map/ppermute | solution.py:164
  78.7 2.3 %constant_dynamic-update-slice_fusion.6 = bf16[2048,2048]{1,0:T(8,128)(2,1)} fusion(bf16[2048,2048]{1,0:T(8,128)(2,1)} %constant_dynamic-update-slice_fusion.7, bf16[256,2048]{1,0:T(8,128)(2,1)} %collective-permute-done), kind=kLoop, calls=%fused_computation.43 | loop fusion | bytes 2097152
  81.0 0.0 collective-permute-done.2
  81.0 0.0 collective-permute-start.6
  81.0 2.4 %constant_dynamic-update-slice_fusion.5 = bf16[2048,2048]{1,0:T(8,128)(2,1)} fusion(bf16[2048,2048]{1,0:T(8,128)(2,1)} %constant_dynamic-update-slice_fusion.6, bf16[256,2048]{1,0:T(8,128)(2,1)} %collective-permute-done.1), kind=kLoop, calls=%fused_computation.42 | loop fusion | bytes 2097152
  83.4 1.0 constant_dynamic-update-slice_fusion.4
  84.4 0.0 collective-permute-done.3
  84.4 2.4 %constant_dynamic-update-slice_fusion.3 = bf16[2048,2048]{1,0:T(8,128)(2,1)} fusion(bf16[2048,2048]{1,0:T(8,128)(2,1)} %constant_dynamic-update-slice_fusion.4, bf16[256,2048]{1,0:T(8,128)(2,1)} %collective-permute-done.3), kind=kLoop, calls=%fused_computation.40 | loop fusion | bytes 2097152
  86.8 0.0 collective-permute-done.4
  86.8 1.0 constant_dynamic-update-slice_fusion.2
  87.8 0.0 collective-permute-done.5
  87.8 1.0 constant_dynamic-update-slice_fusion.1
  88.9 0.0 collective-permute-done.6
  88.9 1.1 constant_dynamic-update-slice_fusion.rows_ref
  90.0 0.0 all-to-all-done.1
  90.0 2.1 %reshape.355 = bf16[512,2176]{1,0:T(8,128)(2,1)} reshape(bf16[128,4,2176]{2,1,0:T(4,128)(2,1)S(1)} %all-to-all-done.1) | data formatting | bytes 4456448 | tf_op jit(solution)/shard_map/reshape | solution.py:190
  92.1 1.1 compare_reduce_fusion
  93.1 0.2 fusion.33
  93.3 2.4 %fusion.11 = (f32[2048]{0:T(1024)S(1)}, f32[512]{0:T(512)S(1)}) fusion(pred[512]{0:T(512)(128)(4,1)S(1)} %compare_reduce_fusion, bf16[512,2176]{1,0:T(8,128)(2,1)} %reshape.355), kind=kLoop, calls=%fused_computation.19 | loop fusion | flops 5240320 | bytes 2107904 | tf_op jit(solution)/shard_map/reduce_sum | solution.py:145
  95.7 3.6 %fusion.26 = f32[512]{0:T(512)S(1)} fusion(bf16[512,2176]{1,0:T(8,128)(2,1)} %reshape.355, f32[512]{0:T(512)S(1)} %add_rsqrt_fusion, pred[512]{0:T(512)(128)(4,1)S(1)} %compare_reduce_fusion), kind=kOutput, calls=%fused_computation.26 | convolution fusion | flops 1075576320 | bytes 2103808 | tf_op jit(solution)/shard_map/dot_general | solution.py:137
  99.3 0.7 select_n.188
  100.1 9.7 %all-to-all-start.2 = ((f32[128,1,4]{2,1,0:T(1,128)}), f32[128,1,4]{2,1,0:T(1,128)S(1)}, u32[]{:S(2)}, u32[]{:S(2)}) async-start(f32[128,1,4]{2,1,0:T(1,128)} %bitcast.8), calls=%async_computation.2 | async-start | bytes 131072 | tf_op jit(solution)/shard_map/all_to_all | solution.py:194
  109.8 0.6 multiply_reduce_fusion
  111.1 0.0 all-gather.2.cloned.1.call-done.cents_ref
  111.1 25.4 %shard_map.67 = f32[2048,1]{1,0:T(8,128)} custom-call(bf16[2048,2048]{1,0:T(8,128)(2,1)} %constant_dynamic-update-slice_fusion.rows_ref, bf16[2048,2048]{1,0:T(8,128)(2,1)} %all-gather.2.cloned.1.call-done.cents_ref, f32[2048,2048]{1,0:T(8,128)} %fusion.9.noise_ref), custom_call_target="tpu_custom_call" | custom-call | tf_op jit(solution)/shard_map/pallas_call | solution.py:118
  136.5 1.6 reduce.1
  138.1 0.6 gather_fusion
  138.6 0.1 bitcast_select_fusion
  138.7 0.6 copy.10
  139.3 0.0 all-to-all-done.2
  139.3 4.8 %all-to-all-start = ((f32[8,1,256]{2,1,0:T(1,128)}), f32[8,1,256]{2,1,0:T(1,128)S(1)}, u32[]{:S(2)}, u32[]{:S(2)}) async-start(f32[8,1,256]{2,1,0:T(1,128)} %copy.10), calls=%async_computation | async-start | bytes 16384 | tf_op jit(solution)/shard_map/all_to_all | solution.py:178
  144.1 0.6 broadcast_multiply_fusion
  144.7 0.5 broadcast.596
  145.3 0.8 reduce.7
  146.1 0.1 reshape.356
  146.2 2.5 %gather_fusion.1 = f32[256]{0:T(256)} fusion(f32[512]{0:T(512)S(1)} %reshape.356, s32[1024]{0:T(1024)S(1)} %pad_clamp_fusion), kind=kCustom, calls=%fused_computation.1 | custom fusion | bytes 3072 | tf_op jit(solution)/shard_map/gather | solution.py:197
  148.7 0.1 all-to-all-done
  148.8 0.6 reduce_max.18
  (10 shorter events, 0.1 us)
Async XLA Ops:
  7.2 104.0 %all-gather.2.cloned.1.call-start = ((), (), s32[]{:S(2)}) async-start(), calls=%async_computation.3 | async-start | bytes 8912896 | tf_op jit(solution)/shard_map/all_gather | solution.py:165
  7.9 36.6 %collective-permute-start = (bf16[256,2048]{1,0:T(8,128)(2,1)}, bf16[256,2048]{1,0:T(8,128)(2,1)}, u32[]{:S(2)}, u32[]{:S(2)}) collective-permute-start(bf16[256,2048]{1,0:T(8,128)(2,1)} %param.4), channel_id=1, source_target_pairs={{0,32},{32,64},{64,96},{96,0},{1,33},{33,65},{65,97},{97,1},{2,34}... | collective-permute-start | bytes 3145736 | tf_op jit(solution)/shard_map/ppermute | solution.py:161
  10.1 65.9 %collective-permute-start.1 = (bf16[256,2048]{1,0:T(8,128)(2,1)}, bf16[256,2048]{1,0:T(8,128)(2,1)}, u32[]{:S(2)}, u32[]{:S(2)}) collective-permute-start(bf16[256,2048]{1,0:T(8,128)(2,1)} %param.4), channel_id=1, source_target_pairs={{0,64},{32,96},{64,0},{96,32},{1,65},{33,97},{65,1},{97,33},{2,66}... | collective-permute-start | bytes 3145736 | tf_op jit(solution)/shard_map/ppermute | solution.py:161
  12.7 68.3 %collective-permute-start.2 = (bf16[256,2048]{1,0:T(8,128)(2,1)}, bf16[256,2048]{1,0:T(8,128)(2,1)S(1)}, u32[]{:S(2)}, u32[]{:S(2)}) collective-permute-start(bf16[256,2048]{1,0:T(8,128)(2,1)} %param.4), channel_id=1, source_target_pairs={{0,96},{32,0},{64,32},{96,64},{1,97},{33,1},{65,33},{97,65},{2,98}... | collective-permute-start | bytes 3145736 | tf_op jit(solution)/shard_map/ppermute | solution.py:161
  13.8 70.6 %collective-permute-start.3 = (bf16[256,2048]{1,0:T(8,128)(2,1)}, bf16[256,2048]{1,0:T(8,128)(2,1)}, u32[]{:S(2)}, u32[]{:S(2)}) collective-permute-start(bf16[256,2048]{1,0:T(8,128)(2,1)} %param.4), channel_id=1, source_target_pairs={{0,1},{1,0},{2,3},{3,2},{4,5},{5,4},{6,7},{7,6},{8,9},{9,8},{10,11... | collective-permute-start | bytes 3145736 | tf_op jit(solution)/shard_map/ppermute | solution.py:164
  22.7 67.2 %all-to-all-start.1 = ((bf16[128,4,2176]{2,1,0:T(4,128)(2,1)}), bf16[128,4,2176]{2,1,0:T(4,128)(2,1)S(1)}, u32[]{:S(2)}, u32[]{:S(2)}) async-start(bf16[128,4,2176]{2,1,0:T(4,128)(2,1)} %reshape.354), calls=%async_computation.1 | async-start | bytes 4456448 | tf_op jit(solution)/shard_map/all_to_all | solution.py:188
  31.2 12.1 %copy-start = (bf16[256,2048]{1,0:T(8,128)(2,1)S(1)}, bf16[256,2048]{1,0:T(8,128)(2,1)}, u32[]{:S(2)}) copy-start(bf16[256,2048]{1,0:T(8,128)(2,1)} %param.4) | copy-start | bytes 3145732
  44.5 42.3 %collective-permute-start.4 = (bf16[256,2048]{1,0:T(8,128)(2,1)}, bf16[256,2048]{1,0:T(8,128)(2,1)S(1)}, u32[]{:S(2)}, u32[]{:S(2)}) collective-permute-start(bf16[256,2048]{1,0:T(8,128)(2,1)} %collective-permute-done), channel_id=1, source_target_pairs={{0,1},{1,0},{2,3},{3,2},{4,5},{5,4},{6,7},{7,6},{8,9},{9,8},{10,11... | collective-permute-start | bytes 3145736 | tf_op jit(solution)/shard_map/ppermute | solution.py:164
  76.0 11.9 %collective-permute-start.5 = (bf16[256,2048]{1,0:T(8,128)(2,1)}, bf16[256,2048]{1,0:T(8,128)(2,1)S(1)}, u32[]{:S(2)}, u32[]{:S(2)}) collective-permute-start(bf16[256,2048]{1,0:T(8,128)(2,1)} %collective-permute-done.1), channel_id=1, source_target_pairs={{0,1},{1,0},{2,3},{3,2},{4,5},{5,4},{6,7},{7,6},{8,9},{9,8},{10,11... | collective-permute-start | bytes 3145736 | tf_op jit(solution)/shard_map/ppermute | solution.py:164
  81.0 7.9 %collective-permute-start.6 = (bf16[256,2048]{1,0:T(8,128)(2,1)S(1)}, bf16[256,2048]{1,0:T(8,128)(2,1)S(1)}, u32[]{:S(2)}, u32[]{:S(2)}) collective-permute-start(bf16[256,2048]{1,0:T(8,128)(2,1)S(1)} %collective-permute-done.2), channel_id=1, source_target_pairs={{0,1},{1,0},{2,3},{3,2},{4,5},{5,4},{6,7},{7,6},{8,9},{9,8},{10,11... | collective-permute-start | bytes 3145736 | tf_op jit(solution)/shard_map/ppermute | solution.py:164
  100.1 39.3 %all-to-all-start.2 = ((f32[128,1,4]{2,1,0:T(1,128)}), f32[128,1,4]{2,1,0:T(1,128)S(1)}, u32[]{:S(2)}, u32[]{:S(2)}) async-start(f32[128,1,4]{2,1,0:T(1,128)} %bitcast.8), calls=%async_computation.2 | async-start | bytes 131072 | tf_op jit(solution)/shard_map/all_to_all | solution.py:194
  139.3 9.4 %all-to-all-start = ((f32[8,1,256]{2,1,0:T(1,128)}), f32[8,1,256]{2,1,0:T(1,128)S(1)}, u32[]{:S(2)}, u32[]{:S(2)}) async-start(f32[8,1,256]{2,1,0:T(1,128)} %copy.10), calls=%async_computation | async-start | bytes 16384 | tf_op jit(solution)/shard_map/all_to_all | solution.py:178
Sparse Core Ops, SparseCore 0:
  10.1 90.6 all-gather.1

commit v12 on v11

--- a/solution.py
+++ b/solution.py
@@ -170,13 +170,6 @@
     cpos = jnp.arange(nz * nx * cent_dev, dtype=jnp.int32)
     cent_dev_ids = ((iy * nz + cpos // (nx * cent_dev)) * nx + cpos // cent_dev % nx) * nc + ic
     cent_ids = cent_dev_ids * cent_dev + cpos % cent_dev
-    noise = gumbel_noise(group_ids[:, None], cent_ids[None, :], salt_word)
-    result = score_max(group, piece, noise)
-    owner = jnp.arange(ny * nc, dtype=jnp.int32)
-    picked = (ic - owner % nc) % nc * ny + (iy - owner // nc) % ny
-    outbound = jnp.take(result.reshape(nc * ny, rows_dev), picked, axis=0)
-    inbound = lax.all_to_all(outbound, ("y", "c"), split_axis=0, concat_axis=0, tiled=True)
-    perturbed_max = jnp.max(inbound, axis=0)
     assigned = cluster[:, 0]
     order = jnp.arange(rows_dev, dtype=jnp.int32)
     same = (assigned[:, None] == assigned[None, :]) & (order[None, :] < order[:, None])
@@ -185,11 +178,19 @@
     flag_width = 128
     tagged = jnp.concatenate([embeddings, jnp.ones((rows_dev, flag_width), jnp.bfloat16)], axis=1)
     outgoing = jnp.zeros((devices * capacity, feature_dim + flag_width), jnp.bfloat16).at[slot].set(tagged)
+    outgoing, piece = lax.optimization_barrier((outgoing, piece))
     received = lax.all_to_all(
         outgoing.reshape(devices, capacity, feature_dim + flag_width), ALL, split_axis=0, concat_axis=0, tiled=True
     ).reshape(devices * capacity, feature_dim + flag_width)
     members = received[:, :feature_dim]
     valid = received[:, feature_dim] > 0.5
+    noise = gumbel_noise(group_ids[:, None], cent_ids[None, :], salt_word)
+    result = score_max(group, piece, noise)
+    owner = jnp.arange(ny * nc, dtype=jnp.int32)
+    picked = (ic - owner % nc) % nc * ny + (iy - owner // nc) % ny
+    outbound = jnp.take(result.reshape(nc * ny, rows_dev), picked, axis=0)
+    inbound = lax.all_to_all(outbound, ("y", "c"), split_axis=0, concat_axis=0, tiled=True)
+    perturbed_max = jnp.max(inbound, axis=0)
     scores, center = cluster_stats(members, valid)
     returned = lax.all_to_all(
         scores.reshape(devices, capacity), ALL, split_axis=0, concat_axis=0, tiled=True

time: 157 us -> 193 us (1.23)
  waiting for transfers between devices: 31.2 us -> 81.8 us
  starting transfers between devices: 33.4 us -> 22.4 us
  other arithmetic: 21.8 us -> 17.9 us
  local copies, waits for them, and re-layouts: 25.3 us -> 27.7 us
  matrix products: 3.61 us -> 1.38 us
    all_to_all x1, waiting for transfers between devices: 0.01 us -> 31 us  [shards(): lax.all_to_all(outgoing.reshape(devices, capacity, feature_dim + flag_wid...]
    all_to_all x1, waiting for transfers between devices: 0.01 us -> 8.94 us  [shards(): lax.all_to_all(scores.reshape(devices, capacity), ALL, split_axis=0, conc...]
    all_to_all x1, starting transfers between devices: 9.73 us -> 4.47 us  [shards(): lax.all_to_all(scores.reshape(devices, capacity), ALL, split_axis=0, conc...]
    all_gather x1, waiting for transfers between devices: 0.02 us -> 4.71 us  [shards(): piece = lax.all_gather(centroids, ('z', 'x'), axis=0, tiled=True)]
    ppermute x3, waiting for transfers between devices: 30.4 us -> 34 us  [shards(): lax.ppermute(embeddings, 'y', [(i, (i + s) % ny) for i in range(ny)])]
    ppermute x4, starting transfers between devices: 5.35 us -> 2.58 us  [shards(): lax.ppermute(p, 'c', swap)]
    unnamed x10 -> x12, local copies, waits for them, and re-layouts: 11.3 us -> 13.9 us
    all_to_all x1, waiting for transfers between devices: 0.08 us -> 2.52 us  [shards(): lax.all_to_all(outbound, ('y', 'c'), split_axis=0, concat_axis=0, tiled=T...]
  transfers between devices with their start and end apart: 11 -> 11, of which waited for: 2 -> 5; matrix products, arithmetic and copies ran while one was open for 32% -> 18% of each run, Pallas kernels for 16% -> 0%
where the time goes in v12:
time: 193 us; the launch traced here: 192 us
  waiting for transfers between devices  81.8 us (42%)
  local copies, waits for them, and re-layouts  27.7 us (14%)
  Pallas kernels  25.4 us (13%)
  starting transfers between devices  22.4 us (12%)
  other arithmetic  17.9 us (9%)
  between operations  15.5 us (8%)
    ppermute x3, waiting for transfers between devices, shards(): lax.ppermute(embeddings, 'y', [(i, (i + s) % ny) for i in range(ny)])  34 us
    all_to_all x1, waiting for transfers between devices, shards(): lax.all_to_all(outgoing.reshape(devices, capacity, feature_dim + flag_wid...  31 us
    pallas_call x1, Pallas kernels, score_max(): pl.pallas_call(score_kernel, out_shape=jax.ShapeDtypeStruct((count, 1), j...  25.4 us
    unnamed x12, local copies, waits for them, and re-layouts  13.9 us
    neg x1, other arithmetic, gumbel_noise(): return -jnp.log(-jnp.log(uniform))  12 us
    all_to_all x1, waiting for transfers between devices, shards(): lax.all_to_all(scores.reshape(devices, capacity), ALL, split_axis=0, conc...  8.94 us
    all_to_all x1, starting transfers between devices, shards(): lax.all_to_all(outgoing.reshape(devices, capacity, feature_dim + flag_wid...  6.46 us
    all_to_all x1, starting transfers between devices, shards(): lax.all_to_all(outbound, ('y', 'c'), split_axis=0, concat_axis=0, tiled=T...  4.96 us
  transfers between devices with their start and end apart: 11, of which 5 were waited for; matrix products, arithmetic and copies ran while one was open for 18% of the time, Pallas kernels for 0%

profile of v12, /device:TPU:1, one launch (start us, length us, event | category | flops | bytes accessed | tf_op | source)
XLA Modules:
  0.0 192.0 jit_solution(5453483918041611360)
XLA Ops:
  7.2 0.0 all-gather.2.cloned.1.call-start
  7.2 0.7 all-gather.2.cloned.1.call-update
  7.9 1.5 collective-permute-start.3
  9.4 2.8 %collective-permute-start.2 = (bf16[256,2048]{1,0:T(8,128)(2,1)}, bf16[256,2048]{1,0:T(8,128)(2,1)}, u32[]{:S(2)}, u32[]{:S(2)}) collective-permute-start(bf16[256,2048]{1,0:T(8,128)(2,1)} %param.4), channel_id=1, source_target_pairs={{0,96},{32,0},{64,32},{96,64},{1,97},{33,1},{65,33},{97,65},{2,98}... | collective-permute-start | bytes 3145736 | tf_op jit(solution)/shard_map/ppermute | solution.py:161
  12.2 0.3 collective-permute-start.1
  12.6 0.7 collective-permute-start
  13.9 0.1 pad_add_fusion
  14.0 0.1 add_multiply_fusion
  14.1 0.1 multiply_bitcast_fusion
  14.2 0.0 copy-start.1
  14.2 0.0 copy-start
  14.2 12.0 %fusion.9.noise_ref = f32[2048,2048]{1,0:T(8,128)} fusion(s32[]{:T(128)} %bitcast.15, s32[2048]{0:T(1024)S(1)} %fusion.46, s32[2048]{0:T(1024)S(1)} %bitcast.17), kind=kLoop, calls=%fused_computation.15 | loop fusion | flops 67108864 | bytes 16793604 | tf_op jit(solution)/shard_map/neg | solution.py:30
  26.3 0.0 copy-done.1
  26.3 0.2 convert_reduce_fusion
  26.5 0.0 copy-done
  26.5 1.1 constant_dynamic-update-slice_fusion.7
  27.6 34.0 %collective-permute-done = bf16[256,2048]{1,0:T(8,128)(2,1)} collective-permute-done((bf16[256,2048]{1,0:T(8,128)(2,1)}, bf16[256,2048]{1,0:T(8,128)(2,1)}, u32[]{:S(2)}, u32[]{:S(2)}) %collective-permute-start) | collective-permute-done | bytes 1048608 | tf_op jit(solution)/shard_map/ppermute | solution.py:161
  61.6 0.5 collective-permute-start.4
  62.1 3.0 %scatter_custom_fusion = bf16[512,2176]{1,0:T(8,128)(2,1)S(1)} fusion(s32[256]{0:T(256)S(1)} %bitcast.20, bf16[256,2048]{1,0:T(8,128)(2,1)S(1)} %copy-done, bf16[]{:T(256)} %constant.177.clone.1, bf16[]{:T(256)} %constant.175.clone.1), kind=kCustom, calls=%fused_computation.27 | custom fusion | bytes 3276804 | tf_op jit(solution)/shard_map/scatter | solution.py:180
  65.1 0.0 collective-permute-done.2
  65.1 0.1 collective-permute-start.6
  65.2 0.0 collective-permute-done.1
  65.2 0.5 collective-permute-start.5
  65.7 2.3 %constant_dynamic-update-slice_fusion.6 = bf16[2048,2048]{1,0:T(8,128)(2,1)} fusion(bf16[2048,2048]{1,0:T(8,128)(2,1)} %constant_dynamic-update-slice_fusion.7, bf16[256,2048]{1,0:T(8,128)(2,1)} %collective-permute-done), kind=kLoop, calls=%fused_computation.43 | loop fusion | bytes 2097152
  68.0 2.4 %constant_dynamic-update-slice_fusion.5 = bf16[2048,2048]{1,0:T(8,128)(2,1)} fusion(bf16[2048,2048]{1,0:T(8,128)(2,1)} %constant_dynamic-update-slice_fusion.6, bf16[256,2048]{1,0:T(8,128)(2,1)} %collective-permute-done.1), kind=kLoop, calls=%fused_computation.42 | loop fusion | bytes 2097152
  70.4 2.3 %constant_dynamic-update-slice_fusion.4 = bf16[2048,2048]{1,0:T(8,128)(2,1)} fusion(bf16[2048,2048]{1,0:T(8,128)(2,1)} %constant_dynamic-update-slice_fusion.5, bf16[256,2048]{1,0:T(8,128)(2,1)} %collective-permute-done.2), kind=kLoop, calls=%fused_computation.41 | loop fusion | bytes 2097152
  72.7 0.0 collective-permute-done.3
  72.7 2.4 %constant_dynamic-update-slice_fusion.3 = bf16[2048,2048]{1,0:T(8,128)(2,1)} fusion(bf16[2048,2048]{1,0:T(8,128)(2,1)} %constant_dynamic-update-slice_fusion.4, bf16[256,2048]{1,0:T(8,128)(2,1)} %collective-permute-done.3), kind=kLoop, calls=%fused_computation.40 | loop fusion | bytes 2097152
  75.1 0.0 collective-permute-done.4
  75.1 2.3 %constant_dynamic-update-slice_fusion.2 = bf16[2048,2048]{1,0:T(8,128)(2,1)} fusion(bf16[2048,2048]{1,0:T(8,128)(2,1)} %constant_dynamic-update-slice_fusion.3, bf16[256,2048]{1,0:T(8,128)(2,1)} %collective-permute-done.4), kind=kLoop, calls=%fused_computation.39 | loop fusion | bytes 2097152
  77.4 0.0 collective-permute-done.5
  77.4 1.0 constant_dynamic-update-slice_fusion.1
  78.5 0.0 collective-permute-done.6
  78.5 1.1 constant_dynamic-update-slice_fusion.rows_ref
  79.5 4.7 %all-gather.2.cloned.1.call-done.cents_ref = bf16[2048,2048]{1,0:T(8,128)(2,1)} async-done(((bf16[128,2048]{1,0:T(8,128)(2,1)}), bf16[2048,2048]{1,0:T(8,128)(2,1)}) %all-gather.2.cloned.1.call-update) | async-done | bytes 8388624 | tf_op jit(solution)/shard_map/all_gather | solution.py:165
  84.2 25.4 %shard_map.67 = f32[2048,1]{1,0:T(8,128)} custom-call(bf16[2048,2048]{1,0:T(8,128)(2,1)} %constant_dynamic-update-slice_fusion.rows_ref, bf16[2048,2048]{1,0:T(8,128)(2,1)} %all-gather.2.cloned.1.call-done.cents_ref, f32[2048,2048]{1,0:T(8,128)} %fusion.9.noise_ref), custom_call_target="tpu_custom_call" | custom-call | tf_op jit(solution)/shard_map/pallas_call | solution.py:118
  109.6 1.6 reduce.1
  111.2 0.6 gather_fusion
  111.7 0.1 bitcast_select_fusion
  111.8 0.6 copy.10
  112.4 5.0 %all-to-all-start = ((f32[8,1,256]{2,1,0:T(1,128)}), f32[8,1,256]{2,1,0:T(1,128)S(1)}, u32[]{:S(2)}, u32[]{:S(2)}) async-start(f32[8,1,256]{2,1,0:T(1,128)} %copy.10), calls=%async_computation | async-start | bytes 16384 | tf_op jit(solution)/shard_map/all_to_all | solution.py:192
  117.4 2.1 %reshape.354 = bf16[128,4,2176]{2,1,0:T(4,128)(2,1)} reshape(bf16[512,2176]{1,0:T(8,128)(2,1)S(1)} %scatter_custom_fusion) | data formatting | bytes 4456448 | tf_op jit(solution)/shard_map/reshape | solution.py:183
  119.5 2.5 %all-to-all-done = f32[8,1,256]{2,1,0:T(1,128)S(1)} async-done(((f32[8,1,256]{2,1,0:T(1,128)}), f32[8,1,256]{2,1,0:T(1,128)S(1)}, u32[]{:S(2)}, u32[]{:S(2)}) %all-to-all-start) | async-done | bytes 8224 | tf_op jit(solution)/shard_map/all_to_all | solution.py:192
  122.0 6.5 %all-to-all-start.1 = ((bf16[128,4,2176]{2,1,0:T(4,128)(2,1)}), bf16[128,4,2176]{2,1,0:T(4,128)(2,1)}, u32[]{:S(2)}, u32[]{:S(2)}) async-start(bf16[128,4,2176]{2,1,0:T(4,128)(2,1)} %reshape.354), calls=%async_computation.1 | async-start | bytes 4456448 | tf_op jit(solution)/shard_map/all_to_all | solution.py:182
  128.5 0.6 reduce_max.18
  129.1 31.0 %all-to-all-done.1 = bf16[128,4,2176]{2,1,0:T(4,128)(2,1)} async-done(((bf16[128,4,2176]{2,1,0:T(4,128)(2,1)}), bf16[128,4,2176]{2,1,0:T(4,128)(2,1)}, u32[]{:S(2)}, u32[]{:S(2)}) %all-to-all-start.1) | async-done | bytes 2228256 | tf_op jit(solution)/shard_map/all_to_all | solution.py:182
  160.0 2.6 %reshape.355 = bf16[512,2176]{1,0:T(8,128)(2,1)S(1)} reshape(bf16[128,4,2176]{2,1,0:T(4,128)(2,1)} %all-to-all-done.1) | data formatting | bytes 4456448 | tf_op jit(solution)/shard_map/reshape | solution.py:184
  162.6 0.1 compare_reduce_fusion
  162.8 0.2 fusion.33
  162.9 0.8 fusion.11
  163.8 0.6 multiply_reduce_fusion
  165.1 1.4 fusion.26
  166.5 0.7 select_n.188
  167.2 4.5 %all-to-all-start.2 = ((f32[128,1,4]{2,1,0:T(1,128)}), f32[128,1,4]{2,1,0:T(1,128)S(1)}, u32[]{:S(2)}, u32[]{:S(2)}) async-start(f32[128,1,4]{2,1,0:T(1,128)} %bitcast.8), calls=%async_computation.2 | async-start | bytes 131072 | tf_op jit(solution)/shard_map/all_to_all | solution.py:195
  171.7 0.6 broadcast_multiply_fusion
  172.3 8.9 %all-to-all-done.2 = f32[128,1,4]{2,1,0:T(1,128)S(1)} async-done(((f32[128,1,4]{2,1,0:T(1,128)}), f32[128,1,4]{2,1,0:T(1,128)S(1)}, u32[]{:S(2)}, u32[]{:S(2)}) %all-to-all-start.2) | async-done | bytes 2080 | tf_op jit(solution)/shard_map/all_to_all | solution.py:195
  181.2 0.5 broadcast.596
  181.7 0.8 reduce.7
  182.6 0.1 reshape.356
  182.7 2.5 %gather_fusion.1 = f32[256]{0:T(256)} fusion(f32[512]{0:T(512)S(1)} %reshape.356, s32[1024]{0:T(1024)S(1)} %pad_clamp_fusion), kind=kCustom, calls=%fused_computation.1 | custom fusion | bytes 3072 | tf_op jit(solution)/shard_map/gather | solution.py:198
  (11 shorter events, 0.1 us)
Async XLA Ops:
  7.2 77.1 %all-gather.2.cloned.1.call-start = ((), (), s32[]{:S(2)}) async-start(), calls=%async_computation.3 | async-start | bytes 8912896 | tf_op jit(solution)/shard_map/all_gather | solution.py:165
  7.9 64.8 %collective-permute-start.3 = (bf16[256,2048]{1,0:T(8,128)(2,1)}, bf16[256,2048]{1,0:T(8,128)(2,1)}, u32[]{:S(2)}, u32[]{:S(2)}) collective-permute-start(bf16[256,2048]{1,0:T(8,128)(2,1)} %param.4), channel_id=1, source_target_pairs={{0,1},{1,0},{2,3},{3,2},{4,5},{5,4},{6,7},{7,6},{8,9},{9,8},{10,11... | collective-permute-start | bytes 3145736 | tf_op jit(solution)/shard_map/ppermute | solution.py:164
  9.4 55.7 %collective-permute-start.2 = (bf16[256,2048]{1,0:T(8,128)(2,1)}, bf16[256,2048]{1,0:T(8,128)(2,1)}, u32[]{:S(2)}, u32[]{:S(2)}) collective-permute-start(bf16[256,2048]{1,0:T(8,128)(2,1)} %param.4), channel_id=1, source_target_pairs={{0,96},{32,0},{64,32},{96,64},{1,97},{33,1},{65,33},{97,65},{2,98}... | collective-permute-start | bytes 3145736 | tf_op jit(solution)/shard_map/ppermute | solution.py:161
  12.2 53.0 %collective-permute-start.1 = (bf16[256,2048]{1,0:T(8,128)(2,1)}, bf16[256,2048]{1,0:T(8,128)(2,1)}, u32[]{:S(2)}, u32[]{:S(2)}) collective-permute-start(bf16[256,2048]{1,0:T(8,128)(2,1)} %param.4), channel_id=1, source_target_pairs={{0,64},{32,96},{64,0},{96,32},{1,65},{33,97},{65,1},{97,33},{2,66}... | collective-permute-start | bytes 3145736 | tf_op jit(solution)/shard_map/ppermute | solution.py:161
  12.6 49.0 %collective-permute-start = (bf16[256,2048]{1,0:T(8,128)(2,1)}, bf16[256,2048]{1,0:T(8,128)(2,1)}, u32[]{:S(2)}, u32[]{:S(2)}) collective-permute-start(bf16[256,2048]{1,0:T(8,128)(2,1)} %param.4), channel_id=1, source_target_pairs={{0,32},{32,64},{64,96},{96,0},{1,33},{33,65},{65,97},{97,1},{2,34}... | collective-permute-start | bytes 3145736 | tf_op jit(solution)/shard_map/ppermute | solution.py:161
  14.2 12.1 %copy-start.1 = (s32[256,1]{0,1:T(1,128)S(1)}, s32[256,1]{0,1:T(1,128)}, u32[]{:S(2)}) copy-start(s32[256,1]{0,1:T(1,128)} %param.6) | copy-start | bytes 3076
  14.2 12.2 %copy-start = (bf16[256,2048]{1,0:T(8,128)(2,1)S(1)}, bf16[256,2048]{1,0:T(8,128)(2,1)}, u32[]{:S(2)}) copy-start(bf16[256,2048]{1,0:T(8,128)(2,1)} %param.4) | copy-start | bytes 3145732
  61.6 13.5 %collective-permute-start.4 = (bf16[256,2048]{1,0:T(8,128)(2,1)}, bf16[256,2048]{1,0:T(8,128)(2,1)}, u32[]{:S(2)}, u32[]{:S(2)}) collective-permute-start(bf16[256,2048]{1,0:T(8,128)(2,1)} %collective-permute-done), channel_id=1, source_target_pairs={{0,1},{1,0},{2,3},{3,2},{4,5},{5,4},{6,7},{7,6},{8,9},{9,8},{10,11... | collective-permute-start | bytes 3145736 | tf_op jit(solution)/shard_map/ppermute | solution.py:164
  65.1 13.4 %collective-permute-start.6 = (bf16[256,2048]{1,0:T(8,128)(2,1)}, bf16[256,2048]{1,0:T(8,128)(2,1)S(1)}, u32[]{:S(2)}, u32[]{:S(2)}) collective-permute-start(bf16[256,2048]{1,0:T(8,128)(2,1)} %collective-permute-done.2), channel_id=1, source_target_pairs={{0,1},{1,0},{2,3},{3,2},{4,5},{5,4},{6,7},{7,6},{8,9},{9,8},{10,11... | collective-permute-start | bytes 3145736 | tf_op jit(solution)/shard_map/ppermute | solution.py:164
  65.2 12.2 %collective-permute-start.5 = (bf16[256,2048]{1,0:T(8,128)(2,1)}, bf16[256,2048]{1,0:T(8,128)(2,1)S(1)}, u32[]{:S(2)}, u32[]{:S(2)}) collective-permute-start(bf16[256,2048]{1,0:T(8,128)(2,1)} %collective-permute-done.1), channel_id=1, source_target_pairs={{0,1},{1,0},{2,3},{3,2},{4,5},{5,4},{6,7},{7,6},{8,9},{9,8},{10,11... | collective-permute-start | bytes 3145736 | tf_op jit(solution)/shard_map/ppermute | solution.py:164
  112.4 9.6 %all-to-all-start = ((f32[8,1,256]{2,1,0:T(1,128)}), f32[8,1,256]{2,1,0:T(1,128)S(1)}, u32[]{:S(2)}, u32[]{:S(2)}) async-start(f32[8,1,256]{2,1,0:T(1,128)} %copy.10), calls=%async_computation | async-start | bytes 16384 | tf_op jit(solution)/shard_map/all_to_all | solution.py:192
  122.0 38.0 %all-to-all-start.1 = ((bf16[128,4,2176]{2,1,0:T(4,128)(2,1)}), bf16[128,4,2176]{2,1,0:T(4,128)(2,1)}, u32[]{:S(2)}, u32[]{:S(2)}) async-start(bf16[128,4,2176]{2,1,0:T(4,128)(2,1)} %reshape.354), calls=%async_computation.1 | async-start | bytes 4456448 | tf_op jit(solution)/shard_map/all_to_all | solution.py:182
  167.2 14.0 %all-to-all-start.2 = ((f32[128,1,4]{2,1,0:T(1,128)}), f32[128,1,4]{2,1,0:T(1,128)S(1)}, u32[]{:S(2)}, u32[]{:S(2)}) async-start(f32[128,1,4]{2,1,0:T(1,128)} %bitcast.8), calls=%async_computation.2 | async-start | bytes 131072 | tf_op jit(solution)/shard_map/all_to_all | solution.py:195
Sparse Core Ops, SparseCore 0:
  10.1 74.0 all-gather.1

commit v13 on v11

--- a/solution.py
+++ b/solution.py
@@ -96,19 +96,28 @@
     return out.reshape((n * x.shape[0],) + x.shape[1:])
 
 
-def score_kernel(rows_ref, cents_ref, noise_ref, out_ref):
+def score_kernel(rows_ref, cents_ref, noise_ref, out_ref, acc_ref):
     scores = lax.dot_general(
         rows_ref[...], cents_ref[...], (((1,), (1,)), ((), ())), preferred_element_type=jnp.float32
     )
-    best = jnp.max(inverse_temp * scores + noise_ref[...], axis=1, keepdims=True)
-
-    @pl.when(pl.program_id(1) == 0)
+    perturbed = inverse_temp * scores + noise_ref[...]
+    lanes = acc_ref.shape[1]
+    folded = perturbed[:, :lanes]
+    for k in range(1, perturbed.shape[1] // lanes):
+        folded = jnp.maximum(folded, perturbed[:, k * lanes:(k + 1) * lanes])
+    step = pl.program_id(1)
+
+    @pl.when(step == 0)
     def _():
-        out_ref[...] = best
-
-    @pl.when(pl.program_id(1) > 0)
+        acc_ref[...] = folded
+
+    @pl.when(step > 0)
     def _():
-        out_ref[...] = jnp.maximum(out_ref[...], best)
+        acc_ref[...] = jnp.maximum(acc_ref[...], folded)
+
+    @pl.when(step == pl.num_programs(1) - 1)
+    def _():
+        out_ref[...] = jnp.max(acc_ref[...], axis=1, keepdims=True)
 
 
 def score_max(rows, cents, noise):
@@ -125,6 +134,7 @@
             pl.BlockSpec((tm, tn), lambda i, j: (i, j)),
         ],
         out_specs=pl.BlockSpec((tm, 1), lambda i, j: (i, 0)),
+        scratch_shapes=[pltpu.VMEM((tm, 128), jnp.float32)],
         compiler_params=pltpu.CompilerParams(dimension_semantics=("parallel", "arbitrary")),
     )(rows, cents, noise)
     return out[:, 0]

time: 157 us -> 156 us (level)
  no operation moved by 1% of the time
where the time goes in v13:
time: 156 us
  starting transfers between devices  33.4 us (21%)
  waiting for transfers between devices  31.2 us (20%)
  local copies, waits for them, and re-layouts  25.3 us (16%)
  Pallas kernels  25.1 us (16%)
  other arithmetic  21.8 us (14%)
  between operations  15.5 us (10%)
  matrix products  3.61 us (2%)
    ppermute x3, waiting for transfers between devices, shards(): lax.ppermute(embeddings, 'y', [(i, (i + s) % ny) for i in range(ny)])  30.4 us
    pallas_call x1, Pallas kernels, score_max(): pl.pallas_call(score_kernel, out_shape=jax.ShapeDtypeStruct((count, 1), j...  25.1 us
    neg x1, other arithmetic, gumbel_noise(): return -jnp.log(-jnp.log(uniform))  12 us
    unnamed x10, local copies, waits for them, and re-layouts  11.3 us
    all_to_all x1, starting transfers between devices, shards(): lax.all_to_all(scores.reshape(devices, capacity), ALL, split_axis=0, conc...  9.73 us
    all_to_all x1, starting transfers between devices, shards(): lax.all_to_all(outgoing.reshape(devices, capacity, feature_dim + flag_wid...  7.56 us
    ppermute x3, starting transfers between devices, shards(): lax.ppermute(embeddings, 'y', [(i, (i + s) % ny) for i in range(ny)])  5.88 us
    ppermute x4, starting transfers between devices, shards(): lax.ppermute(p, 'c', swap)  5.35 us
  transfers between devices with their start and end apart: 11, of which 2 were waited for; matrix products, arithmetic and copies ran while one was open for 32% of the time, Pallas kernels for 16%

profile of v13, /device:TPU:1, one launch (start us, length us, event | category | flops | bytes accessed | tf_op | source)
XLA Modules:
  0.0 155.9 jit_solution(8330511219066355625)
XLA Ops:
  7.2 0.0 all-gather.2.cloned.1.call-start
  7.2 0.7 all-gather.2.cloned.1.call-update
  7.9 2.2 %collective-permute-start = (bf16[256,2048]{1,0:T(8,128)(2,1)}, bf16[256,2048]{1,0:T(8,128)(2,1)}, u32[]{:S(2)}, u32[]{:S(2)}) collective-permute-start(bf16[256,2048]{1,0:T(8,128)(2,1)} %param.4), channel_id=1, source_target_pairs={{0,32},{32,64},{64,96},{96,0},{1,33},{33,65},{65,97},{97,1},{2,34}... | collective-permute-start | bytes 3145736 | tf_op jit(solution)/shard_map/ppermute | solution.py:171
  10.1 2.6 %collective-permute-start.1 = (bf16[256,2048]{1,0:T(8,128)(2,1)}, bf16[256,2048]{1,0:T(8,128)(2,1)}, u32[]{:S(2)}, u32[]{:S(2)}) collective-permute-start(bf16[256,2048]{1,0:T(8,128)(2,1)} %param.4), channel_id=1, source_target_pairs={{0,64},{32,96},{64,0},{96,32},{1,65},{33,97},{65,1},{97,33},{2,66}... | collective-permute-start | bytes 3145736 | tf_op jit(solution)/shard_map/ppermute | solution.py:171
  12.7 1.1 collective-permute-start.2
  13.8 1.5 collective-permute-start.3
  15.3 0.9 convert_reduce_fusion
  16.3 0.7 compare_select_fusion
  16.9 3.6 %scatter_custom_fusion = bf16[512,2176]{1,0:T(8,128)(2,1)S(1)} fusion(s32[256]{0:T(256)S(1)} %bitcast.19, bf16[256,2048]{1,0:T(8,128)(2,1)} %param.4, bf16[]{:T(256)} %constant.193.clone.1, bf16[]{:T(256)} %constant.191.clone.1), kind=kCustom, calls=%fused_computation.27 | custom fusion | bytes 3276804 | tf_op jit(solution)/shard_map/scatter | solution.py:197
  20.6 2.1 %reshape.354 = bf16[128,4,2176]{2,1,0:T(4,128)(2,1)} reshape(bf16[512,2176]{1,0:T(8,128)(2,1)S(1)} %scatter_custom_fusion) | data formatting | bytes 4456448 | tf_op jit(solution)/shard_map/reshape | solution.py:199
  22.7 7.6 %all-to-all-start.1 = ((bf16[128,4,2176]{2,1,0:T(4,128)(2,1)}), bf16[128,4,2176]{2,1,0:T(4,128)(2,1)S(1)}, u32[]{:S(2)}, u32[]{:S(2)}) async-start(bf16[128,4,2176]{2,1,0:T(4,128)(2,1)} %reshape.354), calls=%async_computation.1 | async-start | bytes 4456448 | tf_op jit(solution)/shard_map/all_to_all | solution.py:198
  31.0 0.1 pad_add_fusion
  31.1 0.1 add_multiply_fusion
  31.1 0.1 multiply_bitcast_fusion
  31.2 0.0 copy-start
  31.2 12.0 %fusion.9.noise_ref = f32[2048,2048]{1,0:T(8,128)} fusion(s32[]{:T(128)} %bitcast.15, s32[2048]{0:T(1024)S(1)} %fusion.46, s32[2048]{0:T(1024)S(1)} %bitcast.16), kind=kLoop, calls=%fused_computation.15 | loop fusion | flops 67108864 | bytes 16793604 | tf_op jit(solution)/shard_map/neg | solution.py:30
  43.3 0.0 copy-done
  43.3 1.1 constant_dynamic-update-slice_fusion.7
  44.4 0.0 collective-permute-done
  44.5 1.1 collective-permute-start.4
  45.5 30.4 %collective-permute-done.1 = bf16[256,2048]{1,0:T(8,128)(2,1)} collective-permute-done((bf16[256,2048]{1,0:T(8,128)(2,1)}, bf16[256,2048]{1,0:T(8,128)(2,1)}, u32[]{:S(2)}, u32[]{:S(2)}) %collective-permute-start.1) | collective-permute-done | bytes 1048608 | tf_op jit(solution)/shard_map/ppermute | solution.py:171
  76.0 2.7 %collective-permute-start.5 = (bf16[256,2048]{1,0:T(8,128)(2,1)}, bf16[256,2048]{1,0:T(8,128)(2,1)S(1)}, u32[]{:S(2)}, u32[]{:S(2)}) collective-permute-start(bf16[256,2048]{1,0:T(8,128)(2,1)} %collective-permute-done.1), channel_id=1, source_target_pairs={{0,1},{1,0},{2,3},{3,2},{4,5},{5,4},{6,7},{7,6},{8,9},{9,8},{10,11... | collective-permute-start | bytes 3145736 | tf_op jit(solution)/shard_map/ppermute | solution.py:174
  78.7 2.3 %constant_dynamic-update-slice_fusion.6 = bf16[2048,2048]{1,0:T(8,128)(2,1)} fusion(bf16[2048,2048]{1,0:T(8,128)(2,1)} %constant_dynamic-update-slice_fusion.7, bf16[256,2048]{1,0:T(8,128)(2,1)} %collective-permute-done), kind=kLoop, calls=%fused_computation.43 | loop fusion | bytes 2097152
  81.0 0.0 collective-permute-done.2
  81.0 0.0 collective-permute-start.6
  81.0 2.4 %constant_dynamic-update-slice_fusion.5 = bf16[2048,2048]{1,0:T(8,128)(2,1)} fusion(bf16[2048,2048]{1,0:T(8,128)(2,1)} %constant_dynamic-update-slice_fusion.6, bf16[256,2048]{1,0:T(8,128)(2,1)} %collective-permute-done.1), kind=kLoop, calls=%fused_computation.42 | loop fusion | bytes 2097152
  83.4 1.0 constant_dynamic-update-slice_fusion.4
  84.4 0.0 collective-permute-done.3
  84.4 2.4 %constant_dynamic-update-slice_fusion.3 = bf16[2048,2048]{1,0:T(8,128)(2,1)} fusion(bf16[2048,2048]{1,0:T(8,128)(2,1)} %constant_dynamic-update-slice_fusion.4, bf16[256,2048]{1,0:T(8,128)(2,1)} %collective-permute-done.3), kind=kLoop, calls=%fused_computation.40 | loop fusion | bytes 2097152
  86.8 0.0 collective-permute-done.4
  86.8 1.0 constant_dynamic-update-slice_fusion.2
  87.8 0.0 collective-permute-done.5
  87.8 1.0 constant_dynamic-update-slice_fusion.1
  88.9 0.0 collective-permute-done.6
  88.9 1.1 constant_dynamic-update-slice_fusion.rows_ref
  90.0 0.0 all-to-all-done.1
  90.0 2.1 %reshape.355 = bf16[512,2176]{1,0:T(8,128)(2,1)} reshape(bf16[128,4,2176]{2,1,0:T(4,128)(2,1)S(1)} %all-to-all-done.1) | data formatting | bytes 4456448 | tf_op jit(solution)/shard_map/reshape | solution.py:200
  92.1 1.1 compare_reduce_fusion
  93.1 0.2 fusion.33
  93.3 2.4 %fusion.11 = (f32[2048]{0:T(1024)S(1)}, f32[512]{0:T(512)S(1)}) fusion(pred[512]{0:T(512)(128)(4,1)S(1)} %compare_reduce_fusion, bf16[512,2176]{1,0:T(8,128)(2,1)} %reshape.355), kind=kLoop, calls=%fused_computation.19 | loop fusion | flops 5240320 | bytes 2107904 | tf_op jit(solution)/shard_map/reduce_sum | solution.py:155
  95.7 3.6 %fusion.26 = f32[512]{0:T(512)S(1)} fusion(bf16[512,2176]{1,0:T(8,128)(2,1)} %reshape.355, f32[512]{0:T(512)S(1)} %add_rsqrt_fusion, pred[512]{0:T(512)(128)(4,1)S(1)} %compare_reduce_fusion), kind=kOutput, calls=%fused_computation.26 | convolution fusion | flops 1075576320 | bytes 2103808 | tf_op jit(solution)/shard_map/dot_general | solution.py:147
  99.3 0.7 select_n.188
  100.1 9.7 %all-to-all-start.2 = ((f32[128,1,4]{2,1,0:T(1,128)}), f32[128,1,4]{2,1,0:T(1,128)S(1)}, u32[]{:S(2)}, u32[]{:S(2)}) async-start(f32[128,1,4]{2,1,0:T(1,128)} %bitcast.8), calls=%async_computation.2 | async-start | bytes 131072 | tf_op jit(solution)/shard_map/all_to_all | solution.py:204
  109.8 0.6 multiply_reduce_fusion
  111.1 0.0 all-gather.2.cloned.1.call-done.cents_ref
  111.1 25.1 %shard_map.67 = f32[2048,1]{1,0:T(8,128)} custom-call(bf16[2048,2048]{1,0:T(8,128)(2,1)} %constant_dynamic-update-slice_fusion.rows_ref, bf16[2048,2048]{1,0:T(8,128)(2,1)} %all-gather.2.cloned.1.call-done.cents_ref, f32[2048,2048]{1,0:T(8,128)} %fusion.9.noise_ref), custom_call_target="tpu_custom_call" | custom-call | tf_op jit(solution)/shard_map/pallas_call | solution.py:127
  136.2 1.6 %reduce.1 = f32[2048]{0:T(1024)S(1)} reduce(f32[2048,1]{1,0:T(8,128)} %shard_map.67, f32[]{:T(128)} %constant.203), dimensions={1}, to_apply=%pallas_call.3.reduce_sub_computation | reduce | bytes 16388 | tf_op jit(solution)/shard_map/pallas_call | solution.py:127
  137.8 0.6 gather_fusion
  138.4 0.1 bitcast_select_fusion
  138.4 0.6 copy.10
  139.0 0.0 all-to-all-done.2
  139.0 4.8 %all-to-all-start = ((f32[8,1,256]{2,1,0:T(1,128)}), f32[8,1,256]{2,1,0:T(1,128)S(1)}, u32[]{:S(2)}, u32[]{:S(2)}) async-start(f32[8,1,256]{2,1,0:T(1,128)} %copy.10), calls=%async_computation | async-start | bytes 16384 | tf_op jit(solution)/shard_map/all_to_all | solution.py:188
  143.9 0.6 broadcast_multiply_fusion
  144.5 0.5 broadcast.596
  145.0 0.8 reduce.7
  145.8 0.1 reshape.356
  145.9 2.5 %gather_fusion.1 = f32[256]{0:T(256)} fusion(f32[512]{0:T(512)S(1)} %reshape.356, s32[1024]{0:T(1024)S(1)} %pad_clamp_fusion), kind=kCustom, calls=%fused_computation.1 | custom fusion | bytes 3072 | tf_op jit(solution)/shard_map/gather | solution.py:207
  148.4 0.1 all-to-all-done
  148.5 0.6 reduce_max.18
  (10 shorter events, 0.1 us)
Async XLA Ops:
  7.2 104.0 %all-gather.2.cloned.1.call-start = ((), (), s32[]{:S(2)}) async-start(), calls=%async_computation.3 | async-start | bytes 8912896 | tf_op jit(solution)/shard_map/all_gather | solution.py:175
  7.9 36.6 %collective-permute-start = (bf16[256,2048]{1,0:T(8,128)(2,1)}, bf16[256,2048]{1,0:T(8,128)(2,1)}, u32[]{:S(2)}, u32[]{:S(2)}) collective-permute-start(bf16[256,2048]{1,0:T(8,128)(2,1)} %param.4), channel_id=1, source_target_pairs={{0,32},{32,64},{64,96},{96,0},{1,33},{33,65},{65,97},{97,1},{2,34}... | collective-permute-start | bytes 3145736 | tf_op jit(solution)/shard_map/ppermute | solution.py:171
  10.1 65.9 %collective-permute-start.1 = (bf16[256,2048]{1,0:T(8,128)(2,1)}, bf16[256,2048]{1,0:T(8,128)(2,1)}, u32[]{:S(2)}, u32[]{:S(2)}) collective-permute-start(bf16[256,2048]{1,0:T(8,128)(2,1)} %param.4), channel_id=1, source_target_pairs={{0,64},{32,96},{64,0},{96,32},{1,65},{33,97},{65,1},{97,33},{2,66}... | collective-permute-start | bytes 3145736 | tf_op jit(solution)/shard_map/ppermute | solution.py:171
  12.7 68.3 %collective-permute-start.2 = (bf16[256,2048]{1,0:T(8,128)(2,1)}, bf16[256,2048]{1,0:T(8,128)(2,1)S(1)}, u32[]{:S(2)}, u32[]{:S(2)}) collective-permute-start(bf16[256,2048]{1,0:T(8,128)(2,1)} %param.4), channel_id=1, source_target_pairs={{0,96},{32,0},{64,32},{96,64},{1,97},{33,1},{65,33},{97,65},{2,98}... | collective-permute-start | bytes 3145736 | tf_op jit(solution)/shard_map/ppermute | solution.py:171
  13.8 70.6 %collective-permute-start.3 = (bf16[256,2048]{1,0:T(8,128)(2,1)}, bf16[256,2048]{1,0:T(8,128)(2,1)}, u32[]{:S(2)}, u32[]{:S(2)}) collective-permute-start(bf16[256,2048]{1,0:T(8,128)(2,1)} %param.4), channel_id=1, source_target_pairs={{0,1},{1,0},{2,3},{3,2},{4,5},{5,4},{6,7},{7,6},{8,9},{9,8},{10,11... | collective-permute-start | bytes 3145736 | tf_op jit(solution)/shard_map/ppermute | solution.py:174
  22.7 67.2 %all-to-all-start.1 = ((bf16[128,4,2176]{2,1,0:T(4,128)(2,1)}), bf16[128,4,2176]{2,1,0:T(4,128)(2,1)S(1)}, u32[]{:S(2)}, u32[]{:S(2)}) async-start(bf16[128,4,2176]{2,1,0:T(4,128)(2,1)} %reshape.354), calls=%async_computation.1 | async-start | bytes 4456448 | tf_op jit(solution)/shard_map/all_to_all | solution.py:198
  31.2 12.1 %copy-start = (bf16[256,2048]{1,0:T(8,128)(2,1)S(1)}, bf16[256,2048]{1,0:T(8,128)(2,1)}, u32[]{:S(2)}) copy-start(bf16[256,2048]{1,0:T(8,128)(2,1)} %param.4) | copy-start | bytes 3145732
  44.5 42.3 %collective-permute-start.4 = (bf16[256,2048]{1,0:T(8,128)(2,1)}, bf16[256,2048]{1,0:T(8,128)(2,1)S(1)}, u32[]{:S(2)}, u32[]{:S(2)}) collective-permute-start(bf16[256,2048]{1,0:T(8,128)(2,1)} %collective-permute-done), channel_id=1, source_target_pairs={{0,1},{1,0},{2,3},{3,2},{4,5},{5,4},{6,7},{7,6},{8,9},{9,8},{10,11... | collective-permute-start | bytes 3145736 | tf_op jit(solution)/shard_map/ppermute | solution.py:174
  76.0 11.9 %collective-permute-start.5 = (bf16[256,2048]{1,0:T(8,128)(2,1)}, bf16[256,2048]{1,0:T(8,128)(2,1)S(1)}, u32[]{:S(2)}, u32[]{:S(2)}) collective-permute-start(bf16[256,2048]{1,0:T(8,128)(2,1)} %collective-permute-done.1), channel_id=1, source_target_pairs={{0,1},{1,0},{2,3},{3,2},{4,5},{5,4},{6,7},{7,6},{8,9},{9,8},{10,11... | collective-permute-start | bytes 3145736 | tf_op jit(solution)/shard_map/ppermute | solution.py:174
  81.0 7.9 %collective-permute-start.6 = (bf16[256,2048]{1,0:T(8,128)(2,1)S(1)}, bf16[256,2048]{1,0:T(8,128)(2,1)S(1)}, u32[]{:S(2)}, u32[]{:S(2)}) collective-permute-start(bf16[256,2048]{1,0:T(8,128)(2,1)S(1)} %collective-permute-done.2), channel_id=1, source_target_pairs={{0,1},{1,0},{2,3},{3,2},{4,5},{5,4},{6,7},{7,6},{8,9},{9,8},{10,11... | collective-permute-start | bytes 3145736 | tf_op jit(solution)/shard_map/ppermute | solution.py:174
  100.1 39.0 %all-to-all-start.2 = ((f32[128,1,4]{2,1,0:T(1,128)}), f32[128,1,4]{2,1,0:T(1,128)S(1)}, u32[]{:S(2)}, u32[]{:S(2)}) async-start(f32[128,1,4]{2,1,0:T(1,128)} %bitcast.8), calls=%async_computation.2 | async-start | bytes 131072 | tf_op jit(solution)/shard_map/all_to_all | solution.py:204
  139.0 9.4 %all-to-all-start = ((f32[8,1,256]{2,1,0:T(1,128)}), f32[8,1,256]{2,1,0:T(1,128)S(1)}, u32[]{:S(2)}, u32[]{:S(2)}) async-start(f32[8,1,256]{2,1,0:T(1,128)} %copy.10), calls=%async_computation | async-start | bytes 16384 | tf_op jit(solution)/shard_map/all_to_all | solution.py:188
Sparse Core Ops, SparseCore 0:
  10.1 90.6 all-gather.1

commit v14 on v13

--- a/solution.py
+++ b/solution.py
@@ -180,13 +180,6 @@
     cpos = jnp.arange(nz * nx * cent_dev, dtype=jnp.int32)
     cent_dev_ids = ((iy * nz + cpos // (nx * cent_dev)) * nx + cpos // cent_dev % nx) * nc + ic
     cent_ids = cent_dev_ids * cent_dev + cpos % cent_dev
-    noise = gumbel_noise(group_ids[:, None], cent_ids[None, :], salt_word)
-    result = score_max(group, piece, noise)
-    owner = jnp.arange(ny * nc, dtype=jnp.int32)
-    picked = (ic - owner % nc) % nc * ny + (iy - owner // nc) % ny
-    outbound = jnp.take(result.reshape(nc * ny, rows_dev), picked, axis=0)
-    inbound = lax.all_to_all(outbound, ("y", "c"), split_axis=0, concat_axis=0, tiled=True)
-    perturbed_max = jnp.max(inbound, axis=0)
     assigned = cluster[:, 0]
     order = jnp.arange(rows_dev, dtype=jnp.int32)
     same = (assigned[:, None] == assigned[None, :]) & (order[None, :] < order[:, None])
@@ -195,11 +188,22 @@
     flag_width = 128
     tagged = jnp.concatenate([embeddings, jnp.ones((rows_dev, flag_width), jnp.bfloat16)], axis=1)
     outgoing = jnp.zeros((devices * capacity, feature_dim + flag_width), jnp.bfloat16).at[slot].set(tagged)
+    outgoing, piece = lax.optimization_barrier((outgoing, piece))
     received = lax.all_to_all(
         outgoing.reshape(devices, capacity, feature_dim + flag_width), ALL, split_axis=0, concat_axis=0, tiled=True
     ).reshape(devices * capacity, feature_dim + flag_width)
     members = received[:, :feature_dim]
     valid = received[:, feature_dim] > 0.5
+    noise = gumbel_noise(group_ids[:, None], cent_ids[None, :], salt_word)
+    half = group.shape[0] // 2
+    first = score_max(group[:half], piece, noise[:half])
+    first, received = lax.optimization_barrier((first, received))
+    result = jnp.concatenate([first, score_max(group[half:], piece, noise[half:])])
+    owner = jnp.arange(ny * nc, dtype=jnp.int32)
+    picked = (ic - owner % nc) % nc * ny + (iy - owner // nc) % ny
+    outbound = jnp.take(result.reshape(nc * ny, rows_dev), picked, axis=0)
+    inbound = lax.all_to_all(outbound, ("y", "c"), split_axis=0, concat_axis=0, tiled=True)
+    perturbed_max = jnp.max(inbound, axis=0)
     scores, center = cluster_stats(members, valid)
     returned = lax.all_to_all(
         scores.reshape(devices, capacity), ALL, split_axis=0, concat_axis=0, tiled=True

time: 156 us -> 190 us (1.22)
  waiting for transfers between devices: 31.2 us -> 60.6 us
  other arithmetic: 21.8 us -> 28.1 us
  starting transfers between devices: 33.4 us -> 30 us
  Pallas kernels: 25.1 us -> 28.4 us
  local copies, waits for them, and re-layouts: 25.3 us -> 23.1 us
    all_gather x1, waiting for transfers between devices: 0.02 us -> 52.8 us  [shards(): piece = lax.all_gather(centroids, ('z', 'x'), axis=0, tiled=True)]
    ppermute x3, waiting for transfers between devices: 30.4 us -> 0.01 us  [shards(): lax.ppermute(embeddings, 'y', [(i, (i + s) % ny) for i in range(ny)])]
    unnamed x10 -> x5, local copies, waits for them, and re-layouts: 11.3 us -> 0.02 us
    slice x0 -> x1, local copies, waits for them, and re-layouts: none -> 10.8 us  [shards(): first = score_max(group[:half], piece, noise[:half])]
    all_to_all x1, waiting for transfers between devices: 0.01 us -> 6.95 us  [shards(): lax.all_to_all(scores.reshape(devices, capacity), ALL, split_axis=0, conc...]
    concatenate x0 -> x3, other arithmetic: none -> 6.8 us  [the longest x2 6.79 us: shards(): jnp.concatenate(ring_y + [lax.ppermute(p, 'c', swap) for p in ring_y], ax...]
    pallas_call x1 -> x2, Pallas kernels: 25.1 us -> 28.4 us  [score_max(): pl.pallas_call(score_kernel, out_shape=jax.ShapeDtypeStruct((count, 1), j...]
    ppermute x4, starting transfers between devices: 5.35 us -> 3.2 us  [shards(): lax.ppermute(p, 'c', swap)]
  transfers between devices with their start and end apart: 11 -> 11, of which waited for: 2 -> 3; matrix products, arithmetic and copies ran while one was open for 32% -> 23% of each run, Pallas kernels for 16% -> 15%
where the time goes in v14:
time: 190 us; the launch traced here: 189 us
  waiting for transfers between devices  60.6 us (32%)
  starting transfers between devices  30 us (16%)
  Pallas kernels  28.4 us (15%)
  other arithmetic  28.1 us (15%)
  local copies, waits for them, and re-layouts  23.1 us (12%)
  between operations  15.5 us (8%)
  matrix products  3.61 us (2%)
    all_gather x1, waiting for transfers between devices, shards(): piece = lax.all_gather(centroids, ('z', 'x'), axis=0, tiled=True)  52.8 us
    pallas_call x2, Pallas kernels, score_max(): pl.pallas_call(score_kernel, out_shape=jax.ShapeDtypeStruct((count, 1), j...  28.4 us
    neg x1, other arithmetic, gumbel_noise(): return -jnp.log(-jnp.log(uniform))  12 us
    slice x1, local copies, waits for them, and re-layouts, shards(): first = score_max(group[:half], piece, noise[:half])  10.8 us
    all_to_all x1, starting transfers between devices, shards(): lax.all_to_all(scores.reshape(devices, capacity), ALL, split_axis=0, conc...  8.96 us
    all_to_all x1, starting transfers between devices, shards(): lax.all_to_all(outgoing.reshape(devices, capacity, feature_dim + flag_wid...  7.86 us
    all_to_all x1, waiting for transfers between devices, shards(): lax.all_to_all(scores.reshape(devices, capacity), ALL, split_axis=0, conc...  6.95 us
    concatenate x2, other arithmetic, shards(): jnp.concatenate(ring_y + [lax.ppermute(p, 'c', swap) for p in ring_y], ax...  6.79 us
  transfers between devices with their start and end apart: 11, of which 3 were waited for; matrix products, arithmetic and copies ran while one was open for 23% of the time, Pallas kernels for 15%

profile of v14, /device:TPU:1, one launch (start us, length us, event | category | flops | bytes accessed | tf_op | source)
XLA Modules:
  0.0 189.3 jit_solution(3537025368414738067)
XLA Ops:
  7.2 0.0 all-gather.2.cloned.1.call-start
  7.2 0.7 all-gather.2.cloned.1.call-update
  7.9 2.2 %collective-permute-start = (bf16[256,2048]{1,0:T(8,128)(2,1)}, bf16[256,2048]{1,0:T(8,128)(2,1)}, u32[]{:S(2)}, u32[]{:S(2)}) collective-permute-start(bf16[256,2048]{1,0:T(8,128)(2,1)} %param.4), channel_id=1, source_target_pairs={{0,32},{32,64},{64,96},{96,0},{1,33},{33,65},{65,97},{97,1},{2,34}... | collective-permute-start | bytes 3145736 | tf_op jit(solution)/shard_map/ppermute | solution.py:171
  10.1 2.6 %collective-permute-start.1 = (bf16[256,2048]{1,0:T(8,128)(2,1)}, bf16[256,2048]{1,0:T(8,128)(2,1)}, u32[]{:S(2)}, u32[]{:S(2)}) collective-permute-start(bf16[256,2048]{1,0:T(8,128)(2,1)} %param.4), channel_id=1, source_target_pairs={{0,64},{32,96},{64,0},{96,32},{1,65},{33,97},{65,1},{97,33},{2,66}... | collective-permute-start | bytes 3145736 | tf_op jit(solution)/shard_map/ppermute | solution.py:171
  12.7 1.1 collective-permute-start.2
  13.8 1.5 collective-permute-start.3
  15.3 0.1 pad_add_fusion
  15.4 0.1 add_multiply_fusion
  15.5 0.1 multiply_bitcast_fusion
  16.2 0.0 copy-start.1
  16.3 0.0 copy-start
  16.3 12.0 %fusion.9 = f32[2048,2048]{1,0:T(8,128)} fusion(s32[]{:T(128)} %bitcast.15, s32[2048]{0:T(1024)S(1)} %fusion.46, s32[2048]{0:T(1024)S(1)} %bitcast.16), kind=kLoop, calls=%fused_computation.15 | loop fusion | flops 67108864 | bytes 16793604 | tf_op jit(solution)/shard_map/neg | solution.py:30
  28.3 0.0 copy-done.1
  28.3 0.2 convert_reduce_fusion
  28.5 0.0 copy-done
  28.5 3.0 %scatter_custom_fusion = bf16[512,2176]{1,0:T(8,128)(2,1)S(1)} fusion(s32[256]{0:T(256)S(1)} %bitcast.19, bf16[256,2048]{1,0:T(8,128)(2,1)S(1)} %copy-done, bf16[]{:T(256)} %constant.177.clone.1, bf16[]{:T(256)} %constant.175.clone.1), kind=kCustom, calls=%fused_computation.29 | custom fusion | bytes 3276804 | tf_op jit(solution)/shard_map/scatter | solution.py:190
  31.4 52.8 %all-gather.2.cloned.1.call-done.cents_ref = bf16[2048,2048]{1,0:T(8,128)(2,1)} async-done(((bf16[128,2048]{1,0:T(8,128)(2,1)}), bf16[2048,2048]{1,0:T(8,128)(2,1)}) %all-gather.2.cloned.1.call-update) | async-done | bytes 8388624 | tf_op jit(solution)/shard_map/all_gather | solution.py:175
  84.3 2.1 %reshape.358 = bf16[128,4,2176]{2,1,0:T(4,128)(2,1)} reshape(bf16[512,2176]{1,0:T(8,128)(2,1)S(1)} %scatter_custom_fusion) | data formatting | bytes 4456448 | tf_op jit(solution)/shard_map/reshape | solution.py:193
  86.4 7.9 %all-to-all-start = ((bf16[128,4,2176]{2,1,0:T(4,128)(2,1)}), bf16[128,4,2176]{2,1,0:T(4,128)(2,1)S(1)}, u32[]{:S(2)}, u32[]{:S(2)}) async-start(bf16[128,4,2176]{2,1,0:T(4,128)(2,1)} %reshape.358), calls=%async_computation | async-start | bytes 4456448 | tf_op jit(solution)/shard_map/all_to_all | solution.py:192
  94.3 0.0 collective-permute-done
  94.3 1.1 collective-permute-start.4
  95.5 0.0 collective-permute-done.1
  95.5 0.1 collective-permute-start.5
  95.6 0.0 collective-permute-done.2
  95.6 0.4 collective-permute-start.6
  96.0 10.8 %fusion.70 = (f32[1024,2048]{1,0:T(8,128)}, f32[1024,2048]{1,0:T(8,128)}) fusion(f32[2048,2048]{1,0:T(8,128)} %fusion.9), kind=kLoop, calls=%fused_computation.123 | loop fusion | bytes 33554432 | tf_op jit(solution)/shard_map/slice | solution.py:199
  106.8 3.6 %pad_maximum_fusion.rows_ref = bf16[1024,2048]{1,0:T(8,128)(2,1)} fusion(bf16[256,2048]{1,0:T(8,128)(2,1)} %collective-permute-done.2, bf16[256,2048]{1,0:T(8,128)(2,1)} %collective-permute-done.1, bf16[256,2048]{1,0:T(8,128)(2,1)} %collective-permute-done, bf16[256,2048]{1,0:T(8,128)(2,1)S(1)} %copy-done), kind=kLoop, calls=%fused_computation.20 | loop fusion | flops 16777216 | bytes 8388608 | tf_op jit(solution)/shard_map/concatenate | solution.py:174
  110.4 0.0 collective-permute-done.3
  110.4 0.0 collective-permute-done.4
  110.4 0.0 collective-permute-done.5
  110.4 0.0 collective-permute-done.6
  110.4 3.2 %pad_maximum_fusion.1.rows_ref = bf16[1024,2048]{1,0:T(8,128)(2,1)} fusion(bf16[256,2048]{1,0:T(8,128)(2,1)S(1)} %collective-permute-done.6, bf16[256,2048]{1,0:T(8,128)(2,1)S(1)} %collective-permute-done.5, bf16[256,2048]{1,0:T(8,128)(2,1)S(1)} %collective-permute-done.4, bf16[256,2048]{1,0:T(8,128)(2,1)} %collective-permute-done.3), kind=kLoop, calls=%fused_computation.21 | loop fusion | flops 16777216 | bytes 8388608 | tf_op jit(solution)/shard_map/concatenate | solution.py:174
  113.7 14.2 %shard_map.67 = f32[1024,1]{1,0:T(8,128)} custom-call(bf16[1024,2048]{1,0:T(8,128)(2,1)} %pad_maximum_fusion.rows_ref, bf16[2048,2048]{1,0:T(8,128)(2,1)} %all-gather.2.cloned.1.call-done.cents_ref, f32[1024,2048]{1,0:T(8,128)} %get-tuple-element.11.noise_ref), custom_call_target="tpu_custom_call" | custom-call | tf_op jit(solution)/shard_map/pallas_call | solution.py:127
  127.9 1.2 reduce.1
  129.1 14.2 %shard_map.68 = f32[1024,1]{1,0:T(8,128)} custom-call(bf16[1024,2048]{1,0:T(8,128)(2,1)} %pad_maximum_fusion.1.rows_ref, bf16[2048,2048]{1,0:T(8,128)(2,1)} %all-gather.2.cloned.1.call-done.cents_ref, f32[1024,2048]{1,0:T(8,128)} %get-tuple-element.12.noise_ref), custom_call_target="tpu_custom_call" | custom-call | tf_op jit(solution)/shard_map/pallas_call | solution.py:127
  143.3 1.2 reduce.2
  144.6 0.0 all-to-all-done
  144.6 2.1 %reshape.359 = bf16[512,2176]{1,0:T(8,128)(2,1)} reshape(bf16[128,4,2176]{2,1,0:T(4,128)(2,1)S(1)} %all-to-all-done) | data formatting | bytes 4456448 | tf_op jit(solution)/shard_map/reshape | solution.py:194
  146.7 1.1 compare_reduce_fusion
  147.8 2.4 %fusion.11 = (f32[2048]{0:T(1024)S(1)}, f32[512]{0:T(512)S(1)}) fusion(pred[512]{0:T(512)(128)(4,1)S(1)} %compare_reduce_fusion, bf16[512,2176]{1,0:T(8,128)(2,1)} %reshape.359), kind=kLoop, calls=%fused_computation.19 | loop fusion | flops 5240320 | bytes 2107904 | tf_op jit(solution)/shard_map/reduce_sum | solution.py:155
  150.2 0.2 fusion.33
  150.4 3.6 %fusion.26 = f32[512]{0:T(512)S(1)} fusion(bf16[512,2176]{1,0:T(8,128)(2,1)} %reshape.359, f32[512]{0:T(512)S(1)} %add_rsqrt_fusion, pred[512]{0:T(512)(128)(4,1)S(1)} %compare_reduce_fusion), kind=kOutput, calls=%fused_computation.28 | convolution fusion | flops 1075576320 | bytes 2103808 | tf_op jit(solution)/shard_map/dot_general | solution.py:147
  154.0 0.7 select_n.188
  154.7 9.0 %all-to-all-start.2 = ((f32[128,1,4]{2,1,0:T(1,128)}), f32[128,1,4]{2,1,0:T(1,128)S(1)}, u32[]{:S(2)}, u32[]{:S(2)}) async-start(f32[128,1,4]{2,1,0:T(1,128)} %bitcast.8), calls=%async_computation.2 | async-start | bytes 131072 | tf_op jit(solution)/shard_map/all_to_all | solution.py:208
  163.7 0.6 gather_fusion
  164.3 0.1 bitcast_select_fusion
  164.4 0.6 multiply_reduce_fusion
  165.0 0.6 copy.10
  166.2 6.9 %all-to-all-done.2 = f32[128,1,4]{2,1,0:T(1,128)S(1)} async-done(((f32[128,1,4]{2,1,0:T(1,128)}), f32[128,1,4]{2,1,0:T(1,128)S(1)}, u32[]{:S(2)}, u32[]{:S(2)}) %all-to-all-start.2) | async-done | bytes 2080 | tf_op jit(solution)/shard_map/all_to_all | solution.py:208
  173.2 4.1 %all-to-all-start.1 = ((f32[8,1,256]{2,1,0:T(1,128)}), f32[8,1,256]{2,1,0:T(1,128)S(1)}, u32[]{:S(2)}, u32[]{:S(2)}) async-start(f32[8,1,256]{2,1,0:T(1,128)} %copy.10), calls=%async_computation.1 | async-start | bytes 16384 | tf_op jit(solution)/shard_map/all_to_all | solution.py:205
  177.2 0.6 broadcast_multiply_fusion
  177.8 0.5 broadcast.597
  178.4 0.8 reduce.8
  179.2 0.1 reshape.360
  179.3 2.5 %gather_fusion.1 = f32[256]{0:T(256)} fusion(f32[512]{0:T(512)S(1)} %reshape.360, s32[1024]{0:T(1024)S(1)} %pad_clamp_fusion), kind=kCustom, calls=%fused_computation.1 | custom fusion | bytes 3072 | tf_op jit(solution)/shard_map/gather | solution.py:211
  181.8 0.1 all-to-all-done.1
  181.9 0.6 reduce_max.18
  (13 shorter events, 0.1 us)
Async XLA Ops:
  7.2 77.1 %all-gather.2.cloned.1.call-start = ((), (), s32[]{:S(2)}) async-start(), calls=%async_computation.3 | async-start | bytes 8912896 | tf_op jit(solution)/shard_map/all_gather | solution.py:175
  7.9 86.4 %collective-permute-start = (bf16[256,2048]{1,0:T(8,128)(2,1)}, bf16[256,2048]{1,0:T(8,128)(2,1)}, u32[]{:S(2)}, u32[]{:S(2)}) collective-permute-start(bf16[256,2048]{1,0:T(8,128)(2,1)} %param.4), channel_id=1, source_target_pairs={{0,32},{32,64},{64,96},{96,0},{1,33},{33,65},{65,97},{97,1},{2,34}... | collective-permute-start | bytes 3145736 | tf_op jit(solution)/shard_map/ppermute | solution.py:171
  10.1 85.4 %collective-permute-start.1 = (bf16[256,2048]{1,0:T(8,128)(2,1)}, bf16[256,2048]{1,0:T(8,128)(2,1)}, u32[]{:S(2)}, u32[]{:S(2)}) collective-permute-start(bf16[256,2048]{1,0:T(8,128)(2,1)} %param.4), channel_id=1, source_target_pairs={{0,64},{32,96},{64,0},{96,32},{1,65},{33,97},{65,1},{97,33},{2,66}... | collective-permute-start | bytes 3145736 | tf_op jit(solution)/shard_map/ppermute | solution.py:171
  12.7 82.9 %collective-permute-start.2 = (bf16[256,2048]{1,0:T(8,128)(2,1)}, bf16[256,2048]{1,0:T(8,128)(2,1)}, u32[]{:S(2)}, u32[]{:S(2)}) collective-permute-start(bf16[256,2048]{1,0:T(8,128)(2,1)} %param.4), channel_id=1, source_target_pairs={{0,96},{32,0},{64,32},{96,64},{1,97},{33,1},{65,33},{97,65},{2,98}... | collective-permute-start | bytes 3145736 | tf_op jit(solution)/shard_map/ppermute | solution.py:171
  13.8 96.6 %collective-permute-start.3 = (bf16[256,2048]{1,0:T(8,128)(2,1)}, bf16[256,2048]{1,0:T(8,128)(2,1)}, u32[]{:S(2)}, u32[]{:S(2)}) collective-permute-start(bf16[256,2048]{1,0:T(8,128)(2,1)} %param.4), channel_id=1, source_target_pairs={{0,1},{1,0},{2,3},{3,2},{4,5},{5,4},{6,7},{7,6},{8,9},{9,8},{10,11... | collective-permute-start | bytes 3145736 | tf_op jit(solution)/shard_map/ppermute | solution.py:174
  16.2 12.0 %copy-start.1 = (s32[256,1]{0,1:T(1,128)S(1)}, s32[256,1]{0,1:T(1,128)}, u32[]{:S(2)}) copy-start(s32[256,1]{0,1:T(1,128)} %param.6) | copy-start | bytes 3076
  16.3 12.2 %copy-start = (bf16[256,2048]{1,0:T(8,128)(2,1)S(1)}, bf16[256,2048]{1,0:T(8,128)(2,1)}, u32[]{:S(2)}) copy-start(bf16[256,2048]{1,0:T(8,128)(2,1)} %param.4) | copy-start | bytes 3145732
  86.4 58.2 %all-to-all-start = ((bf16[128,4,2176]{2,1,0:T(4,128)(2,1)}), bf16[128,4,2176]{2,1,0:T(4,128)(2,1)S(1)}, u32[]{:S(2)}, u32[]{:S(2)}) async-start(bf16[128,4,2176]{2,1,0:T(4,128)(2,1)} %reshape.358), calls=%async_computation | async-start | bytes 4456448 | tf_op jit(solution)/shard_map/all_to_all | solution.py:192
  94.3 16.0 %collective-permute-start.4 = (bf16[256,2048]{1,0:T(8,128)(2,1)}, bf16[256,2048]{1,0:T(8,128)(2,1)S(1)}, u32[]{:S(2)}, u32[]{:S(2)}) collective-permute-start(bf16[256,2048]{1,0:T(8,128)(2,1)} %collective-permute-done), channel_id=1, source_target_pairs={{0,1},{1,0},{2,3},{3,2},{4,5},{5,4},{6,7},{7,6},{8,9},{9,8},{10,11... | collective-permute-start | bytes 3145736 | tf_op jit(solution)/shard_map/ppermute | solution.py:174
  95.5 14.9 %collective-permute-start.5 = (bf16[256,2048]{1,0:T(8,128)(2,1)}, bf16[256,2048]{1,0:T(8,128)(2,1)S(1)}, u32[]{:S(2)}, u32[]{:S(2)}) collective-permute-start(bf16[256,2048]{1,0:T(8,128)(2,1)} %collective-permute-done.1), channel_id=1, source_target_pairs={{0,1},{1,0},{2,3},{3,2},{4,5},{5,4},{6,7},{7,6},{8,9},{9,8},{10,11... | collective-permute-start | bytes 3145736 | tf_op jit(solution)/shard_map/ppermute | solution.py:174
  95.6 14.8 %collective-permute-start.6 = (bf16[256,2048]{1,0:T(8,128)(2,1)}, bf16[256,2048]{1,0:T(8,128)(2,1)S(1)}, u32[]{:S(2)}, u32[]{:S(2)}) collective-permute-start(bf16[256,2048]{1,0:T(8,128)(2,1)} %collective-permute-done.2), channel_id=1, source_target_pairs={{0,1},{1,0},{2,3},{3,2},{4,5},{5,4},{6,7},{7,6},{8,9},{9,8},{10,11... | collective-permute-start | bytes 3145736 | tf_op jit(solution)/shard_map/ppermute | solution.py:174
  154.7 18.5 %all-to-all-start.2 = ((f32[128,1,4]{2,1,0:T(1,128)}), f32[128,1,4]{2,1,0:T(1,128)S(1)}, u32[]{:S(2)}, u32[]{:S(2)}) async-start(f32[128,1,4]{2,1,0:T(1,128)} %bitcast.8), calls=%async_computation.2 | async-start | bytes 131072 | tf_op jit(solution)/shard_map/all_to_all | solution.py:208
  173.2 8.7 %all-to-all-start.1 = ((f32[8,1,256]{2,1,0:T(1,128)}), f32[8,1,256]{2,1,0:T(1,128)S(1)}, u32[]{:S(2)}, u32[]{:S(2)}) async-start(f32[8,1,256]{2,1,0:T(1,128)} %copy.10), calls=%async_computation.1 | async-start | bytes 16384 | tf_op jit(solution)/shard_map/all_to_all | solution.py:205
Sparse Core Ops, SparseCore 0:
  10.1 74.0 all-gather.1

commit v15 on v13

--- a/solution.py
+++ b/solution.py
@@ -123,7 +123,7 @@
 def score_max(rows, cents, noise):
     count, width = rows.shape
     tm = min(1024, count)
-    tn = min(512, cents.shape[0])
+    tn = min(1024, cents.shape[0])
     out = pl.pallas_call(
         score_kernel,
         out_shape=jax.ShapeDtypeStruct((count, 1), jnp.float32),

time: 156 us -> 156 us (level)
  no operation moved by 1% of the time
where the time goes in v15:
time: 156 us; the launch traced here: 155 us
  starting transfers between devices  33.4 us (21%)
  waiting for transfers between devices  31.2 us (20%)
  local copies, waits for them, and re-layouts  25.3 us (16%)
  Pallas kernels  24.3 us (16%)
  other arithmetic  21.8 us (14%)
  between operations  15.5 us (10%)
  matrix products  3.61 us (2%)
    ppermute x3, waiting for transfers between devices, shards(): lax.ppermute(embeddings, 'y', [(i, (i + s) % ny) for i in range(ny)])  30.4 us
    pallas_call x1, Pallas kernels, score_max(): pl.pallas_call(score_kernel, out_shape=jax.ShapeDtypeStruct((count, 1), j...  24.3 us
    neg x1, other arithmetic, gumbel_noise(): return -jnp.log(-jnp.log(uniform))  12 us
    unnamed x10, local copies, waits for them, and re-layouts  11.3 us
    all_to_all x1, starting transfers between devices, shards(): lax.all_to_all(scores.reshape(devices, capacity), ALL, split_axis=0, conc...  9.73 us
    all_to_all x1, starting transfers between devices, shards(): lax.all_to_all(outgoing.reshape(devices, capacity, feature_dim + flag_wid...  7.56 us
    ppermute x3, starting transfers between devices, shards(): lax.ppermute(embeddings, 'y', [(i, (i + s) % ny) for i in range(ny)])  5.88 us
    ppermute x4, starting transfers between devices, shards(): lax.ppermute(p, 'c', swap)  5.35 us
  transfers between devices with their start and end apart: 11, of which 2 were waited for; matrix products, arithmetic and copies ran while one was open for 32% of the time, Pallas kernels for 16%

profile of v15, /device:TPU:1, one launch (start us, length us, event | category | flops | bytes accessed | tf_op | source)
XLA Modules:
  0.0 155.1 jit_solution(5249448124489291092)
XLA Ops:
  7.2 0.0 all-gather.2.cloned.1.call-start
  7.2 0.7 all-gather.2.cloned.1.call-update
  7.9 2.2 %collective-permute-start = (bf16[256,2048]{1,0:T(8,128)(2,1)}, bf16[256,2048]{1,0:T(8,128)(2,1)}, u32[]{:S(2)}, u32[]{:S(2)}) collective-permute-start(bf16[256,2048]{1,0:T(8,128)(2,1)} %param.4), channel_id=1, source_target_pairs={{0,32},{32,64},{64,96},{96,0},{1,33},{33,65},{65,97},{97,1},{2,34}... | collective-permute-start | bytes 3145736 | tf_op jit(solution)/shard_map/ppermute | solution.py:171
  10.1 2.6 %collective-permute-start.1 = (bf16[256,2048]{1,0:T(8,128)(2,1)}, bf16[256,2048]{1,0:T(8,128)(2,1)}, u32[]{:S(2)}, u32[]{:S(2)}) collective-permute-start(bf16[256,2048]{1,0:T(8,128)(2,1)} %param.4), channel_id=1, source_target_pairs={{0,64},{32,96},{64,0},{96,32},{1,65},{33,97},{65,1},{97,33},{2,66}... | collective-permute-start | bytes 3145736 | tf_op jit(solution)/shard_map/ppermute | solution.py:171
  12.7 1.1 collective-permute-start.2
  13.8 1.5 collective-permute-start.3
  15.3 0.9 convert_reduce_fusion
  16.3 0.7 compare_select_fusion
  16.9 3.6 %scatter_custom_fusion = bf16[512,2176]{1,0:T(8,128)(2,1)S(1)} fusion(s32[256]{0:T(256)S(1)} %bitcast.19, bf16[256,2048]{1,0:T(8,128)(2,1)} %param.4, bf16[]{:T(256)} %constant.193.clone.1, bf16[]{:T(256)} %constant.191.clone.1), kind=kCustom, calls=%fused_computation.27 | custom fusion | bytes 3276804 | tf_op jit(solution)/shard_map/scatter | solution.py:197
  20.6 2.1 %reshape.354 = bf16[128,4,2176]{2,1,0:T(4,128)(2,1)} reshape(bf16[512,2176]{1,0:T(8,128)(2,1)S(1)} %scatter_custom_fusion) | data formatting | bytes 4456448 | tf_op jit(solution)/shard_map/reshape | solution.py:199
  22.7 7.6 %all-to-all-start.1 = ((bf16[128,4,2176]{2,1,0:T(4,128)(2,1)}), bf16[128,4,2176]{2,1,0:T(4,128)(2,1)S(1)}, u32[]{:S(2)}, u32[]{:S(2)}) async-start(bf16[128,4,2176]{2,1,0:T(4,128)(2,1)} %reshape.354), calls=%async_computation.1 | async-start | bytes 4456448 | tf_op jit(solution)/shard_map/all_to_all | solution.py:198
  31.0 0.1 pad_add_fusion
  31.1 0.1 add_multiply_fusion
  31.1 0.1 multiply_bitcast_fusion
  31.2 0.0 copy-start
  31.2 12.0 %fusion.9.noise_ref = f32[2048,2048]{1,0:T(8,128)} fusion(s32[]{:T(128)} %bitcast.15, s32[2048]{0:T(1024)S(1)} %fusion.46, s32[2048]{0:T(1024)S(1)} %bitcast.16), kind=kLoop, calls=%fused_computation.15 | loop fusion | flops 67108864 | bytes 16793604 | tf_op jit(solution)/shard_map/neg | solution.py:30
  43.3 0.0 copy-done
  43.3 1.1 constant_dynamic-update-slice_fusion.7
  44.4 0.0 collective-permute-done
  44.5 1.1 collective-permute-start.4
  45.5 30.4 %collective-permute-done.1 = bf16[256,2048]{1,0:T(8,128)(2,1)} collective-permute-done((bf16[256,2048]{1,0:T(8,128)(2,1)}, bf16[256,2048]{1,0:T(8,128)(2,1)}, u32[]{:S(2)}, u32[]{:S(2)}) %collective-permute-start.1) | collective-permute-done | bytes 1048608 | tf_op jit(solution)/shard_map/ppermute | solution.py:171
  76.0 2.7 %collective-permute-start.5 = (bf16[256,2048]{1,0:T(8,128)(2,1)}, bf16[256,2048]{1,0:T(8,128)(2,1)S(1)}, u32[]{:S(2)}, u32[]{:S(2)}) collective-permute-start(bf16[256,2048]{1,0:T(8,128)(2,1)} %collective-permute-done.1), channel_id=1, source_target_pairs={{0,1},{1,0},{2,3},{3,2},{4,5},{5,4},{6,7},{7,6},{8,9},{9,8},{10,11... | collective-permute-start | bytes 3145736 | tf_op jit(solution)/shard_map/ppermute | solution.py:174
  78.7 2.3 %constant_dynamic-update-slice_fusion.6 = bf16[2048,2048]{1,0:T(8,128)(2,1)} fusion(bf16[2048,2048]{1,0:T(8,128)(2,1)} %constant_dynamic-update-slice_fusion.7, bf16[256,2048]{1,0:T(8,128)(2,1)} %collective-permute-done), kind=kLoop, calls=%fused_computation.43 | loop fusion | bytes 2097152
  81.0 0.0 collective-permute-done.2
  81.0 0.0 collective-permute-start.6
  81.0 2.4 %constant_dynamic-update-slice_fusion.5 = bf16[2048,2048]{1,0:T(8,128)(2,1)} fusion(bf16[2048,2048]{1,0:T(8,128)(2,1)} %constant_dynamic-update-slice_fusion.6, bf16[256,2048]{1,0:T(8,128)(2,1)} %collective-permute-done.1), kind=kLoop, calls=%fused_computation.42 | loop fusion | bytes 2097152
  83.4 1.0 constant_dynamic-update-slice_fusion.4
  84.4 0.0 collective-permute-done.3
  84.4 2.4 %constant_dynamic-update-slice_fusion.3 = bf16[2048,2048]{1,0:T(8,128)(2,1)} fusion(bf16[2048,2048]{1,0:T(8,128)(2,1)} %constant_dynamic-update-slice_fusion.4, bf16[256,2048]{1,0:T(8,128)(2,1)} %collective-permute-done.3), kind=kLoop, calls=%fused_computation.40 | loop fusion | bytes 2097152
  86.8 0.0 collective-permute-done.4
  86.8 1.0 constant_dynamic-update-slice_fusion.2
  87.8 0.0 collective-permute-done.5
  87.8 1.0 constant_dynamic-update-slice_fusion.1
  88.9 0.0 collective-permute-done.6
  88.9 1.1 constant_dynamic-update-slice_fusion.rows_ref
  90.0 0.0 all-to-all-done.1
  90.0 2.1 %reshape.355 = bf16[512,2176]{1,0:T(8,128)(2,1)} reshape(bf16[128,4,2176]{2,1,0:T(4,128)(2,1)S(1)} %all-to-all-done.1) | data formatting | bytes 4456448 | tf_op jit(solution)/shard_map/reshape | solution.py:200
  92.1 1.1 compare_reduce_fusion
  93.1 0.2 fusion.33
  93.3 2.4 %fusion.11 = (f32[2048]{0:T(1024)S(1)}, f32[512]{0:T(512)S(1)}) fusion(pred[512]{0:T(512)(128)(4,1)S(1)} %compare_reduce_fusion, bf16[512,2176]{1,0:T(8,128)(2,1)} %reshape.355), kind=kLoop, calls=%fused_computation.19 | loop fusion | flops 5240320 | bytes 2107904 | tf_op jit(solution)/shard_map/reduce_sum | solution.py:155
  95.7 3.6 %fusion.26 = f32[512]{0:T(512)S(1)} fusion(bf16[512,2176]{1,0:T(8,128)(2,1)} %reshape.355, f32[512]{0:T(512)S(1)} %add_rsqrt_fusion, pred[512]{0:T(512)(128)(4,1)S(1)} %compare_reduce_fusion), kind=kOutput, calls=%fused_computation.26 | convolution fusion | flops 1075576320 | bytes 2103808 | tf_op jit(solution)/shard_map/dot_general | solution.py:147
  99.3 0.7 select_n.188
  100.1 9.7 %all-to-all-start.2 = ((f32[128,1,4]{2,1,0:T(1,128)}), f32[128,1,4]{2,1,0:T(1,128)S(1)}, u32[]{:S(2)}, u32[]{:S(2)}) async-start(f32[128,1,4]{2,1,0:T(1,128)} %bitcast.8), calls=%async_computation.2 | async-start | bytes 131072 | tf_op jit(solution)/shard_map/all_to_all | solution.py:204
  109.8 0.6 multiply_reduce_fusion
  111.1 0.0 all-gather.2.cloned.1.call-done.cents_ref
  111.1 24.3 %shard_map.67 = f32[2048,1]{1,0:T(8,128)} custom-call(bf16[2048,2048]{1,0:T(8,128)(2,1)} %constant_dynamic-update-slice_fusion.rows_ref, bf16[2048,2048]{1,0:T(8,128)(2,1)} %all-gather.2.cloned.1.call-done.cents_ref, f32[2048,2048]{1,0:T(8,128)} %fusion.9.noise_ref), custom_call_target="tpu_custom_call" | custom-call | tf_op jit(solution)/shard_map/pallas_call | solution.py:127
  135.5 1.6 %reduce.1 = f32[2048]{0:T(1024)S(1)} reduce(f32[2048,1]{1,0:T(8,128)} %shard_map.67, f32[]{:T(128)} %constant.203), dimensions={1}, to_apply=%pallas_call.3.reduce_sub_computation | reduce | bytes 16388 | tf_op jit(solution)/shard_map/pallas_call | solution.py:127
  137.0 0.6 gather_fusion
  137.6 0.1 bitcast_select_fusion
  137.7 0.6 copy.10
  138.3 0.0 all-to-all-done.2
  138.3 4.8 %all-to-all-start = ((f32[8,1,256]{2,1,0:T(1,128)}), f32[8,1,256]{2,1,0:T(1,128)S(1)}, u32[]{:S(2)}, u32[]{:S(2)}) async-start(f32[8,1,256]{2,1,0:T(1,128)} %copy.10), calls=%async_computation | async-start | bytes 16384 | tf_op jit(solution)/shard_map/all_to_all | solution.py:188
  143.1 0.6 broadcast_multiply_fusion
  143.7 0.5 broadcast.596
  144.2 0.8 reduce.7
  145.0 0.1 reshape.356
  145.1 2.5 %gather_fusion.1 = f32[256]{0:T(256)} fusion(f32[512]{0:T(512)S(1)} %reshape.356, s32[1024]{0:T(1024)S(1)} %pad_clamp_fusion), kind=kCustom, calls=%fused_computation.1 | custom fusion | bytes 3072 | tf_op jit(solution)/shard_map/gather | solution.py:207
  147.6 0.1 all-to-all-done
  147.7 0.6 reduce_max.18
  (10 shorter events, 0.1 us)
Async XLA Ops:
  7.2 104.0 %all-gather.2.cloned.1.call-start = ((), (), s32[]{:S(2)}) async-start(), calls=%async_computation.3 | async-start | bytes 8912896 | tf_op jit(solution)/shard_map/all_gather | solution.py:175
  7.9 36.6 %collective-permute-start = (bf16[256,2048]{1,0:T(8,128)(2,1)}, bf16[256,2048]{1,0:T(8,128)(2,1)}, u32[]{:S(2)}, u32[]{:S(2)}) collective-permute-start(bf16[256,2048]{1,0:T(8,128)(2,1)} %param.4), channel_id=1, source_target_pairs={{0,32},{32,64},{64,96},{96,0},{1,33},{33,65},{65,97},{97,1},{2,34}... | collective-permute-start | bytes 3145736 | tf_op jit(solution)/shard_map/ppermute | solution.py:171
  10.1 65.9 %collective-permute-start.1 = (bf16[256,2048]{1,0:T(8,128)(2,1)}, bf16[256,2048]{1,0:T(8,128)(2,1)}, u32[]{:S(2)}, u32[]{:S(2)}) collective-permute-start(bf16[256,2048]{1,0:T(8,128)(2,1)} %param.4), channel_id=1, source_target_pairs={{0,64},{32,96},{64,0},{96,32},{1,65},{33,97},{65,1},{97,33},{2,66}... | collective-permute-start | bytes 3145736 | tf_op jit(solution)/shard_map/ppermute | solution.py:171
  12.7 68.3 %collective-permute-start.2 = (bf16[256,2048]{1,0:T(8,128)(2,1)}, bf16[256,2048]{1,0:T(8,128)(2,1)S(1)}, u32[]{:S(2)}, u32[]{:S(2)}) collective-permute-start(bf16[256,2048]{1,0:T(8,128)(2,1)} %param.4), channel_id=1, source_target_pairs={{0,96},{32,0},{64,32},{96,64},{1,97},{33,1},{65,33},{97,65},{2,98}... | collective-permute-start | bytes 3145736 | tf_op jit(solution)/shard_map/ppermute | solution.py:171
  13.8 70.6 %collective-permute-start.3 = (bf16[256,2048]{1,0:T(8,128)(2,1)}, bf16[256,2048]{1,0:T(8,128)(2,1)}, u32[]{:S(2)}, u32[]{:S(2)}) collective-permute-start(bf16[256,2048]{1,0:T(8,128)(2,1)} %param.4), channel_id=1, source_target_pairs={{0,1},{1,0},{2,3},{3,2},{4,5},{5,4},{6,7},{7,6},{8,9},{9,8},{10,11... | collective-permute-start | bytes 3145736 | tf_op jit(solution)/shard_map/ppermute | solution.py:174
  22.7 67.2 %all-to-all-start.1 = ((bf16[128,4,2176]{2,1,0:T(4,128)(2,1)}), bf16[128,4,2176]{2,1,0:T(4,128)(2,1)S(1)}, u32[]{:S(2)}, u32[]{:S(2)}) async-start(bf16[128,4,2176]{2,1,0:T(4,128)(2,1)} %reshape.354), calls=%async_computation.1 | async-start | bytes 4456448 | tf_op jit(solution)/shard_map/all_to_all | solution.py:198
  31.2 12.1 %copy-start = (bf16[256,2048]{1,0:T(8,128)(2,1)S(1)}, bf16[256,2048]{1,0:T(8,128)(2,1)}, u32[]{:S(2)}) copy-start(bf16[256,2048]{1,0:T(8,128)(2,1)} %param.4) | copy-start | bytes 3145732
  44.5 42.3 %collective-permute-start.4 = (bf16[256,2048]{1,0:T(8,128)(2,1)}, bf16[256,2048]{1,0:T(8,128)(2,1)S(1)}, u32[]{:S(2)}, u32[]{:S(2)}) collective-permute-start(bf16[256,2048]{1,0:T(8,128)(2,1)} %collective-permute-done), channel_id=1, source_target_pairs={{0,1},{1,0},{2,3},{3,2},{4,5},{5,4},{6,7},{7,6},{8,9},{9,8},{10,11... | collective-permute-start | bytes 3145736 | tf_op jit(solution)/shard_map/ppermute | solution.py:174
  76.0 11.9 %collective-permute-start.5 = (bf16[256,2048]{1,0:T(8,128)(2,1)}, bf16[256,2048]{1,0:T(8,128)(2,1)S(1)}, u32[]{:S(2)}, u32[]{:S(2)}) collective-permute-start(bf16[256,2048]{1,0:T(8,128)(2,1)} %collective-permute-done.1), channel_id=1, source_target_pairs={{0,1},{1,0},{2,3},{3,2},{4,5},{5,4},{6,7},{7,6},{8,9},{9,8},{10,11... | collective-permute-start | bytes 3145736 | tf_op jit(solution)/shard_map/ppermute | solution.py:174
  81.0 7.9 %collective-permute-start.6 = (bf16[256,2048]{1,0:T(8,128)(2,1)S(1)}, bf16[256,2048]{1,0:T(8,128)(2,1)S(1)}, u32[]{:S(2)}, u32[]{:S(2)}) collective-permute-start(bf16[256,2048]{1,0:T(8,128)(2,1)S(1)} %collective-permute-done.2), channel_id=1, source_target_pairs={{0,1},{1,0},{2,3},{3,2},{4,5},{5,4},{6,7},{7,6},{8,9},{9,8},{10,11... | collective-permute-start | bytes 3145736 | tf_op jit(solution)/shard_map/ppermute | solution.py:174
  100.1 38.2 %all-to-all-start.2 = ((f32[128,1,4]{2,1,0:T(1,128)}), f32[128,1,4]{2,1,0:T(1,128)S(1)}, u32[]{:S(2)}, u32[]{:S(2)}) async-start(f32[128,1,4]{2,1,0:T(1,128)} %bitcast.8), calls=%async_computation.2 | async-start | bytes 131072 | tf_op jit(solution)/shard_map/all_to_all | solution.py:204
  138.3 9.4 %all-to-all-start = ((f32[8,1,256]{2,1,0:T(1,128)}), f32[8,1,256]{2,1,0:T(1,128)S(1)}, u32[]{:S(2)}, u32[]{:S(2)}) async-start(f32[8,1,256]{2,1,0:T(1,128)} %copy.10), calls=%async_computation | async-start | bytes 16384 | tf_op jit(solution)/shard_map/all_to_all | solution.py:188
Sparse Core Ops, SparseCore 0:
  10.1 90.6 all-gather.1

commit v16 on v13

--- a/solution.py
+++ b/solution.py
@@ -122,7 +122,7 @@
 
 def score_max(rows, cents, noise):
     count, width = rows.shape
-    tm = min(1024, count)
+    tm = min(2048, count)
     tn = min(512, cents.shape[0])
     out = pl.pallas_call(
         score_kernel,

time: 156 us -> 157 us (level)
  no operation moved by 1% of the time
where the time goes in v16:
time: 157 us; the launch traced here: 156 us
  starting transfers between devices  33.4 us (21%)
  waiting for transfers between devices  31.2 us (20%)
  local copies, waits for them, and re-layouts  25.3 us (16%)
  Pallas kernels  25.3 us (16%)
  other arithmetic  21.8 us (14%)
  between operations  15.5 us (10%)
  matrix products  3.61 us (2%)
    ppermute x3, waiting for transfers between devices, shards(): lax.ppermute(embeddings, 'y', [(i, (i + s) % ny) for i in range(ny)])  30.4 us
    pallas_call x1, Pallas kernels, score_max(): pl.pallas_call(score_kernel, out_shape=jax.ShapeDtypeStruct((count, 1), j...  25.3 us
    neg x1, other arithmetic, gumbel_noise(): return -jnp.log(-jnp.log(uniform))  12 us
    unnamed x10, local copies, waits for them, and re-layouts  11.3 us
    all_to_all x1, starting transfers between devices, shards(): lax.all_to_all(scores.reshape(devices, capacity), ALL, split_axis=0, conc...  9.73 us
    all_to_all x1, starting transfers between devices, shards(): lax.all_to_all(outgoing.reshape(devices, capacity, feature_dim + flag_wid...  7.56 us
    ppermute x3, starting transfers between devices, shards(): lax.ppermute(embeddings, 'y', [(i, (i + s) % ny) for i in range(ny)])  5.88 us
    ppermute x4, starting transfers between devices, shards(): lax.ppermute(p, 'c', swap)  5.35 us
  transfers between devices with their start and end apart: 11, of which 2 were waited for; matrix products, arithmetic and copies ran while one was open for 32% of the time, Pallas kernels for 16%

profile of v16, /device:TPU:1, one launch (start us, length us, event | category | flops | bytes accessed | tf_op | source)
XLA Modules:
  0.0 156.1 jit_solution(12860975822165293212)
XLA Ops:
  7.2 0.0 all-gather.2.cloned.1.call-start
  7.2 0.7 all-gather.2.cloned.1.call-update
  7.9 2.2 %collective-permute-start = (bf16[256,2048]{1,0:T(8,128)(2,1)}, bf16[256,2048]{1,0:T(8,128)(2,1)}, u32[]{:S(2)}, u32[]{:S(2)}) collective-permute-start(bf16[256,2048]{1,0:T(8,128)(2,1)} %param.4), channel_id=1, source_target_pairs={{0,32},{32,64},{64,96},{96,0},{1,33},{33,65},{65,97},{97,1},{2,34}... | collective-permute-start | bytes 3145736 | tf_op jit(solution)/shard_map/ppermute | solution.py:171
  10.1 2.6 %collective-permute-start.1 = (bf16[256,2048]{1,0:T(8,128)(2,1)}, bf16[256,2048]{1,0:T(8,128)(2,1)}, u32[]{:S(2)}, u32[]{:S(2)}) collective-permute-start(bf16[256,2048]{1,0:T(8,128)(2,1)} %param.4), channel_id=1, source_target_pairs={{0,64},{32,96},{64,0},{96,32},{1,65},{33,97},{65,1},{97,33},{2,66}... | collective-permute-start | bytes 3145736 | tf_op jit(solution)/shard_map/ppermute | solution.py:171
  12.7 1.1 collective-permute-start.2
  13.8 1.5 collective-permute-start.3
  15.3 0.9 convert_reduce_fusion
  16.3 0.7 compare_select_fusion
  16.9 3.6 %scatter_custom_fusion = bf16[512,2176]{1,0:T(8,128)(2,1)S(1)} fusion(s32[256]{0:T(256)S(1)} %bitcast.19, bf16[256,2048]{1,0:T(8,128)(2,1)} %param.4, bf16[]{:T(256)} %constant.193.clone.1, bf16[]{:T(256)} %constant.191.clone.1), kind=kCustom, calls=%fused_computation.27 | custom fusion | bytes 3276804 | tf_op jit(solution)/shard_map/scatter | solution.py:197
  20.6 2.1 %reshape.354 = bf16[128,4,2176]{2,1,0:T(4,128)(2,1)} reshape(bf16[512,2176]{1,0:T(8,128)(2,1)S(1)} %scatter_custom_fusion) | data formatting | bytes 4456448 | tf_op jit(solution)/shard_map/reshape | solution.py:199
  22.7 7.6 %all-to-all-start.1 = ((bf16[128,4,2176]{2,1,0:T(4,128)(2,1)}), bf16[128,4,2176]{2,1,0:T(4,128)(2,1)S(1)}, u32[]{:S(2)}, u32[]{:S(2)}) async-start(bf16[128,4,2176]{2,1,0:T(4,128)(2,1)} %reshape.354), calls=%async_computation.1 | async-start | bytes 4456448 | tf_op jit(solution)/shard_map/all_to_all | solution.py:198
  31.0 0.1 pad_add_fusion
  31.1 0.1 add_multiply_fusion
  31.1 0.1 multiply_bitcast_fusion
  31.2 0.0 copy-start
  31.2 12.0 %fusion.9.noise_ref = f32[2048,2048]{1,0:T(8,128)} fusion(s32[]{:T(128)} %bitcast.15, s32[2048]{0:T(1024)S(1)} %fusion.46, s32[2048]{0:T(1024)S(1)} %bitcast.16), kind=kLoop, calls=%fused_computation.15 | loop fusion | flops 67108864 | bytes 16793604 | tf_op jit(solution)/shard_map/neg | solution.py:30
  43.3 0.0 copy-done
  43.3 1.1 constant_dynamic-update-slice_fusion.7
  44.4 0.0 collective-permute-done
  44.5 1.1 collective-permute-start.4
  45.5 30.4 %collective-permute-done.1 = bf16[256,2048]{1,0:T(8,128)(2,1)} collective-permute-done((bf16[256,2048]{1,0:T(8,128)(2,1)}, bf16[256,2048]{1,0:T(8,128)(2,1)}, u32[]{:S(2)}, u32[]{:S(2)}) %collective-permute-start.1) | collective-permute-done | bytes 1048608 | tf_op jit(solution)/shard_map/ppermute | solution.py:171
  76.0 2.7 %collective-permute-start.5 = (bf16[256,2048]{1,0:T(8,128)(2,1)}, bf16[256,2048]{1,0:T(8,128)(2,1)S(1)}, u32[]{:S(2)}, u32[]{:S(2)}) collective-permute-start(bf16[256,2048]{1,0:T(8,128)(2,1)} %collective-permute-done.1), channel_id=1, source_target_pairs={{0,1},{1,0},{2,3},{3,2},{4,5},{5,4},{6,7},{7,6},{8,9},{9,8},{10,11... | collective-permute-start | bytes 3145736 | tf_op jit(solution)/shard_map/ppermute | solution.py:174
  78.7 2.3 %constant_dynamic-update-slice_fusion.6 = bf16[2048,2048]{1,0:T(8,128)(2,1)} fusion(bf16[2048,2048]{1,0:T(8,128)(2,1)} %constant_dynamic-update-slice_fusion.7, bf16[256,2048]{1,0:T(8,128)(2,1)} %collective-permute-done), kind=kLoop, calls=%fused_computation.43 | loop fusion | bytes 2097152
  81.0 0.0 collective-permute-done.2
  81.0 0.0 collective-permute-start.6
  81.0 2.4 %constant_dynamic-update-slice_fusion.5 = bf16[2048,2048]{1,0:T(8,128)(2,1)} fusion(bf16[2048,2048]{1,0:T(8,128)(2,1)} %constant_dynamic-update-slice_fusion.6, bf16[256,2048]{1,0:T(8,128)(2,1)} %collective-permute-done.1), kind=kLoop, calls=%fused_computation.42 | loop fusion | bytes 2097152
  83.4 1.0 constant_dynamic-update-slice_fusion.4
  84.4 0.0 collective-permute-done.3
  84.4 2.4 %constant_dynamic-update-slice_fusion.3 = bf16[2048,2048]{1,0:T(8,128)(2,1)} fusion(bf16[2048,2048]{1,0:T(8,128)(2,1)} %constant_dynamic-update-slice_fusion.4, bf16[256,2048]{1,0:T(8,128)(2,1)} %collective-permute-done.3), kind=kLoop, calls=%fused_computation.40 | loop fusion | bytes 2097152
  86.8 0.0 collective-permute-done.4
  86.8 1.0 constant_dynamic-update-slice_fusion.2
  87.8 0.0 collective-permute-done.5
  87.8 1.0 constant_dynamic-update-slice_fusion.1
  88.9 0.0 collective-permute-done.6
  88.9 1.1 constant_dynamic-update-slice_fusion.rows_ref
  90.0 0.0 all-to-all-done.1
  90.0 2.1 %reshape.355 = bf16[512,2176]{1,0:T(8,128)(2,1)} reshape(bf16[128,4,2176]{2,1,0:T(4,128)(2,1)S(1)} %all-to-all-done.1) | data formatting | bytes 4456448 | tf_op jit(solution)/shard_map/reshape | solution.py:200
  92.1 1.1 compare_reduce_fusion
  93.1 0.2 fusion.33
  93.3 2.4 %fusion.11 = (f32[2048]{0:T(1024)S(1)}, f32[512]{0:T(512)S(1)}) fusion(pred[512]{0:T(512)(128)(4,1)S(1)} %compare_reduce_fusion, bf16[512,2176]{1,0:T(8,128)(2,1)} %reshape.355), kind=kLoop, calls=%fused_computation.19 | loop fusion | flops 5240320 | bytes 2107904 | tf_op jit(solution)/shard_map/reduce_sum | solution.py:155
  95.7 3.6 %fusion.26 = f32[512]{0:T(512)S(1)} fusion(bf16[512,2176]{1,0:T(8,128)(2,1)} %reshape.355, f32[512]{0:T(512)S(1)} %add_rsqrt_fusion, pred[512]{0:T(512)(128)(4,1)S(1)} %compare_reduce_fusion), kind=kOutput, calls=%fused_computation.26 | convolution fusion | flops 1075576320 | bytes 2103808 | tf_op jit(solution)/shard_map/dot_general | solution.py:147
  99.3 0.7 select_n.188
  100.1 9.7 %all-to-all-start.2 = ((f32[128,1,4]{2,1,0:T(1,128)}), f32[128,1,4]{2,1,0:T(1,128)S(1)}, u32[]{:S(2)}, u32[]{:S(2)}) async-start(f32[128,1,4]{2,1,0:T(1,128)} %bitcast.8), calls=%async_computation.2 | async-start | bytes 131072 | tf_op jit(solution)/shard_map/all_to_all | solution.py:204
  109.8 0.6 multiply_reduce_fusion
  111.1 0.0 all-gather.2.cloned.1.call-done.cents_ref
  111.1 25.3 %shard_map.67 = f32[2048,1]{1,0:T(8,128)} custom-call(bf16[2048,2048]{1,0:T(8,128)(2,1)} %constant_dynamic-update-slice_fusion.rows_ref, bf16[2048,2048]{1,0:T(8,128)(2,1)} %all-gather.2.cloned.1.call-done.cents_ref, f32[2048,2048]{1,0:T(8,128)} %fusion.9.noise_ref), custom_call_target="tpu_custom_call" | custom-call | tf_op jit(solution)/shard_map/pallas_call | solution.py:127
  136.4 1.6 %reduce.1 = f32[2048]{0:T(1024)S(1)} reduce(f32[2048,1]{1,0:T(8,128)} %shard_map.67, f32[]{:T(128)} %constant.203), dimensions={1}, to_apply=%pallas_call.3.reduce_sub_computation | reduce | bytes 16388 | tf_op jit(solution)/shard_map/pallas_call | solution.py:127
  138.0 0.6 gather_fusion
  138.6 0.1 bitcast_select_fusion
  138.6 0.6 copy.10
  139.2 0.0 all-to-all-done.2
  139.2 4.8 %all-to-all-start = ((f32[8,1,256]{2,1,0:T(1,128)}), f32[8,1,256]{2,1,0:T(1,128)S(1)}, u32[]{:S(2)}, u32[]{:S(2)}) async-start(f32[8,1,256]{2,1,0:T(1,128)} %copy.10), calls=%async_computation | async-start | bytes 16384 | tf_op jit(solution)/shard_map/all_to_all | solution.py:188
  144.1 0.6 broadcast_multiply_fusion
  144.7 0.5 broadcast.596
  145.2 0.8 reduce.7
  146.0 0.1 reshape.356
  146.1 2.5 %gather_fusion.1 = f32[256]{0:T(256)} fusion(f32[512]{0:T(512)S(1)} %reshape.356, s32[1024]{0:T(1024)S(1)} %pad_clamp_fusion), kind=kCustom, calls=%fused_computation.1 | custom fusion | bytes 3072 | tf_op jit(solution)/shard_map/gather | solution.py:207
  148.6 0.1 all-to-all-done
  148.7 0.6 reduce_max.18
  (10 shorter events, 0.1 us)
Async XLA Ops:
  7.2 104.0 %all-gather.2.cloned.1.call-start = ((), (), s32[]{:S(2)}) async-start(), calls=%async_computation.3 | async-start | bytes 8912896 | tf_op jit(solution)/shard_map/all_gather | solution.py:175
  7.9 36.6 %collective-permute-start = (bf16[256,2048]{1,0:T(8,128)(2,1)}, bf16[256,2048]{1,0:T(8,128)(2,1)}, u32[]{:S(2)}, u32[]{:S(2)}) collective-permute-start(bf16[256,2048]{1,0:T(8,128)(2,1)} %param.4), channel_id=1, source_target_pairs={{0,32},{32,64},{64,96},{96,0},{1,33},{33,65},{65,97},{97,1},{2,34}... | collective-permute-start | bytes 3145736 | tf_op jit(solution)/shard_map/ppermute | solution.py:171
  10.1 65.9 %collective-permute-start.1 = (bf16[256,2048]{1,0:T(8,128)(2,1)}, bf16[256,2048]{1,0:T(8,128)(2,1)}, u32[]{:S(2)}, u32[]{:S(2)}) collective-permute-start(bf16[256,2048]{1,0:T(8,128)(2,1)} %param.4), channel_id=1, source_target_pairs={{0,64},{32,96},{64,0},{96,32},{1,65},{33,97},{65,1},{97,33},{2,66}... | collective-permute-start | bytes 3145736 | tf_op jit(solution)/shard_map/ppermute | solution.py:171
  12.7 68.3 %collective-permute-start.2 = (bf16[256,2048]{1,0:T(8,128)(2,1)}, bf16[256,2048]{1,0:T(8,128)(2,1)S(1)}, u32[]{:S(2)}, u32[]{:S(2)}) collective-permute-start(bf16[256,2048]{1,0:T(8,128)(2,1)} %param.4), channel_id=1, source_target_pairs={{0,96},{32,0},{64,32},{96,64},{1,97},{33,1},{65,33},{97,65},{2,98}... | collective-permute-start | bytes 3145736 | tf_op jit(solution)/shard_map/ppermute | solution.py:171
  13.8 70.6 %collective-permute-start.3 = (bf16[256,2048]{1,0:T(8,128)(2,1)}, bf16[256,2048]{1,0:T(8,128)(2,1)}, u32[]{:S(2)}, u32[]{:S(2)}) collective-permute-start(bf16[256,2048]{1,0:T(8,128)(2,1)} %param.4), channel_id=1, source_target_pairs={{0,1},{1,0},{2,3},{3,2},{4,5},{5,4},{6,7},{7,6},{8,9},{9,8},{10,11... | collective-permute-start | bytes 3145736 | tf_op jit(solution)/shard_map/ppermute | solution.py:174
  22.7 67.2 %all-to-all-start.1 = ((bf16[128,4,2176]{2,1,0:T(4,128)(2,1)}), bf16[128,4,2176]{2,1,0:T(4,128)(2,1)S(1)}, u32[]{:S(2)}, u32[]{:S(2)}) async-start(bf16[128,4,2176]{2,1,0:T(4,128)(2,1)} %reshape.354), calls=%async_computation.1 | async-start | bytes 4456448 | tf_op jit(solution)/shard_map/all_to_all | solution.py:198
  31.2 12.1 %copy-start = (bf16[256,2048]{1,0:T(8,128)(2,1)S(1)}, bf16[256,2048]{1,0:T(8,128)(2,1)}, u32[]{:S(2)}) copy-start(bf16[256,2048]{1,0:T(8,128)(2,1)} %param.4) | copy-start | bytes 3145732
  44.5 42.3 %collective-permute-start.4 = (bf16[256,2048]{1,0:T(8,128)(2,1)}, bf16[256,2048]{1,0:T(8,128)(2,1)S(1)}, u32[]{:S(2)}, u32[]{:S(2)}) collective-permute-start(bf16[256,2048]{1,0:T(8,128)(2,1)} %collective-permute-done), channel_id=1, source_target_pairs={{0,1},{1,0},{2,3},{3,2},{4,5},{5,4},{6,7},{7,6},{8,9},{9,8},{10,11... | collective-permute-start | bytes 3145736 | tf_op jit(solution)/shard_map/ppermute | solution.py:174
  76.0 11.9 %collective-permute-start.5 = (bf16[256,2048]{1,0:T(8,128)(2,1)}, bf16[256,2048]{1,0:T(8,128)(2,1)S(1)}, u32[]{:S(2)}, u32[]{:S(2)}) collective-permute-start(bf16[256,2048]{1,0:T(8,128)(2,1)} %collective-permute-done.1), channel_id=1, source_target_pairs={{0,1},{1,0},{2,3},{3,2},{4,5},{5,4},{6,7},{7,6},{8,9},{9,8},{10,11... | collective-permute-start | bytes 3145736 | tf_op jit(solution)/shard_map/ppermute | solution.py:174
  81.0 7.9 %collective-permute-start.6 = (bf16[256,2048]{1,0:T(8,128)(2,1)S(1)}, bf16[256,2048]{1,0:T(8,128)(2,1)S(1)}, u32[]{:S(2)}, u32[]{:S(2)}) collective-permute-start(bf16[256,2048]{1,0:T(8,128)(2,1)S(1)} %collective-permute-done.2), channel_id=1, source_target_pairs={{0,1},{1,0},{2,3},{3,2},{4,5},{5,4},{6,7},{7,6},{8,9},{9,8},{10,11... | collective-permute-start | bytes 3145736 | tf_op jit(solution)/shard_map/ppermute | solution.py:174
  100.1 39.2 %all-to-all-start.2 = ((f32[128,1,4]{2,1,0:T(1,128)}), f32[128,1,4]{2,1,0:T(1,128)S(1)}, u32[]{:S(2)}, u32[]{:S(2)}) async-start(f32[128,1,4]{2,1,0:T(1,128)} %bitcast.8), calls=%async_computation.2 | async-start | bytes 131072 | tf_op jit(solution)/shard_map/all_to_all | solution.py:204
  139.2 9.4 %all-to-all-start = ((f32[8,1,256]{2,1,0:T(1,128)}), f32[8,1,256]{2,1,0:T(1,128)S(1)}, u32[]{:S(2)}, u32[]{:S(2)}) async-start(f32[8,1,256]{2,1,0:T(1,128)} %copy.10), calls=%async_computation | async-start | bytes 16384 | tf_op jit(solution)/shard_map/all_to_all | solution.py:188
Sparse Core Ops, SparseCore 0:
  10.1 90.6 all-gather.1

commit v17 on v15

--- a/solution.py
+++ b/solution.py
@@ -96,15 +96,13 @@
     return out.reshape((n * x.shape[0],) + x.shape[1:])
 
 
-def score_kernel(rows_ref, cents_ref, noise_ref, out_ref, acc_ref):
+def score_kernel(cents_ref, rows_ref, noise_ref, out_ref, acc_ref):
     scores = lax.dot_general(
-        rows_ref[...], cents_ref[...], (((1,), (1,)), ((), ())), preferred_element_type=jnp.float32
+        cents_ref[...], rows_ref[...], (((1,), (1,)), ((), ())), preferred_element_type=jnp.float32
     )
     perturbed = inverse_temp * scores + noise_ref[...]
-    lanes = acc_ref.shape[1]
-    folded = perturbed[:, :lanes]
-    for k in range(1, perturbed.shape[1] // lanes):
-        folded = jnp.maximum(folded, perturbed[:, k * lanes:(k + 1) * lanes])
+    depth = acc_ref.shape[0]
+    folded = jnp.max(perturbed.reshape(perturbed.shape[0] // depth, depth, perturbed.shape[1]), axis=0)
     step = pl.program_id(1)
 
     @pl.when(step == 0)
@@ -117,27 +115,27 @@
 
     @pl.when(step == pl.num_programs(1) - 1)
     def _():
-        out_ref[...] = jnp.max(acc_ref[...], axis=1, keepdims=True)
-
-
-def score_max(rows, cents, noise):
+        out_ref[...] = jnp.max(acc_ref[...], axis=0, keepdims=True)
+
+
+def score_max(rows, cents, noise_t):
     count, width = rows.shape
     tm = min(1024, count)
     tn = min(1024, cents.shape[0])
     out = pl.pallas_call(
         score_kernel,
-        out_shape=jax.ShapeDtypeStruct((count, 1), jnp.float32),
+        out_shape=jax.ShapeDtypeStruct((1, count), jnp.float32),
         grid=(count // tm, cents.shape[0] // tn),
         in_specs=[
+            pl.BlockSpec((tn, width), lambda i, j: (j, 0)),
             pl.BlockSpec((tm, width), lambda i, j: (i, 0)),
-            pl.BlockSpec((tn, width), lambda i, j: (j, 0)),
-            pl.BlockSpec((tm, tn), lambda i, j: (i, j)),
+            pl.BlockSpec((tn, tm), lambda i, j: (j, i)),
         ],
-        out_specs=pl.BlockSpec((tm, 1), lambda i, j: (i, 0)),
-        scratch_shapes=[pltpu.VMEM((tm, 128), jnp.float32)],
+        out_specs=pl.BlockSpec((1, tm), lambda i, j: (0, i)),
+        scratch_shapes=[pltpu.VMEM((8, tm), jnp.float32)],
         compiler_params=pltpu.CompilerParams(dimension_semantics=("parallel", "arbitrary")),
-    )(rows, cents, noise)
-    return out[:, 0]
+    )(cents, rows, noise_t)
+    return out[0]
 
 
 def cluster_stats(members, valid):
@@ -180,8 +178,8 @@
     cpos = jnp.arange(nz * nx * cent_dev, dtype=jnp.int32)
     cent_dev_ids = ((iy * nz + cpos // (nx * cent_dev)) * nx + cpos // cent_dev % nx) * nc + ic
     cent_ids = cent_dev_ids * cent_dev + cpos % cent_dev
-    noise = gumbel_noise(group_ids[:, None], cent_ids[None, :], salt_word)
-    result = score_max(group, piece, noise)
+    noise_t = gumbel_noise(group_ids[None, :], cent_ids[:, None], salt_word)
+    result = score_max(group, piece, noise_t)
     owner = jnp.arange(ny * nc, dtype=jnp.int32)
     picked = (ic - owner % nc) % nc * ny + (iy - owner // nc) % ny
     outbound = jnp.take(result.reshape(nc * ny, rows_dev), picked, axis=0)

time: 156 us -> 155 us (level)
  transfers between devices with their start and end apart: 11 -> 11, of which waited for: 2 -> 2; matrix products, arithmetic and copies ran while one was open for 32% -> 32% of each run, Pallas kernels for 16% -> 15%
where the time goes in v17:
time: 155 us
  starting transfers between devices  33.4 us (22%)
  waiting for transfers between devices  31.7 us (20%)
  local copies, waits for them, and re-layouts  25.3 us (16%)
  Pallas kernels  23.6 us (15%)
  other arithmetic  21.6 us (14%)
  between operations  15.5 us (10%)
  matrix products  3.61 us (2%)
    ppermute x3, waiting for transfers between devices, shards(): lax.ppermute(embeddings, 'y', [(i, (i + s) % ny) for i in range(ny)])  30.4 us
    pallas_call x1, Pallas kernels, score_max(): pl.pallas_call(score_kernel, out_shape=jax.ShapeDtypeStruct((1, count), j...  23.6 us
    neg x1, other arithmetic, gumbel_noise(): return -jnp.log(-jnp.log(uniform))  12 us
    unnamed x10, local copies, waits for them, and re-layouts  11.3 us
    all_to_all x1, starting transfers between devices, shards(): lax.all_to_all(scores.reshape(devices, capacity), ALL, split_axis=0, conc...  9.73 us
    all_to_all x1, starting transfers between devices, shards(): lax.all_to_all(outgoing.reshape(devices, capacity, feature_dim + flag_wid...  7.56 us
    ppermute x3, starting transfers between devices, shards(): lax.ppermute(embeddings, 'y', [(i, (i + s) % ny) for i in range(ny)])  5.88 us
    ppermute x4, starting transfers between devices, shards(): lax.ppermute(p, 'c', swap)  5.35 us
  transfers between devices with their start and end apart: 11, of which 2 were waited for; matrix products, arithmetic and copies ran while one was open for 32% of the time, Pallas kernels for 15%

profile of v17, /device:TPU:1, one launch (start us, length us, event | category | flops | bytes accessed | tf_op | source)
XLA Modules:
  0.0 154.7 jit_solution(3981592812080545057)
XLA Ops:
  7.2 0.0 all-gather.2.cloned.1.call-start
  7.2 0.7 all-gather.2.cloned.1.call-update
  7.9 2.2 %collective-permute-start = (bf16[256,2048]{1,0:T(8,128)(2,1)}, bf16[256,2048]{1,0:T(8,128)(2,1)}, u32[]{:S(2)}, u32[]{:S(2)}) collective-permute-start(bf16[256,2048]{1,0:T(8,128)(2,1)} %param.4), channel_id=1, source_target_pairs={{0,32},{32,64},{64,96},{96,0},{1,33},{33,65},{65,97},{97,1},{2,34}... | collective-permute-start | bytes 3145736 | tf_op jit(solution)/shard_map/ppermute | solution.py:169
  10.1 2.6 %collective-permute-start.1 = (bf16[256,2048]{1,0:T(8,128)(2,1)}, bf16[256,2048]{1,0:T(8,128)(2,1)}, u32[]{:S(2)}, u32[]{:S(2)}) collective-permute-start(bf16[256,2048]{1,0:T(8,128)(2,1)} %param.4), channel_id=1, source_target_pairs={{0,64},{32,96},{64,0},{96,32},{1,65},{33,97},{65,1},{97,33},{2,66}... | collective-permute-start | bytes 3145736 | tf_op jit(solution)/shard_map/ppermute | solution.py:169
  12.7 1.1 collective-permute-start.2
  13.8 1.5 collective-permute-start.3
  15.3 0.9 convert_reduce_fusion
  16.3 0.7 compare_select_fusion
  16.9 3.6 %scatter_custom_fusion = bf16[512,2176]{1,0:T(8,128)(2,1)S(1)} fusion(s32[256]{0:T(256)S(1)} %bitcast.19, bf16[256,2048]{1,0:T(8,128)(2,1)} %param.4, bf16[]{:T(256)} %constant.193.clone.1, bf16[]{:T(256)} %constant.191.clone.1), kind=kCustom, calls=%fused_computation.27 | custom fusion | bytes 3276804 | tf_op jit(solution)/shard_map/scatter | solution.py:195
  20.6 2.1 %reshape.354 = bf16[128,4,2176]{2,1,0:T(4,128)(2,1)} reshape(bf16[512,2176]{1,0:T(8,128)(2,1)S(1)} %scatter_custom_fusion) | data formatting | bytes 4456448 | tf_op jit(solution)/shard_map/reshape | solution.py:197
  22.7 7.6 %all-to-all-start.1 = ((bf16[128,4,2176]{2,1,0:T(4,128)(2,1)}), bf16[128,4,2176]{2,1,0:T(4,128)(2,1)S(1)}, u32[]{:S(2)}, u32[]{:S(2)}) async-start(bf16[128,4,2176]{2,1,0:T(4,128)(2,1)} %reshape.354), calls=%async_computation.1 | async-start | bytes 4456448 | tf_op jit(solution)/shard_map/all_to_all | solution.py:196
  31.0 0.1 pad_add_fusion
  31.1 0.1 add_multiply_fusion
  31.1 0.1 multiply_bitcast_fusion
  31.2 0.0 copy-start
  31.2 12.0 %fusion.9.noise_ref = f32[2048,2048]{1,0:T(8,128)} fusion(s32[]{:T(128)} %bitcast.15, s32[2048]{0:T(1024)S(1)} %fusion.46, s32[2048]{0:T(1024)S(1)} %bitcast.16), kind=kLoop, calls=%fused_computation.15 | loop fusion | flops 67108864 | bytes 16793604 | tf_op jit(solution)/shard_map/neg | solution.py:30
  43.3 0.0 copy-done
  43.3 1.1 constant_dynamic-update-slice_fusion.7
  44.4 0.0 collective-permute-done
  44.5 1.1 collective-permute-start.4
  45.5 30.4 %collective-permute-done.1 = bf16[256,2048]{1,0:T(8,128)(2,1)} collective-permute-done((bf16[256,2048]{1,0:T(8,128)(2,1)}, bf16[256,2048]{1,0:T(8,128)(2,1)}, u32[]{:S(2)}, u32[]{:S(2)}) %collective-permute-start.1) | collective-permute-done | bytes 1048608 | tf_op jit(solution)/shard_map/ppermute | solution.py:169
  76.0 2.7 %collective-permute-start.5 = (bf16[256,2048]{1,0:T(8,128)(2,1)}, bf16[256,2048]{1,0:T(8,128)(2,1)S(1)}, u32[]{:S(2)}, u32[]{:S(2)}) collective-permute-start(bf16[256,2048]{1,0:T(8,128)(2,1)} %collective-permute-done.1), channel_id=1, source_target_pairs={{0,1},{1,0},{2,3},{3,2},{4,5},{5,4},{6,7},{7,6},{8,9},{9,8},{10,11... | collective-permute-start | bytes 3145736 | tf_op jit(solution)/shard_map/ppermute | solution.py:172
  78.7 2.3 %constant_dynamic-update-slice_fusion.6 = bf16[2048,2048]{1,0:T(8,128)(2,1)} fusion(bf16[2048,2048]{1,0:T(8,128)(2,1)} %constant_dynamic-update-slice_fusion.7, bf16[256,2048]{1,0:T(8,128)(2,1)} %collective-permute-done), kind=kLoop, calls=%fused_computation.43 | loop fusion | bytes 2097152
  81.0 0.0 collective-permute-done.2
  81.0 0.0 collective-permute-start.6
  81.0 2.4 %constant_dynamic-update-slice_fusion.5 = bf16[2048,2048]{1,0:T(8,128)(2,1)} fusion(bf16[2048,2048]{1,0:T(8,128)(2,1)} %constant_dynamic-update-slice_fusion.6, bf16[256,2048]{1,0:T(8,128)(2,1)} %collective-permute-done.1), kind=kLoop, calls=%fused_computation.42 | loop fusion | bytes 2097152
  83.4 1.0 constant_dynamic-update-slice_fusion.4
  84.4 0.0 collective-permute-done.3
  84.4 2.4 %constant_dynamic-update-slice_fusion.3 = bf16[2048,2048]{1,0:T(8,128)(2,1)} fusion(bf16[2048,2048]{1,0:T(8,128)(2,1)} %constant_dynamic-update-slice_fusion.4, bf16[256,2048]{1,0:T(8,128)(2,1)} %collective-permute-done.3), kind=kLoop, calls=%fused_computation.40 | loop fusion | bytes 2097152
  86.8 0.0 collective-permute-done.4
  86.8 1.0 constant_dynamic-update-slice_fusion.2
  87.8 0.0 collective-permute-done.5
  87.8 1.0 constant_dynamic-update-slice_fusion.1
  88.9 0.0 collective-permute-done.6
  88.9 1.1 constant_dynamic-update-slice_fusion.rows_ref
  90.0 0.0 all-to-all-done.1
  90.0 2.1 %reshape.355 = bf16[512,2176]{1,0:T(8,128)(2,1)} reshape(bf16[128,4,2176]{2,1,0:T(4,128)(2,1)S(1)} %all-to-all-done.1) | data formatting | bytes 4456448 | tf_op jit(solution)/shard_map/reshape | solution.py:198
  92.1 1.1 compare_reduce_fusion
  93.1 0.2 fusion.33
  93.3 2.4 %fusion.11 = (f32[2048]{0:T(1024)S(1)}, f32[512]{0:T(512)S(1)}) fusion(pred[512]{0:T(512)(128)(4,1)S(1)} %compare_reduce_fusion, bf16[512,2176]{1,0:T(8,128)(2,1)} %reshape.355), kind=kLoop, calls=%fused_computation.19 | loop fusion | flops 5240320 | bytes 2107904 | tf_op jit(solution)/shard_map/reduce_sum | solution.py:153
  95.7 3.6 %fusion.26 = f32[512]{0:T(512)S(1)} fusion(bf16[512,2176]{1,0:T(8,128)(2,1)} %reshape.355, f32[512]{0:T(512)S(1)} %add_rsqrt_fusion, pred[512]{0:T(512)(128)(4,1)S(1)} %compare_reduce_fusion), kind=kOutput, calls=%fused_computation.26 | convolution fusion | flops 1075576320 | bytes 2103808 | tf_op jit(solution)/shard_map/dot_general | solution.py:145
  99.3 0.7 select_n.188
  100.1 9.7 %all-to-all-start.2 = ((f32[128,1,4]{2,1,0:T(1,128)}), f32[128,1,4]{2,1,0:T(1,128)S(1)}, u32[]{:S(2)}, u32[]{:S(2)}) async-start(f32[128,1,4]{2,1,0:T(1,128)} %bitcast.8), calls=%async_computation.2 | async-start | bytes 131072 | tf_op jit(solution)/shard_map/all_to_all | solution.py:202
  109.8 0.6 multiply_reduce_fusion
  111.1 0.0 all-gather.2.cloned.1.call-done.cents_ref
  111.1 23.6 %shard_map.67 = f32[1,2048]{1,0:T(1,128)} custom-call(bf16[2048,2048]{1,0:T(8,128)(2,1)} %all-gather.2.cloned.1.call-done.cents_ref, bf16[2048,2048]{1,0:T(8,128)(2,1)} %constant_dynamic-update-slice_fusion.rows_ref, f32[2048,2048]{1,0:T(8,128)} %fusion.9.noise_ref), custom_call_target="tpu_custom_call" | custom-call | tf_op jit(solution)/shard_map/pallas_call | solution.py:125
  134.7 0.5 broadcast.598
  135.3 1.4 reduce.9
  136.6 0.6 gather_fusion
  137.2 0.1 bitcast_select_fusion
  137.3 0.6 copy.10
  137.9 0.0 all-to-all-done.2
  137.9 4.8 %all-to-all-start = ((f32[8,1,256]{2,1,0:T(1,128)}), f32[8,1,256]{2,1,0:T(1,128)S(1)}, u32[]{:S(2)}, u32[]{:S(2)}) async-start(f32[8,1,256]{2,1,0:T(1,128)} %copy.10), calls=%async_computation | async-start | bytes 16384 | tf_op jit(solution)/shard_map/all_to_all | solution.py:186
  142.7 0.6 broadcast_multiply_fusion
  143.3 0.8 reduce.10
  144.1 0.1 reshape.356
  144.2 2.5 %gather_fusion.1 = f32[256]{0:T(256)} fusion(f32[512]{0:T(512)S(1)} %reshape.356, s32[1024]{0:T(1024)S(1)} %pad_clamp_fusion), kind=kCustom, calls=%fused_computation.1 | custom fusion | bytes 3072 | tf_op jit(solution)/shard_map/gather | solution.py:205
  146.7 0.6 all-to-all-done
  147.3 0.6 reduce_max.18
  (10 shorter events, 0.1 us)
Async XLA Ops:
  7.2 103.9 %all-gather.2.cloned.1.call-start = ((), (), s32[]{:S(2)}) async-start(), calls=%async_computation.3 | async-start | bytes 8912896 | tf_op jit(solution)/shard_map/all_gather | solution.py:173
  7.9 36.6 %collective-permute-start = (bf16[256,2048]{1,0:T(8,128)(2,1)}, bf16[256,2048]{1,0:T(8,128)(2,1)}, u32[]{:S(2)}, u32[]{:S(2)}) collective-permute-start(bf16[256,2048]{1,0:T(8,128)(2,1)} %param.4), channel_id=1, source_target_pairs={{0,32},{32,64},{64,96},{96,0},{1,33},{33,65},{65,97},{97,1},{2,34}... | collective-permute-start | bytes 3145736 | tf_op jit(solution)/shard_map/ppermute | solution.py:169
  10.1 65.9 %collective-permute-start.1 = (bf16[256,2048]{1,0:T(8,128)(2,1)}, bf16[256,2048]{1,0:T(8,128)(2,1)}, u32[]{:S(2)}, u32[]{:S(2)}) collective-permute-start(bf16[256,2048]{1,0:T(8,128)(2,1)} %param.4), channel_id=1, source_target_pairs={{0,64},{32,96},{64,0},{96,32},{1,65},{33,97},{65,1},{97,33},{2,66}... | collective-permute-start | bytes 3145736 | tf_op jit(solution)/shard_map/ppermute | solution.py:169
  12.7 68.3 %collective-permute-start.2 = (bf16[256,2048]{1,0:T(8,128)(2,1)}, bf16[256,2048]{1,0:T(8,128)(2,1)S(1)}, u32[]{:S(2)}, u32[]{:S(2)}) collective-permute-start(bf16[256,2048]{1,0:T(8,128)(2,1)} %param.4), channel_id=1, source_target_pairs={{0,96},{32,0},{64,32},{96,64},{1,97},{33,1},{65,33},{97,65},{2,98}... | collective-permute-start | bytes 3145736 | tf_op jit(solution)/shard_map/ppermute | solution.py:169
  13.8 70.6 %collective-permute-start.3 = (bf16[256,2048]{1,0:T(8,128)(2,1)}, bf16[256,2048]{1,0:T(8,128)(2,1)}, u32[]{:S(2)}, u32[]{:S(2)}) collective-permute-start(bf16[256,2048]{1,0:T(8,128)(2,1)} %param.4), channel_id=1, source_target_pairs={{0,1},{1,0},{2,3},{3,2},{4,5},{5,4},{6,7},{7,6},{8,9},{9,8},{10,11... | collective-permute-start | bytes 3145736 | tf_op jit(solution)/shard_map/ppermute | solution.py:172
  22.7 67.2 %all-to-all-start.1 = ((bf16[128,4,2176]{2,1,0:T(4,128)(2,1)}), bf16[128,4,2176]{2,1,0:T(4,128)(2,1)S(1)}, u32[]{:S(2)}, u32[]{:S(2)}) async-start(bf16[128,4,2176]{2,1,0:T(4,128)(2,1)} %reshape.354), calls=%async_computation.1 | async-start | bytes 4456448 | tf_op jit(solution)/shard_map/all_to_all | solution.py:196
  31.2 12.1 %copy-start = (bf16[256,2048]{1,0:T(8,128)(2,1)S(1)}, bf16[256,2048]{1,0:T(8,128)(2,1)}, u32[]{:S(2)}) copy-start(bf16[256,2048]{1,0:T(8,128)(2,1)} %param.4) | copy-start | bytes 3145732
  44.5 42.3 %collective-permute-start.4 = (bf16[256,2048]{1,0:T(8,128)(2,1)}, bf16[256,2048]{1,0:T(8,128)(2,1)S(1)}, u32[]{:S(2)}, u32[]{:S(2)}) collective-permute-start(bf16[256,2048]{1,0:T(8,128)(2,1)} %collective-permute-done), channel_id=1, source_target_pairs={{0,1},{1,0},{2,3},{3,2},{4,5},{5,4},{6,7},{7,6},{8,9},{9,8},{10,11... | collective-permute-start | bytes 3145736 | tf_op jit(solution)/shard_map/ppermute | solution.py:172
  76.0 11.9 %collective-permute-start.5 = (bf16[256,2048]{1,0:T(8,128)(2,1)}, bf16[256,2048]{1,0:T(8,128)(2,1)S(1)}, u32[]{:S(2)}, u32[]{:S(2)}) collective-permute-start(bf16[256,2048]{1,0:T(8,128)(2,1)} %collective-permute-done.1), channel_id=1, source_target_pairs={{0,1},{1,0},{2,3},{3,2},{4,5},{5,4},{6,7},{7,6},{8,9},{9,8},{10,11... | collective-permute-start | bytes 3145736 | tf_op jit(solution)/shard_map/ppermute | solution.py:172
  81.0 7.9 %collective-permute-start.6 = (bf16[256,2048]{1,0:T(8,128)(2,1)S(1)}, bf16[256,2048]{1,0:T(8,128)(2,1)S(1)}, u32[]{:S(2)}, u32[]{:S(2)}) collective-permute-start(bf16[256,2048]{1,0:T(8,128)(2,1)S(1)} %collective-permute-done.2), channel_id=1, source_target_pairs={{0,1},{1,0},{2,3},{3,2},{4,5},{5,4},{6,7},{7,6},{8,9},{9,8},{10,11... | collective-permute-start | bytes 3145736 | tf_op jit(solution)/shard_map/ppermute | solution.py:172
  100.1 37.8 %all-to-all-start.2 = ((f32[128,1,4]{2,1,0:T(1,128)}), f32[128,1,4]{2,1,0:T(1,128)S(1)}, u32[]{:S(2)}, u32[]{:S(2)}) async-start(f32[128,1,4]{2,1,0:T(1,128)} %bitcast.8), calls=%async_computation.2 | async-start | bytes 131072 | tf_op jit(solution)/shard_map/all_to_all | solution.py:202
  137.9 9.4 %all-to-all-start = ((f32[8,1,256]{2,1,0:T(1,128)}), f32[8,1,256]{2,1,0:T(1,128)S(1)}, u32[]{:S(2)}, u32[]{:S(2)}) async-start(f32[8,1,256]{2,1,0:T(1,128)} %copy.10), calls=%async_computation | async-start | bytes 16384 | tf_op jit(solution)/shard_map/all_to_all | solution.py:186
Sparse Core Ops, SparseCore 0:
  10.1 90.6 all-gather.1

commit v18 on v17

--- a/solution.py
+++ b/solution.py
@@ -202,7 +202,11 @@
     returned = lax.all_to_all(
         scores.reshape(devices, capacity), ALL, split_axis=0, concat_axis=0, tiled=True
     )
-    dedup_score = returned.reshape(devices * capacity)[slot]
+    back = returned.reshape(devices, capacity)
+    hit = assigned[:, None] == jnp.arange(devices, dtype=jnp.int32)[None, :]
+    by_owner = jnp.sum(jnp.where(hit[:, :, None], back[None, :, :], 0.0), axis=1)
+    by_rank = rank[:, None] == jnp.arange(capacity, dtype=jnp.int32)[None, :]
+    dedup_score = jnp.sum(jnp.where(by_rank, by_owner, 0.0), axis=1)
     return (perturbed_max, dedup_score, center[None, :])
 
 

time: 155 us -> 163 us (1.052)
  waiting for transfers between devices: 31.7 us -> 42.6 us
  local copies, waits for them, and re-layouts: 25.3 us -> 22.7 us
    all_to_all x1, waiting for transfers between devices: 0.01 us -> 7.6 us  [shards(): lax.all_to_all(scores.reshape(devices, capacity), ALL, split_axis=0, conc...]
    all_to_all x1, waiting for transfers between devices: 0.59 us -> 4.05 us  [shards(): lax.all_to_all(outbound, ('y', 'c'), split_axis=0, concat_axis=0, tiled=T...]
    gather x1 -> x0, local copies, waits for them, and re-layouts: 2.51 us -> none  [shards(): dedup_score = returned.reshape(devices * capacity)[slot]]
    unnamed x10 -> x12, local copies, waits for them, and re-layouts: 11.3 us -> 11.3 us
  transfers between devices with their start and end apart: 11 -> 11, of which waited for: 2 -> 3; matrix products, arithmetic and copies ran while one was open for 32% -> 27% of each run, Pallas kernels for 15% -> 0%
where the time goes in v18:
time: 163 us
  waiting for transfers between devices  42.6 us (26%)
  starting transfers between devices  32.7 us (20%)
  Pallas kernels  23.6 us (14%)
  local copies, waits for them, and re-layouts  22.7 us (14%)
  other arithmetic  21.7 us (13%)
  between operations  15.5 us (10%)
  matrix products  3.61 us (2%)
    ppermute x3, waiting for transfers between devices, shards(): lax.ppermute(embeddings, 'y', [(i, (i + s) % ny) for i in range(ny)])  30.2 us
    pallas_call x1, Pallas kernels, score_max(): pl.pallas_call(score_kernel, out_shape=jax.ShapeDtypeStruct((1, count), j...  23.6 us
    neg x1, other arithmetic, gumbel_noise(): return -jnp.log(-jnp.log(uniform))  12 us
    unnamed x12, local copies, waits for them, and re-layouts  11.3 us
    all_to_all x1, starting transfers between devices, shards(): lax.all_to_all(scores.reshape(devices, capacity), ALL, split_axis=0, conc...  9.73 us
    all_to_all x1, waiting for transfers between devices, shards(): lax.all_to_all(scores.reshape(devices, capacity), ALL, split_axis=0, conc...  7.6 us
    all_to_all x1, starting transfers between devices, shards(): lax.all_to_all(outgoing.reshape(devices, capacity, feature_dim + flag_wid...  7.56 us
    ppermute x3, starting transfers between devices, shards(): lax.ppermute(embeddings, 'y', [(i, (i + s) % ny) for i in range(ny)])  5.88 us
  transfers between devices with their start and end apart: 11, of which 3 were waited for; matrix products, arithmetic and copies ran while one was open for 27% of the time, Pallas kernels for 0%

profile of v18, /device:TPU:1, one launch (start us, length us, event | category | flops | bytes accessed | tf_op | source)
XLA Modules:
  0.0 162.6 jit_solution(844052180874677754)
XLA Ops:
  7.2 0.0 all-gather.2.cloned.1.call-start
  7.2 0.7 all-gather.2.cloned.1.call-update
  7.9 2.2 %collective-permute-start = (bf16[256,2048]{1,0:T(8,128)(2,1)}, bf16[256,2048]{1,0:T(8,128)(2,1)}, u32[]{:S(2)}, u32[]{:S(2)}) collective-permute-start(bf16[256,2048]{1,0:T(8,128)(2,1)} %param.4), channel_id=1, source_target_pairs={{0,32},{32,64},{64,96},{96,0},{1,33},{33,65},{65,97},{97,1},{2,34}... | collective-permute-start | bytes 3145736 | tf_op jit(solution)/shard_map/ppermute | solution.py:169
  10.1 2.6 %collective-permute-start.1 = (bf16[256,2048]{1,0:T(8,128)(2,1)}, bf16[256,2048]{1,0:T(8,128)(2,1)}, u32[]{:S(2)}, u32[]{:S(2)}) collective-permute-start(bf16[256,2048]{1,0:T(8,128)(2,1)} %param.4), channel_id=1, source_target_pairs={{0,64},{32,96},{64,0},{96,32},{1,65},{33,97},{65,1},{97,33},{2,66}... | collective-permute-start | bytes 3145736 | tf_op jit(solution)/shard_map/ppermute | solution.py:169
  12.7 1.1 collective-permute-start.2
  13.8 1.5 collective-permute-start.3
  15.3 0.9 convert_reduce_fusion
  16.3 0.7 compare_select_fusion
  16.9 3.6 %scatter_custom_fusion = bf16[512,2176]{1,0:T(8,128)(2,1)S(1)} fusion(s32[256]{0:T(256)S(1)} %bitcast.23, bf16[256,2048]{1,0:T(8,128)(2,1)} %param.4, bf16[]{:T(256)} %constant.193.clone.1, bf16[]{:T(256)} %constant.191.clone.1), kind=kCustom, calls=%fused_computation.26 | custom fusion | bytes 3276804 | tf_op jit(solution)/shard_map/scatter | solution.py:195
  20.6 2.1 %reshape.375 = bf16[128,4,2176]{2,1,0:T(4,128)(2,1)} reshape(bf16[512,2176]{1,0:T(8,128)(2,1)S(1)} %scatter_custom_fusion) | data formatting | bytes 4456448 | tf_op jit(solution)/shard_map/reshape | solution.py:197
  22.7 7.6 %all-to-all-start.1 = ((bf16[128,4,2176]{2,1,0:T(4,128)(2,1)}), bf16[128,4,2176]{2,1,0:T(4,128)(2,1)S(1)}, u32[]{:S(2)}, u32[]{:S(2)}) async-start(bf16[128,4,2176]{2,1,0:T(4,128)(2,1)} %reshape.375), calls=%async_computation.1 | async-start | bytes 4456448 | tf_op jit(solution)/shard_map/all_to_all | solution.py:196
  31.0 0.1 pad_add_fusion
  31.1 0.1 add_multiply_fusion
  31.1 0.1 multiply_bitcast_fusion
  31.2 0.0 copy-start
  31.2 0.0 copy-start.1
  31.2 12.0 %fusion.9.noise_ref = f32[2048,2048]{1,0:T(8,128)} fusion(s32[]{:T(128)} %bitcast.16, s32[2048]{0:T(1024)S(1)} %fusion.46, s32[2048]{0:T(1024)S(1)} %bitcast.18), kind=kLoop, calls=%fused_computation.14 | loop fusion | flops 67108864 | bytes 16793604 | tf_op jit(solution)/shard_map/neg | solution.py:30
  43.3 0.0 copy-done
  43.3 1.1 constant_dynamic-update-slice_fusion.7
  44.4 0.0 copy-done.1
  44.4 0.1 iota_compare_fusion.2
  44.6 0.0 collective-permute-done
  44.6 1.1 collective-permute-start.4
  45.7 30.2 %collective-permute-done.1 = bf16[256,2048]{1,0:T(8,128)(2,1)} collective-permute-done((bf16[256,2048]{1,0:T(8,128)(2,1)}, bf16[256,2048]{1,0:T(8,128)(2,1)}, u32[]{:S(2)}, u32[]{:S(2)}) %collective-permute-start.1) | collective-permute-done | bytes 1048608 | tf_op jit(solution)/shard_map/ppermute | solution.py:169
  76.0 2.7 %collective-permute-start.5 = (bf16[256,2048]{1,0:T(8,128)(2,1)}, bf16[256,2048]{1,0:T(8,128)(2,1)S(1)}, u32[]{:S(2)}, u32[]{:S(2)}) collective-permute-start(bf16[256,2048]{1,0:T(8,128)(2,1)} %collective-permute-done.1), channel_id=1, source_target_pairs={{0,1},{1,0},{2,3},{3,2},{4,5},{5,4},{6,7},{7,6},{8,9},{9,8},{10,11... | collective-permute-start | bytes 3145736 | tf_op jit(solution)/shard_map/ppermute | solution.py:172
  78.7 2.3 %constant_dynamic-update-slice_fusion.6 = bf16[2048,2048]{1,0:T(8,128)(2,1)} fusion(bf16[2048,2048]{1,0:T(8,128)(2,1)} %constant_dynamic-update-slice_fusion.7, bf16[256,2048]{1,0:T(8,128)(2,1)} %collective-permute-done), kind=kLoop, calls=%fused_computation.44 | loop fusion | bytes 2097152
  81.0 0.0 collective-permute-done.2
  81.0 0.0 collective-permute-start.6
  81.0 2.4 %constant_dynamic-update-slice_fusion.5 = bf16[2048,2048]{1,0:T(8,128)(2,1)} fusion(bf16[2048,2048]{1,0:T(8,128)(2,1)} %constant_dynamic-update-slice_fusion.6, bf16[256,2048]{1,0:T(8,128)(2,1)} %collective-permute-done.1), kind=kLoop, calls=%fused_computation.43 | loop fusion | bytes 2097152
  83.4 1.0 constant_dynamic-update-slice_fusion.4
  84.4 0.0 collective-permute-done.3
  84.4 2.4 %constant_dynamic-update-slice_fusion.3 = bf16[2048,2048]{1,0:T(8,128)(2,1)} fusion(bf16[2048,2048]{1,0:T(8,128)(2,1)} %constant_dynamic-update-slice_fusion.4, bf16[256,2048]{1,0:T(8,128)(2,1)} %collective-permute-done.3), kind=kLoop, calls=%fused_computation.41 | loop fusion | bytes 2097152
  86.8 0.0 collective-permute-done.4
  86.8 1.0 constant_dynamic-update-slice_fusion.2
  87.8 0.0 collective-permute-done.5
  87.8 1.0 constant_dynamic-update-slice_fusion.1
  88.9 0.0 collective-permute-done.6
  88.9 1.1 constant_dynamic-update-slice_fusion.rows_ref
  90.0 0.0 all-to-all-done.1
  90.0 2.1 %reshape.376 = bf16[512,2176]{1,0:T(8,128)(2,1)} reshape(bf16[128,4,2176]{2,1,0:T(4,128)(2,1)S(1)} %all-to-all-done.1) | data formatting | bytes 4456448 | tf_op jit(solution)/shard_map/reshape | solution.py:198
  92.1 1.1 compare_reduce_fusion
  93.1 0.2 fusion.33
  93.3 2.4 %fusion.11 = (f32[2048]{0:T(1024)S(1)}, f32[512]{0:T(512)S(1)}) fusion(pred[512]{0:T(512)(128)(4,1)S(1)} %compare_reduce_fusion, bf16[512,2176]{1,0:T(8,128)(2,1)} %reshape.376), kind=kLoop, calls=%fused_computation.18 | loop fusion | flops 5240320 | bytes 2107904 | tf_op jit(solution)/shard_map/reduce_sum | solution.py:153
  95.7 3.6 %fusion.26 = f32[512]{0:T(512)S(1)} fusion(bf16[512,2176]{1,0:T(8,128)(2,1)} %reshape.376, f32[512]{0:T(512)S(1)} %add_rsqrt_fusion, pred[512]{0:T(512)(128)(4,1)S(1)} %compare_reduce_fusion), kind=kOutput, calls=%fused_computation.25 | convolution fusion | flops 1075576320 | bytes 2103808 | tf_op jit(solution)/shard_map/dot_general | solution.py:145
  99.3 0.7 select_n.195
  100.1 9.7 %all-to-all-start.2 = ((f32[128,1,4]{2,1,0:T(1,128)}), f32[128,1,4]{2,1,0:T(1,128)S(1)}, u32[]{:S(2)}, u32[]{:S(2)}) async-start(f32[128,1,4]{2,1,0:T(1,128)} %bitcast.8), calls=%async_computation.2 | async-start | bytes 131072 | tf_op jit(solution)/shard_map/all_to_all | solution.py:202
  109.8 0.6 multiply_reduce_fusion
  111.1 0.6 broadcast_multiply_fusion
  111.7 7.6 %all-to-all-done.2 = f32[128,1,4]{2,1,0:T(1,128)S(1)} async-done(((f32[128,1,4]{2,1,0:T(1,128)}), f32[128,1,4]{2,1,0:T(1,128)S(1)}, u32[]{:S(2)}, u32[]{:S(2)}) %all-to-all-start.2) | async-done | bytes 2080 | tf_op jit(solution)/shard_map/all_to_all | solution.py:202
  119.3 0.1 copy.12
  119.3 0.2 select_reduce_fusion
  119.6 0.0 all-gather.2.cloned.1.call-done.cents_ref
  119.6 23.6 %shard_map.67 = f32[1,2048]{1,0:T(1,128)} custom-call(bf16[2048,2048]{1,0:T(8,128)(2,1)} %all-gather.2.cloned.1.call-done.cents_ref, bf16[2048,2048]{1,0:T(8,128)(2,1)} %constant_dynamic-update-slice_fusion.rows_ref, f32[2048,2048]{1,0:T(8,128)} %fusion.9.noise_ref), custom_call_target="tpu_custom_call" | custom-call | tf_op jit(solution)/shard_map/pallas_call | solution.py:125
  143.2 0.5 broadcast.596
  143.8 1.4 reduce.6
  145.1 0.6 gather_fusion
  145.7 0.1 bitcast_select_fusion
  145.8 0.6 copy.10
  146.4 4.1 %all-to-all-start = ((f32[8,1,256]{2,1,0:T(1,128)}), f32[8,1,256]{2,1,0:T(1,128)S(1)}, u32[]{:S(2)}, u32[]{:S(2)}) async-start(f32[8,1,256]{2,1,0:T(1,128)} %copy.10), calls=%async_computation | async-start | bytes 16384 | tf_op jit(solution)/shard_map/all_to_all | solution.py:186
  150.5 0.6 select_reduce_fusion.1
  151.1 4.1 %all-to-all-done = f32[8,1,256]{2,1,0:T(1,128)S(1)} async-done(((f32[8,1,256]{2,1,0:T(1,128)}), f32[8,1,256]{2,1,0:T(1,128)S(1)}, u32[]{:S(2)}, u32[]{:S(2)}) %all-to-all-start) | async-done | bytes 8224 | tf_op jit(solution)/shard_map/all_to_all | solution.py:186
  155.1 0.6 reduce_max.18
  (9 shorter events, 0.1 us)
Async XLA Ops:
  7.2 112.4 %all-gather.2.cloned.1.call-start = ((), (), s32[]{:S(2)}) async-start(), calls=%async_computation.3 | async-start | bytes 8912896 | tf_op jit(solution)/shard_map/all_gather | solution.py:173
  7.9 36.7 %collective-permute-start = (bf16[256,2048]{1,0:T(8,128)(2,1)}, bf16[256,2048]{1,0:T(8,128)(2,1)}, u32[]{:S(2)}, u32[]{:S(2)}) collective-permute-start(bf16[256,2048]{1,0:T(8,128)(2,1)} %param.4), channel_id=1, source_target_pairs={{0,32},{32,64},{64,96},{96,0},{1,33},{33,65},{65,97},{97,1},{2,34}... | collective-permute-start | bytes 3145736 | tf_op jit(solution)/shard_map/ppermute | solution.py:169
  10.1 65.9 %collective-permute-start.1 = (bf16[256,2048]{1,0:T(8,128)(2,1)}, bf16[256,2048]{1,0:T(8,128)(2,1)}, u32[]{:S(2)}, u32[]{:S(2)}) collective-permute-start(bf16[256,2048]{1,0:T(8,128)(2,1)} %param.4), channel_id=1, source_target_pairs={{0,64},{32,96},{64,0},{96,32},{1,65},{33,97},{65,1},{97,33},{2,66}... | collective-permute-start | bytes 3145736 | tf_op jit(solution)/shard_map/ppermute | solution.py:169
  12.7 68.3 %collective-permute-start.2 = (bf16[256,2048]{1,0:T(8,128)(2,1)}, bf16[256,2048]{1,0:T(8,128)(2,1)S(1)}, u32[]{:S(2)}, u32[]{:S(2)}) collective-permute-start(bf16[256,2048]{1,0:T(8,128)(2,1)} %param.4), channel_id=1, source_target_pairs={{0,96},{32,0},{64,32},{96,64},{1,97},{33,1},{65,33},{97,65},{2,98}... | collective-permute-start | bytes 3145736 | tf_op jit(solution)/shard_map/ppermute | solution.py:169
  13.8 70.6 %collective-permute-start.3 = (bf16[256,2048]{1,0:T(8,128)(2,1)}, bf16[256,2048]{1,0:T(8,128)(2,1)}, u32[]{:S(2)}, u32[]{:S(2)}) collective-permute-start(bf16[256,2048]{1,0:T(8,128)(2,1)} %param.4), channel_id=1, source_target_pairs={{0,1},{1,0},{2,3},{3,2},{4,5},{5,4},{6,7},{7,6},{8,9},{9,8},{10,11... | collective-permute-start | bytes 3145736 | tf_op jit(solution)/shard_map/ppermute | solution.py:172
  22.7 67.2 %all-to-all-start.1 = ((bf16[128,4,2176]{2,1,0:T(4,128)(2,1)}), bf16[128,4,2176]{2,1,0:T(4,128)(2,1)S(1)}, u32[]{:S(2)}, u32[]{:S(2)}) async-start(bf16[128,4,2176]{2,1,0:T(4,128)(2,1)} %reshape.375), calls=%async_computation.1 | async-start | bytes 4456448 | tf_op jit(solution)/shard_map/all_to_all | solution.py:196
  31.2 12.0 %copy-start = (bf16[256,2048]{1,0:T(8,128)(2,1)S(1)}, bf16[256,2048]{1,0:T(8,128)(2,1)}, u32[]{:S(2)}) copy-start(bf16[256,2048]{1,0:T(8,128)(2,1)} %param.4) | copy-start | bytes 3145732
  31.2 13.2 %copy-start.1 = (s32[256,1]{0,1:T(1,128)S(1)}, s32[256,1]{0,1:T(1,128)}, u32[]{:S(2)}) copy-start(s32[256,1]{0,1:T(1,128)} %param.6) | copy-start | bytes 3076
  44.6 42.2 %collective-permute-start.4 = (bf16[256,2048]{1,0:T(8,128)(2,1)}, bf16[256,2048]{1,0:T(8,128)(2,1)S(1)}, u32[]{:S(2)}, u32[]{:S(2)}) collective-permute-start(bf16[256,2048]{1,0:T(8,128)(2,1)} %collective-permute-done), channel_id=1, source_target_pairs={{0,1},{1,0},{2,3},{3,2},{4,5},{5,4},{6,7},{7,6},{8,9},{9,8},{10,11... | collective-permute-start | bytes 3145736 | tf_op jit(solution)/shard_map/ppermute | solution.py:172
  76.0 11.9 %collective-permute-start.5 = (bf16[256,2048]{1,0:T(8,128)(2,1)}, bf16[256,2048]{1,0:T(8,128)(2,1)S(1)}, u32[]{:S(2)}, u32[]{:S(2)}) collective-permute-start(bf16[256,2048]{1,0:T(8,128)(2,1)} %collective-permute-done.1), channel_id=1, source_target_pairs={{0,1},{1,0},{2,3},{3,2},{4,5},{5,4},{6,7},{7,6},{8,9},{9,8},{10,11... | collective-permute-start | bytes 3145736 | tf_op jit(solution)/shard_map/ppermute | solution.py:172
  81.0 7.9 %collective-permute-start.6 = (bf16[256,2048]{1,0:T(8,128)(2,1)S(1)}, bf16[256,2048]{1,0:T(8,128)(2,1)S(1)}, u32[]{:S(2)}, u32[]{:S(2)}) collective-permute-start(bf16[256,2048]{1,0:T(8,128)(2,1)S(1)} %collective-permute-done.2), channel_id=1, source_target_pairs={{0,1},{1,0},{2,3},{3,2},{4,5},{5,4},{6,7},{7,6},{8,9},{9,8},{10,11... | collective-permute-start | bytes 3145736 | tf_op jit(solution)/shard_map/ppermute | solution.py:172
  100.1 19.2 %all-to-all-start.2 = ((f32[128,1,4]{2,1,0:T(1,128)}), f32[128,1,4]{2,1,0:T(1,128)S(1)}, u32[]{:S(2)}, u32[]{:S(2)}) async-start(f32[128,1,4]{2,1,0:T(1,128)} %bitcast.8), calls=%async_computation.2 | async-start | bytes 131072 | tf_op jit(solution)/shard_map/all_to_all | solution.py:202
  146.4 8.7 %all-to-all-start = ((f32[8,1,256]{2,1,0:T(1,128)}), f32[8,1,256]{2,1,0:T(1,128)S(1)}, u32[]{:S(2)}, u32[]{:S(2)}) async-start(f32[8,1,256]{2,1,0:T(1,128)} %copy.10), calls=%async_computation | async-start | bytes 16384 | tf_op jit(solution)/shard_map/all_to_all | solution.py:186
Sparse Core Ops, SparseCore 0:
  10.1 90.6 all-gather.1
